TPU v7x, 32 devices: a whole 2x2x4 slice. The times are simulated.
32 devices in a mesh: groups: 2 (over y), rows: 4 (over z), cols: 2 (over x), sub: 2 (over core).
Axes of the slice: x: 2, y: 2, z: 4, core: 2. Of those that a mesh axis runs over, the one named last changes fastest.
Arguments:
- tile_index: int32 [64, 2], P(('groups', 'rows', 'cols', 'sub')), parts along dimension 0, may hold values from 0 to 7, as said below
- tile_values: bfloat16 [64, 256, 256], P(('groups', 'rows', 'cols', 'sub')), parts along dimension 0, may hold values from -0.125 to 0.125
- onsite_energy: float32 [4096], P(('groups', 'rows', 'cols')), parts along dimension 0, may hold values from 0.5 to 4
- start_block: float32 [4096, 64], P(('groups', 'rows', 'cols')), parts along dimension 0, may hold values from -6 to 6
- previous_block: float32 [4096, 64], P(('groups', 'rows', 'cols')), parts along dimension 0, may hold values from -6 to 6
- previous_coupling: float32 [128, 64], P('groups'), parts along dimension 0, may hold values from -0.6 to 0.6
- stored_basis: float32 [8, 4096, 64], P('sub', ('groups', 'rows', 'cols')), parts along dimension 1, may hold values from -6 to 6
Outputs:
- new_blocks: float32 [1, 4096, 64], P(None, ('groups', 'rows', 'cols')), parts along dimension 1
- diagonal_blocks: float32 [1, 128, 64], P(None, 'groups'), parts along dimension 1
- coupling_blocks: float32 [1, 128, 64], P(None, 'groups'), parts along dimension 1
There are 2 independent parts, one for each index of `groups`. A program takes and returns all parts, laid end to end along the dimension named above; each array names one. Nothing has to cross between parts.
Inputs may be any that keep to these rules, and one draw needn't show every extreme that they name: `tile_index`: tile rows of a device's tiles lie in the rows of the operator that the device's index of rows and cols holds; tile columns lie in the rows held by some index of rows with the same index of cols. Tiles may repeat.
All inputs are finite; a program needn't handle non-finite values.
Results may differ from a plain program's by a relative error of at most 0.0019.
Values may be sent and summed in bfloat16 or wider, within the bound.
No kernel may reach another device: no remote copies, remote signals or barrier semaphores. Data moves between devices by JAX's collectives and lax.ppermute only.
A program may use at most 64 MiB of HBM per device.

v0:
```python
import jax
import jax.numpy as jnp
from jax import lax
from jax.sharding import PartitionSpec as P

BLOCK = 64
TILE = 256


highest = lax.Precision.HIGHEST


def apply_operator(tile_index, tile_values, onsite_energy, current):
    local_rows = current.shape[0]
    tile_rows = local_rows // TILE
    band_count = lax.axis_size("rows")
    column_count = lax.axis_size("cols")
    narrow = current.astype(jnp.bfloat16)
    own_tiles = narrow.reshape(tile_rows, TILE, BLOCK)
    local_row = tile_index[:, 0] % tile_rows
    column = tile_index[:, 1]
    source = column // tile_rows // column_count * tile_rows + column % tile_rows
    gathered = lax.all_gather(own_tiles, "rows", axis=0, tiled=True)
    pulled = jnp.einsum(
        "kab,kbn->kan", tile_values, gathered[source], preferred_element_type=jnp.float32
    )
    pushed = jnp.einsum(
        "kab,kan->kbn", tile_values, own_tiles[local_row], preferred_element_type=jnp.float32
    )
    slot_count = band_count * tile_rows
    slot_range = jnp.arange(slot_count, dtype=jnp.int32)
    push_onehot = (source[None, :] == slot_range[:, None]).astype(jnp.float32)
    terms = jnp.einsum("sk,kbn->sbn", push_onehot, pushed, precision=highest)
    received = lax.psum_scatter(terms, "rows", scatter_dimension=0, tiled=True)
    row_onehot = (local_row[None, :] == jnp.arange(tile_rows, dtype=jnp.int32)[:, None]).astype(
        jnp.float32
    )
    partial_total = received + jnp.einsum("tk,kan->tan", row_onehot, pulled, precision=highest)
    total = lax.psum(partial_total, "sub")
    return total.reshape(local_rows, BLOCK) + onsite_energy[:, None] * current


def local(
    tile_index,
    tile_values,
    onsite_energy,
    start_block,
    previous_block,
    previous_coupling,
    stored_basis,
):
    local_rows = start_block.shape[0]
    total_rows = local_rows * lax.axis_size("rows") * lax.axis_size("cols")
    coupling = jnp.triu(previous_coupling)
    correlation_local = jnp.einsum("kib,ic->kbc", stored_basis, start_block, precision=highest)
    correlation = lax.psum(correlation_local, ("rows", "cols")) / total_rows
    images = apply_operator(tile_index, tile_values, onsite_energy, start_block)
    images = images - jnp.dot(previous_block, coupling.T, precision=highest)
    diagonal_local = jnp.dot(start_block.T, images, precision=highest)
    stored_local = jnp.einsum("kib,ic->kbc", stored_basis, images, precision=highest)
    raw_diagonal, raw_stored = lax.psum((diagonal_local, stored_local), ("rows", "cols"))
    diagonal = raw_diagonal / total_rows
    projection = raw_stored / total_rows - jnp.einsum(
        "kbc,cd->kbd", correlation, diagonal, precision=highest
    )
    images = images - jnp.dot(start_block, diagonal, precision=highest)
    removal_local = jnp.einsum("kib,kbc->ic", stored_basis, projection, precision=highest)
    removal = lax.psum(removal_local, "sub")
    images = images - removal
    gram_local = jnp.dot(images.T, images, precision=highest)
    gram = lax.psum(gram_local, ("rows", "cols")) / total_rows
    lower_factor = jnp.linalg.cholesky(gram)
    following = lax.linalg.triangular_solve(
        lower_factor, images, left_side=False, lower=True, transpose_a=True
    )
    new_list = [following]
    diagonal_list = [diagonal]
    coupling_list = [lower_factor.T]
    return (jnp.stack(new_list), jnp.stack(diagonal_list), jnp.stack(coupling_list))


def solution(mesh):
    return jax.shard_map(
        local,
        mesh=mesh,
        in_specs=(
            P(("groups", "rows", "cols", "sub"), None),
            P(("groups", "rows", "cols", "sub"), None, None),
            P(("groups", "rows", "cols")),
            P(("groups", "rows", "cols"), None),
            P(("groups", "rows", "cols"), None),
            P("groups", None),
            P("sub", ("groups", "rows", "cols"), None),
        ),
        out_specs=(
            P(None, ("groups", "rows", "cols"), None),
            P(None, "groups", None),
            P(None, "groups", None),
        ),
        check_vma=False,
    )
```

profile of v0, /device:TPU:0, one launch (start us, length us, event | category | flops | bytes accessed | tf_op | source)
XLA Modules:
  0.0 217.6 jit_solution(17785886655713540770)
XLA Ops:
  7.2 0.9 convert_element_type.2
  8.1 0.9 fusion.27
  9.0 0.2 fusion.15
  9.2 0.5 fusion.5
  9.7 0.8 copy.31
  10.6 15.6 %all-gather = bf16[1024,64]{0,1:T(8,128)(2,1)S(1)} all-gather(bf16[256,64]{0,1:T(8,128)(2,1)S(1)} %convert_element_type.2), channel_id=2, replica_groups=mesh['groups'=2,'rows'=4,'cols'=2,'sub'=2] {'rows'}, dimensions={0}, use_global_device_ids=true | all-gather | bytes 163840 | tf_op jit(solution)/shard_map/all_gather | solution.py:23
  26.2 0.6 gather_fusion
  26.8 0.2 convolution_bitcast_fusion.1
  27.0 9.0 %fusion.3 = f32[1,256,64]{0,1,2:T(8,128)} fusion(f32[2,256,64]{1,2,0:T(8,128)S(1)} %convolution_bitcast_fusion.1), kind=kOutput, calls=%fused_computation.13 | convolution fusion | flops 393216 | bytes 196608 | tf_op jit(solution)/shard_map/tk,kan->tan/dot_general | solution.py:38
  36.0 5.2 %copy.42 = f32[1,256,64]{1,2,0:T(8,128)S(1)} copy(f32[1,256,64]{0,1,2:T(8,128)} %fusion.3) | data formatting | bytes 131072 | tf_op jit(solution)/shard_map/tk,kan->tan/dot_general | solution.py:38
  41.2 1.2 fusion.8
  42.4 1.5 add_bitcast_fusion
  43.9 18.8 %all-reduce.5.cloned.1.call-done = f32[256,64]{0,1:T(8,128)} async-done(((f32[256,64]{0,1:T(8,128)}), f32[256,64]{0,1:T(8,128)}) %all-reduce.5.cloned.1.call-update) | async-done | bytes 65552 | tf_op jit(solution)/shard_map/psum | solution.py:39
  62.8 1.1 fusion.2
  63.9 1.2 convolution_bitcast_fusion
  65.1 0.2 convolution_bitcast_fusion.6
  65.3 37.4 %psum.43 = f32[64,64]{0,1:T(8,128)S(1)} all-reduce(f32[64,64]{0,1:T(8,128)S(1)} %convolution_bitcast_fusion.6), channel_id=1, replica_groups=mesh['groups'=2,'rows'=4,'cols'=2,'sub'=2] {'rows','cols'}, use_global_device_ids=true, to_apply=%region_2.3 | all-reduce | flops 4096 | bytes 32768 | tf_op jit(solution)/shard_map/psum | solution.py:61
  102.7 36.2 %all-reduce.9.cloned.1.call-done = (f32[4,64,64]{1,2,0:T(8,128)}, f32[4,64,64]{1,2,0:T(8,128)}) async-done(((f32[4,64,64]{1,2,0:T(8,128)}, f32[4,64,64]{1,2,0:T(8,128)}), (f32[4,64,64]{1,2,0:T(8,128)}, f32[4,64,64]{1,2,0:T(8,128)})) %all-reduce.9.cloned.1.call-update) | async-done | bytes 131088 | tf_op jit(solution)/shard_map/psum | solution.py:56
  138.9 1.2 convolution_subtract_fusion
  140.1 0.9 convolution_bitcast_fusion.5
  141.1 0.7 copy.39
  141.8 16.8 %all-reduce.7.cloned.1.call-done = f32[256,64]{0,1:T(8,128)} async-done(((f32[256,64]{0,1:T(8,128)}), f32[256,64]{0,1:T(8,128)}) %all-reduce.7.cloned.1.call-update) | async-done | bytes 65552 | tf_op jit(solution)/shard_map/psum | solution.py:68
  158.6 1.0 fusion.1
  159.7 0.2 fusion.35
  159.9 37.4 %psum.47 = f32[64,64]{0,1:T(8,128)S(1)} all-reduce(f32[64,64]{0,1:T(8,128)S(1)} %fusion.35), channel_id=1, replica_groups=mesh['groups'=2,'rows'=4,'cols'=2,'sub'=2] {'rows','cols'}, use_global_device_ids=true, to_apply=%region_6.7 | all-reduce | flops 4096 | bytes 32768 | tf_op jit(solution)/shard_map/psum | solution.py:71
  197.3 0.1 copy.38
  197.4 5.8 %cholesky.15 = f32[64,64]{1,0:T(8,128)S(1)} custom-call(f32[64,64]{1,0:T(8,128)S(1)} %fusion.13), custom_call_target="Cholesky" | custom-call | tf_op jit(solution)/shard_map/jit(cholesky)/cholesky | solution.py:72
  203.3 0.6 compare_reduce_fusion
  203.9 0.7 fusion.20
  204.6 4.9 %custom-call.6 = f32[1,64,64]{1,2,0:T(8,128)S(1)} custom-call(f32[1,64,64]{2,1,0:T(8,128)S(1)} %get-tuple-element.20), custom_call_target="InvertDiagBlocksLowerTriangular" | custom-call | tf_op jit(solution)/shard_map/triangular_solve | solution.py:73
  209.5 0.9 convolution_bitcast_fusion.2
  210.4 0.7 copy.40
  (29 shorter events, 0.4 us)
Async XLA Ops:
  7.2 1.9 copy-start
  7.2 35.2 %reduce-scatter.2.cloned.1.call-start = ((), (), s32[]{:S(2)}) async-start(), calls=%async_computation.1 | async-start | bytes 327680 | tf_op jit(solution)/shard_map/reduce_scatter | solution.py:34
  10.5 52.2 %all-reduce.5.cloned.1.call-start = ((), (), s32[]{:S(2)}) async-start(), calls=%async_computation.2 | async-start | bytes 131072 | tf_op jit(solution)/shard_map/psum | solution.py:39
  27.0 14.2 %copy-start.1 = (f32[4,256,64]{1,2,0:T(8,128)S(1)}, f32[4,256,64]{1,2,0:T(8,128)}, u32[]{:S(2)}) copy-start(f32[4,256,64]{1,2,0:T(8,128)} %param.13) | copy-start | bytes 786436
  27.0 14.2 %copy-start.2 = (f32[256,64]{0,1:T(8,128)S(1)}, f32[256,64]{0,1:T(8,128)}, u32[]{:S(2)}) copy-start(f32[256,64]{0,1:T(8,128)} %param.10) | copy-start | bytes 196612
  27.0 35.8 %copy-start.3 = (f32[256,64]{0,1:T(8,128)S(1)}, f32[256,64]{0,1:T(8,128)}, u32[]{:S(2)}) copy-start(f32[256,64]{0,1:T(8,128)} %param.11) | copy-start | bytes 196612
  27.0 35.7 %copy-start.4 = (f32[64,64]{1,0:T(8,128)S(1)}, f32[64,64]{1,0:T(8,128)}, u32[]{:S(2)}) copy-start(f32[64,64]{1,0:T(8,128)} %param.12) | copy-start | bytes 49156
  27.0 35.7 %copy-start.5 = (f32[256]{0:T(256)S(1)}, f32[256]{0:T(256)}, u32[]{:S(2)}) copy-start(f32[256]{0:T(256)} %param.9) | copy-start | bytes 3076
  43.9 95.0 %all-reduce.9.cloned.1.call-start = ((), (), s32[]{:S(2)}) async-start(), calls=%async_computation.4 | async-start | bytes 524288 | tf_op jit(solution)/shard_map/psum | solution.py:56
  65.0 93.6 %all-reduce.7.cloned.1.call-start = ((), (), s32[]{:S(2)}) async-start(), calls=%async_computation.3 | async-start | bytes 131072 | tf_op jit(solution)/shard_map/psum | solution.py:68
Sparse Core Ops, SparseCore 0:
  10.6 22.8 reduce-scatter.1
  44.0 18.7 all-reduce.4
  66.2 72.6 all-reduce.8
  141.6 16.9 all-reduce.6
where the time goes:
time: 218 us
  blocking collectives  90.4 us (41%)
  waiting for transfers between devices  71.9 us (33%)
  matrix products  17.8 us (8%)
  other arithmetic  15.4 us (7%)
  between operations  13.9 us (6%)
  local copies, waits for them, and re-layouts  8.02 us (4%)
    psum x1, blocking collectives, local(): gram = lax.psum(gram_local, ('rows', 'cols')) / total_rows  37.4 us
    psum x1, blocking collectives, local(): lax.psum((diagonal_local, stored_local), ('rows', 'cols'))  37.4 us
    psum x1, waiting for transfers between devices, local(): correlation = lax.psum(correlation_local, ('rows', 'cols')) / total_rows  36.2 us
    psum x1, waiting for transfers between devices, apply_operator(): total = lax.psum(partial_total, 'sub')  18.8 us
    psum x1, waiting for transfers between devices, local(): removal = lax.psum(removal_local, 'sub')  16.8 us
    all_gather x1, blocking collectives, apply_operator(): gathered = lax.all_gather(own_tiles, 'rows', axis=0, tiled=True)  15.6 us
    dot_general x1, matrix products, apply_operator(): jnp.einsum('tk,kan->tan', row_onehot, pulled, precision=highest)  8.95 us
    another operation x3, other arithmetic, local(): lower_factor = jnp.linalg.cholesky(gram)  6.52 us
  transfers between devices with their start and end apart: 4, of which 3 were waited for; matrix products, arithmetic and copies ran while one was open for 8% of the time, Pallas kernels for 0%

commit v1 on v0

v1 whole, which is shorter than its diff:
```python
import functools

import jax
import jax.numpy as jnp
from jax import lax
from jax.experimental import pallas as pl
from jax.experimental.pallas import tpu as pltpu
from jax.sharding import PartitionSpec as P

f32 = jnp.float32
bf16 = jnp.bfloat16
GROUP = 16
HIGHEST = lax.Precision.HIGHEST
GRANT = 16 * 1024 * 1024
NN = (((1,), (0,)), ((), ()))
NT = (((1,), (1,)), ((), ()))


def split(x):
    high = x.astype(bf16)
    return high, (x - high.astype(f32)).astype(bf16)


def dot_bf16(a, b, dims):
    return lax.dot_general(a, b, dims, preferred_element_type=f32)


def dot_split(a, b, dims):
    (ah, al), (bh, bl) = a, b
    return dot_bf16(ah, bh, dims) + dot_bf16(ah, bl, dims) + dot_bf16(al, bh, dims)


def dot_exact(a, b, dims):
    return lax.dot_general(a, b, dims, precision=HIGHEST, preferred_element_type=f32)


def fold(x, parts):
    rows = x.shape[0] // parts
    return jnp.concatenate([x[i * rows : (i + 1) * rows] for i in range(parts)], axis=1)


def unfold(x, parts):
    lanes = x.shape[1] // parts
    return jnp.concatenate([x[:, i * lanes : (i + 1) * lanes] for i in range(parts)], axis=0)


def call(kernel, outs, ins, scratch=(), work=40000000):
    spaces = {"v": pltpu.VMEM, "h": pltpu.HBM}
    return pl.pallas_call(
        kernel,
        out_shape=[jax.ShapeDtypeStruct(s, d) for s, d in outs],
        in_specs=[pl.BlockSpec(memory_space=spaces[c]) for c in ins],
        out_specs=[pl.BlockSpec(memory_space=pltpu.VMEM)] * len(outs),
        scratch_shapes=list(scratch),
        cost_estimate=pl.CostEstimate(flops=work, bytes_accessed=1000000, transcendentals=0),
        compiler_params=pltpu.CompilerParams(vmem_limit_bytes=GRANT),
    )


def prepare_kernel(
    x_hbm, e_hbm, p_hbm, c_hbm, s_hbm, t_hbm, i_hbm,
    base_ref, corr_ref, x_ref, xs_ref, ss_ref, t_ref, i_ref,
    e_ref, p_ref, c_ref, s_ref, sems,
):
    pairs = (
        (s_hbm, s_ref), (x_hbm, x_ref), (p_hbm, p_ref), (c_hbm, c_ref),
        (e_hbm, e_ref), (t_hbm, t_ref), (i_hbm, i_ref),
    )
    copies = [pltpu.make_async_copy(a, b, sems.at[k]) for k, (a, b) in enumerate(pairs)]
    for copy in copies:
        copy.start()
    for copy in copies[:5]:
        copy.wait()
    block = x_ref.shape[0]
    row = lax.broadcasted_iota(jnp.int32, (block, block), 0)
    column = lax.broadcasted_iota(jnp.int32, (block, block), 1)
    coupling = jnp.where(row <= column, c_ref[...], 0.0)
    x = x_ref[...]
    xs = split(x)
    ss = split(s_ref[...])
    for half in range(2):
        xs_ref[half] = xs[half]
        ss_ref[half] = ss[half]
    base_ref[...] = e_ref[...] * x - dot_split(split(coupling), split(p_ref[...]), NN)
    corr = dot_split(xs, ss, NT)
    chunk = corr_ref.shape[1]
    for band in range(corr_ref.shape[0]):
        corr_ref[band] = corr[band * chunk : (band + 1) * chunk]
    for copy in copies[5:]:
        copy.wait()


def tile_columns(index_refs, shape):
    found = []
    for ref in index_refs:
        index = ref[...]
        for k in range(ref.shape[0]):
            found.append(jnp.broadcast_to(index[k : k + 1, 1:2], shape))
    return found


def target_band(me, core, pair):
    return jnp.bitwise_xor(me, jnp.where(core == 0, pair[0], pair[1]))


def push_kernel(pairs, columns, i_ref, j_ref, xs_ref, corr_ref, t_ref, u_ref, *outs):
    block, rows = xs_ref.shape[1:]
    x = xs_ref[0]
    me, core = lax.axis_index("rows"), lax.axis_index("sub")
    targets = tile_columns((i_ref, j_ref), (block, rows))
    products = [dot_bf16(x, ref[k], NN) for ref in (t_ref, u_ref) for k in range(ref.shape[0])]

    def pushed(band):
        first = band * columns
        total = jnp.zeros((block, rows), f32)
        for target, product in zip(targets, products):
            inside = (target >= first) & (target < first + columns)
            total = total + jnp.where(inside, product, 0.0)
        return total

    parity = jnp.bitwise_and(me, 1)
    outs[0][...] = jnp.concatenate([pushed(me), corr_ref[parity]], axis=0)
    for ref, pair in zip(outs[1:], pairs):
        message = jnp.concatenate([x.astype(f32), pushed(target_band(me, core, pair))], axis=0)
        if pair[0] != pair[1]:
            ref[...] = message.astype(bf16)
        else:
            message = jnp.where(core == 0, message[:, : rows // 2], message[:, rows // 2 :])
            halves = [unfold(h.astype(f32), 2) for h in split(corr_ref[1 - parity])]
            ref[...] = jnp.concatenate([message, *halves], axis=0).astype(bf16)


def image_kernel(pairs, columns, parts, i_ref, j_ref, base_ref, xs_ref, ss_ref, t_ref, u_ref, own_ref, *refs):
    received, (y_ref, send_ref) = refs[:-2], refs[-2:]
    block, rows = base_ref.shape
    xs = (xs_ref[0], xs_ref[1])
    me, core = lax.axis_index("rows"), lax.axis_index("sub")
    y = base_ref[...] + own_ref[0:block]
    corr = own_ref[block:]
    blocks = [(me, xs[0].astype(f32))]
    for k, pair in enumerate(pairs):
        mine, other = received[2 * k][...].astype(f32), received[2 * k + 1][...].astype(f32)
        if pair[0] != pair[1]:
            found = [(target_band(me, core, pair), mine), (target_band(me, core, pair[::-1]), other)]
        else:
            parts_of = mine[2 * block :]
            count = parts_of.shape[0] // 2
            corr = corr + fold(parts_of[:count] + parts_of[count:], 2)
            mine, other = mine[: 2 * block], other[: 2 * block]
            first, second = jnp.where(core == 0, mine, other), jnp.where(core == 0, other, mine)
            found = [(jnp.bitwise_xor(me, pair[0]), jnp.concatenate([first, second], axis=1))]
        for band, message in found:
            blocks.append((band, message[0:block]))
            y = y + message[block:]
    tiles = [ref[k] for ref in (t_ref, u_ref) for k in range(ref.shape[0])]
    for target, tile in zip(tile_columns((i_ref, j_ref), (block, rows)), tiles):
        source = jnp.zeros((block, rows), f32)
        for band, held in blocks:
            first = band * columns
            inside = (target >= first) & (target < first + columns)
            source = jnp.where(inside, held, source)
        y = y + dot_bf16(source.astype(bf16), tile, NT)
    y_ref[...] = y
    halves = split(y)
    stored = dot_split(halves, (ss_ref[0], ss_ref[1]), NT)
    diagonal = fold(dot_split(halves, xs, NT), parts)
    middle = diagonal.shape[0] // 2
    diagonal = jnp.where(core == 0, diagonal[:middle], diagonal[middle:])
    send_ref[...] = jnp.concatenate([stored, diagonal, corr], axis=0)


def combine_kernel(block, small, mine_ref, other_ref, total_ref, send_ref):
    total = mine_ref[...] + other_ref[...]
    total_ref[...] = total
    high, low = split(total[block : block + small])
    message = [total[0:block], high.astype(f32), low.astype(f32), total[block + small :]]
    send_ref[...] = jnp.concatenate(message, axis=0).astype(bf16)


def project_kernel(steps, block, small, total_rows, total_ref, ss_ref, *refs):
    received, out_ref = refs[:-1], refs[-1]
    me, core = lax.axis_index("rows"), lax.axis_index("sub")
    total = total_ref[...]
    stored, diagonal = total[0:block], total[block : block + small]
    same, other = total[block + small :], jnp.zeros((block // 2, total.shape[1]), f32)
    for step, ref in zip(steps, received):
        message = ref[...].astype(f32)
        stored = stored + message[0:block]
        diagonal = diagonal + message[block : block + small]
        diagonal = diagonal + message[block + small : block + 2 * small]
        part = message[block + 2 * small :]
        if step % 2:
            other = other + part
        else:
            same = same + part
    even = jnp.bitwise_and(me, 1) == 0
    first, second = jnp.where(even, same, other), jnp.where(even, other, same)
    scale = 1.0 / total_rows
    weights = jnp.concatenate([stored, first, second], axis=0) * scale
    out_ref[0 : 2 * block, :] = dot_split(split(weights), (ss_ref[0], ss_ref[1]), NN)
    out_ref[2 * block : 2 * block + small, :] = jnp.where(core == 0, diagonal * scale, 0.0)
    out_ref[2 * block + small :, :] = jnp.where(core == 0, 0.0, diagonal * scale)


def gram_kernel(parts, mine_ref, other_ref, x_ref, y_ref, images_ref, send_ref, diagonal_ref):
    block = x_ref.shape[0]
    both = mine_ref[...] + other_ref[...]
    diagonal = unfold(both[2 * block :], parts)
    reduced = x_ref[...] - both[block : 2 * block]
    images = y_ref[...] - both[0:block] - dot_split(split(diagonal), split(reduced), NN)
    images_ref[...] = images
    diagonal_ref[...] = diagonal
    message = fold(dot_exact(images, images, NT), 2)
    for device in range(send_ref.shape[0]):
        send_ref[device] = message


def factor_kernel(total_rows, got_ref, images_ref, d_ref, following_ref, coupling_ref, diagonal_ref):
    block = images_ref.shape[0]
    half, lanes = block // 2, 2 * block
    gram = got_ref[0]
    for device in range(1, got_ref.shape[0]):
        gram = gram + got_ref[device]
    gram = gram * (1.0 / total_rows)
    row = lax.broadcasted_iota(jnp.int32, (block, lanes), 0)
    column = lax.broadcasted_iota(jnp.int32, (block, lanes), 1)
    left = column < block
    m = jnp.concatenate([gram, pltpu.roll(gram, block, 1)], axis=0)
    m = jnp.where(left, m, jnp.where(column == row + block, 1.0, 0.0))
    finished = []
    for start in range(0, block, GROUP):
        spread = [
            jnp.broadcast_to(m[:, start + p : start + p + 1], m.shape) for p in range(GROUP)
        ]
        for p in range(GROUP):
            at = p % 8
            root = lax.rsqrt(spread[p][at : at + 1])
            lower = spread[p] * root
            done = m[at : at + 1] * root
            finished.append(done)
            for q in range(p + 1, GROUP):
                pivot = q - p + at
                spread[q] = spread[q] - lower * lower[pivot : pivot + 1]
            m = m - lower * done
            if at == 7:
                m = m[8:]
                spread = [column[8:] for column in spread]
    done = jnp.concatenate(finished, axis=0)
    coupling_ref[...] = jnp.where((row <= column) & left, done, 0.0)[:, 0:block]
    inverse = jnp.where((row + block >= column) & ~left, done, 0.0)
    images = images_ref[...]
    following_ref[...] = dot_exact(inverse, jnp.concatenate([images, images], axis=0), NN)
    diagonal_ref[...] = d_ref[...].T


def exchange(x, axis, distance):
    return lax.ppermute(x, axis, [(i, i ^ distance) for i in range(lax.axis_size(axis))])


def local(
    tile_index,
    tile_values,
    onsite_energy,
    start_block,
    previous_block,
    previous_coupling,
    stored_basis,
):
    rows, block = start_block.shape
    bands, columns = lax.axis_size("rows"), lax.axis_size("cols")
    cores = lax.axis_size("sub")
    stored = stored_basis.shape[0]
    width = stored * block
    total_rows = rows * bands * columns
    peers = bands * columns
    parts = width // block
    chunk = block // 2
    assert rows == tile_values.shape[1] and cores == 2 and width == rows
    assert bands > 1 and columns > 1 and bands & (bands - 1) == 0 and columns & (columns - 1) == 0
    half = (block, rows)
    swap = [(0, 1), (1, 0)]
    other_tiles = lax.ppermute(tile_values, "sub", swap)
    other_index = lax.ppermute(tile_index, "sub", swap)
    base, corr, x, xs, ss, tiles, index = call(
        prepare_kernel,
        [
            (half, f32), ((2, chunk, width), f32), (half, f32), ((2,) + half, bf16),
            ((2, width, rows), bf16), (tile_values.shape, bf16), (tile_index.shape, jnp.int32),
        ],
        "hhhhhhh",
        [
            pltpu.VMEM((1, rows), f32), pltpu.VMEM(half, f32), pltpu.VMEM((block, block), f32),
            pltpu.VMEM((width, rows), f32), pltpu.SemaphoreType.DMA((7,)),
        ],
    )(
        *(
            pltpu.with_memory_space_constraint(a, pltpu.HBM)
            for a in (
                start_block.T, onsite_energy.reshape(1, rows), previous_block.T, previous_coupling,
                stored_basis.transpose(0, 2, 1).reshape(width, rows), tile_values, tile_index,
            )
        )
    )
    pairs = [(step, step - 1) for step in range(bands - 1, 1, -2)] + [(1, 1)]
    sends = call(
        functools.partial(push_kernel, pairs, columns),
        [((block + chunk, rows), f32)]
        + [((2 * block, rows) if a != b else (4 * block, rows // 2), bf16) for a, b in pairs],
        "vvvvvv",
    )(index, other_index, xs, corr, tiles, other_tiles)
    received = []
    for send, pair in zip(sends[1:], pairs):
        moves = [(2 * r + c, 2 * (r ^ pair[c]) + c) for r in range(bands) for c in range(2)]
        received.append(lax.ppermute(send, ("rows", "sub"), moves))
    received = [y for x in received for y in (x, lax.ppermute(x, "sub", swap))]
    small = block // parts // 2
    y, mine = call(
        functools.partial(image_kernel, pairs, columns, parts),
        [(half, f32), ((block + small + chunk, rows), f32)],
        "v" * (8 + len(received)),
    )(index, other_index, base, xs, ss, tiles, other_tiles, sends[0], *received)
    distances = [2**k for k in range(columns.bit_length() - 1)]
    for distance in distances[:-1]:
        mine = mine + exchange(mine, "cols", distance)
    total, send = call(
        functools.partial(combine_kernel, block, small),
        [(mine.shape, f32), ((block + 2 * small + chunk, rows), bf16)],
        "vv",
    )(mine, exchange(mine, "cols", distances[-1]))
    steps = [*range(2, bands), 1]
    (mine,) = call(
        functools.partial(project_kernel, steps, block, small, total_rows),
        [((2 * block + 2 * small, rows), f32)],
        "v" * (1 + bands),
    )(total, ss, *(exchange(send, "rows", step) for step in steps))
    other = lax.ppermute(mine, "sub", swap)
    images, send, diagonal = call(
        functools.partial(gram_kernel, parts),
        [(half, f32), ((peers, block // 2, 2 * block), f32), ((block, block), f32)],
        "vvvv",
    )(mine, other, x, y)
    got = lax.all_to_all(send, ("rows", "cols"), 0, 0, tiled=True)
    following, coupling, diagonal = call(
        functools.partial(factor_kernel, total_rows),
        [(half, f32), ((block, block), f32), ((block, block), f32)],
        "vvv",
    )(got, images, diagonal)
    return following.T[None], diagonal[None], coupling[None]


def solution(mesh):
    return jax.shard_map(
        local,
        mesh=mesh,
        in_specs=(
            P(("groups", "rows", "cols", "sub"), None),
            P(("groups", "rows", "cols", "sub"), None, None),
            P(("groups", "rows", "cols")),
            P(("groups", "rows", "cols"), None),
            P(("groups", "rows", "cols"), None),
            P("groups", None),
            P("sub", ("groups", "rows", "cols"), None),
        ),
        out_specs=(
            P(None, ("groups", "rows", "cols"), None),
            P(None, "groups", None),
            P(None, "groups", None),
        ),
        check_vma=False,
    )
```

time: 218 us -> 44.1 us (0.20)
  blocking collectives: 90.4 us -> 11.4 us
  waiting for transfers between devices: 71.9 us -> 15.7 us
  matrix products: 17.8 us -> 0 us
  other arithmetic: 15.4 us -> 0 us
  between operations: 13.9 us -> 0.69 us
  starting transfers between devices: 0.16 us -> 10.9 us
  local copies, waits for them, and re-layouts: 8.02 us -> 0 us
  Pallas kernels: 0 us -> 5.11 us
    psum x2 -> x0, blocking collectives: 74.8 us -> none  [the longest x1 37.4 us: local(): gram = lax.psum(gram_local, ('rows', 'cols')) / total_rows]
    psum x3 -> x0, waiting for transfers between devices: 71.9 us -> none  [the longest x1 36.2 us: local(): correlation = lax.psum(correlation_local, ('rows', 'cols')) / total_rows]
    dot_general x12 -> x0, matrix products: 16.9 us -> none  [the longest x1 8.95 us: apply_operator(): jnp.einsum('tk,kan->tan', row_onehot, pulled, precision=highest)]
    ppermute x0 -> x11, waiting for transfers between devices: none -> 15.7 us  [the longest x4 8.86 us: exchange(): lax.ppermute(x, axis, [(i, i ^ distance) for i in range(lax.axis_size(axi...]
    all_gather x1 -> x0, blocking collectives: 15.6 us -> none  [apply_operator(): gathered = lax.all_gather(own_tiles, 'rows', axis=0, tiled=True)]
    another operation x6 -> x0, other arithmetic: 12.1 us -> none  [the longest x3 6.52 us: local(): lower_factor = jnp.linalg.cholesky(gram)]
    all_to_all x0 -> x1, blocking collectives: none -> 11.4 us  [local(): got = lax.all_to_all(send, ('rows', 'cols'), 0, 0, tiled=True)]
    ppermute x0 -> x11, starting transfers between devices: none -> 10.9 us  [the longest x4 5.1 us: exchange(): lax.ppermute(x, axis, [(i, i ^ distance) for i in range(lax.axis_size(axi...]
  transfers between devices with their start and end apart: 4 -> 11, of which waited for: 3 -> 8; matrix products, arithmetic and copies ran while one was open for 8% -> 0% of each run, Pallas kernels for 0% -> 3%
where the time goes in v1:
time: 44.1 us; the launch traced here: 43.9 us
  waiting for transfers between devices  15.7 us (36%)
  blocking collectives  11.4 us (26%)
  starting transfers between devices  10.9 us (25%)
  Pallas kernels  5.11 us (12%)
  between operations  0.69 us (2%)
    all_to_all x1, blocking collectives, local(): got = lax.all_to_all(send, ('rows', 'cols'), 0, 0, tiled=True)  11.4 us
    ppermute x4, waiting for transfers between devices, exchange(): lax.ppermute(x, axis, [(i, i ^ distance) for i in range(lax.axis_size(axi...  8.86 us
    ppermute x4, starting transfers between devices, exchange(): lax.ppermute(x, axis, [(i, i ^ distance) for i in range(lax.axis_size(axi...  5.1 us
    ppermute x2, starting transfers between devices, local(): received.append(lax.ppermute(send, ('rows', 'sub'), moves))  5.09 us
    ppermute x2, waiting for transfers between devices, local(): received.append(lax.ppermute(send, ('rows', 'sub'), moves))  4.26 us
    pallas_call x1, Pallas kernels, local(): call(functools.partial(factor_kernel, total_rows), [(half, f32), ((block,...  2.07 us
    ppermute x1, waiting for transfers between devices, local(): other = lax.ppermute(mine, 'sub', swap)  1.36 us
    pallas_call x1, Pallas kernels, local(): call(prepare_kernel, [(half, f32), ((2, chunk, width), f32), (half, f32),...  1.29 us
  transfers between devices with their start and end apart: 11, of which 8 were waited for; matrix products, arithmetic and copies ran while one was open for 0% of the time, Pallas kernels for 3%

profile of v1, /device:TPU:0, one launch (start us, length us, event | category | flops | bytes accessed | tf_op | source)
XLA Modules:
  0.0 43.9 jit_solution(11523257743319470953)
XLA Ops:
  0.6 0.6 %collective-permute-start.1 = (bf16[2,256,256]{2,1,0:T(8,128)(2,1)}, bf16[2,256,256]{2,1,0:T(8,128)(2,1)S(1)}, u32[]{:S(2)}, u32[]{:S(2)}) collective-permute-start(bf16[2,256,256]{2,1,0:T(8,128)(2,1)} %t_hbm.1), channel_id=1, source_target_pairs={{0,1},{1,0},{2,3},{3,2},{4,5},{5,4},{6,7},{7,6},{8,9},{9,8},{10,11... | collective-permute-start | bytes 786440 | tf_op jit(solution)/shard_map/ppermute | solution.py:282
  1.2 0.1 collective-permute-start
  1.3 1.3 %shard_map.94 = (f32[64,256]{1,0:T(8,128)S(1)}, f32[2,32,256]{2,1,0:T(8,128)S(1)}, f32[64,256]{1,0:T(8,128)S(1)}, bf16[2,64,256]{2,1,0:T(8,128)(2,1)S(1)}, bf16[...) custom-call(f32[64,256]{1,0:T(8,128)} %bitcast.12, f32[1,256]{1,0:T(1,128)} %bitcast.14, ...), custom_call_target="tpu_custom_call" | custom-call | flops 40000000 | bytes 1000000 | tf_op jit(solution)/shard_map/pallas_call | solution.py:284
  2.6 0.0 collective-permute-done.j_ref
  2.6 0.0 collective-permute-done.1.u_ref
  2.6 0.2 shard_map.95
  2.8 5.1 %collective-permute-start.2 = (bf16[128,256]{1,0:T(8,128)(2,1)S(1)}, bf16[128,256]{1,0:T(8,128)(2,1)S(1)}, u32[]{:S(2)}, u32[]{:S(2)}) collective-permute-start(bf16[128,256]{1,0:T(8,128)(2,1)S(1)} %get-tuple-element.30), channel_id=1, source_target_pairs={{0,12},{1,9},{4,8},{5,13},{8,4},{9,1},{12,0},{13,5},{2,14},{3,11},... | collective-permute-start | bytes 196616 | tf_op jit(solution)/shard_map/ppermute | solution.py:314
  7.9 0.0 collective-permute-start.4
  7.9 2.9 %collective-permute-done.2.refs_0_ = bf16[128,256]{1,0:T(8,128)(2,1)S(1)} collective-permute-done((bf16[128,256]{1,0:T(8,128)(2,1)S(1)}, bf16[128,256]{1,0:T(8,128)(2,1)S(1)}, u32[]{:S(2)}, u32[]{:S(2)}) %collective-permute-start.2) | collective-permute-done | bytes 65568 | tf_op jit(solution)/shard_map/ppermute | solution.py:314
  10.9 0.0 collective-permute-start.3
  10.9 1.3 %collective-permute-done.4.refs_2_ = bf16[256,128]{1,0:T(8,128)(2,1)S(1)} collective-permute-done((bf16[256,128]{1,0:T(8,128)(2,1)S(1)}, bf16[256,128]{1,0:T(8,128)(2,1)S(1)}, u32[]{:S(2)}, u32[]{:S(2)}) %collective-permute-start.4) | collective-permute-done | bytes 65568 | tf_op jit(solution)/shard_map/ppermute | solution.py:314
  12.2 0.0 collective-permute-start.5
  12.2 0.0 collective-permute-done.3.refs_1_
  12.2 1.2 %collective-permute-done.5.refs_3_ = bf16[256,128]{1,0:T(8,128)(2,1)S(1)} collective-permute-done((bf16[256,128]{1,0:T(8,128)(2,1)S(1)}, bf16[256,128]{1,0:T(8,128)(2,1)S(1)}, u32[]{:S(2)}, u32[]{:S(2)}) %collective-permute-start.5) | collective-permute-done | bytes 65568 | tf_op jit(solution)/shard_map/ppermute | solution.py:315
  13.4 0.8 %shard_map.96 = (f32[64,256]{1,0:T(8,128)S(1)}, f32[104,256]{1,0:T(8,128)S(1)}) custom-call(s32[2,2]{1,0:T(2,128)S(1)} %get-tuple-element.23.i_ref, s32[2,2]{1,0:T(2,128)S(1)} %collective-permute-done.j_ref, f32[64,256]{1,0:T(8,128)S(1)} %get-tuple-element.24.base_ref, bf16[2,64,256]{2,1,0:T(8,128)(2,1)S(1)} %get-tuple-element.25.xs_ref, ...), custom_call_target="tpu_custom_call" | custom-call | flops 40000000 | bytes 1000000 | tf_op jit(solution)/shard_map/pallas_call | solution.py:317
  14.2 1.5 %collective-permute-start.6 = (f32[104,256]{1,0:T(8,128)S(1)}, f32[104,256]{1,0:T(8,128)S(1)}, u32[]{:S(2)}, u32[]{:S(2)}) collective-permute-start(f32[104,256]{1,0:T(8,128)S(1)} %get-tuple-element.32.mine_ref), channel_id=1, source_target_pairs={{0,2},{2,0},{1,3},{3,1},{4,6},{6,4},{5,7},{7,5},{8,10},{10,8},{9,1... | collective-permute-start | bytes 319496 | tf_op jit(solution)/shard_map/ppermute | solution.py:257
  15.8 3.5 %collective-permute-done.6.other_ref = f32[104,256]{1,0:T(8,128)S(1)} collective-permute-done((f32[104,256]{1,0:T(8,128)S(1)}, f32[104,256]{1,0:T(8,128)S(1)}, u32[]{:S(2)}, u32[]{:S(2)}) %collective-permute-start.6) | collective-permute-done | bytes 106528 | tf_op jit(solution)/shard_map/ppermute | solution.py:257
  19.3 0.9 %collective-permute-start.9 = (bf16[112,256]{1,0:T(8,128)(2,1)S(1)}, bf16[112,256]{1,0:T(8,128)(2,1)S(1)}, u32[]{:S(2)}, u32[]{:S(2)}) collective-permute-start(bf16[112,256]{1,0:T(8,128)(2,1)S(1)} %get-tuple-element.34), channel_id=1, source_target_pairs={{0,4},{4,0},{8,12},{12,8},{1,5},{5,1},{9,13},{13,9},{2,6},{6,2},{1... | collective-permute-start | bytes 172040 | tf_op jit(solution)/shard_map/ppermute | solution.py:257
  20.2 1.6 %collective-permute-start.8 = (bf16[112,256]{1,0:T(8,128)(2,1)S(1)}, bf16[112,256]{1,0:T(8,128)(2,1)S(1)}, u32[]{:S(2)}, u32[]{:S(2)}) collective-permute-start(bf16[112,256]{1,0:T(8,128)(2,1)S(1)} %get-tuple-element.34), channel_id=1, source_target_pairs={{0,12},{4,8},{8,4},{12,0},{1,13},{5,9},{9,5},{13,1},{2,14},{6,10},... | collective-permute-start | bytes 172040 | tf_op jit(solution)/shard_map/ppermute | solution.py:257
  21.8 1.1 %collective-permute-start.7 = (bf16[112,256]{1,0:T(8,128)(2,1)S(1)}, bf16[112,256]{1,0:T(8,128)(2,1)S(1)}, u32[]{:S(2)}, u32[]{:S(2)}) collective-permute-start(bf16[112,256]{1,0:T(8,128)(2,1)S(1)} %get-tuple-element.34), channel_id=1, source_target_pairs={{0,8},{4,12},{8,0},{12,4},{1,9},{5,13},{9,1},{13,5},{2,10},{6,14},... | collective-permute-start | bytes 172040 | tf_op jit(solution)/shard_map/ppermute | solution.py:257
  22.9 0.7 %collective-permute-done.9.refs_2_ = bf16[112,256]{1,0:T(8,128)(2,1)S(1)} collective-permute-done((bf16[112,256]{1,0:T(8,128)(2,1)S(1)}, bf16[112,256]{1,0:T(8,128)(2,1)S(1)}, u32[]{:S(2)}, u32[]{:S(2)}) %collective-permute-start.9) | collective-permute-done | bytes 57376 | tf_op jit(solution)/shard_map/ppermute | solution.py:257
  23.6 2.6 %collective-permute-done.8.refs_1_ = bf16[112,256]{1,0:T(8,128)(2,1)S(1)} collective-permute-done((bf16[112,256]{1,0:T(8,128)(2,1)S(1)}, bf16[112,256]{1,0:T(8,128)(2,1)S(1)}, u32[]{:S(2)}, u32[]{:S(2)}) %collective-permute-start.8) | collective-permute-done | bytes 57376 | tf_op jit(solution)/shard_map/ppermute | solution.py:257
  26.2 2.0 %collective-permute-done.7.refs_0_ = bf16[112,256]{1,0:T(8,128)(2,1)S(1)} collective-permute-done((bf16[112,256]{1,0:T(8,128)(2,1)S(1)}, bf16[112,256]{1,0:T(8,128)(2,1)S(1)}, u32[]{:S(2)}, u32[]{:S(2)}) %collective-permute-start.7) | collective-permute-done | bytes 57376 | tf_op jit(solution)/shard_map/ppermute | solution.py:257
  28.2 0.2 shard_map.98.mine_ref
  28.4 0.1 collective-permute-start.10
  28.5 1.4 %collective-permute-done.10.other_ref = f32[144,256]{1,0:T(8,128)S(1)} collective-permute-done((f32[144,256]{1,0:T(8,128)S(1)}, f32[144,256]{1,0:T(8,128)S(1)}, u32[]{:S(2)}, u32[]{:S(2)}) %collective-permute-start.10) | collective-permute-done | bytes 147488 | tf_op jit(solution)/shard_map/ppermute | solution.py:336
  29.8 0.5 %shard_map.99 = (f32[64,256]{1,0:T(8,128)S(1)}, f32[8,32,128]{2,1,0:T(8,128)S(1)}, f32[64,64]{1,0:T(8,128)S(1)}) custom-call(f32[144,256]{1,0:T(8,128)S(1)} %shard_map.98.mine_ref, f32[144,256]{1,0:T(8,128)S(1)} %collective-permute-done.10.other_ref, f32[64,256]{1,0:T(8,128)S(1)} %get-tuple-element.35.x_ref, f32[64,256]{1,0:T(8,128)S(1)} %get-tuple-element.36.y_ref), custom_call_target="tpu_custom_call" | custom-call | flops 40000000 | bytes 1000000 | tf_op jit(solution)/shard_map/pallas_call | solution.py:337
  30.4 11.4 %all_to_all.5.got_ref = f32[8,32,128]{2,1,0:T(8,128)S(1)} all-to-all(f32[8,32,128]{2,1,0:T(8,128)S(1)} %get-tuple-element.37), channel_id=1, replica_groups=mesh['groups'=2,'rows'=4,'cols'=2,'sub'=2] {'rows','cols'}, dimensions={0} | all-to-all | bytes 262144 | tf_op jit(solution)/shard_map/all_to_all | solution.py:342
  41.8 2.1 %shard_map.100 = (f32[64,256]{1,0:T(8,128)}, f32[64,64]{1,0:T(8,128)}, f32[64,64]{1,0:T(8,128)}) custom-call(f32[8,32,128]{2,1,0:T(8,128)S(1)} %all_to_all.5.got_ref, f32[64,256]{1,0:T(8,128)S(1)} %get-tuple-element.38.images_ref, f32[64,64]{1,0:T(8,128)S(1)} %get-tuple-element.39.d_ref), custom_call_target="tpu_custom_call" | custom-call | flops 40000000 | bytes 1000000 | tf_op jit(solution)/shard_map/pallas_call | solution.py:343
  (1 shorter events, 0.0 us)
Async XLA Ops:
  0.6 2.0 %collective-permute-start.1 = (bf16[2,256,256]{2,1,0:T(8,128)(2,1)}, bf16[2,256,256]{2,1,0:T(8,128)(2,1)S(1)}, u32[]{:S(2)}, u32[]{:S(2)}) collective-permute-start(bf16[2,256,256]{2,1,0:T(8,128)(2,1)} %t_hbm.1), channel_id=1, source_target_pairs={{0,1},{1,0},{2,3},{3,2},{4,5},{5,4},{6,7},{7,6},{8,9},{9,8},{10,11... | collective-permute-start | bytes 786440 | tf_op jit(solution)/shard_map/ppermute | solution.py:282
  1.2 1.4 %collective-permute-start = (s32[2,2]{1,0:T(2,128)}, s32[2,2]{1,0:T(2,128)S(1)}, u32[]{:S(2)}, u32[]{:S(2)}) collective-permute-start(s32[2,2]{1,0:T(2,128)} %i_hbm.1), channel_id=1, source_target_pairs={{0,1},{1,0},{2,3},{3,2},{4,5},{5,4},{6,7},{7,6},{8,9},{9,8},{10,11... | collective-permute-start | bytes 56 | tf_op jit(solution)/shard_map/ppermute | solution.py:283
  2.8 8.0 %collective-permute-start.2 = (bf16[128,256]{1,0:T(8,128)(2,1)S(1)}, bf16[128,256]{1,0:T(8,128)(2,1)S(1)}, u32[]{:S(2)}, u32[]{:S(2)}) collective-permute-start(bf16[128,256]{1,0:T(8,128)(2,1)S(1)} %get-tuple-element.30), channel_id=1, source_target_pairs={{0,12},{1,9},{4,8},{5,13},{8,4},{9,1},{12,0},{13,5},{2,14},{3,11},... | collective-permute-start | bytes 196616 | tf_op jit(solution)/shard_map/ppermute | solution.py:314
  7.9 4.3 %collective-permute-start.4 = (bf16[256,128]{1,0:T(8,128)(2,1)S(1)}, bf16[256,128]{1,0:T(8,128)(2,1)S(1)}, u32[]{:S(2)}, u32[]{:S(2)}) collective-permute-start(bf16[256,128]{1,0:T(8,128)(2,1)S(1)} %get-tuple-element.31), channel_id=1, source_target_pairs={{0,4},{1,5},{4,0},{5,1},{8,12},{9,13},{12,8},{13,9},{2,6},{3,7},{6... | collective-permute-start | bytes 196616 | tf_op jit(solution)/shard_map/ppermute | solution.py:314
  10.9 1.3 %collective-permute-start.3 = (bf16[128,256]{1,0:T(8,128)(2,1)S(1)}, bf16[128,256]{1,0:T(8,128)(2,1)S(1)}, u32[]{:S(2)}, u32[]{:S(2)}) collective-permute-start(bf16[128,256]{1,0:T(8,128)(2,1)S(1)} %collective-permute-done.2.refs_0_), channel_id=1, source_target_pairs={{0,1},{1,0},{2,3},{3,2},{4,5},{5,4},{6,7},{7,6},{8,9},{9,8},{10,11... | collective-permute-start | bytes 196616 | tf_op jit(solution)/shard_map/ppermute | solution.py:315
  12.2 1.3 %collective-permute-start.5 = (bf16[256,128]{1,0:T(8,128)(2,1)S(1)}, bf16[256,128]{1,0:T(8,128)(2,1)S(1)}, u32[]{:S(2)}, u32[]{:S(2)}) collective-permute-start(bf16[256,128]{1,0:T(8,128)(2,1)S(1)} %collective-permute-done.4.refs_2_), channel_id=1, source_target_pairs={{0,1},{1,0},{2,3},{3,2},{4,5},{5,4},{6,7},{7,6},{8,9},{9,8},{10,11... | collective-permute-start | bytes 196616 | tf_op jit(solution)/shard_map/ppermute | solution.py:315
  14.2 5.1 %collective-permute-start.6 = (f32[104,256]{1,0:T(8,128)S(1)}, f32[104,256]{1,0:T(8,128)S(1)}, u32[]{:S(2)}, u32[]{:S(2)}) collective-permute-start(f32[104,256]{1,0:T(8,128)S(1)} %get-tuple-element.32.mine_ref), channel_id=1, source_target_pairs={{0,2},{2,0},{1,3},{3,1},{4,6},{6,4},{5,7},{7,5},{8,10},{10,8},{9,1... | collective-permute-start | bytes 319496 | tf_op jit(solution)/shard_map/ppermute | solution.py:257
  19.3 4.2 %collective-permute-start.9 = (bf16[112,256]{1,0:T(8,128)(2,1)S(1)}, bf16[112,256]{1,0:T(8,128)(2,1)S(1)}, u32[]{:S(2)}, u32[]{:S(2)}) collective-permute-start(bf16[112,256]{1,0:T(8,128)(2,1)S(1)} %get-tuple-element.34), channel_id=1, source_target_pairs={{0,4},{4,0},{8,12},{12,8},{1,5},{5,1},{9,13},{13,9},{2,6},{6,2},{1... | collective-permute-start | bytes 172040 | tf_op jit(solution)/shard_map/ppermute | solution.py:257
  20.2 6.0 %collective-permute-start.8 = (bf16[112,256]{1,0:T(8,128)(2,1)S(1)}, bf16[112,256]{1,0:T(8,128)(2,1)S(1)}, u32[]{:S(2)}, u32[]{:S(2)}) collective-permute-start(bf16[112,256]{1,0:T(8,128)(2,1)S(1)} %get-tuple-element.34), channel_id=1, source_target_pairs={{0,12},{4,8},{8,4},{12,0},{1,13},{5,9},{9,5},{13,1},{2,14},{6,10},... | collective-permute-start | bytes 172040 | tf_op jit(solution)/shard_map/ppermute | solution.py:257
  21.8 6.4 %collective-permute-start.7 = (bf16[112,256]{1,0:T(8,128)(2,1)S(1)}, bf16[112,256]{1,0:T(8,128)(2,1)S(1)}, u32[]{:S(2)}, u32[]{:S(2)}) collective-permute-start(bf16[112,256]{1,0:T(8,128)(2,1)S(1)} %get-tuple-element.34), channel_id=1, source_target_pairs={{0,8},{4,12},{8,0},{12,4},{1,9},{5,13},{9,1},{13,5},{2,10},{6,14},... | collective-permute-start | bytes 172040 | tf_op jit(solution)/shard_map/ppermute | solution.py:257
  28.4 1.4 %collective-permute-start.10 = (f32[144,256]{1,0:T(8,128)S(1)}, f32[144,256]{1,0:T(8,128)S(1)}, u32[]{:S(2)}, u32[]{:S(2)}) collective-permute-start(f32[144,256]{1,0:T(8,128)S(1)} %shard_map.98.mine_ref), channel_id=1, source_target_pairs={{0,1},{1,0},{2,3},{3,2},{4,5},{5,4},{6,7},{7,6},{8,9},{9,8},{10,11... | collective-permute-start | bytes 442376 | tf_op jit(solution)/shard_map/ppermute | solution.py:336

commit v2 on v1

--- a/solution.py
+++ b/solution.py
@@ -59,8 +59,8 @@
 
 def prepare_kernel(
     x_hbm, e_hbm, p_hbm, c_hbm, s_hbm, t_hbm, i_hbm,
-    base_ref, corr_ref, x_ref, xs_ref, ss_ref, t_ref, i_ref,
-    e_ref, p_ref, c_ref, s_ref, sems,
+    base_ref, corr_ref, sx_ref, t_ref, i_ref,
+    x_ref, e_ref, p_ref, c_ref, s_ref, sems,
 ):
     pairs = (
         (s_hbm, s_ref), (x_hbm, x_ref), (p_hbm, p_ref), (c_hbm, c_ref),
@@ -79,8 +79,7 @@
     xs = split(x)
     ss = split(s_ref[...])
     for half in range(2):
-        xs_ref[half] = xs[half]
-        ss_ref[half] = ss[half]
+        sx_ref[half] = jnp.concatenate([ss[half], xs[half]], axis=0)
     base_ref[...] = e_ref[...] * x - dot_split(split(coupling), split(p_ref[...]), NN)
     corr = dot_split(xs, ss, NT)
     chunk = corr_ref.shape[1]
@@ -103,9 +102,10 @@
     return jnp.bitwise_xor(me, jnp.where(core == 0, pair[0], pair[1]))
 
 
-def push_kernel(pairs, columns, i_ref, j_ref, xs_ref, corr_ref, t_ref, u_ref, *outs):
-    block, rows = xs_ref.shape[1:]
-    x = xs_ref[0]
+def push_kernel(pairs, columns, i_ref, j_ref, sx_ref, corr_ref, t_ref, u_ref, *outs):
+    width, rows = corr_ref.shape[2], sx_ref.shape[2]
+    block = sx_ref.shape[1] - width
+    x = sx_ref[0, width:]
     me, core = lax.axis_index("rows"), lax.axis_index("sub")
     targets = tile_columns((i_ref, j_ref), (block, rows))
     products = [dot_bf16(x, ref[k], NN) for ref in (t_ref, u_ref) for k in range(ref.shape[0])]
@@ -130,14 +130,13 @@
             ref[...] = jnp.concatenate([message, *halves], axis=0).astype(bf16)
 
 
-def image_kernel(pairs, columns, parts, i_ref, j_ref, base_ref, xs_ref, ss_ref, t_ref, u_ref, own_ref, *refs):
-    received, (y_ref, send_ref) = refs[:-2], refs[-2:]
+def image_kernel(pairs, columns, i_ref, j_ref, base_ref, sx_ref, t_ref, u_ref, own_ref, *refs):
+    received, send_ref = refs[:-1], refs[-1]
     block, rows = base_ref.shape
-    xs = (xs_ref[0], xs_ref[1])
     me, core = lax.axis_index("rows"), lax.axis_index("sub")
     y = base_ref[...] + own_ref[0:block]
     corr = own_ref[block:]
-    blocks = [(me, xs[0].astype(f32))]
+    blocks = [(me, sx_ref[0, sx_ref.shape[1] - block :].astype(f32))]
     for k, pair in enumerate(pairs):
         mine, other = received[2 * k][...].astype(f32), received[2 * k + 1][...].astype(f32)
         if pair[0] != pair[1]:
@@ -160,26 +159,34 @@
             inside = (target >= first) & (target < first + columns)
             source = jnp.where(inside, held, source)
         y = y + dot_bf16(source.astype(bf16), tile, NT)
-    y_ref[...] = y
-    halves = split(y)
-    stored = dot_split(halves, (ss_ref[0], ss_ref[1]), NT)
-    diagonal = fold(dot_split(halves, xs, NT), parts)
-    middle = diagonal.shape[0] // 2
-    diagonal = jnp.where(core == 0, diagonal[:middle], diagonal[middle:])
-    send_ref[...] = jnp.concatenate([stored, diagonal, corr], axis=0)
-
-
-def combine_kernel(block, small, mine_ref, other_ref, total_ref, send_ref):
-    total = mine_ref[...] + other_ref[...]
-    total_ref[...] = total
+    send_ref[0:block, :] = y
+    send_ref[block:, :] = corr
+
+
+def pack(total, block, small):
     high, low = split(total[block : block + small])
     message = [total[0:block], high.astype(f32), low.astype(f32), total[block + small :]]
-    send_ref[...] = jnp.concatenate(message, axis=0).astype(bf16)
-
-
-def project_kernel(steps, block, small, total_rows, total_ref, ss_ref, *refs):
-    received, out_ref = refs[:-1], refs[-1]
+    return jnp.concatenate(message, axis=0).astype(bf16)
+
+
+def inner_kernel(block, parts, mine_ref, other_ref, sx_ref, sy_ref, total_ref, *send_refs):
+    width = sx_ref.shape[1] - block
+    stored = diagonal = 0.0
+    for y_ref, s_ref in ((mine_ref, sx_ref), (other_ref, sy_ref)):
+        halves = split(y_ref[0:block])
+        stored = stored + dot_split(halves, (s_ref[0, :width], s_ref[1, :width]), NT)
+        diagonal = diagonal + dot_split(halves, (s_ref[0, width:], s_ref[1, width:]), NT)
+    corr = mine_ref[block:] + other_ref[block:]
+    total = jnp.concatenate([stored, fold(diagonal, parts), corr], axis=0)
+    total_ref[...] = total
+    for ref in send_refs:
+        ref[...] = pack(total, block, block // parts)
+
+
+def project_kernel(steps, block, parts, total_rows, total_ref, sx_ref, sy_ref, *refs):
+    received, (out_ref, diagonal_ref) = refs[:-2], refs[-2:]
     me, core = lax.axis_index("rows"), lax.axis_index("sub")
+    small = block // parts
     total = total_ref[...]
     stored, diagonal = total[0:block], total[block : block + small]
     same, other = total[block + small :], jnp.zeros((block // 2, total.shape[1]), f32)
@@ -194,33 +201,44 @@
         else:
             same = same + part
     even = jnp.bitwise_and(me, 1) == 0
-    first, second = jnp.where(even, same, other), jnp.where(even, other, same)
+    corr = jnp.concatenate([jnp.where(even, same, other), jnp.where(even, other, same)], axis=0)
     scale = 1.0 / total_rows
-    weights = jnp.concatenate([stored, first, second], axis=0) * scale
-    out_ref[0 : 2 * block, :] = dot_split(split(weights), (ss_ref[0], ss_ref[1]), NN)
-    out_ref[2 * block : 2 * block + small, :] = jnp.where(core == 0, diagonal * scale, 0.0)
-    out_ref[2 * block + small :, :] = jnp.where(core == 0, 0.0, diagonal * scale)
-
-
-def gram_kernel(parts, mine_ref, other_ref, x_ref, y_ref, images_ref, send_ref, diagonal_ref):
-    block = x_ref.shape[0]
-    both = mine_ref[...] + other_ref[...]
-    diagonal = unfold(both[2 * block :], parts)
-    reduced = x_ref[...] - both[block : 2 * block]
-    images = y_ref[...] - both[0:block] - dot_split(split(diagonal), split(reduced), NN)
+    diagonal = unfold(diagonal * scale, parts)
+    diagonal_ref[...] = diagonal
+    projection = stored * scale - dot_split(split(diagonal), split(corr * scale), NN)
+    weights = split(jnp.concatenate([projection, jnp.where(core == 0, diagonal, 0.0)], axis=1))
+    for k, ref in enumerate((sx_ref, sy_ref)):
+        out_ref[k * block : (k + 1) * block, :] = dot_split(weights, (ref[0], ref[1]), NN)
+
+
+def gram_kernel(mine_ref, other_ref, y_ref, z_ref, images_ref, full_ref, half_ref):
+    block = images_ref.shape[0]
+    removed = mine_ref[...] + other_ref[...]
+    images = y_ref[0:block] - removed[0:block]
     images_ref[...] = images
-    diagonal_ref[...] = diagonal
-    message = fold(dot_exact(images, images, NT), 2)
-    for device in range(send_ref.shape[0]):
-        send_ref[device] = message
-
-
-def factor_kernel(total_rows, got_ref, images_ref, d_ref, following_ref, coupling_ref, diagonal_ref):
+    gram = 0.0
+    for x in (images, z_ref[0:block] - removed[block:]):
+        halves = split(x)
+        gram = gram + dot_split(halves, halves, NT)
+    gram = fold(gram, 2)
+    full_ref[...] = gram
+    middle = half_ref.shape[0]
+    half_ref[...] = jnp.where(lax.axis_index("sub") == 0, gram[:middle], gram[middle:])
+
+
+def factor_kernel(pairs, total_rows, own_ref, images_ref, d_ref, *refs):
+    received, (following_ref, coupling_ref, diagonal_ref) = refs[:-3], refs[-3:]
     block = images_ref.shape[0]
-    half, lanes = block // 2, 2 * block
-    gram = got_ref[0]
-    for device in range(1, got_ref.shape[0]):
-        gram = gram + got_ref[device]
+    lanes = 2 * block
+    core = lax.axis_index("sub")
+    gram = own_ref[...]
+    for k, pair in enumerate(pairs):
+        mine, other = received[2 * k][...], received[2 * k + 1][...]
+        if pair[0] != pair[1]:
+            gram = gram + (mine + other)
+        else:
+            first, second = jnp.where(core == 0, mine, other), jnp.where(core == 0, other, mine)
+            gram = gram + jnp.concatenate([first, second], axis=0)
     gram = gram * (1.0 / total_rows)
     row = lax.broadcasted_iota(jnp.int32, (block, lanes), 0)
     column = lax.broadcasted_iota(jnp.int32, (block, lanes), 1)
@@ -272,7 +290,6 @@
     stored = stored_basis.shape[0]
     width = stored * block
     total_rows = rows * bands * columns
-    peers = bands * columns
     parts = width // block
     chunk = block // 2
     assert rows == tile_values.shape[1] and cores == 2 and width == rows
@@ -281,70 +298,80 @@
     swap = [(0, 1), (1, 0)]
     other_tiles = lax.ppermute(tile_values, "sub", swap)
     other_index = lax.ppermute(tile_index, "sub", swap)
-    base, corr, x, xs, ss, tiles, index = call(
+    prepare = call(
         prepare_kernel,
         [
-            (half, f32), ((2, chunk, width), f32), (half, f32), ((2,) + half, bf16),
-            ((2, width, rows), bf16), (tile_values.shape, bf16), (tile_index.shape, jnp.int32),
+            (half, f32), ((2, chunk, width), f32), ((2, width + block, rows), bf16),
+            (tile_values.shape, bf16), (tile_index.shape, jnp.int32),
         ],
         "hhhhhhh",
         [
-            pltpu.VMEM((1, rows), f32), pltpu.VMEM(half, f32), pltpu.VMEM((block, block), f32),
-            pltpu.VMEM((width, rows), f32), pltpu.SemaphoreType.DMA((7,)),
+            pltpu.VMEM(half, f32), pltpu.VMEM((1, rows), f32), pltpu.VMEM(half, f32),
+            pltpu.VMEM((block, block), f32), pltpu.VMEM((width, rows), f32),
+            pltpu.SemaphoreType.DMA((7,)),
         ],
-    )(
-        *(
-            pltpu.with_memory_space_constraint(a, pltpu.HBM)
-            for a in (
-                start_block.T, onsite_energy.reshape(1, rows), previous_block.T, previous_coupling,
-                stored_basis.transpose(0, 2, 1).reshape(width, rows), tile_values, tile_index,
-            )
-        )
-    )
-    pairs = [(step, step - 1) for step in range(bands - 1, 1, -2)] + [(1, 1)]
+    )
+    sources = (
+        start_block.T, onsite_energy.reshape(1, rows), previous_block.T, previous_coupling,
+        stored_basis.transpose(0, 2, 1).reshape(width, rows), tile_values, tile_index,
+    )
+    base, corr, sx, tiles, index = prepare(
+        *(pltpu.with_memory_space_constraint(a, pltpu.HBM) for a in sources)
+    )
+    pairs = [(step - 1, step) for step in range(bands - 1, 1, -2)] + [(1, 1)]
+
+    def serve(sends):
+        received = []
+        for send, pair in zip(sends, pairs):
+            moves = [(2 * r + c, 2 * (r ^ pair[c]) + c) for r in range(bands) for c in range(2)]
+            received.append(lax.ppermute(send, ("rows", "sub"), moves))
+        return [y for x in received for y in (x, lax.ppermute(x, "sub", swap))]
+
     sends = call(
         functools.partial(push_kernel, pairs, columns),
         [((block + chunk, rows), f32)]
         + [((2 * block, rows) if a != b else (4 * block, rows // 2), bf16) for a, b in pairs],
         "vvvvvv",
-    )(index, other_index, xs, corr, tiles, other_tiles)
-    received = []
-    for send, pair in zip(sends[1:], pairs):
-        moves = [(2 * r + c, 2 * (r ^ pair[c]) + c) for r in range(bands) for c in range(2)]
-        received.append(lax.ppermute(send, ("rows", "sub"), moves))
-    received = [y for x in received for y in (x, lax.ppermute(x, "sub", swap))]
-    small = block // parts // 2
-    y, mine = call(
-        functools.partial(image_kernel, pairs, columns, parts),
-        [(half, f32), ((block + small + chunk, rows), f32)],
-        "v" * (8 + len(received)),
-    )(index, other_index, base, xs, ss, tiles, other_tiles, sends[0], *received)
-    distances = [2**k for k in range(columns.bit_length() - 1)]
-    for distance in distances[:-1]:
-        mine = mine + exchange(mine, "cols", distance)
-    total, send = call(
-        functools.partial(combine_kernel, block, small),
-        [(mine.shape, f32), ((block + 2 * small + chunk, rows), bf16)],
-        "vv",
-    )(mine, exchange(mine, "cols", distances[-1]))
+    )(index, other_index, sx, corr, tiles, other_tiles)
+    sy = exchange(sx, "cols", 1)
+    received = serve(sends[1:])
+    (mine,) = call(
+        functools.partial(image_kernel, pairs, columns),
+        [((block + chunk, rows), f32)],
+        "v" * (7 + len(received)),
+    )(index, other_index, base, sx, tiles, other_tiles, sends[0], *received)
+    other = exchange(mine, "cols", 1)
+    distances = [2**k for k in range(1, columns.bit_length() - 1)]
+    small = block // parts
+    total, *send = call(
+        functools.partial(inner_kernel, block, parts),
+        [((block + small + chunk, rows), f32)]
+        + [((block + 2 * small + chunk, rows), bf16)] * (not distances),
+        "vvvv",
+    )(mine, other, sx, sy)
+    for distance in distances:
+        total = total + exchange(total, "cols", distance)
+    send = send[0] if send else pack(total, block, small)
     steps = [*range(2, bands), 1]
-    (mine,) = call(
-        functools.partial(project_kernel, steps, block, small, total_rows),
-        [((2 * block + 2 * small, rows), f32)],
-        "v" * (1 + bands),
-    )(total, ss, *(exchange(send, "rows", step) for step in steps))
-    other = lax.ppermute(mine, "sub", swap)
-    images, send, diagonal = call(
-        functools.partial(gram_kernel, parts),
-        [(half, f32), ((peers, block // 2, 2 * block), f32), ((block, block), f32)],
+    removed, diagonal = call(
+        functools.partial(project_kernel, steps, block, parts, total_rows),
+        [((2 * block, rows), f32), ((block, block), f32)],
+        "v" * (2 + bands),
+    )(total, sx, sy, *(exchange(send, "rows", step) for step in steps))
+    images, full, part = call(
+        gram_kernel,
+        [(half, f32), ((block // 2, 2 * block), f32), ((block // 4, 2 * block), f32)],
         "vvvv",
-    )(mine, other, x, y)
-    got = lax.all_to_all(send, ("rows", "cols"), 0, 0, tiled=True)
+    )(removed, lax.ppermute(removed, "sub", swap), mine, other)
+    for distance in distances:
+        full = full + exchange(full, "cols", distance)
+        middle = part.shape[0]
+        part = jnp.where(lax.axis_index("sub") == 0, full[:middle], full[middle:])
     following, coupling, diagonal = call(
-        functools.partial(factor_kernel, total_rows),
+        functools.partial(factor_kernel, pairs, total_rows),
         [(half, f32), ((block, block), f32), ((block, block), f32)],
-        "vvv",
-    )(got, images, diagonal)
+        "v" * (3 + 2 * len(pairs)),
+    )(full, images, diagonal, *serve([full] * (len(pairs) - 1) + [part]))
     return following.T[None], diagonal[None], coupling[None]
 
 

time: 44.1 us -> 41.4 us (0.939)
  blocking collectives: 11.4 us -> 0 us
  starting transfers between devices: 10.9 us -> 15.4 us
  waiting for transfers between devices: 15.7 us -> 20 us
    all_to_all x1 -> x0, blocking collectives: 11.4 us -> none  [local(): got = lax.all_to_all(send, ('rows', 'cols'), 0, 0, tiled=True)]
    ppermute x5 -> x9, starting transfers between devices: 5.16 us -> 7.67 us  [the longest x4 6.98 us: serve(): received.append(lax.ppermute(send, ('rows', 'sub'), moves))]
    ppermute x4 -> x5, starting transfers between devices: 5.1 us -> 7 us  [exchange(): lax.ppermute(x, axis, [(i, i ^ distance) for i in range(lax.axis_size(axi...]
    ppermute x5 -> x9, waiting for transfers between devices: 6.87 us -> 8.72 us  [the longest x4 5.4 us: serve(): received.append(lax.ppermute(send, ('rows', 'sub'), moves))]
    ppermute x4 -> x5, waiting for transfers between devices: 8.86 us -> 10.3 us  [exchange(): lax.ppermute(x, axis, [(i, i ^ distance) for i in range(lax.axis_size(axi...]
    ppermute x1, waiting for transfers between devices: 0.01 us -> 0.95 us  [local(): other_index = lax.ppermute(tile_index, 'sub', swap)]
  transfers between devices with their start and end apart: 11 -> 16, of which waited for: 8 -> 11; matrix products, arithmetic and copies ran while one was open for 0% -> 0% of each run, Pallas kernels for 3% -> 5%
where the time goes in v2:
time: 41.4 us; the launch traced here: 41.3 us
  waiting for transfers between devices  20 us (48%)
  starting transfers between devices  15.4 us (37%)
  Pallas kernels  5.18 us (13%)
  between operations  0.69 us (2%)
    ppermute x5, waiting for transfers between devices, exchange(): lax.ppermute(x, axis, [(i, i ^ distance) for i in range(lax.axis_size(axi...  10.3 us
    ppermute x5, starting transfers between devices, exchange(): lax.ppermute(x, axis, [(i, i ^ distance) for i in range(lax.axis_size(axi...  7 us
    ppermute x4, starting transfers between devices, serve(): received.append(lax.ppermute(send, ('rows', 'sub'), moves))  6.98 us
    ppermute x4, waiting for transfers between devices, serve(): received.append(lax.ppermute(send, ('rows', 'sub'), moves))  5.4 us
    pallas_call x1, Pallas kernels, local(): call(functools.partial(factor_kernel, pairs, total_rows), [(half, f32), (...  2.07 us
    ppermute x4, waiting for transfers between devices, serve(): return [y for x in received for y in (x, lax.ppermute(x, 'sub', swap))]  1.98 us
    ppermute x1, waiting for transfers between devices, local(): lax.ppermute(removed, 'sub', swap)  1.33 us
    pallas_call x1, Pallas kernels, local(): prepare(*(pltpu.with_memory_space_constraint(a, pltpu.HBM) for a in sourc...  1.29 us
  transfers between devices with their start and end apart: 16, of which 11 were waited for; matrix products, arithmetic and copies ran while one was open for 0% of the time, Pallas kernels for 5%

profile of v2, /device:TPU:0, one launch (start us, length us, event | category | flops | bytes accessed | tf_op | source)
XLA Modules:
  0.0 41.3 jit_solution(3239366558397723122)
XLA Ops:
  0.6 0.6 %collective-permute-start.1 = (bf16[2,256,256]{2,1,0:T(8,128)(2,1)}, bf16[2,256,256]{2,1,0:T(8,128)(2,1)S(1)}, u32[]{:S(2)}, u32[]{:S(2)}) collective-permute-start(bf16[2,256,256]{2,1,0:T(8,128)(2,1)} %t_hbm.1), channel_id=1, source_target_pairs={{0,1},{1,0},{2,3},{3,2},{4,5},{5,4},{6,7},{7,6},{8,9},{9,8},{10,11... | collective-permute-start | bytes 786440 | tf_op jit(solution)/shard_map/ppermute | solution.py:299
  1.2 1.3 %shard_map.94 = (f32[64,256]{1,0:T(8,128)S(1)}, f32[2,32,256]{2,1,0:T(8,128)S(1)}, bf16[2,320,256]{2,1,0:T(8,128)(2,1)S(1)}, bf16[2,256,256]{2,1,0:T(8,128)(2,1)S(1)}, s32[2,2]{1,0:T(2,128)S(1)}) custom-call(f32[64,256]{1,0:T(8,128)} %bitcast.12, f32[1,256]{1,0:T(1,128)} %bitcast.14, f32[64,256]{1,0:T(8,128)} %bitcast.13, f32[64,64]{1,0:T(8,128)} %c_hbm.1, ...), custom_call_target="tpu_custom_call" | custom-call | flops 40000000 | bytes 1000000 | tf_op jit(solution)/shard_map/pallas_call | solution.py:318
  2.5 2.6 %collective-permute-start.7 = (bf16[2,320,256]{2,1,0:T(8,128)(2,1)S(1)}, bf16[2,320,256]{2,1,0:T(8,128)(2,1)S(1)}, u32[]{:S(2)}, u32[]{:S(2)}) collective-permute-start(bf16[2,320,256]{2,1,0:T(8,128)(2,1)S(1)} %get-tuple-element.23.sx_ref), channel_id=1, source_target_pairs={{0,2},{2,0},{1,3},{3,1},{4,6},{6,4},{5,7},{7,5},{8,10},{10,8},{9,1... | collective-permute-start | bytes 983048 | tf_op jit(solution)/shard_map/ppermute | solution.py:275
  5.1 0.2 collective-permute-start
  5.3 0.9 %collective-permute-done.j_ref = s32[2,2]{1,0:T(2,128)S(1)} collective-permute-done((s32[2,2]{1,0:T(2,128)S(1)}, s32[2,2]{1,0:T(2,128)S(1)}, u32[]{:S(2)}, u32[]{:S(2)}) %collective-permute-start) | collective-permute-done | bytes 48 | tf_op jit(solution)/shard_map/ppermute | solution.py:300
  6.2 0.2 shard_map.95
  6.5 2.7 %collective-permute-start.2 = (bf16[128,256]{1,0:T(8,128)(2,1)S(1)}, bf16[128,256]{1,0:T(8,128)(2,1)S(1)}, u32[]{:S(2)}, u32[]{:S(2)}) collective-permute-start(bf16[128,256]{1,0:T(8,128)(2,1)S(1)} %get-tuple-element.27), channel_id=1, source_target_pairs={{0,8},{1,13},{4,12},{5,9},{8,0},{9,5},{12,4},{13,1},{2,10},{3,15},... | collective-permute-start | bytes 196616 | tf_op jit(solution)/shard_map/ppermute | solution.py:327
  9.1 1.6 %collective-permute-start.4 = (bf16[256,128]{1,0:T(8,128)(2,1)S(1)}, bf16[256,128]{1,0:T(8,128)(2,1)S(1)}, u32[]{:S(2)}, u32[]{:S(2)}) collective-permute-start(bf16[256,128]{1,0:T(8,128)(2,1)S(1)} %get-tuple-element.28), channel_id=1, source_target_pairs={{0,4},{1,5},{4,0},{5,1},{8,12},{9,13},{12,8},{13,9},{2,6},{3,7},{6... | collective-permute-start | bytes 196616 | tf_op jit(solution)/shard_map/ppermute | solution.py:327
  10.7 2.2 %collective-permute-done.2.refs_0_ = bf16[128,256]{1,0:T(8,128)(2,1)S(1)} collective-permute-done((bf16[128,256]{1,0:T(8,128)(2,1)S(1)}, bf16[128,256]{1,0:T(8,128)(2,1)S(1)}, u32[]{:S(2)}, u32[]{:S(2)}) %collective-permute-start.2) | collective-permute-done | bytes 65568 | tf_op jit(solution)/shard_map/ppermute | solution.py:327
  12.9 1.3 %collective-permute-done.4.refs_2_ = bf16[256,128]{1,0:T(8,128)(2,1)S(1)} collective-permute-done((bf16[256,128]{1,0:T(8,128)(2,1)S(1)}, bf16[256,128]{1,0:T(8,128)(2,1)S(1)}, u32[]{:S(2)}, u32[]{:S(2)}) %collective-permute-start.4) | collective-permute-done | bytes 65568 | tf_op jit(solution)/shard_map/ppermute | solution.py:327
  14.2 0.1 collective-permute-start.5
  14.3 1.1 %collective-permute-done.5.refs_3_ = bf16[256,128]{1,0:T(8,128)(2,1)S(1)} collective-permute-done((bf16[256,128]{1,0:T(8,128)(2,1)S(1)}, bf16[256,128]{1,0:T(8,128)(2,1)S(1)}, u32[]{:S(2)}, u32[]{:S(2)}) %collective-permute-start.5) | collective-permute-done | bytes 65568 | tf_op jit(solution)/shard_map/ppermute | solution.py:328
  15.4 0.3 shard_map.96.mine_ref.y_ref
  15.8 0.9 %collective-permute-start.6 = (f32[96,256]{1,0:T(8,128)S(1)}, f32[96,256]{1,0:T(8,128)S(1)}, u32[]{:S(2)}, u32[]{:S(2)}) collective-permute-start(f32[96,256]{1,0:T(8,128)S(1)} %shard_map.96.mine_ref.y_ref), channel_id=1, source_target_pairs={{0,2},{2,0},{1,3},{3,1},{4,6},{6,4},{5,7},{7,5},{8,10},{10,8},{9,1... | collective-permute-start | bytes 294920 | tf_op jit(solution)/shard_map/ppermute | solution.py:275
  16.7 4.0 %collective-permute-done.6.other_ref.z_ref = f32[96,256]{1,0:T(8,128)S(1)} collective-permute-done((f32[96,256]{1,0:T(8,128)S(1)}, f32[96,256]{1,0:T(8,128)S(1)}, u32[]{:S(2)}, u32[]{:S(2)}) %collective-permute-start.6) | collective-permute-done | bytes 98336 | tf_op jit(solution)/shard_map/ppermute | solution.py:275
  20.7 0.5 %shard_map.97 = (f32[112,256]{1,0:T(8,128)S(1)}, bf16[128,256]{1,0:T(8,128)(2,1)S(1)}) custom-call(f32[96,256]{1,0:T(8,128)S(1)} %shard_map.96.mine_ref.y_ref, f32[96,256]{1,0:T(8,128)S(1)} %collective-permute-done.6.other_ref.z_ref, bf16[2,320,256]{2,1,0:T(8,128)(2,1)S(1)} %get-tuple-element.23.sx_ref, bf16[2,320,256]{2,1,0:T(8,128)(2,1)S(1)} %collective-permute-done.7.sy_ref), custom_call_target="tpu_custom_call" | custom-call | flops 40000000 | bytes 1000000 | tf_op jit(solution)/shard_map/pallas_call | solution.py:346
  21.2 1.4 %collective-permute-start.10 = (bf16[128,256]{1,0:T(8,128)(2,1)S(1)}, bf16[128,256]{1,0:T(8,128)(2,1)S(1)}, u32[]{:S(2)}, u32[]{:S(2)}) collective-permute-start(bf16[128,256]{1,0:T(8,128)(2,1)S(1)} %get-tuple-element.30), channel_id=1, source_target_pairs={{0,4},{4,0},{8,12},{12,8},{1,5},{5,1},{9,13},{13,9},{2,6},{6,2},{1... | collective-permute-start | bytes 196616 | tf_op jit(solution)/shard_map/ppermute | solution.py:275
  22.5 1.5 %collective-permute-start.9 = (bf16[128,256]{1,0:T(8,128)(2,1)S(1)}, bf16[128,256]{1,0:T(8,128)(2,1)S(1)}, u32[]{:S(2)}, u32[]{:S(2)}) collective-permute-start(bf16[128,256]{1,0:T(8,128)(2,1)S(1)} %get-tuple-element.30), channel_id=1, source_target_pairs={{0,12},{4,8},{8,4},{12,0},{1,13},{5,9},{9,5},{13,1},{2,14},{6,10},... | collective-permute-start | bytes 196616 | tf_op jit(solution)/shard_map/ppermute | solution.py:275
  24.1 0.7 %collective-permute-start.8 = (bf16[128,256]{1,0:T(8,128)(2,1)S(1)}, bf16[128,256]{1,0:T(8,128)(2,1)S(1)}, u32[]{:S(2)}, u32[]{:S(2)}) collective-permute-start(bf16[128,256]{1,0:T(8,128)(2,1)S(1)} %get-tuple-element.30), channel_id=1, source_target_pairs={{0,8},{4,12},{8,0},{12,4},{1,9},{5,13},{9,1},{13,5},{2,10},{6,14},... | collective-permute-start | bytes 196616 | tf_op jit(solution)/shard_map/ppermute | solution.py:275
  24.7 0.8 %collective-permute-done.10.refs_2_ = bf16[128,256]{1,0:T(8,128)(2,1)S(1)} collective-permute-done((bf16[128,256]{1,0:T(8,128)(2,1)S(1)}, bf16[128,256]{1,0:T(8,128)(2,1)S(1)}, u32[]{:S(2)}, u32[]{:S(2)}) %collective-permute-start.10) | collective-permute-done | bytes 65568 | tf_op jit(solution)/shard_map/ppermute | solution.py:275
  25.5 3.1 %collective-permute-done.9.refs_1_ = bf16[128,256]{1,0:T(8,128)(2,1)S(1)} collective-permute-done((bf16[128,256]{1,0:T(8,128)(2,1)S(1)}, bf16[128,256]{1,0:T(8,128)(2,1)S(1)}, u32[]{:S(2)}, u32[]{:S(2)}) %collective-permute-start.9) | collective-permute-done | bytes 65568 | tf_op jit(solution)/shard_map/ppermute | solution.py:275
  28.6 2.4 %collective-permute-done.8.refs_0_ = bf16[128,256]{1,0:T(8,128)(2,1)S(1)} collective-permute-done((bf16[128,256]{1,0:T(8,128)(2,1)S(1)}, bf16[128,256]{1,0:T(8,128)(2,1)S(1)}, u32[]{:S(2)}, u32[]{:S(2)}) %collective-permute-start.8) | collective-permute-done | bytes 65568 | tf_op jit(solution)/shard_map/ppermute | solution.py:275
  31.0 0.5 %shard_map.98 = (f32[128,256]{1,0:T(8,128)S(1)}, f32[64,64]{1,0:T(8,128)S(1)}) custom-call(f32[112,256]{1,0:T(8,128)S(1)} %get-tuple-element.29.total_ref, bf16[2,320,256]{2,1,0:T(8,128)(2,1)S(1)} %get-tuple-element.23.sx_ref, bf16[2,320,256]{2,1,0:T(8,128)(2,1)S(1)} %collective-permute-done.7.sy_ref, bf16[128,256]{1,0:T(8,128)(2,1)S(1)} %collective-permute-done.8.refs_0_, ...), custom_call_target="tpu_custom_call" | custom-call | flops 40000000 | bytes 1000000 | tf_op jit(solution)/shard_map/pallas_call | solution.py:356
  31.5 0.1 collective-permute-start.11
  31.6 1.3 %collective-permute-done.11.other_ref = f32[128,256]{1,0:T(8,128)S(1)} collective-permute-done((f32[128,256]{1,0:T(8,128)S(1)}, f32[128,256]{1,0:T(8,128)S(1)}, u32[]{:S(2)}, u32[]{:S(2)}) %collective-permute-start.11) | collective-permute-done | bytes 131104 | tf_op jit(solution)/shard_map/ppermute | solution.py:365
  32.9 0.3 shard_map.99
  33.2 0.6 %collective-permute-start.12 = (f32[32,128]{1,0:T(8,128)S(1)}, f32[32,128]{1,0:T(8,128)S(1)}, u32[]{:S(2)}, u32[]{:S(2)}) collective-permute-start(f32[32,128]{1,0:T(8,128)S(1)} %get-tuple-element.32.own_ref), channel_id=1, source_target_pairs={{0,8},{1,13},{4,12},{5,9},{8,0},{9,5},{12,4},{13,1},{2,10},{3,15},... | collective-permute-start | bytes 49160 | tf_op jit(solution)/shard_map/ppermute | solution.py:327
  33.8 2.2 %collective-permute-start.14 = (f32[16,128]{1,0:T(8,128)S(1)}, f32[16,128]{1,0:T(8,128)S(1)}, u32[]{:S(2)}, u32[]{:S(2)}) collective-permute-start(f32[16,128]{1,0:T(8,128)S(1)} %get-tuple-element.35), channel_id=1, source_target_pairs={{0,4},{1,5},{4,0},{5,1},{8,12},{9,13},{12,8},{13,9},{2,6},{3,7},{6... | collective-permute-start | bytes 24584 | tf_op jit(solution)/shard_map/ppermute | solution.py:327
  36.0 1.9 %collective-permute-done.12.refs_0_ = f32[32,128]{1,0:T(8,128)S(1)} collective-permute-done((f32[32,128]{1,0:T(8,128)S(1)}, f32[32,128]{1,0:T(8,128)S(1)}, u32[]{:S(2)}, u32[]{:S(2)}) %collective-permute-start.12) | collective-permute-done | bytes 16416 | tf_op jit(solution)/shard_map/ppermute | solution.py:327
  37.9 0.5 %collective-permute-start.15 = (f32[16,128]{1,0:T(8,128)S(1)}, f32[16,128]{1,0:T(8,128)S(1)}, u32[]{:S(2)}, u32[]{:S(2)}) collective-permute-start(f32[16,128]{1,0:T(8,128)S(1)} %collective-permute-done.14.refs_2_), channel_id=1, source_target_pairs={{0,1},{1,0},{2,3},{3,2},{4,5},{5,4},{6,7},{7,6},{8,9},{9,8},{10,11... | collective-permute-start | bytes 24584 | tf_op jit(solution)/shard_map/ppermute | solution.py:328
  38.4 0.8 %collective-permute-done.15.refs_3_ = f32[16,128]{1,0:T(8,128)S(1)} collective-permute-done((f32[16,128]{1,0:T(8,128)S(1)}, f32[16,128]{1,0:T(8,128)S(1)}, u32[]{:S(2)}, u32[]{:S(2)}) %collective-permute-start.15) | collective-permute-done | bytes 8224 | tf_op jit(solution)/shard_map/ppermute | solution.py:328
  39.2 2.1 %shard_map.100 = (f32[64,256]{1,0:T(8,128)}, f32[64,64]{1,0:T(8,128)}, f32[64,64]{1,0:T(8,128)}) custom-call(f32[32,128]{1,0:T(8,128)S(1)} %get-tuple-element.32.own_ref, f32[64,256]{1,0:T(8,128)S(1)} %get-tuple-element.33.images_ref, f32[64,64]{1,0:T(8,128)S(1)} %get-tuple-element.34.d_ref, f32[32,128]{1,0:T(8,128)S(1)} %collective-permute-done.12.refs_0_, ...), custom_call_target="tpu_custom_call" | custom-call | flops 40000000 | bytes 1000000 | tf_op jit(solution)/shard_map/pallas_call | solution.py:370
  (9 shorter events, 0.0 us)
Async XLA Ops:
  0.6 5.6 %collective-permute-start.1 = (bf16[2,256,256]{2,1,0:T(8,128)(2,1)}, bf16[2,256,256]{2,1,0:T(8,128)(2,1)S(1)}, u32[]{:S(2)}, u32[]{:S(2)}) collective-permute-start(bf16[2,256,256]{2,1,0:T(8,128)(2,1)} %t_hbm.1), channel_id=1, source_target_pairs={{0,1},{1,0},{2,3},{3,2},{4,5},{5,4},{6,7},{7,6},{8,9},{9,8},{10,11... | collective-permute-start | bytes 786440 | tf_op jit(solution)/shard_map/ppermute | solution.py:299
  2.5 2.6 %copy-start = (s32[2,2]{1,0:T(2,128)S(1)}, s32[2,2]{1,0:T(2,128)}, u32[]{:S(2)}) copy-start(s32[2,2]{1,0:T(2,128)} %i_hbm.1) | copy-start | bytes 52
  2.5 14.2 %collective-permute-start.7 = (bf16[2,320,256]{2,1,0:T(8,128)(2,1)S(1)}, bf16[2,320,256]{2,1,0:T(8,128)(2,1)S(1)}, u32[]{:S(2)}, u32[]{:S(2)}) collective-permute-start(bf16[2,320,256]{2,1,0:T(8,128)(2,1)S(1)} %get-tuple-element.23.sx_ref), channel_id=1, source_target_pairs={{0,2},{2,0},{1,3},{3,1},{4,6},{6,4},{5,7},{7,5},{8,10},{10,8},{9,1... | collective-permute-start | bytes 983048 | tf_op jit(solution)/shard_map/ppermute | solution.py:275
  5.1 1.2 %collective-permute-start = (s32[2,2]{1,0:T(2,128)S(1)}, s32[2,2]{1,0:T(2,128)S(1)}, u32[]{:S(2)}, u32[]{:S(2)}) collective-permute-start(s32[2,2]{1,0:T(2,128)S(1)} %copy-done), channel_id=1, source_target_pairs={{0,1},{1,0},{2,3},{3,2},{4,5},{5,4},{6,7},{7,6},{8,9},{9,8},{10,11... | collective-permute-start | bytes 56 | tf_op jit(solution)/shard_map/ppermute | solution.py:300
  6.5 6.4 %collective-permute-start.2 = (bf16[128,256]{1,0:T(8,128)(2,1)S(1)}, bf16[128,256]{1,0:T(8,128)(2,1)S(1)}, u32[]{:S(2)}, u32[]{:S(2)}) collective-permute-start(bf16[128,256]{1,0:T(8,128)(2,1)S(1)} %get-tuple-element.27), channel_id=1, source_target_pairs={{0,8},{1,13},{4,12},{5,9},{8,0},{9,5},{12,4},{13,1},{2,10},{3,15},... | collective-permute-start | bytes 196616 | tf_op jit(solution)/shard_map/ppermute | solution.py:327
  9.1 5.1 %collective-permute-start.4 = (bf16[256,128]{1,0:T(8,128)(2,1)S(1)}, bf16[256,128]{1,0:T(8,128)(2,1)S(1)}, u32[]{:S(2)}, u32[]{:S(2)}) collective-permute-start(bf16[256,128]{1,0:T(8,128)(2,1)S(1)} %get-tuple-element.28), channel_id=1, source_target_pairs={{0,4},{1,5},{4,0},{5,1},{8,12},{9,13},{12,8},{13,9},{2,6},{3,7},{6... | collective-permute-start | bytes 196616 | tf_op jit(solution)/shard_map/ppermute | solution.py:327
  12.9 1.4 %collective-permute-start.3 = (bf16[128,256]{1,0:T(8,128)(2,1)S(1)}, bf16[128,256]{1,0:T(8,128)(2,1)S(1)}, u32[]{:S(2)}, u32[]{:S(2)}) collective-permute-start(bf16[128,256]{1,0:T(8,128)(2,1)S(1)} %collective-permute-done.2.refs_0_), channel_id=1, source_target_pairs={{0,1},{1,0},{2,3},{3,2},{4,5},{5,4},{6,7},{7,6},{8,9},{9,8},{10,11... | collective-permute-start | bytes 196616 | tf_op jit(solution)/shard_map/ppermute | solution.py:328
  14.2 1.3 %collective-permute-start.5 = (bf16[256,128]{1,0:T(8,128)(2,1)S(1)}, bf16[256,128]{1,0:T(8,128)(2,1)S(1)}, u32[]{:S(2)}, u32[]{:S(2)}) collective-permute-start(bf16[256,128]{1,0:T(8,128)(2,1)S(1)} %collective-permute-done.4.refs_2_), channel_id=1, source_target_pairs={{0,1},{1,0},{2,3},{3,2},{4,5},{5,4},{6,7},{7,6},{8,9},{9,8},{10,11... | collective-permute-start | bytes 196616 | tf_op jit(solution)/shard_map/ppermute | solution.py:328
  15.8 4.9 %collective-permute-start.6 = (f32[96,256]{1,0:T(8,128)S(1)}, f32[96,256]{1,0:T(8,128)S(1)}, u32[]{:S(2)}, u32[]{:S(2)}) collective-permute-start(f32[96,256]{1,0:T(8,128)S(1)} %shard_map.96.mine_ref.y_ref), channel_id=1, source_target_pairs={{0,2},{2,0},{1,3},{3,1},{4,6},{6,4},{5,7},{7,5},{8,10},{10,8},{9,1... | collective-permute-start | bytes 294920 | tf_op jit(solution)/shard_map/ppermute | solution.py:275
  21.2 4.3 %collective-permute-start.10 = (bf16[128,256]{1,0:T(8,128)(2,1)S(1)}, bf16[128,256]{1,0:T(8,128)(2,1)S(1)}, u32[]{:S(2)}, u32[]{:S(2)}) collective-permute-start(bf16[128,256]{1,0:T(8,128)(2,1)S(1)} %get-tuple-element.30), channel_id=1, source_target_pairs={{0,4},{4,0},{8,12},{12,8},{1,5},{5,1},{9,13},{13,9},{2,6},{6,2},{1... | collective-permute-start | bytes 196616 | tf_op jit(solution)/shard_map/ppermute | solution.py:275
  22.5 6.1 %collective-permute-start.9 = (bf16[128,256]{1,0:T(8,128)(2,1)S(1)}, bf16[128,256]{1,0:T(8,128)(2,1)S(1)}, u32[]{:S(2)}, u32[]{:S(2)}) collective-permute-start(bf16[128,256]{1,0:T(8,128)(2,1)S(1)} %get-tuple-element.30), channel_id=1, source_target_pairs={{0,12},{4,8},{8,4},{12,0},{1,13},{5,9},{9,5},{13,1},{2,14},{6,10},... | collective-permute-start | bytes 196616 | tf_op jit(solution)/shard_map/ppermute | solution.py:275
  24.1 7.0 %collective-permute-start.8 = (bf16[128,256]{1,0:T(8,128)(2,1)S(1)}, bf16[128,256]{1,0:T(8,128)(2,1)S(1)}, u32[]{:S(2)}, u32[]{:S(2)}) collective-permute-start(bf16[128,256]{1,0:T(8,128)(2,1)S(1)} %get-tuple-element.30), channel_id=1, source_target_pairs={{0,8},{4,12},{8,0},{12,4},{1,9},{5,13},{9,1},{13,5},{2,10},{6,14},... | collective-permute-start | bytes 196616 | tf_op jit(solution)/shard_map/ppermute | solution.py:275
  31.5 1.4 %collective-permute-start.11 = (f32[128,256]{1,0:T(8,128)S(1)}, f32[128,256]{1,0:T(8,128)S(1)}, u32[]{:S(2)}, u32[]{:S(2)}) collective-permute-start(f32[128,256]{1,0:T(8,128)S(1)} %get-tuple-element.31.mine_ref), channel_id=1, source_target_pairs={{0,1},{1,0},{2,3},{3,2},{4,5},{5,4},{6,7},{7,6},{8,9},{9,8},{10,11... | collective-permute-start | bytes 393224 | tf_op jit(solution)/shard_map/ppermute | solution.py:365
  33.2 4.7 %collective-permute-start.12 = (f32[32,128]{1,0:T(8,128)S(1)}, f32[32,128]{1,0:T(8,128)S(1)}, u32[]{:S(2)}, u32[]{:S(2)}) collective-permute-start(f32[32,128]{1,0:T(8,128)S(1)} %get-tuple-element.32.own_ref), channel_id=1, source_target_pairs={{0,8},{1,13},{4,12},{5,9},{8,0},{9,5},{12,4},{13,1},{2,10},{3,15},... | collective-permute-start | bytes 49160 | tf_op jit(solution)/shard_map/ppermute | solution.py:327
  33.8 4.1 %collective-permute-start.14 = (f32[16,128]{1,0:T(8,128)S(1)}, f32[16,128]{1,0:T(8,128)S(1)}, u32[]{:S(2)}, u32[]{:S(2)}) collective-permute-start(f32[16,128]{1,0:T(8,128)S(1)} %get-tuple-element.35), channel_id=1, source_target_pairs={{0,4},{1,5},{4,0},{5,1},{8,12},{9,13},{12,8},{13,9},{2,6},{3,7},{6... | collective-permute-start | bytes 24584 | tf_op jit(solution)/shard_map/ppermute | solution.py:327
  37.9 1.3 %collective-permute-start.13 = (f32[32,128]{1,0:T(8,128)S(1)}, f32[32,128]{1,0:T(8,128)S(1)}, u32[]{:S(2)}, u32[]{:S(2)}) collective-permute-start(f32[32,128]{1,0:T(8,128)S(1)} %collective-permute-done.12.refs_0_), channel_id=1, source_target_pairs={{0,1},{1,0},{2,3},{3,2},{4,5},{5,4},{6,7},{7,6},{8,9},{9,8},{10,11... | collective-permute-start | bytes 49160 | tf_op jit(solution)/shard_map/ppermute | solution.py:328
  37.9 1.3 %collective-permute-start.15 = (f32[16,128]{1,0:T(8,128)S(1)}, f32[16,128]{1,0:T(8,128)S(1)}, u32[]{:S(2)}, u32[]{:S(2)}) collective-permute-start(f32[16,128]{1,0:T(8,128)S(1)} %collective-permute-done.14.refs_2_), channel_id=1, source_target_pairs={{0,1},{1,0},{2,3},{3,2},{4,5},{5,4},{6,7},{7,6},{8,9},{9,8},{10,11... | collective-permute-start | bytes 24584 | tf_op jit(solution)/shard_map/ppermute | solution.py:328

commit v3 on v2

--- a/solution.py
+++ b/solution.py
@@ -10,7 +10,6 @@
 f32 = jnp.float32
 bf16 = jnp.bfloat16
 GROUP = 16
-HIGHEST = lax.Precision.HIGHEST
 GRANT = 16 * 1024 * 1024
 NN = (((1,), (0,)), ((), ()))
 NT = (((1,), (1,)), ((), ()))
@@ -28,10 +27,6 @@
 def dot_split(a, b, dims):
     (ah, al), (bh, bl) = a, b
     return dot_bf16(ah, bh, dims) + dot_bf16(ah, bl, dims) + dot_bf16(al, bh, dims)
-
-
-def dot_exact(a, b, dims):
-    return lax.dot_general(a, b, dims, precision=HIGHEST, preferred_element_type=f32)
 
 
 def fold(x, parts):
@@ -267,7 +262,8 @@
     coupling_ref[...] = jnp.where((row <= column) & left, done, 0.0)[:, 0:block]
     inverse = jnp.where((row + block >= column) & ~left, done, 0.0)
     images = images_ref[...]
-    following_ref[...] = dot_exact(inverse, jnp.concatenate([images, images], axis=0), NN)
+    images = jnp.concatenate([images, images], axis=0)
+    following_ref[...] = dot_split(split(inverse), split(images), NN)
     diagonal_ref[...] = d_ref[...].T
 
 

time: 41.4 us -> 41.4 us (level)
  no operation moved by 1% of the time
where the time goes in v3:
time: 41.4 us; the launch traced here: 41.3 us
  waiting for transfers between devices  20 us (48%)
  starting transfers between devices  15.4 us (37%)
  Pallas kernels  5.13 us (12%)
  between operations  0.69 us (2%)
    ppermute x5, waiting for transfers between devices, exchange(): lax.ppermute(x, axis, [(i, i ^ distance) for i in range(lax.axis_size(axi...  10.3 us
    ppermute x5, starting transfers between devices, exchange(): lax.ppermute(x, axis, [(i, i ^ distance) for i in range(lax.axis_size(axi...  7 us
    ppermute x4, starting transfers between devices, serve(): received.append(lax.ppermute(send, ('rows', 'sub'), moves))  6.98 us
    ppermute x4, waiting for transfers between devices, serve(): received.append(lax.ppermute(send, ('rows', 'sub'), moves))  5.4 us
    pallas_call x1, Pallas kernels, local(): call(functools.partial(factor_kernel, pairs, total_rows), [(half, f32), (...  2.03 us
    ppermute x4, waiting for transfers between devices, serve(): return [y for x in received for y in (x, lax.ppermute(x, 'sub', swap))]  1.98 us
    ppermute x1, waiting for transfers between devices, local(): lax.ppermute(removed, 'sub', swap)  1.33 us
    pallas_call x1, Pallas kernels, local(): prepare(*(pltpu.with_memory_space_constraint(a, pltpu.HBM) for a in sourc...  1.29 us
  transfers between devices with their start and end apart: 16, of which 11 were waited for; matrix products, arithmetic and copies ran while one was open for 0% of the time, Pallas kernels for 5%

profile of v3, /device:TPU:0, one launch (start us, length us, event | category | flops | bytes accessed | tf_op | source)
XLA Modules:
  0.0 41.3 jit_solution(18227720342119579122)
XLA Ops:
  0.6 0.6 %collective-permute-start.1 = (bf16[2,256,256]{2,1,0:T(8,128)(2,1)}, bf16[2,256,256]{2,1,0:T(8,128)(2,1)S(1)}, u32[]{:S(2)}, u32[]{:S(2)}) collective-permute-start(bf16[2,256,256]{2,1,0:T(8,128)(2,1)} %t_hbm.1), channel_id=1, source_target_pairs={{0,1},{1,0},{2,3},{3,2},{4,5},{5,4},{6,7},{7,6},{8,9},{9,8},{10,11... | collective-permute-start | bytes 786440 | tf_op jit(solution)/shard_map/ppermute | solution.py:295
  1.2 1.3 %shard_map.94 = (f32[64,256]{1,0:T(8,128)S(1)}, f32[2,32,256]{2,1,0:T(8,128)S(1)}, bf16[2,320,256]{2,1,0:T(8,128)(2,1)S(1)}, bf16[2,256,256]{2,1,0:T(8,128)(2,1)S(1)}, s32[2,2]{1,0:T(2,128)S(1)}) custom-call(f32[64,256]{1,0:T(8,128)} %bitcast.12, f32[1,256]{1,0:T(1,128)} %bitcast.14, f32[64,256]{1,0:T(8,128)} %bitcast.13, f32[64,64]{1,0:T(8,128)} %c_hbm.1, ...), custom_call_target="tpu_custom_call" | custom-call | flops 40000000 | bytes 1000000 | tf_op jit(solution)/shard_map/pallas_call | solution.py:314
  2.5 2.6 %collective-permute-start.7 = (bf16[2,320,256]{2,1,0:T(8,128)(2,1)S(1)}, bf16[2,320,256]{2,1,0:T(8,128)(2,1)S(1)}, u32[]{:S(2)}, u32[]{:S(2)}) collective-permute-start(bf16[2,320,256]{2,1,0:T(8,128)(2,1)S(1)} %get-tuple-element.23.sx_ref), channel_id=1, source_target_pairs={{0,2},{2,0},{1,3},{3,1},{4,6},{6,4},{5,7},{7,5},{8,10},{10,8},{9,1... | collective-permute-start | bytes 983048 | tf_op jit(solution)/shard_map/ppermute | solution.py:271
  5.1 0.2 collective-permute-start
  5.3 0.9 %collective-permute-done.j_ref = s32[2,2]{1,0:T(2,128)S(1)} collective-permute-done((s32[2,2]{1,0:T(2,128)S(1)}, s32[2,2]{1,0:T(2,128)S(1)}, u32[]{:S(2)}, u32[]{:S(2)}) %collective-permute-start) | collective-permute-done | bytes 48 | tf_op jit(solution)/shard_map/ppermute | solution.py:296
  6.2 0.2 shard_map.95
  6.5 2.7 %collective-permute-start.2 = (bf16[128,256]{1,0:T(8,128)(2,1)S(1)}, bf16[128,256]{1,0:T(8,128)(2,1)S(1)}, u32[]{:S(2)}, u32[]{:S(2)}) collective-permute-start(bf16[128,256]{1,0:T(8,128)(2,1)S(1)} %get-tuple-element.27), channel_id=1, source_target_pairs={{0,8},{1,13},{4,12},{5,9},{8,0},{9,5},{12,4},{13,1},{2,10},{3,15},... | collective-permute-start | bytes 196616 | tf_op jit(solution)/shard_map/ppermute | solution.py:323
  9.1 1.6 %collective-permute-start.4 = (bf16[256,128]{1,0:T(8,128)(2,1)S(1)}, bf16[256,128]{1,0:T(8,128)(2,1)S(1)}, u32[]{:S(2)}, u32[]{:S(2)}) collective-permute-start(bf16[256,128]{1,0:T(8,128)(2,1)S(1)} %get-tuple-element.28), channel_id=1, source_target_pairs={{0,4},{1,5},{4,0},{5,1},{8,12},{9,13},{12,8},{13,9},{2,6},{3,7},{6... | collective-permute-start | bytes 196616 | tf_op jit(solution)/shard_map/ppermute | solution.py:323
  10.7 2.2 %collective-permute-done.2.refs_0_ = bf16[128,256]{1,0:T(8,128)(2,1)S(1)} collective-permute-done((bf16[128,256]{1,0:T(8,128)(2,1)S(1)}, bf16[128,256]{1,0:T(8,128)(2,1)S(1)}, u32[]{:S(2)}, u32[]{:S(2)}) %collective-permute-start.2) | collective-permute-done | bytes 65568 | tf_op jit(solution)/shard_map/ppermute | solution.py:323
  12.9 1.3 %collective-permute-done.4.refs_2_ = bf16[256,128]{1,0:T(8,128)(2,1)S(1)} collective-permute-done((bf16[256,128]{1,0:T(8,128)(2,1)S(1)}, bf16[256,128]{1,0:T(8,128)(2,1)S(1)}, u32[]{:S(2)}, u32[]{:S(2)}) %collective-permute-start.4) | collective-permute-done | bytes 65568 | tf_op jit(solution)/shard_map/ppermute | solution.py:323
  14.2 0.1 collective-permute-start.5
  14.3 1.1 %collective-permute-done.5.refs_3_ = bf16[256,128]{1,0:T(8,128)(2,1)S(1)} collective-permute-done((bf16[256,128]{1,0:T(8,128)(2,1)S(1)}, bf16[256,128]{1,0:T(8,128)(2,1)S(1)}, u32[]{:S(2)}, u32[]{:S(2)}) %collective-permute-start.5) | collective-permute-done | bytes 65568 | tf_op jit(solution)/shard_map/ppermute | solution.py:324
  15.4 0.3 shard_map.96.mine_ref.y_ref
  15.8 0.9 %collective-permute-start.6 = (f32[96,256]{1,0:T(8,128)S(1)}, f32[96,256]{1,0:T(8,128)S(1)}, u32[]{:S(2)}, u32[]{:S(2)}) collective-permute-start(f32[96,256]{1,0:T(8,128)S(1)} %shard_map.96.mine_ref.y_ref), channel_id=1, source_target_pairs={{0,2},{2,0},{1,3},{3,1},{4,6},{6,4},{5,7},{7,5},{8,10},{10,8},{9,1... | collective-permute-start | bytes 294920 | tf_op jit(solution)/shard_map/ppermute | solution.py:271
  16.7 4.0 %collective-permute-done.6.other_ref.z_ref = f32[96,256]{1,0:T(8,128)S(1)} collective-permute-done((f32[96,256]{1,0:T(8,128)S(1)}, f32[96,256]{1,0:T(8,128)S(1)}, u32[]{:S(2)}, u32[]{:S(2)}) %collective-permute-start.6) | collective-permute-done | bytes 98336 | tf_op jit(solution)/shard_map/ppermute | solution.py:271
  20.7 0.5 %shard_map.97 = (f32[112,256]{1,0:T(8,128)S(1)}, bf16[128,256]{1,0:T(8,128)(2,1)S(1)}) custom-call(f32[96,256]{1,0:T(8,128)S(1)} %shard_map.96.mine_ref.y_ref, f32[96,256]{1,0:T(8,128)S(1)} %collective-permute-done.6.other_ref.z_ref, bf16[2,320,256]{2,1,0:T(8,128)(2,1)S(1)} %get-tuple-element.23.sx_ref, bf16[2,320,256]{2,1,0:T(8,128)(2,1)S(1)} %collective-permute-done.7.sy_ref), custom_call_target="tpu_custom_call" | custom-call | flops 40000000 | bytes 1000000 | tf_op jit(solution)/shard_map/pallas_call | solution.py:342
  21.2 1.4 %collective-permute-start.10 = (bf16[128,256]{1,0:T(8,128)(2,1)S(1)}, bf16[128,256]{1,0:T(8,128)(2,1)S(1)}, u32[]{:S(2)}, u32[]{:S(2)}) collective-permute-start(bf16[128,256]{1,0:T(8,128)(2,1)S(1)} %get-tuple-element.30), channel_id=1, source_target_pairs={{0,4},{4,0},{8,12},{12,8},{1,5},{5,1},{9,13},{13,9},{2,6},{6,2},{1... | collective-permute-start | bytes 196616 | tf_op jit(solution)/shard_map/ppermute | solution.py:271
  22.5 1.5 %collective-permute-start.9 = (bf16[128,256]{1,0:T(8,128)(2,1)S(1)}, bf16[128,256]{1,0:T(8,128)(2,1)S(1)}, u32[]{:S(2)}, u32[]{:S(2)}) collective-permute-start(bf16[128,256]{1,0:T(8,128)(2,1)S(1)} %get-tuple-element.30), channel_id=1, source_target_pairs={{0,12},{4,8},{8,4},{12,0},{1,13},{5,9},{9,5},{13,1},{2,14},{6,10},... | collective-permute-start | bytes 196616 | tf_op jit(solution)/shard_map/ppermute | solution.py:271
  24.1 0.7 %collective-permute-start.8 = (bf16[128,256]{1,0:T(8,128)(2,1)S(1)}, bf16[128,256]{1,0:T(8,128)(2,1)S(1)}, u32[]{:S(2)}, u32[]{:S(2)}) collective-permute-start(bf16[128,256]{1,0:T(8,128)(2,1)S(1)} %get-tuple-element.30), channel_id=1, source_target_pairs={{0,8},{4,12},{8,0},{12,4},{1,9},{5,13},{9,1},{13,5},{2,10},{6,14},... | collective-permute-start | bytes 196616 | tf_op jit(solution)/shard_map/ppermute | solution.py:271
  24.7 0.8 %collective-permute-done.10.refs_2_ = bf16[128,256]{1,0:T(8,128)(2,1)S(1)} collective-permute-done((bf16[128,256]{1,0:T(8,128)(2,1)S(1)}, bf16[128,256]{1,0:T(8,128)(2,1)S(1)}, u32[]{:S(2)}, u32[]{:S(2)}) %collective-permute-start.10) | collective-permute-done | bytes 65568 | tf_op jit(solution)/shard_map/ppermute | solution.py:271
  25.5 3.1 %collective-permute-done.9.refs_1_ = bf16[128,256]{1,0:T(8,128)(2,1)S(1)} collective-permute-done((bf16[128,256]{1,0:T(8,128)(2,1)S(1)}, bf16[128,256]{1,0:T(8,128)(2,1)S(1)}, u32[]{:S(2)}, u32[]{:S(2)}) %collective-permute-start.9) | collective-permute-done | bytes 65568 | tf_op jit(solution)/shard_map/ppermute | solution.py:271
  28.6 2.4 %collective-permute-done.8.refs_0_ = bf16[128,256]{1,0:T(8,128)(2,1)S(1)} collective-permute-done((bf16[128,256]{1,0:T(8,128)(2,1)S(1)}, bf16[128,256]{1,0:T(8,128)(2,1)S(1)}, u32[]{:S(2)}, u32[]{:S(2)}) %collective-permute-start.8) | collective-permute-done | bytes 65568 | tf_op jit(solution)/shard_map/ppermute | solution.py:271
  31.0 0.5 %shard_map.98 = (f32[128,256]{1,0:T(8,128)S(1)}, f32[64,64]{1,0:T(8,128)S(1)}) custom-call(f32[112,256]{1,0:T(8,128)S(1)} %get-tuple-element.29.total_ref, bf16[2,320,256]{2,1,0:T(8,128)(2,1)S(1)} %get-tuple-element.23.sx_ref, bf16[2,320,256]{2,1,0:T(8,128)(2,1)S(1)} %collective-permute-done.7.sy_ref, bf16[128,256]{1,0:T(8,128)(2,1)S(1)} %collective-permute-done.8.refs_0_, ...), custom_call_target="tpu_custom_call" | custom-call | flops 40000000 | bytes 1000000 | tf_op jit(solution)/shard_map/pallas_call | solution.py:352
  31.5 0.1 collective-permute-start.11
  31.6 1.3 %collective-permute-done.11.other_ref = f32[128,256]{1,0:T(8,128)S(1)} collective-permute-done((f32[128,256]{1,0:T(8,128)S(1)}, f32[128,256]{1,0:T(8,128)S(1)}, u32[]{:S(2)}, u32[]{:S(2)}) %collective-permute-start.11) | collective-permute-done | bytes 131104 | tf_op jit(solution)/shard_map/ppermute | solution.py:361
  32.9 0.3 shard_map.99
  33.2 0.6 %collective-permute-start.12 = (f32[32,128]{1,0:T(8,128)S(1)}, f32[32,128]{1,0:T(8,128)S(1)}, u32[]{:S(2)}, u32[]{:S(2)}) collective-permute-start(f32[32,128]{1,0:T(8,128)S(1)} %get-tuple-element.32.own_ref), channel_id=1, source_target_pairs={{0,8},{1,13},{4,12},{5,9},{8,0},{9,5},{12,4},{13,1},{2,10},{3,15},... | collective-permute-start | bytes 49160 | tf_op jit(solution)/shard_map/ppermute | solution.py:323
  33.8 2.2 %collective-permute-start.14 = (f32[16,128]{1,0:T(8,128)S(1)}, f32[16,128]{1,0:T(8,128)S(1)}, u32[]{:S(2)}, u32[]{:S(2)}) collective-permute-start(f32[16,128]{1,0:T(8,128)S(1)} %get-tuple-element.35), channel_id=1, source_target_pairs={{0,4},{1,5},{4,0},{5,1},{8,12},{9,13},{12,8},{13,9},{2,6},{3,7},{6... | collective-permute-start | bytes 24584 | tf_op jit(solution)/shard_map/ppermute | solution.py:323
  36.0 1.9 %collective-permute-done.12.refs_0_ = f32[32,128]{1,0:T(8,128)S(1)} collective-permute-done((f32[32,128]{1,0:T(8,128)S(1)}, f32[32,128]{1,0:T(8,128)S(1)}, u32[]{:S(2)}, u32[]{:S(2)}) %collective-permute-start.12) | collective-permute-done | bytes 16416 | tf_op jit(solution)/shard_map/ppermute | solution.py:323
  37.9 0.5 %collective-permute-start.15 = (f32[16,128]{1,0:T(8,128)S(1)}, f32[16,128]{1,0:T(8,128)S(1)}, u32[]{:S(2)}, u32[]{:S(2)}) collective-permute-start(f32[16,128]{1,0:T(8,128)S(1)} %collective-permute-done.14.refs_2_), channel_id=1, source_target_pairs={{0,1},{1,0},{2,3},{3,2},{4,5},{5,4},{6,7},{7,6},{8,9},{9,8},{10,11... | collective-permute-start | bytes 24584 | tf_op jit(solution)/shard_map/ppermute | solution.py:324
  38.4 0.8 %collective-permute-done.15.refs_3_ = f32[16,128]{1,0:T(8,128)S(1)} collective-permute-done((f32[16,128]{1,0:T(8,128)S(1)}, f32[16,128]{1,0:T(8,128)S(1)}, u32[]{:S(2)}, u32[]{:S(2)}) %collective-permute-start.15) | collective-permute-done | bytes 8224 | tf_op jit(solution)/shard_map/ppermute | solution.py:324
  39.2 2.0 %shard_map.100 = (f32[64,256]{1,0:T(8,128)}, f32[64,64]{1,0:T(8,128)}, f32[64,64]{1,0:T(8,128)}) custom-call(f32[32,128]{1,0:T(8,128)S(1)} %get-tuple-element.32.own_ref, f32[64,256]{1,0:T(8,128)S(1)} %get-tuple-element.33.images_ref, f32[64,64]{1,0:T(8,128)S(1)} %get-tuple-element.34.d_ref, f32[32,128]{1,0:T(8,128)S(1)} %collective-permute-done.12.refs_0_, ...), custom_call_target="tpu_custom_call" | custom-call | flops 40000000 | bytes 1000000 | tf_op jit(solution)/shard_map/pallas_call | solution.py:366
  (9 shorter events, 0.0 us)
Async XLA Ops:
  0.6 5.6 %collective-permute-start.1 = (bf16[2,256,256]{2,1,0:T(8,128)(2,1)}, bf16[2,256,256]{2,1,0:T(8,128)(2,1)S(1)}, u32[]{:S(2)}, u32[]{:S(2)}) collective-permute-start(bf16[2,256,256]{2,1,0:T(8,128)(2,1)} %t_hbm.1), channel_id=1, source_target_pairs={{0,1},{1,0},{2,3},{3,2},{4,5},{5,4},{6,7},{7,6},{8,9},{9,8},{10,11... | collective-permute-start | bytes 786440 | tf_op jit(solution)/shard_map/ppermute | solution.py:295
  2.5 2.6 %copy-start = (s32[2,2]{1,0:T(2,128)S(1)}, s32[2,2]{1,0:T(2,128)}, u32[]{:S(2)}) copy-start(s32[2,2]{1,0:T(2,128)} %i_hbm.1) | copy-start | bytes 52
  2.5 14.2 %collective-permute-start.7 = (bf16[2,320,256]{2,1,0:T(8,128)(2,1)S(1)}, bf16[2,320,256]{2,1,0:T(8,128)(2,1)S(1)}, u32[]{:S(2)}, u32[]{:S(2)}) collective-permute-start(bf16[2,320,256]{2,1,0:T(8,128)(2,1)S(1)} %get-tuple-element.23.sx_ref), channel_id=1, source_target_pairs={{0,2},{2,0},{1,3},{3,1},{4,6},{6,4},{5,7},{7,5},{8,10},{10,8},{9,1... | collective-permute-start | bytes 983048 | tf_op jit(solution)/shard_map/ppermute | solution.py:271
  5.1 1.2 %collective-permute-start = (s32[2,2]{1,0:T(2,128)S(1)}, s32[2,2]{1,0:T(2,128)S(1)}, u32[]{:S(2)}, u32[]{:S(2)}) collective-permute-start(s32[2,2]{1,0:T(2,128)S(1)} %copy-done), channel_id=1, source_target_pairs={{0,1},{1,0},{2,3},{3,2},{4,5},{5,4},{6,7},{7,6},{8,9},{9,8},{10,11... | collective-permute-start | bytes 56 | tf_op jit(solution)/shard_map/ppermute | solution.py:296
  6.5 6.4 %collective-permute-start.2 = (bf16[128,256]{1,0:T(8,128)(2,1)S(1)}, bf16[128,256]{1,0:T(8,128)(2,1)S(1)}, u32[]{:S(2)}, u32[]{:S(2)}) collective-permute-start(bf16[128,256]{1,0:T(8,128)(2,1)S(1)} %get-tuple-element.27), channel_id=1, source_target_pairs={{0,8},{1,13},{4,12},{5,9},{8,0},{9,5},{12,4},{13,1},{2,10},{3,15},... | collective-permute-start | bytes 196616 | tf_op jit(solution)/shard_map/ppermute | solution.py:323
  9.1 5.1 %collective-permute-start.4 = (bf16[256,128]{1,0:T(8,128)(2,1)S(1)}, bf16[256,128]{1,0:T(8,128)(2,1)S(1)}, u32[]{:S(2)}, u32[]{:S(2)}) collective-permute-start(bf16[256,128]{1,0:T(8,128)(2,1)S(1)} %get-tuple-element.28), channel_id=1, source_target_pairs={{0,4},{1,5},{4,0},{5,1},{8,12},{9,13},{12,8},{13,9},{2,6},{3,7},{6... | collective-permute-start | bytes 196616 | tf_op jit(solution)/shard_map/ppermute | solution.py:323
  12.9 1.4 %collective-permute-start.3 = (bf16[128,256]{1,0:T(8,128)(2,1)S(1)}, bf16[128,256]{1,0:T(8,128)(2,1)S(1)}, u32[]{:S(2)}, u32[]{:S(2)}) collective-permute-start(bf16[128,256]{1,0:T(8,128)(2,1)S(1)} %collective-permute-done.2.refs_0_), channel_id=1, source_target_pairs={{0,1},{1,0},{2,3},{3,2},{4,5},{5,4},{6,7},{7,6},{8,9},{9,8},{10,11... | collective-permute-start | bytes 196616 | tf_op jit(solution)/shard_map/ppermute | solution.py:324
  14.2 1.3 %collective-permute-start.5 = (bf16[256,128]{1,0:T(8,128)(2,1)S(1)}, bf16[256,128]{1,0:T(8,128)(2,1)S(1)}, u32[]{:S(2)}, u32[]{:S(2)}) collective-permute-start(bf16[256,128]{1,0:T(8,128)(2,1)S(1)} %collective-permute-done.4.refs_2_), channel_id=1, source_target_pairs={{0,1},{1,0},{2,3},{3,2},{4,5},{5,4},{6,7},{7,6},{8,9},{9,8},{10,11... | collective-permute-start | bytes 196616 | tf_op jit(solution)/shard_map/ppermute | solution.py:324
  15.8 4.9 %collective-permute-start.6 = (f32[96,256]{1,0:T(8,128)S(1)}, f32[96,256]{1,0:T(8,128)S(1)}, u32[]{:S(2)}, u32[]{:S(2)}) collective-permute-start(f32[96,256]{1,0:T(8,128)S(1)} %shard_map.96.mine_ref.y_ref), channel_id=1, source_target_pairs={{0,2},{2,0},{1,3},{3,1},{4,6},{6,4},{5,7},{7,5},{8,10},{10,8},{9,1... | collective-permute-start | bytes 294920 | tf_op jit(solution)/shard_map/ppermute | solution.py:271
  21.2 4.3 %collective-permute-start.10 = (bf16[128,256]{1,0:T(8,128)(2,1)S(1)}, bf16[128,256]{1,0:T(8,128)(2,1)S(1)}, u32[]{:S(2)}, u32[]{:S(2)}) collective-permute-start(bf16[128,256]{1,0:T(8,128)(2,1)S(1)} %get-tuple-element.30), channel_id=1, source_target_pairs={{0,4},{4,0},{8,12},{12,8},{1,5},{5,1},{9,13},{13,9},{2,6},{6,2},{1... | collective-permute-start | bytes 196616 | tf_op jit(solution)/shard_map/ppermute | solution.py:271
  22.5 6.1 %collective-permute-start.9 = (bf16[128,256]{1,0:T(8,128)(2,1)S(1)}, bf16[128,256]{1,0:T(8,128)(2,1)S(1)}, u32[]{:S(2)}, u32[]{:S(2)}) collective-permute-start(bf16[128,256]{1,0:T(8,128)(2,1)S(1)} %get-tuple-element.30), channel_id=1, source_target_pairs={{0,12},{4,8},{8,4},{12,0},{1,13},{5,9},{9,5},{13,1},{2,14},{6,10},... | collective-permute-start | bytes 196616 | tf_op jit(solution)/shard_map/ppermute | solution.py:271
  24.1 7.0 %collective-permute-start.8 = (bf16[128,256]{1,0:T(8,128)(2,1)S(1)}, bf16[128,256]{1,0:T(8,128)(2,1)S(1)}, u32[]{:S(2)}, u32[]{:S(2)}) collective-permute-start(bf16[128,256]{1,0:T(8,128)(2,1)S(1)} %get-tuple-element.30), channel_id=1, source_target_pairs={{0,8},{4,12},{8,0},{12,4},{1,9},{5,13},{9,1},{13,5},{2,10},{6,14},... | collective-permute-start | bytes 196616 | tf_op jit(solution)/shard_map/ppermute | solution.py:271
  31.5 1.4 %collective-permute-start.11 = (f32[128,256]{1,0:T(8,128)S(1)}, f32[128,256]{1,0:T(8,128)S(1)}, u32[]{:S(2)}, u32[]{:S(2)}) collective-permute-start(f32[128,256]{1,0:T(8,128)S(1)} %get-tuple-element.31.mine_ref), channel_id=1, source_target_pairs={{0,1},{1,0},{2,3},{3,2},{4,5},{5,4},{6,7},{7,6},{8,9},{9,8},{10,11... | collective-permute-start | bytes 393224 | tf_op jit(solution)/shard_map/ppermute | solution.py:361
  33.2 4.7 %collective-permute-start.12 = (f32[32,128]{1,0:T(8,128)S(1)}, f32[32,128]{1,0:T(8,128)S(1)}, u32[]{:S(2)}, u32[]{:S(2)}) collective-permute-start(f32[32,128]{1,0:T(8,128)S(1)} %get-tuple-element.32.own_ref), channel_id=1, source_target_pairs={{0,8},{1,13},{4,12},{5,9},{8,0},{9,5},{12,4},{13,1},{2,10},{3,15},... | collective-permute-start | bytes 49160 | tf_op jit(solution)/shard_map/ppermute | solution.py:323
  33.8 4.1 %collective-permute-start.14 = (f32[16,128]{1,0:T(8,128)S(1)}, f32[16,128]{1,0:T(8,128)S(1)}, u32[]{:S(2)}, u32[]{:S(2)}) collective-permute-start(f32[16,128]{1,0:T(8,128)S(1)} %get-tuple-element.35), channel_id=1, source_target_pairs={{0,4},{1,5},{4,0},{5,1},{8,12},{9,13},{12,8},{13,9},{2,6},{3,7},{6... | collective-permute-start | bytes 24584 | tf_op jit(solution)/shard_map/ppermute | solution.py:323
  37.9 1.3 %collective-permute-start.13 = (f32[32,128]{1,0:T(8,128)S(1)}, f32[32,128]{1,0:T(8,128)S(1)}, u32[]{:S(2)}, u32[]{:S(2)}) collective-permute-start(f32[32,128]{1,0:T(8,128)S(1)} %collective-permute-done.12.refs_0_), channel_id=1, source_target_pairs={{0,1},{1,0},{2,3},{3,2},{4,5},{5,4},{6,7},{7,6},{8,9},{9,8},{10,11... | collective-permute-start | bytes 49160 | tf_op jit(solution)/shard_map/ppermute | solution.py:324
  37.9 1.3 %collective-permute-start.15 = (f32[16,128]{1,0:T(8,128)S(1)}, f32[16,128]{1,0:T(8,128)S(1)}, u32[]{:S(2)}, u32[]{:S(2)}) collective-permute-start(f32[16,128]{1,0:T(8,128)S(1)} %collective-permute-done.14.refs_2_), channel_id=1, source_target_pairs={{0,1},{1,0},{2,3},{3,2},{4,5},{5,4},{6,7},{7,6},{8,9},{9,8},{10,11... | collective-permute-start | bytes 24584 | tf_op jit(solution)/shard_map/ppermute | solution.py:324

commit v4 on v3

--- a/solution.py
+++ b/solution.py
@@ -54,7 +54,7 @@
 
 def prepare_kernel(
     x_hbm, e_hbm, p_hbm, c_hbm, s_hbm, t_hbm, i_hbm,
-    base_ref, corr_ref, sx_ref, t_ref, i_ref,
+    base_ref, corr_ref, high_ref, low_ref, t_ref, i_ref,
     x_ref, e_ref, p_ref, c_ref, s_ref, sems,
 ):
     pairs = (
@@ -73,8 +73,8 @@
     x = x_ref[...]
     xs = split(x)
     ss = split(s_ref[...])
-    for half in range(2):
-        sx_ref[half] = jnp.concatenate([ss[half], xs[half]], axis=0)
+    for k, ref in enumerate((high_ref, low_ref)):
+        ref[...] = jnp.concatenate([ss[k], xs[k]], axis=0)
     base_ref[...] = e_ref[...] * x - dot_split(split(coupling), split(p_ref[...]), NN)
     corr = dot_split(xs, ss, NT)
     chunk = corr_ref.shape[1]
@@ -97,10 +97,10 @@
     return jnp.bitwise_xor(me, jnp.where(core == 0, pair[0], pair[1]))
 
 
-def push_kernel(pairs, columns, i_ref, j_ref, sx_ref, corr_ref, t_ref, u_ref, *outs):
-    width, rows = corr_ref.shape[2], sx_ref.shape[2]
-    block = sx_ref.shape[1] - width
-    x = sx_ref[0, width:]
+def push_kernel(pairs, columns, i_ref, j_ref, high_ref, corr_ref, t_ref, u_ref, *outs):
+    width, rows = corr_ref.shape[2], high_ref.shape[1]
+    block = high_ref.shape[0] - width
+    x = high_ref[width:]
     me, core = lax.axis_index("rows"), lax.axis_index("sub")
     targets = tile_columns((i_ref, j_ref), (block, rows))
     products = [dot_bf16(x, ref[k], NN) for ref in (t_ref, u_ref) for k in range(ref.shape[0])]
@@ -125,13 +125,14 @@
             ref[...] = jnp.concatenate([message, *halves], axis=0).astype(bf16)
 
 
-def image_kernel(pairs, columns, i_ref, j_ref, base_ref, sx_ref, t_ref, u_ref, own_ref, *refs):
-    received, send_ref = refs[:-1], refs[-1]
+def image_kernel(pairs, columns, parts, i_ref, j_ref, base_ref, high_ref, low_ref, t_ref, u_ref, own_ref, *refs):
+    received, (y_ref, send_ref, late_ref) = refs[:-3], refs[-3:]
     block, rows = base_ref.shape
+    width = high_ref.shape[0] - block
     me, core = lax.axis_index("rows"), lax.axis_index("sub")
     y = base_ref[...] + own_ref[0:block]
     corr = own_ref[block:]
-    blocks = [(me, sx_ref[0, sx_ref.shape[1] - block :].astype(f32))]
+    blocks = [(me, high_ref[width:].astype(f32))]
     for k, pair in enumerate(pairs):
         mine, other = received[2 * k][...].astype(f32), received[2 * k + 1][...].astype(f32)
         if pair[0] != pair[1]:
@@ -154,8 +155,12 @@
             inside = (target >= first) & (target < first + columns)
             source = jnp.where(inside, held, source)
         y = y + dot_bf16(source.astype(bf16), tile, NT)
-    send_ref[0:block, :] = y
-    send_ref[block:, :] = corr
+    y_ref[...] = y
+    halves = split(y)
+    stored = dot_split(halves, (high_ref[:width], low_ref[:width]), NT)
+    diagonal = dot_split(halves, (high_ref[width:], low_ref[width:]), NT)
+    send_ref[...] = jnp.concatenate([stored, fold(diagonal, parts), corr], axis=0)
+    late_ref[...] = jnp.concatenate([low_ref[...], *halves], axis=0)
 
 
 def pack(total, block, small):
@@ -164,21 +169,14 @@
     return jnp.concatenate(message, axis=0).astype(bf16)
 
 
-def inner_kernel(block, parts, mine_ref, other_ref, sx_ref, sy_ref, total_ref, *send_refs):
-    width = sx_ref.shape[1] - block
-    stored = diagonal = 0.0
-    for y_ref, s_ref in ((mine_ref, sx_ref), (other_ref, sy_ref)):
-        halves = split(y_ref[0:block])
-        stored = stored + dot_split(halves, (s_ref[0, :width], s_ref[1, :width]), NT)
-        diagonal = diagonal + dot_split(halves, (s_ref[0, width:], s_ref[1, width:]), NT)
-    corr = mine_ref[block:] + other_ref[block:]
-    total = jnp.concatenate([stored, fold(diagonal, parts), corr], axis=0)
+def combine_kernel(block, small, mine_ref, other_ref, total_ref, *send_refs):
+    total = mine_ref[...] + other_ref[...]
     total_ref[...] = total
     for ref in send_refs:
-        ref[...] = pack(total, block, block // parts)
-
-
-def project_kernel(steps, block, parts, total_rows, total_ref, sx_ref, sy_ref, *refs):
+        ref[...] = pack(total, block, small)
+
+
+def project_kernel(steps, block, parts, total_rows, total_ref, high_ref, low_ref, near_ref, late_ref, *refs):
     received, (out_ref, diagonal_ref) = refs[:-2], refs[-2:]
     me, core = lax.axis_index("rows"), lax.axis_index("sub")
     small = block // parts
@@ -202,17 +200,18 @@
     diagonal_ref[...] = diagonal
     projection = stored * scale - dot_split(split(diagonal), split(corr * scale), NN)
     weights = split(jnp.concatenate([projection, jnp.where(core == 0, diagonal, 0.0)], axis=1))
-    for k, ref in enumerate((sx_ref, sy_ref)):
-        out_ref[k * block : (k + 1) * block, :] = dot_split(weights, (ref[0], ref[1]), NN)
-
-
-def gram_kernel(mine_ref, other_ref, y_ref, z_ref, images_ref, full_ref, half_ref):
+    out_ref[0:block, :] = dot_split(weights, (high_ref[...], low_ref[...]), NN)
+    out_ref[block:, :] = dot_split(weights, (near_ref[...], late_ref[: low_ref.shape[0]]), NN)
+
+
+def gram_kernel(mine_ref, other_ref, y_ref, late_ref, images_ref, full_ref, half_ref):
     block = images_ref.shape[0]
     removed = mine_ref[...] + other_ref[...]
-    images = y_ref[0:block] - removed[0:block]
+    images = y_ref[...] - removed[0:block]
     images_ref[...] = images
+    halves = late_ref[late_ref.shape[0] - 2 * block :].astype(f32)
     gram = 0.0
-    for x in (images, z_ref[0:block] - removed[block:]):
+    for x in (images, halves[0:block] + halves[block:] - removed[block:]):
         halves = split(x)
         gram = gram + dot_split(halves, halves, NT)
     gram = fold(gram, 2)
@@ -297,7 +296,7 @@
     prepare = call(
         prepare_kernel,
         [
-            (half, f32), ((2, chunk, width), f32), ((2, width + block, rows), bf16),
+            (half, f32), ((2, chunk, width), f32), *[((width + block, rows), bf16)] * 2,
             (tile_values.shape, bf16), (tile_index.shape, jnp.int32),
         ],
         "hhhhhhh",
@@ -311,7 +310,7 @@
         start_block.T, onsite_energy.reshape(1, rows), previous_block.T, previous_coupling,
         stored_basis.transpose(0, 2, 1).reshape(width, rows), tile_values, tile_index,
     )
-    base, corr, sx, tiles, index = prepare(
+    base, corr, high, low, tiles, index = prepare(
         *(pltpu.with_memory_space_constraint(a, pltpu.HBM) for a in sources)
     )
     pairs = [(step - 1, step) for step in range(bands - 1, 1, -2)] + [(1, 1)]
@@ -328,23 +327,24 @@
         [((block + chunk, rows), f32)]
         + [((2 * block, rows) if a != b else (4 * block, rows // 2), bf16) for a, b in pairs],
         "vvvvvv",
-    )(index, other_index, sx, corr, tiles, other_tiles)
-    sy = exchange(sx, "cols", 1)
+    )(index, other_index, high, corr, tiles, other_tiles)
+    near = exchange(high, "cols", 1)
     received = serve(sends[1:])
-    (mine,) = call(
-        functools.partial(image_kernel, pairs, columns),
-        [((block + chunk, rows), f32)],
-        "v" * (7 + len(received)),
-    )(index, other_index, base, sx, tiles, other_tiles, sends[0], *received)
+    small = block // parts
+    y, mine, late = call(
+        functools.partial(image_kernel, pairs, columns, parts),
+        [(half, f32), ((block + small + chunk, rows), f32), ((width + 3 * block, rows), bf16)],
+        "v" * (8 + len(received)),
+    )(index, other_index, base, high, low, tiles, other_tiles, sends[0], *received)
     other = exchange(mine, "cols", 1)
+    late = exchange(late, "cols", 1)
     distances = [2**k for k in range(1, columns.bit_length() - 1)]
-    small = block // parts
     total, *send = call(
-        functools.partial(inner_kernel, block, parts),
+        functools.partial(combine_kernel, block, small),
         [((block + small + chunk, rows), f32)]
         + [((block + 2 * small + chunk, rows), bf16)] * (not distances),
-        "vvvv",
-    )(mine, other, sx, sy)
+        "vv",
+    )(mine, other)
     for distance in distances:
         total = total + exchange(total, "cols", distance)
     send = send[0] if send else pack(total, block, small)
@@ -352,13 +352,13 @@
     removed, diagonal = call(
         functools.partial(project_kernel, steps, block, parts, total_rows),
         [((2 * block, rows), f32), ((block, block), f32)],
-        "v" * (2 + bands),
-    )(total, sx, sy, *(exchange(send, "rows", step) for step in steps))
+        "v" * (4 + bands),
+    )(total, high, low, near, late, *(exchange(send, "rows", step) for step in steps))
     images, full, part = call(
         gram_kernel,
         [(half, f32), ((block // 2, 2 * block), f32), ((block // 4, 2 * block), f32)],
         "vvvv",
-    )(removed, lax.ppermute(removed, "sub", swap), mine, other)
+    )(removed, lax.ppermute(removed, "sub", swap), y, late)
     for distance in distances:
         full = full + exchange(full, "cols", distance)
         middle = part.shape[0]

time: 41.4 us -> 43.7 us (1.056)
  starting transfers between devices: 15.4 us -> 16.8 us
  waiting for transfers between devices: 20 us -> 21 us
    ppermute x5 -> x6, starting transfers between devices: 7 us -> 8.1 us  [exchange(): lax.ppermute(x, axis, [(i, i ^ distance) for i in range(lax.axis_size(axi...]
    ppermute x1, waiting for transfers between devices: 0.95 us -> 0.01 us  [local(): other_index = lax.ppermute(tile_index, 'sub', swap)]
    ppermute x4, starting transfers between devices: 6.98 us -> 7.92 us  [serve(): received.append(lax.ppermute(send, ('rows', 'sub'), moves))]
    ppermute x5 -> x6, waiting for transfers between devices: 10.3 us -> 11.1 us  [exchange(): lax.ppermute(x, axis, [(i, i ^ distance) for i in range(lax.axis_size(axi...]
    ppermute x4, waiting for transfers between devices: 5.4 us -> 6.15 us  [serve(): received.append(lax.ppermute(send, ('rows', 'sub'), moves))]
    ppermute x4, starting transfers between devices: 0.62 us -> 0.04 us  [serve(): return [y for x in received for y in (x, lax.ppermute(x, 'sub', swap))]]
  transfers between devices with their start and end apart: 16 -> 17, of which waited for: 11 -> 11; matrix products, arithmetic and copies ran while one was open for 0% -> 0% of each run, Pallas kernels for 5% -> 3%
where the time goes in v4:
time: 43.7 us; the launch traced here: 43.6 us
  waiting for transfers between devices  21 us (48%)
  starting transfers between devices  16.8 us (38%)
  Pallas kernels  5.15 us (12%)
  between operations  0.7 us (2%)
    ppermute x6, waiting for transfers between devices, exchange(): lax.ppermute(x, axis, [(i, i ^ distance) for i in range(lax.axis_size(axi...  11.1 us
    ppermute x6, starting transfers between devices, exchange(): lax.ppermute(x, axis, [(i, i ^ distance) for i in range(lax.axis_size(axi...  8.1 us
    ppermute x4, starting transfers between devices, serve(): received.append(lax.ppermute(send, ('rows', 'sub'), moves))  7.92 us
    ppermute x4, waiting for transfers between devices, serve(): received.append(lax.ppermute(send, ('rows', 'sub'), moves))  6.15 us
    ppermute x4, waiting for transfers between devices, serve(): return [y for x in received for y in (x, lax.ppermute(x, 'sub', swap))]  2.39 us
    pallas_call x1, Pallas kernels, local(): call(functools.partial(factor_kernel, pairs, total_rows), [(half, f32), (...  2.03 us
    ppermute x1, waiting for transfers between devices, local(): lax.ppermute(removed, 'sub', swap)  1.33 us
    pallas_call x1, Pallas kernels, local(): prepare(*(pltpu.with_memory_space_constraint(a, pltpu.HBM) for a in sourc...  1.29 us
  transfers between devices with their start and end apart: 17, of which 11 were waited for; matrix products, arithmetic and copies ran while one was open for 0% of the time, Pallas kernels for 3%

profile of v4, /device:TPU:0, one launch (start us, length us, event | category | flops | bytes accessed | tf_op | source)
XLA Modules:
  0.0 43.6 jit_solution(13873951400461677008)
XLA Ops:
  0.6 0.6 %collective-permute-start.1 = (bf16[2,256,256]{2,1,0:T(8,128)(2,1)}, bf16[2,256,256]{2,1,0:T(8,128)(2,1)S(1)}, u32[]{:S(2)}, u32[]{:S(2)}) collective-permute-start(bf16[2,256,256]{2,1,0:T(8,128)(2,1)} %t_hbm.1), channel_id=1, source_target_pairs={{0,1},{1,0},{2,3},{3,2},{4,5},{5,4},{6,7},{7,6},{8,9},{9,8},{10,11... | collective-permute-start | bytes 786440 | tf_op jit(solution)/shard_map/ppermute | solution.py:294
  1.2 0.1 collective-permute-start
  1.3 1.3 %shard_map.94 = (f32[64,256]{1,0:T(8,128)S(1)}, f32[2,32,256]{2,1,0:T(8,128)S(1)}, bf16[320,256]{1,0:T(8,128)(2,1)S(1)}, bf16[320,256]{1,0:T(8,128)(2,1)S(1)}, b...) custom-call(f32[64,256]{1,0:T(8,128)} %bitcast.12, f32[1,256]{1,0:T(1,128)} %bitcast.14, f32[64,256]{1,0:T(8,128)} %bitcast.13, ...), custom_call_target="tpu_custom_call" | custom-call | flops 40000000 | bytes 1000000 | tf_op jit(solution)/shard_map/pallas_call | solution.py:313
  2.6 0.0 collective-permute-done.j_ref
  2.6 0.2 shard_map.95
  2.8 4.1 %collective-permute-start.2 = (bf16[128,256]{1,0:T(8,128)(2,1)S(1)}, bf16[128,256]{1,0:T(8,128)(2,1)S(1)}, u32[]{:S(2)}, u32[]{:S(2)}) collective-permute-start(bf16[128,256]{1,0:T(8,128)(2,1)S(1)} %get-tuple-element.32), channel_id=1, source_target_pairs={{0,8},{1,13},{4,12},{5,9},{8,0},{9,5},{12,4},{13,1},{2,10},{3,15},... | collective-permute-start | bytes 196616 | tf_op jit(solution)/shard_map/ppermute | solution.py:322
  6.9 1.6 %collective-permute-start.4 = (bf16[256,128]{1,0:T(8,128)(2,1)S(1)}, bf16[256,128]{1,0:T(8,128)(2,1)S(1)}, u32[]{:S(2)}, u32[]{:S(2)}) collective-permute-start(bf16[256,128]{1,0:T(8,128)(2,1)S(1)} %get-tuple-element.33), channel_id=1, source_target_pairs={{0,4},{1,5},{4,0},{5,1},{8,12},{9,13},{12,8},{13,9},{2,6},{3,7},{6... | collective-permute-start | bytes 196616 | tf_op jit(solution)/shard_map/ppermute | solution.py:322
  8.5 1.9 %collective-permute-done.2.refs_0_ = bf16[128,256]{1,0:T(8,128)(2,1)S(1)} collective-permute-done((bf16[128,256]{1,0:T(8,128)(2,1)S(1)}, bf16[128,256]{1,0:T(8,128)(2,1)S(1)}, u32[]{:S(2)}, u32[]{:S(2)}) %collective-permute-start.2) | collective-permute-done | bytes 65568 | tf_op jit(solution)/shard_map/ppermute | solution.py:322
  10.4 1.3 %collective-permute-done.4.refs_2_ = bf16[256,128]{1,0:T(8,128)(2,1)S(1)} collective-permute-done((bf16[256,128]{1,0:T(8,128)(2,1)S(1)}, bf16[256,128]{1,0:T(8,128)(2,1)S(1)}, u32[]{:S(2)}, u32[]{:S(2)}) %collective-permute-start.4) | collective-permute-done | bytes 65568 | tf_op jit(solution)/shard_map/ppermute | solution.py:322
  11.8 0.0 collective-permute-start.5
  11.8 1.2 %collective-permute-done.5.refs_3_ = bf16[256,128]{1,0:T(8,128)(2,1)S(1)} collective-permute-done((bf16[256,128]{1,0:T(8,128)(2,1)S(1)}, bf16[256,128]{1,0:T(8,128)(2,1)S(1)}, u32[]{:S(2)}, u32[]{:S(2)}) %collective-permute-start.5) | collective-permute-done | bytes 65568 | tf_op jit(solution)/shard_map/ppermute | solution.py:323
  13.0 0.8 %shard_map.96 = (f32[64,256]{1,0:T(8,128)S(1)}, f32[112,256]{1,0:T(8,128)S(1)}, bf16[448,256]{1,0:T(8,128)(2,1)S(1)}) custom-call(s32[2,2]{1,0:T(2,128)S(1)} %get-tuple-element.25.i_ref, s32[2,2]{1,0:T(2,128)S(1)} %collective-permute-done.j_ref, f32[64,256]{1,0:T(8,128)S(1)} %get-tuple-element.26.base_ref, bf16[320,256]{1,0:T(8,128)(2,1)S(1)} %get-tuple-element.27.high_ref, ...), custom_call_target="tpu_custom_call" | custom-call | flops 40000000 | bytes 1000000 | tf_op jit(solution)/shard_map/pallas_call | solution.py:334
  13.8 1.6 %collective-permute-start.8 = (bf16[448,256]{1,0:T(8,128)(2,1)S(1)}, bf16[448,256]{1,0:T(8,128)(2,1)S(1)}, u32[]{:S(2)}, u32[]{:S(2)}) collective-permute-start(bf16[448,256]{1,0:T(8,128)(2,1)S(1)} %get-tuple-element.36), channel_id=1, source_target_pairs={{0,2},{2,0},{1,3},{3,1},{4,6},{6,4},{5,7},{7,5},{8,10},{10,8},{9,1... | collective-permute-start | bytes 688136 | tf_op jit(solution)/shard_map/ppermute | solution.py:270
  15.4 0.5 %collective-permute-start.6 = (f32[112,256]{1,0:T(8,128)S(1)}, f32[112,256]{1,0:T(8,128)S(1)}, u32[]{:S(2)}, u32[]{:S(2)}) collective-permute-start(f32[112,256]{1,0:T(8,128)S(1)} %get-tuple-element.34.mine_ref), channel_id=1, source_target_pairs={{0,2},{2,0},{1,3},{3,1},{4,6},{6,4},{5,7},{7,5},{8,10},{10,8},{9,1... | collective-permute-start | bytes 344072 | tf_op jit(solution)/shard_map/ppermute | solution.py:270
  15.9 1.6 %collective-permute-start.7 = (bf16[320,256]{1,0:T(8,128)(2,1)S(1)}, bf16[320,256]{1,0:T(8,128)(2,1)S(1)}, u32[]{:S(2)}, u32[]{:S(2)}) collective-permute-start(bf16[320,256]{1,0:T(8,128)(2,1)S(1)} %get-tuple-element.27.high_ref), channel_id=1, source_target_pairs={{0,2},{2,0},{1,3},{3,1},{4,6},{6,4},{5,7},{7,5},{8,10},{10,8},{9,1... | collective-permute-start | bytes 491528 | tf_op jit(solution)/shard_map/ppermute | solution.py:270
  17.4 7.3 %collective-permute-done.6.other_ref = f32[112,256]{1,0:T(8,128)S(1)} collective-permute-done((f32[112,256]{1,0:T(8,128)S(1)}, f32[112,256]{1,0:T(8,128)S(1)}, u32[]{:S(2)}, u32[]{:S(2)}) %collective-permute-start.6) | collective-permute-done | bytes 114720 | tf_op jit(solution)/shard_map/ppermute | solution.py:270
  24.8 2.8 %collective-permute-start.10 = (bf16[128,256]{1,0:T(8,128)(2,1)S(1)}, bf16[128,256]{1,0:T(8,128)(2,1)S(1)}, u32[]{:S(2)}, u32[]{:S(2)}) collective-permute-start(bf16[128,256]{1,0:T(8,128)(2,1)S(1)} %get-tuple-element.37), channel_id=1, source_target_pairs={{0,12},{4,8},{8,4},{12,0},{1,13},{5,9},{9,5},{13,1},{2,14},{6,10},... | collective-permute-start | bytes 196616 | tf_op jit(solution)/shard_map/ppermute | solution.py:270
  27.6 1.6 %collective-permute-start.9 = (bf16[128,256]{1,0:T(8,128)(2,1)S(1)}, bf16[128,256]{1,0:T(8,128)(2,1)S(1)}, u32[]{:S(2)}, u32[]{:S(2)}) collective-permute-start(bf16[128,256]{1,0:T(8,128)(2,1)S(1)} %get-tuple-element.37), channel_id=1, source_target_pairs={{0,8},{4,12},{8,0},{12,4},{1,9},{5,13},{9,1},{13,5},{2,10},{6,14},... | collective-permute-start | bytes 196616 | tf_op jit(solution)/shard_map/ppermute | solution.py:270
  29.3 1.8 %collective-permute-done.10.refs_1_ = bf16[128,256]{1,0:T(8,128)(2,1)S(1)} collective-permute-done((bf16[128,256]{1,0:T(8,128)(2,1)S(1)}, bf16[128,256]{1,0:T(8,128)(2,1)S(1)}, u32[]{:S(2)}, u32[]{:S(2)}) %collective-permute-start.10) | collective-permute-done | bytes 65568 | tf_op jit(solution)/shard_map/ppermute | solution.py:270
  31.0 1.4 %collective-permute-done.11.refs_2_ = bf16[128,256]{1,0:T(8,128)(2,1)S(1)} collective-permute-done((bf16[128,256]{1,0:T(8,128)(2,1)S(1)}, bf16[128,256]{1,0:T(8,128)(2,1)S(1)}, u32[]{:S(2)}, u32[]{:S(2)}) %collective-permute-start.11) | collective-permute-done | bytes 65568 | tf_op jit(solution)/shard_map/ppermute | solution.py:270
  32.4 0.6 %collective-permute-done.9.refs_0_ = bf16[128,256]{1,0:T(8,128)(2,1)S(1)} collective-permute-done((bf16[128,256]{1,0:T(8,128)(2,1)S(1)}, bf16[128,256]{1,0:T(8,128)(2,1)S(1)}, u32[]{:S(2)}, u32[]{:S(2)}) %collective-permute-start.9) | collective-permute-done | bytes 65568 | tf_op jit(solution)/shard_map/ppermute | solution.py:270
  33.0 0.5 %shard_map.98 = (f32[128,256]{1,0:T(8,128)S(1)}, f32[64,64]{1,0:T(8,128)S(1)}) custom-call(f32[112,256]{1,0:T(8,128)S(1)} %get-tuple-element.35.total_ref, bf16[320,256]{1,0:T(8,128)(2,1)S(1)} %get-tuple-element.27.high_ref, bf16[320,256]{1,0:T(8,128)(2,1)S(1)} %get-tuple-element.28.low_ref, bf16[320,256]{1,0:T(8,128)(2,1)S(1)} %collective-permute-done.7.near_ref, ...), custom_call_target="tpu_custom_call" | custom-call | flops 40000000 | bytes 1000000 | tf_op jit(solution)/shard_map/pallas_call | solution.py:352
  33.5 0.1 collective-permute-start.12
  33.6 1.3 %collective-permute-done.12.other_ref = f32[128,256]{1,0:T(8,128)S(1)} collective-permute-done((f32[128,256]{1,0:T(8,128)S(1)}, f32[128,256]{1,0:T(8,128)S(1)}, u32[]{:S(2)}, u32[]{:S(2)}) %collective-permute-start.12) | collective-permute-done | bytes 131104 | tf_op jit(solution)/shard_map/ppermute | solution.py:361
  34.9 0.3 shard_map.99
  35.2 1.5 %collective-permute-start.13 = (f32[32,128]{1,0:T(8,128)S(1)}, f32[32,128]{1,0:T(8,128)S(1)}, u32[]{:S(2)}, u32[]{:S(2)}) collective-permute-start(f32[32,128]{1,0:T(8,128)S(1)} %get-tuple-element.40.own_ref), channel_id=1, source_target_pairs={{0,8},{1,13},{4,12},{5,9},{8,0},{9,5},{12,4},{13,1},{2,10},{3,15},... | collective-permute-start | bytes 49160 | tf_op jit(solution)/shard_map/ppermute | solution.py:322
  36.7 0.8 %collective-permute-start.15 = (f32[16,128]{1,0:T(8,128)S(1)}, f32[16,128]{1,0:T(8,128)S(1)}, u32[]{:S(2)}, u32[]{:S(2)}) collective-permute-start(f32[16,128]{1,0:T(8,128)S(1)} %get-tuple-element.43), channel_id=1, source_target_pairs={{0,4},{1,5},{4,0},{5,1},{8,12},{9,13},{12,8},{13,9},{2,6},{3,7},{6... | collective-permute-start | bytes 24584 | tf_op jit(solution)/shard_map/ppermute | solution.py:322
  37.5 2.4 %collective-permute-done.13.refs_0_ = f32[32,128]{1,0:T(8,128)S(1)} collective-permute-done((f32[32,128]{1,0:T(8,128)S(1)}, f32[32,128]{1,0:T(8,128)S(1)}, u32[]{:S(2)}, u32[]{:S(2)}) %collective-permute-start.13) | collective-permute-done | bytes 16416 | tf_op jit(solution)/shard_map/ppermute | solution.py:322
  39.9 0.5 %collective-permute-done.15.refs_2_ = f32[16,128]{1,0:T(8,128)S(1)} collective-permute-done((f32[16,128]{1,0:T(8,128)S(1)}, f32[16,128]{1,0:T(8,128)S(1)}, u32[]{:S(2)}, u32[]{:S(2)}) %collective-permute-start.15) | collective-permute-done | bytes 8224 | tf_op jit(solution)/shard_map/ppermute | solution.py:322
  40.4 0.0 collective-permute-start.16
  40.4 1.1 %collective-permute-done.16.refs_3_ = f32[16,128]{1,0:T(8,128)S(1)} collective-permute-done((f32[16,128]{1,0:T(8,128)S(1)}, f32[16,128]{1,0:T(8,128)S(1)}, u32[]{:S(2)}, u32[]{:S(2)}) %collective-permute-start.16) | collective-permute-done | bytes 8224 | tf_op jit(solution)/shard_map/ppermute | solution.py:323
  41.6 2.0 %shard_map.100 = (f32[64,256]{1,0:T(8,128)}, f32[64,64]{1,0:T(8,128)}, f32[64,64]{1,0:T(8,128)}) custom-call(f32[32,128]{1,0:T(8,128)S(1)} %get-tuple-element.40.own_ref, f32[64,256]{1,0:T(8,128)S(1)} %get-tuple-element.41.images_ref, f32[64,64]{1,0:T(8,128)S(1)} %get-tuple-element.42.d_ref, f32[32,128]{1,0:T(8,128)S(1)} %collective-permute-done.13.refs_0_, ...), custom_call_target="tpu_custom_call" | custom-call | flops 40000000 | bytes 1000000 | tf_op jit(solution)/shard_map/pallas_call | solution.py:366
  (9 shorter events, 0.0 us)
Async XLA Ops:
  0.6 2.0 %collective-permute-start.1 = (bf16[2,256,256]{2,1,0:T(8,128)(2,1)}, bf16[2,256,256]{2,1,0:T(8,128)(2,1)S(1)}, u32[]{:S(2)}, u32[]{:S(2)}) collective-permute-start(bf16[2,256,256]{2,1,0:T(8,128)(2,1)} %t_hbm.1), channel_id=1, source_target_pairs={{0,1},{1,0},{2,3},{3,2},{4,5},{5,4},{6,7},{7,6},{8,9},{9,8},{10,11... | collective-permute-start | bytes 786440 | tf_op jit(solution)/shard_map/ppermute | solution.py:294
  1.2 1.4 %collective-permute-start = (s32[2,2]{1,0:T(2,128)}, s32[2,2]{1,0:T(2,128)S(1)}, u32[]{:S(2)}, u32[]{:S(2)}) collective-permute-start(s32[2,2]{1,0:T(2,128)} %i_hbm.1), channel_id=1, source_target_pairs={{0,1},{1,0},{2,3},{3,2},{4,5},{5,4},{6,7},{7,6},{8,9},{9,8},{10,11... | collective-permute-start | bytes 56 | tf_op jit(solution)/shard_map/ppermute | solution.py:295
  2.8 7.6 %collective-permute-start.2 = (bf16[128,256]{1,0:T(8,128)(2,1)S(1)}, bf16[128,256]{1,0:T(8,128)(2,1)S(1)}, u32[]{:S(2)}, u32[]{:S(2)}) collective-permute-start(bf16[128,256]{1,0:T(8,128)(2,1)S(1)} %get-tuple-element.32), channel_id=1, source_target_pairs={{0,8},{1,13},{4,12},{5,9},{8,0},{9,5},{12,4},{13,1},{2,10},{3,15},... | collective-permute-start | bytes 196616 | tf_op jit(solution)/shard_map/ppermute | solution.py:322
  6.9 4.9 %collective-permute-start.4 = (bf16[256,128]{1,0:T(8,128)(2,1)S(1)}, bf16[256,128]{1,0:T(8,128)(2,1)S(1)}, u32[]{:S(2)}, u32[]{:S(2)}) collective-permute-start(bf16[256,128]{1,0:T(8,128)(2,1)S(1)} %get-tuple-element.33), channel_id=1, source_target_pairs={{0,4},{1,5},{4,0},{5,1},{8,12},{9,13},{12,8},{13,9},{2,6},{3,7},{6... | collective-permute-start | bytes 196616 | tf_op jit(solution)/shard_map/ppermute | solution.py:322
  10.4 1.4 %collective-permute-start.3 = (bf16[128,256]{1,0:T(8,128)(2,1)S(1)}, bf16[128,256]{1,0:T(8,128)(2,1)S(1)}, u32[]{:S(2)}, u32[]{:S(2)}) collective-permute-start(bf16[128,256]{1,0:T(8,128)(2,1)S(1)} %collective-permute-done.2.refs_0_), channel_id=1, source_target_pairs={{0,1},{1,0},{2,3},{3,2},{4,5},{5,4},{6,7},{7,6},{8,9},{9,8},{10,11... | collective-permute-start | bytes 196616 | tf_op jit(solution)/shard_map/ppermute | solution.py:323
  11.8 1.3 %collective-permute-start.5 = (bf16[256,128]{1,0:T(8,128)(2,1)S(1)}, bf16[256,128]{1,0:T(8,128)(2,1)S(1)}, u32[]{:S(2)}, u32[]{:S(2)}) collective-permute-start(bf16[256,128]{1,0:T(8,128)(2,1)S(1)} %collective-permute-done.4.refs_2_), channel_id=1, source_target_pairs={{0,1},{1,0},{2,3},{3,2},{4,5},{5,4},{6,7},{7,6},{8,9},{9,8},{10,11... | collective-permute-start | bytes 196616 | tf_op jit(solution)/shard_map/ppermute | solution.py:323
  13.8 19.2 %collective-permute-start.8 = (bf16[448,256]{1,0:T(8,128)(2,1)S(1)}, bf16[448,256]{1,0:T(8,128)(2,1)S(1)}, u32[]{:S(2)}, u32[]{:S(2)}) collective-permute-start(bf16[448,256]{1,0:T(8,128)(2,1)S(1)} %get-tuple-element.36), channel_id=1, source_target_pairs={{0,2},{2,0},{1,3},{3,1},{4,6},{6,4},{5,7},{7,5},{8,10},{10,8},{9,1... | collective-permute-start | bytes 688136 | tf_op jit(solution)/shard_map/ppermute | solution.py:270
  15.4 9.4 %collective-permute-start.6 = (f32[112,256]{1,0:T(8,128)S(1)}, f32[112,256]{1,0:T(8,128)S(1)}, u32[]{:S(2)}, u32[]{:S(2)}) collective-permute-start(f32[112,256]{1,0:T(8,128)S(1)} %get-tuple-element.34.mine_ref), channel_id=1, source_target_pairs={{0,2},{2,0},{1,3},{3,1},{4,6},{6,4},{5,7},{7,5},{8,10},{10,8},{9,1... | collective-permute-start | bytes 344072 | tf_op jit(solution)/shard_map/ppermute | solution.py:270
  15.9 13.4 %collective-permute-start.7 = (bf16[320,256]{1,0:T(8,128)(2,1)S(1)}, bf16[320,256]{1,0:T(8,128)(2,1)S(1)}, u32[]{:S(2)}, u32[]{:S(2)}) collective-permute-start(bf16[320,256]{1,0:T(8,128)(2,1)S(1)} %get-tuple-element.27.high_ref), channel_id=1, source_target_pairs={{0,2},{2,0},{1,3},{3,1},{4,6},{6,4},{5,7},{7,5},{8,10},{10,8},{9,1... | collective-permute-start | bytes 491528 | tf_op jit(solution)/shard_map/ppermute | solution.py:270
  24.8 6.2 %collective-permute-start.10 = (bf16[128,256]{1,0:T(8,128)(2,1)S(1)}, bf16[128,256]{1,0:T(8,128)(2,1)S(1)}, u32[]{:S(2)}, u32[]{:S(2)}) collective-permute-start(bf16[128,256]{1,0:T(8,128)(2,1)S(1)} %get-tuple-element.37), channel_id=1, source_target_pairs={{0,12},{4,8},{8,4},{12,0},{1,13},{5,9},{9,5},{13,1},{2,14},{6,10},... | collective-permute-start | bytes 196616 | tf_op jit(solution)/shard_map/ppermute | solution.py:270
  27.6 4.8 %collective-permute-start.11 = (bf16[128,256]{1,0:T(8,128)(2,1)S(1)}, bf16[128,256]{1,0:T(8,128)(2,1)S(1)}, u32[]{:S(2)}, u32[]{:S(2)}) collective-permute-start(bf16[128,256]{1,0:T(8,128)(2,1)S(1)} %get-tuple-element.37), channel_id=1, source_target_pairs={{0,4},{4,0},{8,12},{12,8},{1,5},{5,1},{9,13},{13,9},{2,6},{6,2},{1... | collective-permute-start | bytes 196616 | tf_op jit(solution)/shard_map/ppermute | solution.py:270
  27.6 5.4 %collective-permute-start.9 = (bf16[128,256]{1,0:T(8,128)(2,1)S(1)}, bf16[128,256]{1,0:T(8,128)(2,1)S(1)}, u32[]{:S(2)}, u32[]{:S(2)}) collective-permute-start(bf16[128,256]{1,0:T(8,128)(2,1)S(1)} %get-tuple-element.37), channel_id=1, source_target_pairs={{0,8},{4,12},{8,0},{12,4},{1,9},{5,13},{9,1},{13,5},{2,10},{6,14},... | collective-permute-start | bytes 196616 | tf_op jit(solution)/shard_map/ppermute | solution.py:270
  33.5 1.4 %collective-permute-start.12 = (f32[128,256]{1,0:T(8,128)S(1)}, f32[128,256]{1,0:T(8,128)S(1)}, u32[]{:S(2)}, u32[]{:S(2)}) collective-permute-start(f32[128,256]{1,0:T(8,128)S(1)} %get-tuple-element.38.mine_ref), channel_id=1, source_target_pairs={{0,1},{1,0},{2,3},{3,2},{4,5},{5,4},{6,7},{7,6},{8,9},{9,8},{10,11... | collective-permute-start | bytes 393224 | tf_op jit(solution)/shard_map/ppermute | solution.py:361
  35.2 4.7 %collective-permute-start.13 = (f32[32,128]{1,0:T(8,128)S(1)}, f32[32,128]{1,0:T(8,128)S(1)}, u32[]{:S(2)}, u32[]{:S(2)}) collective-permute-start(f32[32,128]{1,0:T(8,128)S(1)} %get-tuple-element.40.own_ref), channel_id=1, source_target_pairs={{0,8},{1,13},{4,12},{5,9},{8,0},{9,5},{12,4},{13,1},{2,10},{3,15},... | collective-permute-start | bytes 49160 | tf_op jit(solution)/shard_map/ppermute | solution.py:322
  36.7 3.7 %collective-permute-start.15 = (f32[16,128]{1,0:T(8,128)S(1)}, f32[16,128]{1,0:T(8,128)S(1)}, u32[]{:S(2)}, u32[]{:S(2)}) collective-permute-start(f32[16,128]{1,0:T(8,128)S(1)} %get-tuple-element.43), channel_id=1, source_target_pairs={{0,4},{1,5},{4,0},{5,1},{8,12},{9,13},{12,8},{13,9},{2,6},{3,7},{6... | collective-permute-start | bytes 24584 | tf_op jit(solution)/shard_map/ppermute | solution.py:322
  39.9 1.7 %collective-permute-start.14 = (f32[32,128]{1,0:T(8,128)S(1)}, f32[32,128]{1,0:T(8,128)S(1)}, u32[]{:S(2)}, u32[]{:S(2)}) collective-permute-start(f32[32,128]{1,0:T(8,128)S(1)} %collective-permute-done.13.refs_0_), channel_id=1, source_target_pairs={{0,1},{1,0},{2,3},{3,2},{4,5},{5,4},{6,7},{7,6},{8,9},{9,8},{10,11... | collective-permute-start | bytes 49160 | tf_op jit(solution)/shard_map/ppermute | solution.py:323
  40.4 1.2 %collective-permute-start.16 = (f32[16,128]{1,0:T(8,128)S(1)}, f32[16,128]{1,0:T(8,128)S(1)}, u32[]{:S(2)}, u32[]{:S(2)}) collective-permute-start(f32[16,128]{1,0:T(8,128)S(1)} %collective-permute-done.15.refs_2_), channel_id=1, source_target_pairs={{0,1},{1,0},{2,3},{3,2},{4,5},{5,4},{6,7},{7,6},{8,9},{9,8},{10,11... | collective-permute-start | bytes 24584 | tf_op jit(solution)/shard_map/ppermute | solution.py:323

commit v5 on v4

--- a/solution.py
+++ b/solution.py
@@ -320,7 +320,10 @@
         for send, pair in zip(sends, pairs):
             moves = [(2 * r + c, 2 * (r ^ pair[c]) + c) for r in range(bands) for c in range(2)]
             received.append(lax.ppermute(send, ("rows", "sub"), moves))
-        return [y for x in received for y in (x, lax.ppermute(x, "sub", swap))]
+        swapped = []
+        for x, pair in zip(received, pairs):
+            swapped += [x, lax.ppermute(x, "sub", swap)]
+        return swapped
 
     sends = call(
         functools.partial(push_kernel, pairs, columns),

time: 43.7 us -> 43.7 us (level)
  no operation moved by 1% of the time
where the time goes in v5:
time: 43.7 us; the launch traced here: 43.6 us
  waiting for transfers between devices  21 us (48%)
  starting transfers between devices  16.8 us (38%)
  Pallas kernels  5.15 us (12%)
  between operations  0.7 us (2%)
    ppermute x6, waiting for transfers between devices, exchange(): lax.ppermute(x, axis, [(i, i ^ distance) for i in range(lax.axis_size(axi...  11.1 us
    ppermute x6, starting transfers between devices, exchange(): lax.ppermute(x, axis, [(i, i ^ distance) for i in range(lax.axis_size(axi...  8.1 us
    ppermute x4, starting transfers between devices, serve(): received.append(lax.ppermute(send, ('rows', 'sub'), moves))  7.92 us
    ppermute x4, waiting for transfers between devices, serve(): received.append(lax.ppermute(send, ('rows', 'sub'), moves))  6.15 us
    ppermute x4, waiting for transfers between devices, serve(): swapped += [x, lax.ppermute(x, 'sub', swap)]  2.39 us
    pallas_call x1, Pallas kernels, local(): call(functools.partial(factor_kernel, pairs, total_rows), [(half, f32), (...  2.03 us
    ppermute x1, waiting for transfers between devices, local(): lax.ppermute(removed, 'sub', swap)  1.33 us
    pallas_call x1, Pallas kernels, local(): prepare(*(pltpu.with_memory_space_constraint(a, pltpu.HBM) for a in sourc...  1.29 us
  transfers between devices with their start and end apart: 17, of which 11 were waited for; matrix products, arithmetic and copies ran while one was open for 0% of the time, Pallas kernels for 3%

profile of v5, /device:TPU:0, one launch (start us, length us, event | category | flops | bytes accessed | tf_op | source)
XLA Modules:
  0.0 43.6 jit_solution(13873951400461677008)
XLA Ops:
  0.6 0.6 %collective-permute-start.1 = (bf16[2,256,256]{2,1,0:T(8,128)(2,1)}, bf16[2,256,256]{2,1,0:T(8,128)(2,1)S(1)}, u32[]{:S(2)}, u32[]{:S(2)}) collective-permute-start(bf16[2,256,256]{2,1,0:T(8,128)(2,1)} %t_hbm.1), channel_id=1, source_target_pairs={{0,1},{1,0},{2,3},{3,2},{4,5},{5,4},{6,7},{7,6},{8,9},{9,8},{10,11... | collective-permute-start | bytes 786440 | tf_op jit(solution)/shard_map/ppermute | solution.py:294
  1.2 0.1 collective-permute-start
  1.3 1.3 %shard_map.94 = (f32[64,256]{1,0:T(8,128)S(1)}, f32[2,32,256]{2,1,0:T(8,128)S(1)}, bf16[320,256]{1,0:T(8,128)(2,1)S(1)}, bf16[320,256]{1,0:T(8,128)(2,1)S(1)}, b...) custom-call(f32[64,256]{1,0:T(8,128)} %bitcast.12, f32[1,256]{1,0:T(1,128)} %bitcast.14, f32[64,256]{1,0:T(8,128)} %bitcast.13, ...), custom_call_target="tpu_custom_call" | custom-call | flops 40000000 | bytes 1000000 | tf_op jit(solution)/shard_map/pallas_call | solution.py:313
  2.6 0.0 collective-permute-done.j_ref
  2.6 0.2 shard_map.95
  2.8 4.1 %collective-permute-start.2 = (bf16[128,256]{1,0:T(8,128)(2,1)S(1)}, bf16[128,256]{1,0:T(8,128)(2,1)S(1)}, u32[]{:S(2)}, u32[]{:S(2)}) collective-permute-start(bf16[128,256]{1,0:T(8,128)(2,1)S(1)} %get-tuple-element.32), channel_id=1, source_target_pairs={{0,8},{1,13},{4,12},{5,9},{8,0},{9,5},{12,4},{13,1},{2,10},{3,15},... | collective-permute-start | bytes 196616 | tf_op jit(solution)/shard_map/ppermute | solution.py:322
  6.9 1.6 %collective-permute-start.4 = (bf16[256,128]{1,0:T(8,128)(2,1)S(1)}, bf16[256,128]{1,0:T(8,128)(2,1)S(1)}, u32[]{:S(2)}, u32[]{:S(2)}) collective-permute-start(bf16[256,128]{1,0:T(8,128)(2,1)S(1)} %get-tuple-element.33), channel_id=1, source_target_pairs={{0,4},{1,5},{4,0},{5,1},{8,12},{9,13},{12,8},{13,9},{2,6},{3,7},{6... | collective-permute-start | bytes 196616 | tf_op jit(solution)/shard_map/ppermute | solution.py:322
  8.5 1.9 %collective-permute-done.2.refs_0_ = bf16[128,256]{1,0:T(8,128)(2,1)S(1)} collective-permute-done((bf16[128,256]{1,0:T(8,128)(2,1)S(1)}, bf16[128,256]{1,0:T(8,128)(2,1)S(1)}, u32[]{:S(2)}, u32[]{:S(2)}) %collective-permute-start.2) | collective-permute-done | bytes 65568 | tf_op jit(solution)/shard_map/ppermute | solution.py:322
  10.4 1.3 %collective-permute-done.4.refs_2_ = bf16[256,128]{1,0:T(8,128)(2,1)S(1)} collective-permute-done((bf16[256,128]{1,0:T(8,128)(2,1)S(1)}, bf16[256,128]{1,0:T(8,128)(2,1)S(1)}, u32[]{:S(2)}, u32[]{:S(2)}) %collective-permute-start.4) | collective-permute-done | bytes 65568 | tf_op jit(solution)/shard_map/ppermute | solution.py:322
  11.8 0.0 collective-permute-start.5
  11.8 1.2 %collective-permute-done.5.refs_3_ = bf16[256,128]{1,0:T(8,128)(2,1)S(1)} collective-permute-done((bf16[256,128]{1,0:T(8,128)(2,1)S(1)}, bf16[256,128]{1,0:T(8,128)(2,1)S(1)}, u32[]{:S(2)}, u32[]{:S(2)}) %collective-permute-start.5) | collective-permute-done | bytes 65568 | tf_op jit(solution)/shard_map/ppermute | solution.py:325
  13.0 0.8 %shard_map.96 = (f32[64,256]{1,0:T(8,128)S(1)}, f32[112,256]{1,0:T(8,128)S(1)}, bf16[448,256]{1,0:T(8,128)(2,1)S(1)}) custom-call(s32[2,2]{1,0:T(2,128)S(1)} %get-tuple-element.25.i_ref, s32[2,2]{1,0:T(2,128)S(1)} %collective-permute-done.j_ref, f32[64,256]{1,0:T(8,128)S(1)} %get-tuple-element.26.base_ref, bf16[320,256]{1,0:T(8,128)(2,1)S(1)} %get-tuple-element.27.high_ref, ...), custom_call_target="tpu_custom_call" | custom-call | flops 40000000 | bytes 1000000 | tf_op jit(solution)/shard_map/pallas_call | solution.py:337
  13.8 1.6 %collective-permute-start.8 = (bf16[448,256]{1,0:T(8,128)(2,1)S(1)}, bf16[448,256]{1,0:T(8,128)(2,1)S(1)}, u32[]{:S(2)}, u32[]{:S(2)}) collective-permute-start(bf16[448,256]{1,0:T(8,128)(2,1)S(1)} %get-tuple-element.36), channel_id=1, source_target_pairs={{0,2},{2,0},{1,3},{3,1},{4,6},{6,4},{5,7},{7,5},{8,10},{10,8},{9,1... | collective-permute-start | bytes 688136 | tf_op jit(solution)/shard_map/ppermute | solution.py:270
  15.4 0.5 %collective-permute-start.6 = (f32[112,256]{1,0:T(8,128)S(1)}, f32[112,256]{1,0:T(8,128)S(1)}, u32[]{:S(2)}, u32[]{:S(2)}) collective-permute-start(f32[112,256]{1,0:T(8,128)S(1)} %get-tuple-element.34.mine_ref), channel_id=1, source_target_pairs={{0,2},{2,0},{1,3},{3,1},{4,6},{6,4},{5,7},{7,5},{8,10},{10,8},{9,1... | collective-permute-start | bytes 344072 | tf_op jit(solution)/shard_map/ppermute | solution.py:270
  15.9 1.6 %collective-permute-start.7 = (bf16[320,256]{1,0:T(8,128)(2,1)S(1)}, bf16[320,256]{1,0:T(8,128)(2,1)S(1)}, u32[]{:S(2)}, u32[]{:S(2)}) collective-permute-start(bf16[320,256]{1,0:T(8,128)(2,1)S(1)} %get-tuple-element.27.high_ref), channel_id=1, source_target_pairs={{0,2},{2,0},{1,3},{3,1},{4,6},{6,4},{5,7},{7,5},{8,10},{10,8},{9,1... | collective-permute-start | bytes 491528 | tf_op jit(solution)/shard_map/ppermute | solution.py:270
  17.4 7.3 %collective-permute-done.6.other_ref = f32[112,256]{1,0:T(8,128)S(1)} collective-permute-done((f32[112,256]{1,0:T(8,128)S(1)}, f32[112,256]{1,0:T(8,128)S(1)}, u32[]{:S(2)}, u32[]{:S(2)}) %collective-permute-start.6) | collective-permute-done | bytes 114720 | tf_op jit(solution)/shard_map/ppermute | solution.py:270
  24.8 2.8 %collective-permute-start.10 = (bf16[128,256]{1,0:T(8,128)(2,1)S(1)}, bf16[128,256]{1,0:T(8,128)(2,1)S(1)}, u32[]{:S(2)}, u32[]{:S(2)}) collective-permute-start(bf16[128,256]{1,0:T(8,128)(2,1)S(1)} %get-tuple-element.37), channel_id=1, source_target_pairs={{0,12},{4,8},{8,4},{12,0},{1,13},{5,9},{9,5},{13,1},{2,14},{6,10},... | collective-permute-start | bytes 196616 | tf_op jit(solution)/shard_map/ppermute | solution.py:270
  27.6 1.6 %collective-permute-start.9 = (bf16[128,256]{1,0:T(8,128)(2,1)S(1)}, bf16[128,256]{1,0:T(8,128)(2,1)S(1)}, u32[]{:S(2)}, u32[]{:S(2)}) collective-permute-start(bf16[128,256]{1,0:T(8,128)(2,1)S(1)} %get-tuple-element.37), channel_id=1, source_target_pairs={{0,8},{4,12},{8,0},{12,4},{1,9},{5,13},{9,1},{13,5},{2,10},{6,14},... | collective-permute-start | bytes 196616 | tf_op jit(solution)/shard_map/ppermute | solution.py:270
  29.3 1.8 %collective-permute-done.10.refs_1_ = bf16[128,256]{1,0:T(8,128)(2,1)S(1)} collective-permute-done((bf16[128,256]{1,0:T(8,128)(2,1)S(1)}, bf16[128,256]{1,0:T(8,128)(2,1)S(1)}, u32[]{:S(2)}, u32[]{:S(2)}) %collective-permute-start.10) | collective-permute-done | bytes 65568 | tf_op jit(solution)/shard_map/ppermute | solution.py:270
  31.0 1.4 %collective-permute-done.11.refs_2_ = bf16[128,256]{1,0:T(8,128)(2,1)S(1)} collective-permute-done((bf16[128,256]{1,0:T(8,128)(2,1)S(1)}, bf16[128,256]{1,0:T(8,128)(2,1)S(1)}, u32[]{:S(2)}, u32[]{:S(2)}) %collective-permute-start.11) | collective-permute-done | bytes 65568 | tf_op jit(solution)/shard_map/ppermute | solution.py:270
  32.4 0.6 %collective-permute-done.9.refs_0_ = bf16[128,256]{1,0:T(8,128)(2,1)S(1)} collective-permute-done((bf16[128,256]{1,0:T(8,128)(2,1)S(1)}, bf16[128,256]{1,0:T(8,128)(2,1)S(1)}, u32[]{:S(2)}, u32[]{:S(2)}) %collective-permute-start.9) | collective-permute-done | bytes 65568 | tf_op jit(solution)/shard_map/ppermute | solution.py:270
  33.0 0.5 %shard_map.98 = (f32[128,256]{1,0:T(8,128)S(1)}, f32[64,64]{1,0:T(8,128)S(1)}) custom-call(f32[112,256]{1,0:T(8,128)S(1)} %get-tuple-element.35.total_ref, bf16[320,256]{1,0:T(8,128)(2,1)S(1)} %get-tuple-element.27.high_ref, bf16[320,256]{1,0:T(8,128)(2,1)S(1)} %get-tuple-element.28.low_ref, bf16[320,256]{1,0:T(8,128)(2,1)S(1)} %collective-permute-done.7.near_ref, ...), custom_call_target="tpu_custom_call" | custom-call | flops 40000000 | bytes 1000000 | tf_op jit(solution)/shard_map/pallas_call | solution.py:355
  33.5 0.1 collective-permute-start.12
  33.6 1.3 %collective-permute-done.12.other_ref = f32[128,256]{1,0:T(8,128)S(1)} collective-permute-done((f32[128,256]{1,0:T(8,128)S(1)}, f32[128,256]{1,0:T(8,128)S(1)}, u32[]{:S(2)}, u32[]{:S(2)}) %collective-permute-start.12) | collective-permute-done | bytes 131104 | tf_op jit(solution)/shard_map/ppermute | solution.py:364
  34.9 0.3 shard_map.99
  35.2 1.5 %collective-permute-start.13 = (f32[32,128]{1,0:T(8,128)S(1)}, f32[32,128]{1,0:T(8,128)S(1)}, u32[]{:S(2)}, u32[]{:S(2)}) collective-permute-start(f32[32,128]{1,0:T(8,128)S(1)} %get-tuple-element.40.own_ref), channel_id=1, source_target_pairs={{0,8},{1,13},{4,12},{5,9},{8,0},{9,5},{12,4},{13,1},{2,10},{3,15},... | collective-permute-start | bytes 49160 | tf_op jit(solution)/shard_map/ppermute | solution.py:322
  36.7 0.8 %collective-permute-start.15 = (f32[16,128]{1,0:T(8,128)S(1)}, f32[16,128]{1,0:T(8,128)S(1)}, u32[]{:S(2)}, u32[]{:S(2)}) collective-permute-start(f32[16,128]{1,0:T(8,128)S(1)} %get-tuple-element.43), channel_id=1, source_target_pairs={{0,4},{1,5},{4,0},{5,1},{8,12},{9,13},{12,8},{13,9},{2,6},{3,7},{6... | collective-permute-start | bytes 24584 | tf_op jit(solution)/shard_map/ppermute | solution.py:322
  37.5 2.4 %collective-permute-done.13.refs_0_ = f32[32,128]{1,0:T(8,128)S(1)} collective-permute-done((f32[32,128]{1,0:T(8,128)S(1)}, f32[32,128]{1,0:T(8,128)S(1)}, u32[]{:S(2)}, u32[]{:S(2)}) %collective-permute-start.13) | collective-permute-done | bytes 16416 | tf_op jit(solution)/shard_map/ppermute | solution.py:322
  39.9 0.5 %collective-permute-done.15.refs_2_ = f32[16,128]{1,0:T(8,128)S(1)} collective-permute-done((f32[16,128]{1,0:T(8,128)S(1)}, f32[16,128]{1,0:T(8,128)S(1)}, u32[]{:S(2)}, u32[]{:S(2)}) %collective-permute-start.15) | collective-permute-done | bytes 8224 | tf_op jit(solution)/shard_map/ppermute | solution.py:322
  40.4 0.0 collective-permute-start.16
  40.4 1.1 %collective-permute-done.16.refs_3_ = f32[16,128]{1,0:T(8,128)S(1)} collective-permute-done((f32[16,128]{1,0:T(8,128)S(1)}, f32[16,128]{1,0:T(8,128)S(1)}, u32[]{:S(2)}, u32[]{:S(2)}) %collective-permute-start.16) | collective-permute-done | bytes 8224 | tf_op jit(solution)/shard_map/ppermute | solution.py:325
  41.6 2.0 %shard_map.100 = (f32[64,256]{1,0:T(8,128)}, f32[64,64]{1,0:T(8,128)}, f32[64,64]{1,0:T(8,128)}) custom-call(f32[32,128]{1,0:T(8,128)S(1)} %get-tuple-element.40.own_ref, f32[64,256]{1,0:T(8,128)S(1)} %get-tuple-element.41.images_ref, f32[64,64]{1,0:T(8,128)S(1)} %get-tuple-element.42.d_ref, f32[32,128]{1,0:T(8,128)S(1)} %collective-permute-done.13.refs_0_, ...), custom_call_target="tpu_custom_call" | custom-call | flops 40000000 | bytes 1000000 | tf_op jit(solution)/shard_map/pallas_call | solution.py:369
  (9 shorter events, 0.0 us)
Async XLA Ops:
  0.6 2.0 %collective-permute-start.1 = (bf16[2,256,256]{2,1,0:T(8,128)(2,1)}, bf16[2,256,256]{2,1,0:T(8,128)(2,1)S(1)}, u32[]{:S(2)}, u32[]{:S(2)}) collective-permute-start(bf16[2,256,256]{2,1,0:T(8,128)(2,1)} %t_hbm.1), channel_id=1, source_target_pairs={{0,1},{1,0},{2,3},{3,2},{4,5},{5,4},{6,7},{7,6},{8,9},{9,8},{10,11... | collective-permute-start | bytes 786440 | tf_op jit(solution)/shard_map/ppermute | solution.py:294
  1.2 1.4 %collective-permute-start = (s32[2,2]{1,0:T(2,128)}, s32[2,2]{1,0:T(2,128)S(1)}, u32[]{:S(2)}, u32[]{:S(2)}) collective-permute-start(s32[2,2]{1,0:T(2,128)} %i_hbm.1), channel_id=1, source_target_pairs={{0,1},{1,0},{2,3},{3,2},{4,5},{5,4},{6,7},{7,6},{8,9},{9,8},{10,11... | collective-permute-start | bytes 56 | tf_op jit(solution)/shard_map/ppermute | solution.py:295
  2.8 7.6 %collective-permute-start.2 = (bf16[128,256]{1,0:T(8,128)(2,1)S(1)}, bf16[128,256]{1,0:T(8,128)(2,1)S(1)}, u32[]{:S(2)}, u32[]{:S(2)}) collective-permute-start(bf16[128,256]{1,0:T(8,128)(2,1)S(1)} %get-tuple-element.32), channel_id=1, source_target_pairs={{0,8},{1,13},{4,12},{5,9},{8,0},{9,5},{12,4},{13,1},{2,10},{3,15},... | collective-permute-start | bytes 196616 | tf_op jit(solution)/shard_map/ppermute | solution.py:322
  6.9 4.9 %collective-permute-start.4 = (bf16[256,128]{1,0:T(8,128)(2,1)S(1)}, bf16[256,128]{1,0:T(8,128)(2,1)S(1)}, u32[]{:S(2)}, u32[]{:S(2)}) collective-permute-start(bf16[256,128]{1,0:T(8,128)(2,1)S(1)} %get-tuple-element.33), channel_id=1, source_target_pairs={{0,4},{1,5},{4,0},{5,1},{8,12},{9,13},{12,8},{13,9},{2,6},{3,7},{6... | collective-permute-start | bytes 196616 | tf_op jit(solution)/shard_map/ppermute | solution.py:322
  10.4 1.4 %collective-permute-start.3 = (bf16[128,256]{1,0:T(8,128)(2,1)S(1)}, bf16[128,256]{1,0:T(8,128)(2,1)S(1)}, u32[]{:S(2)}, u32[]{:S(2)}) collective-permute-start(bf16[128,256]{1,0:T(8,128)(2,1)S(1)} %collective-permute-done.2.refs_0_), channel_id=1, source_target_pairs={{0,1},{1,0},{2,3},{3,2},{4,5},{5,4},{6,7},{7,6},{8,9},{9,8},{10,11... | collective-permute-start | bytes 196616 | tf_op jit(solution)/shard_map/ppermute | solution.py:325
  11.8 1.3 %collective-permute-start.5 = (bf16[256,128]{1,0:T(8,128)(2,1)S(1)}, bf16[256,128]{1,0:T(8,128)(2,1)S(1)}, u32[]{:S(2)}, u32[]{:S(2)}) collective-permute-start(bf16[256,128]{1,0:T(8,128)(2,1)S(1)} %collective-permute-done.4.refs_2_), channel_id=1, source_target_pairs={{0,1},{1,0},{2,3},{3,2},{4,5},{5,4},{6,7},{7,6},{8,9},{9,8},{10,11... | collective-permute-start | bytes 196616 | tf_op jit(solution)/shard_map/ppermute | solution.py:325
  13.8 19.2 %collective-permute-start.8 = (bf16[448,256]{1,0:T(8,128)(2,1)S(1)}, bf16[448,256]{1,0:T(8,128)(2,1)S(1)}, u32[]{:S(2)}, u32[]{:S(2)}) collective-permute-start(bf16[448,256]{1,0:T(8,128)(2,1)S(1)} %get-tuple-element.36), channel_id=1, source_target_pairs={{0,2},{2,0},{1,3},{3,1},{4,6},{6,4},{5,7},{7,5},{8,10},{10,8},{9,1... | collective-permute-start | bytes 688136 | tf_op jit(solution)/shard_map/ppermute | solution.py:270
  15.4 9.4 %collective-permute-start.6 = (f32[112,256]{1,0:T(8,128)S(1)}, f32[112,256]{1,0:T(8,128)S(1)}, u32[]{:S(2)}, u32[]{:S(2)}) collective-permute-start(f32[112,256]{1,0:T(8,128)S(1)} %get-tuple-element.34.mine_ref), channel_id=1, source_target_pairs={{0,2},{2,0},{1,3},{3,1},{4,6},{6,4},{5,7},{7,5},{8,10},{10,8},{9,1... | collective-permute-start | bytes 344072 | tf_op jit(solution)/shard_map/ppermute | solution.py:270
  15.9 13.4 %collective-permute-start.7 = (bf16[320,256]{1,0:T(8,128)(2,1)S(1)}, bf16[320,256]{1,0:T(8,128)(2,1)S(1)}, u32[]{:S(2)}, u32[]{:S(2)}) collective-permute-start(bf16[320,256]{1,0:T(8,128)(2,1)S(1)} %get-tuple-element.27.high_ref), channel_id=1, source_target_pairs={{0,2},{2,0},{1,3},{3,1},{4,6},{6,4},{5,7},{7,5},{8,10},{10,8},{9,1... | collective-permute-start | bytes 491528 | tf_op jit(solution)/shard_map/ppermute | solution.py:270
  24.8 6.2 %collective-permute-start.10 = (bf16[128,256]{1,0:T(8,128)(2,1)S(1)}, bf16[128,256]{1,0:T(8,128)(2,1)S(1)}, u32[]{:S(2)}, u32[]{:S(2)}) collective-permute-start(bf16[128,256]{1,0:T(8,128)(2,1)S(1)} %get-tuple-element.37), channel_id=1, source_target_pairs={{0,12},{4,8},{8,4},{12,0},{1,13},{5,9},{9,5},{13,1},{2,14},{6,10},... | collective-permute-start | bytes 196616 | tf_op jit(solution)/shard_map/ppermute | solution.py:270
  27.6 4.8 %collective-permute-start.11 = (bf16[128,256]{1,0:T(8,128)(2,1)S(1)}, bf16[128,256]{1,0:T(8,128)(2,1)S(1)}, u32[]{:S(2)}, u32[]{:S(2)}) collective-permute-start(bf16[128,256]{1,0:T(8,128)(2,1)S(1)} %get-tuple-element.37), channel_id=1, source_target_pairs={{0,4},{4,0},{8,12},{12,8},{1,5},{5,1},{9,13},{13,9},{2,6},{6,2},{1... | collective-permute-start | bytes 196616 | tf_op jit(solution)/shard_map/ppermute | solution.py:270
  27.6 5.4 %collective-permute-start.9 = (bf16[128,256]{1,0:T(8,128)(2,1)S(1)}, bf16[128,256]{1,0:T(8,128)(2,1)S(1)}, u32[]{:S(2)}, u32[]{:S(2)}) collective-permute-start(bf16[128,256]{1,0:T(8,128)(2,1)S(1)} %get-tuple-element.37), channel_id=1, source_target_pairs={{0,8},{4,12},{8,0},{12,4},{1,9},{5,13},{9,1},{13,5},{2,10},{6,14},... | collective-permute-start | bytes 196616 | tf_op jit(solution)/shard_map/ppermute | solution.py:270
  33.5 1.4 %collective-permute-start.12 = (f32[128,256]{1,0:T(8,128)S(1)}, f32[128,256]{1,0:T(8,128)S(1)}, u32[]{:S(2)}, u32[]{:S(2)}) collective-permute-start(f32[128,256]{1,0:T(8,128)S(1)} %get-tuple-element.38.mine_ref), channel_id=1, source_target_pairs={{0,1},{1,0},{2,3},{3,2},{4,5},{5,4},{6,7},{7,6},{8,9},{9,8},{10,11... | collective-permute-start | bytes 393224 | tf_op jit(solution)/shard_map/ppermute | solution.py:364
  35.2 4.7 %collective-permute-start.13 = (f32[32,128]{1,0:T(8,128)S(1)}, f32[32,128]{1,0:T(8,128)S(1)}, u32[]{:S(2)}, u32[]{:S(2)}) collective-permute-start(f32[32,128]{1,0:T(8,128)S(1)} %get-tuple-element.40.own_ref), channel_id=1, source_target_pairs={{0,8},{1,13},{4,12},{5,9},{8,0},{9,5},{12,4},{13,1},{2,10},{3,15},... | collective-permute-start | bytes 49160 | tf_op jit(solution)/shard_map/ppermute | solution.py:322
  36.7 3.7 %collective-permute-start.15 = (f32[16,128]{1,0:T(8,128)S(1)}, f32[16,128]{1,0:T(8,128)S(1)}, u32[]{:S(2)}, u32[]{:S(2)}) collective-permute-start(f32[16,128]{1,0:T(8,128)S(1)} %get-tuple-element.43), channel_id=1, source_target_pairs={{0,4},{1,5},{4,0},{5,1},{8,12},{9,13},{12,8},{13,9},{2,6},{3,7},{6... | collective-permute-start | bytes 24584 | tf_op jit(solution)/shard_map/ppermute | solution.py:322
  39.9 1.7 %collective-permute-start.14 = (f32[32,128]{1,0:T(8,128)S(1)}, f32[32,128]{1,0:T(8,128)S(1)}, u32[]{:S(2)}, u32[]{:S(2)}) collective-permute-start(f32[32,128]{1,0:T(8,128)S(1)} %collective-permute-done.13.refs_0_), channel_id=1, source_target_pairs={{0,1},{1,0},{2,3},{3,2},{4,5},{5,4},{6,7},{7,6},{8,9},{9,8},{10,11... | collective-permute-start | bytes 49160 | tf_op jit(solution)/shard_map/ppermute | solution.py:325
  40.4 1.2 %collective-permute-start.16 = (f32[16,128]{1,0:T(8,128)S(1)}, f32[16,128]{1,0:T(8,128)S(1)}, u32[]{:S(2)}, u32[]{:S(2)}) collective-permute-start(f32[16,128]{1,0:T(8,128)S(1)} %collective-permute-done.15.refs_2_), channel_id=1, source_target_pairs={{0,1},{1,0},{2,3},{3,2},{4,5},{5,4},{6,7},{7,6},{8,9},{9,8},{10,11... | collective-permute-start | bytes 24584 | tf_op jit(solution)/shard_map/ppermute | solution.py:325

commit v6 on v5

--- a/solution.py
+++ b/solution.py
@@ -126,7 +126,7 @@
 
 
 def image_kernel(pairs, columns, parts, i_ref, j_ref, base_ref, high_ref, low_ref, t_ref, u_ref, own_ref, *refs):
-    received, (y_ref, send_ref, late_ref) = refs[:-3], refs[-3:]
+    received, (y_ref, send_ref) = refs[:-2], refs[-2:]
     block, rows = base_ref.shape
     width = high_ref.shape[0] - block
     me, core = lax.axis_index("rows"), lax.axis_index("sub")
@@ -160,7 +160,6 @@
     stored = dot_split(halves, (high_ref[:width], low_ref[:width]), NT)
     diagonal = dot_split(halves, (high_ref[width:], low_ref[width:]), NT)
     send_ref[...] = jnp.concatenate([stored, fold(diagonal, parts), corr], axis=0)
-    late_ref[...] = jnp.concatenate([low_ref[...], *halves], axis=0)
 
 
 def pack(total, block, small):
@@ -176,7 +175,7 @@
         ref[...] = pack(total, block, small)
 
 
-def project_kernel(steps, block, parts, total_rows, total_ref, high_ref, low_ref, near_ref, late_ref, *refs):
+def project_kernel(steps, block, parts, total_rows, total_ref, high_ref, low_ref, near_ref, *refs):
     received, (out_ref, diagonal_ref) = refs[:-2], refs[-2:]
     me, core = lax.axis_index("rows"), lax.axis_index("sub")
     small = block // parts
@@ -200,18 +199,19 @@
     diagonal_ref[...] = diagonal
     projection = stored * scale - dot_split(split(diagonal), split(corr * scale), NN)
     weights = split(jnp.concatenate([projection, jnp.where(core == 0, diagonal, 0.0)], axis=1))
-    out_ref[0:block, :] = dot_split(weights, (high_ref[...], low_ref[...]), NN)
-    out_ref[block:, :] = dot_split(weights, (near_ref[...], late_ref[: low_ref.shape[0]]), NN)
-
-
-def gram_kernel(mine_ref, other_ref, y_ref, late_ref, images_ref, full_ref, half_ref):
+    for k, ref in enumerate((high_ref, near_ref)):
+        rounded = dot_bf16(weights[0], ref[...], NN) + dot_bf16(weights[1], ref[...], NN)
+        out_ref[k * block : (k + 1) * block, :] = rounded
+    out_ref[2 * block :, :] = dot_bf16(weights[0], low_ref[...], NN)
+
+
+def gram_kernel(mine_ref, other_ref, y_ref, z_ref, images_ref, full_ref, half_ref):
     block = images_ref.shape[0]
     removed = mine_ref[...] + other_ref[...]
     images = y_ref[...] - removed[0:block]
-    images_ref[...] = images
-    halves = late_ref[late_ref.shape[0] - 2 * block :].astype(f32)
+    images_ref[...] = images - removed[2 * block :]
     gram = 0.0
-    for x in (images, halves[0:block] + halves[block:] - removed[block:]):
+    for x in (images, z_ref[...] - removed[block : 2 * block]):
         halves = split(x)
         gram = gram + dot_split(halves, halves, NT)
     gram = fold(gram, 2)
@@ -334,13 +334,13 @@
     near = exchange(high, "cols", 1)
     received = serve(sends[1:])
     small = block // parts
-    y, mine, late = call(
+    y, mine = call(
         functools.partial(image_kernel, pairs, columns, parts),
-        [(half, f32), ((block + small + chunk, rows), f32), ((width + 3 * block, rows), bf16)],
+        [(half, f32), ((block + small + chunk, rows), f32)],
         "v" * (8 + len(received)),
     )(index, other_index, base, high, low, tiles, other_tiles, sends[0], *received)
     other = exchange(mine, "cols", 1)
-    late = exchange(late, "cols", 1)
+    late = exchange(y, "cols", 1)
     distances = [2**k for k in range(1, columns.bit_length() - 1)]
     total, *send = call(
         functools.partial(combine_kernel, block, small),
@@ -352,11 +352,15 @@
         total = total + exchange(total, "cols", distance)
     send = send[0] if send else pack(total, block, small)
     steps = [*range(2, bands), 1]
-    removed, diagonal = call(
+    received = []
+    for step in steps:
+        received.append(exchange(send, "rows", step))
+    project = call(
         functools.partial(project_kernel, steps, block, parts, total_rows),
-        [((2 * block, rows), f32), ((block, block), f32)],
-        "v" * (4 + bands),
-    )(total, high, low, near, late, *(exchange(send, "rows", step) for step in steps))
+        [((3 * block, rows), f32), ((block, block), f32)],
+        "v" * (3 + bands),
+    )
+    removed, diagonal = project(total, high, low, near, *received)
     images, full, part = call(
         gram_kernel,
         [(half, f32), ((block // 2, 2 * block), f32), ((block // 4, 2 * block), f32)],

time: 43.7 us -> 42.9 us (0.982)
  waiting for transfers between devices: 21 us -> 20.4 us
    ppermute x1, waiting for transfers between devices: 1.33 us -> 0.01 us  [local(): lax.ppermute(removed, 'sub', swap)]
    ppermute x6, waiting for transfers between devices: 11.1 us -> 11.9 us  [exchange(): lax.ppermute(x, axis, [(i, i ^ distance) for i in range(lax.axis_size(axi...]
    ppermute x4, starting transfers between devices: 7.92 us -> 7.24 us  [serve(): received.append(lax.ppermute(send, ('rows', 'sub'), moves))]
    ppermute x4, starting transfers between devices: 0.04 us -> 0.52 us  [serve(): swapped += [x, lax.ppermute(x, 'sub', swap)]]
  transfers between devices with their start and end apart: 17 -> 17, of which waited for: 11 -> 10; matrix products, arithmetic and copies ran while one was open for 0% -> 0% of each run, Pallas kernels for 3% -> 3%
where the time goes in v6:
time: 42.9 us; the launch traced here: 42.8 us
  waiting for transfers between devices  20.4 us (48%)
  starting transfers between devices  16.6 us (39%)
  Pallas kernels  5.14 us (12%)
  between operations  0.69 us (2%)
    ppermute x6, waiting for transfers between devices, exchange(): lax.ppermute(x, axis, [(i, i ^ distance) for i in range(lax.axis_size(axi...  11.9 us
    ppermute x6, starting transfers between devices, exchange(): lax.ppermute(x, axis, [(i, i ^ distance) for i in range(lax.axis_size(axi...  8.13 us
    ppermute x4, starting transfers between devices, serve(): received.append(lax.ppermute(send, ('rows', 'sub'), moves))  7.24 us
    ppermute x4, waiting for transfers between devices, serve(): received.append(lax.ppermute(send, ('rows', 'sub'), moves))  6.34 us
    ppermute x4, waiting for transfers between devices, serve(): swapped += [x, lax.ppermute(x, 'sub', swap)]  2.07 us
    pallas_call x1, Pallas kernels, local(): call(functools.partial(factor_kernel, pairs, total_rows), [(half, f32), (...  2.03 us
    pallas_call x1, Pallas kernels, local(): prepare(*(pltpu.with_memory_space_constraint(a, pltpu.HBM) for a in sourc...  1.29 us
  transfers between devices with their start and end apart: 17, of which 10 were waited for; matrix products, arithmetic and copies ran while one was open for 0% of the time, Pallas kernels for 3%

profile of v6, /device:TPU:0, one launch (start us, length us, event | category | flops | bytes accessed | tf_op | source)
XLA Modules:
  0.0 42.8 jit_solution(7815541873316719027)
XLA Ops:
  0.6 0.6 %collective-permute-start.1 = (bf16[2,256,256]{2,1,0:T(8,128)(2,1)}, bf16[2,256,256]{2,1,0:T(8,128)(2,1)S(1)}, u32[]{:S(2)}, u32[]{:S(2)}) collective-permute-start(bf16[2,256,256]{2,1,0:T(8,128)(2,1)} %t_hbm.1), channel_id=1, source_target_pairs={{0,1},{1,0},{2,3},{3,2},{4,5},{5,4},{6,7},{7,6},{8,9},{9,8},{10,11... | collective-permute-start | bytes 786440 | tf_op jit(solution)/shard_map/ppermute | solution.py:294
  1.2 0.1 collective-permute-start
  1.3 1.3 %shard_map.94 = (f32[64,256]{1,0:T(8,128)S(1)}, f32[2,32,256]{2,1,0:T(8,128)S(1)}, bf16[320,256]{1,0:T(8,128)(2,1)S(1)}, bf16[320,256]{1,0:T(8,128)(2,1)S(1)}, b...) custom-call(f32[64,256]{1,0:T(8,128)} %bitcast.12, f32[1,256]{1,0:T(1,128)} %bitcast.14, f32[64,256]{1,0:T(8,128)} %bitcast.13, ...), custom_call_target="tpu_custom_call" | custom-call | flops 40000000 | bytes 1000000 | tf_op jit(solution)/shard_map/pallas_call | solution.py:313
  2.6 0.0 collective-permute-done.j_ref
  2.6 0.2 shard_map.95
  2.8 4.1 %collective-permute-start.2 = (bf16[128,256]{1,0:T(8,128)(2,1)S(1)}, bf16[128,256]{1,0:T(8,128)(2,1)S(1)}, u32[]{:S(2)}, u32[]{:S(2)}) collective-permute-start(bf16[128,256]{1,0:T(8,128)(2,1)S(1)} %get-tuple-element.31), channel_id=1, source_target_pairs={{0,8},{1,13},{4,12},{5,9},{8,0},{9,5},{12,4},{13,1},{2,10},{3,15},... | collective-permute-start | bytes 196616 | tf_op jit(solution)/shard_map/ppermute | solution.py:322
  6.9 1.6 %collective-permute-start.4 = (bf16[256,128]{1,0:T(8,128)(2,1)S(1)}, bf16[256,128]{1,0:T(8,128)(2,1)S(1)}, u32[]{:S(2)}, u32[]{:S(2)}) collective-permute-start(bf16[256,128]{1,0:T(8,128)(2,1)S(1)} %get-tuple-element.32), channel_id=1, source_target_pairs={{0,4},{1,5},{4,0},{5,1},{8,12},{9,13},{12,8},{13,9},{2,6},{3,7},{6... | collective-permute-start | bytes 196616 | tf_op jit(solution)/shard_map/ppermute | solution.py:322
  8.5 1.9 %collective-permute-done.2.refs_0_ = bf16[128,256]{1,0:T(8,128)(2,1)S(1)} collective-permute-done((bf16[128,256]{1,0:T(8,128)(2,1)S(1)}, bf16[128,256]{1,0:T(8,128)(2,1)S(1)}, u32[]{:S(2)}, u32[]{:S(2)}) %collective-permute-start.2) | collective-permute-done | bytes 65568 | tf_op jit(solution)/shard_map/ppermute | solution.py:322
  10.4 1.3 %collective-permute-done.4.refs_2_ = bf16[256,128]{1,0:T(8,128)(2,1)S(1)} collective-permute-done((bf16[256,128]{1,0:T(8,128)(2,1)S(1)}, bf16[256,128]{1,0:T(8,128)(2,1)S(1)}, u32[]{:S(2)}, u32[]{:S(2)}) %collective-permute-start.4) | collective-permute-done | bytes 65568 | tf_op jit(solution)/shard_map/ppermute | solution.py:322
  11.8 0.0 collective-permute-start.5
  11.8 1.2 %collective-permute-done.5.refs_3_ = bf16[256,128]{1,0:T(8,128)(2,1)S(1)} collective-permute-done((bf16[256,128]{1,0:T(8,128)(2,1)S(1)}, bf16[256,128]{1,0:T(8,128)(2,1)S(1)}, u32[]{:S(2)}, u32[]{:S(2)}) %collective-permute-start.5) | collective-permute-done | bytes 65568 | tf_op jit(solution)/shard_map/ppermute | solution.py:325
  13.0 0.8 %shard_map.96 = (f32[64,256]{1,0:T(8,128)S(1)}, f32[112,256]{1,0:T(8,128)S(1)}) custom-call(s32[2,2]{1,0:T(2,128)S(1)} %get-tuple-element.24.i_ref, s32[2,2]{1,0:T(2,128)S(1)} %collective-permute-done.j_ref, f32[64,256]{1,0:T(8,128)S(1)} %get-tuple-element.25.base_ref, bf16[320,256]{1,0:T(8,128)(2,1)S(1)} %get-tuple-element.26.high_ref, ...), custom_call_target="tpu_custom_call" | custom-call | flops 40000000 | bytes 1000000 | tf_op jit(solution)/shard_map/pallas_call | solution.py:337
  13.8 1.6 %collective-permute-start.6 = (f32[112,256]{1,0:T(8,128)S(1)}, f32[112,256]{1,0:T(8,128)S(1)}, u32[]{:S(2)}, u32[]{:S(2)}) collective-permute-start(f32[112,256]{1,0:T(8,128)S(1)} %get-tuple-element.33.mine_ref), channel_id=1, source_target_pairs={{0,2},{2,0},{1,3},{3,1},{4,6},{6,4},{5,7},{7,5},{8,10},{10,8},{9,1... | collective-permute-start | bytes 344072 | tf_op jit(solution)/shard_map/ppermute | solution.py:270
  15.4 0.5 %collective-permute-start.7 = (bf16[320,256]{1,0:T(8,128)(2,1)S(1)}, bf16[320,256]{1,0:T(8,128)(2,1)S(1)}, u32[]{:S(2)}, u32[]{:S(2)}) collective-permute-start(bf16[320,256]{1,0:T(8,128)(2,1)S(1)} %get-tuple-element.26.high_ref), channel_id=1, source_target_pairs={{0,2},{2,0},{1,3},{3,1},{4,6},{6,4},{5,7},{7,5},{8,10},{10,8},{9,1... | collective-permute-start | bytes 491528 | tf_op jit(solution)/shard_map/ppermute | solution.py:270
  15.9 4.0 %collective-permute-done.6.other_ref = f32[112,256]{1,0:T(8,128)S(1)} collective-permute-done((f32[112,256]{1,0:T(8,128)S(1)}, f32[112,256]{1,0:T(8,128)S(1)}, u32[]{:S(2)}, u32[]{:S(2)}) %collective-permute-start.6) | collective-permute-done | bytes 114720 | tf_op jit(solution)/shard_map/ppermute | solution.py:270
  19.9 1.6 %collective-permute-start.10 = (bf16[128,256]{1,0:T(8,128)(2,1)S(1)}, bf16[128,256]{1,0:T(8,128)(2,1)S(1)}, u32[]{:S(2)}, u32[]{:S(2)}) collective-permute-start(bf16[128,256]{1,0:T(8,128)(2,1)S(1)} %get-tuple-element.35), channel_id=1, source_target_pairs={{0,4},{4,0},{8,12},{12,8},{1,5},{5,1},{9,13},{13,9},{2,6},{6,2},{1... | collective-permute-start | bytes 196616 | tf_op jit(solution)/shard_map/ppermute | solution.py:270
  21.5 1.8 %collective-permute-start.8 = (bf16[128,256]{1,0:T(8,128)(2,1)S(1)}, bf16[128,256]{1,0:T(8,128)(2,1)S(1)}, u32[]{:S(2)}, u32[]{:S(2)}) collective-permute-start(bf16[128,256]{1,0:T(8,128)(2,1)S(1)} %get-tuple-element.35), channel_id=1, source_target_pairs={{0,8},{4,12},{8,0},{12,4},{1,9},{5,13},{9,1},{13,5},{2,10},{6,14},... | collective-permute-start | bytes 196616 | tf_op jit(solution)/shard_map/ppermute | solution.py:270
  23.3 1.1 %collective-permute-start.9 = (bf16[128,256]{1,0:T(8,128)(2,1)S(1)}, bf16[128,256]{1,0:T(8,128)(2,1)S(1)}, u32[]{:S(2)}, u32[]{:S(2)}) collective-permute-start(bf16[128,256]{1,0:T(8,128)(2,1)S(1)} %get-tuple-element.35), channel_id=1, source_target_pairs={{0,12},{4,8},{8,4},{12,0},{1,13},{5,9},{9,5},{13,1},{2,14},{6,10},... | collective-permute-start | bytes 196616 | tf_op jit(solution)/shard_map/ppermute | solution.py:270
  24.3 0.5 %collective-permute-done.10.refs_2_ = bf16[128,256]{1,0:T(8,128)(2,1)S(1)} collective-permute-done((bf16[128,256]{1,0:T(8,128)(2,1)S(1)}, bf16[128,256]{1,0:T(8,128)(2,1)S(1)}, u32[]{:S(2)}, u32[]{:S(2)}) %collective-permute-start.10) | collective-permute-done | bytes 65568 | tf_op jit(solution)/shard_map/ppermute | solution.py:270
  24.9 3.1 %collective-permute-done.8.refs_0_ = bf16[128,256]{1,0:T(8,128)(2,1)S(1)} collective-permute-done((bf16[128,256]{1,0:T(8,128)(2,1)S(1)}, bf16[128,256]{1,0:T(8,128)(2,1)S(1)}, u32[]{:S(2)}, u32[]{:S(2)}) %collective-permute-start.8) | collective-permute-done | bytes 65568 | tf_op jit(solution)/shard_map/ppermute | solution.py:270
  28.0 1.4 %collective-permute-done.9.refs_1_ = bf16[128,256]{1,0:T(8,128)(2,1)S(1)} collective-permute-done((bf16[128,256]{1,0:T(8,128)(2,1)S(1)}, bf16[128,256]{1,0:T(8,128)(2,1)S(1)}, u32[]{:S(2)}, u32[]{:S(2)}) %collective-permute-start.9) | collective-permute-done | bytes 65568 | tf_op jit(solution)/shard_map/ppermute | solution.py:270
  29.4 0.5 %shard_map.98 = (f32[192,256]{1,0:T(8,128)S(1)}, f32[64,64]{1,0:T(8,128)S(1)}) custom-call(f32[112,256]{1,0:T(8,128)S(1)} %get-tuple-element.34.total_ref, bf16[320,256]{1,0:T(8,128)(2,1)S(1)} %get-tuple-element.26.high_ref, bf16[320,256]{1,0:T(8,128)(2,1)S(1)} %get-tuple-element.27.low_ref, bf16[320,256]{1,0:T(8,128)(2,1)S(1)} %collective-permute-done.7.near_ref, ...), custom_call_target="tpu_custom_call" | custom-call | flops 40000000 | bytes 1000000 | tf_op jit(solution)/shard_map/pallas_call | solution.py:363
  29.9 0.1 collective-permute-start.11
  30.0 1.6 %collective-permute-start.12 = (f32[64,256]{1,0:T(8,128)S(1)}, f32[64,256]{1,0:T(8,128)S(1)}, u32[]{:S(2)}, u32[]{:S(2)}) collective-permute-start(f32[64,256]{1,0:T(8,128)S(1)} %get-tuple-element.37.y_ref), channel_id=1, source_target_pairs={{0,2},{2,0},{1,3},{3,1},{4,6},{6,4},{5,7},{7,5},{8,10},{10,8},{9,1... | collective-permute-start | bytes 196616 | tf_op jit(solution)/shard_map/ppermute | solution.py:270
  31.6 2.9 %collective-permute-done.12.z_ref = f32[64,256]{1,0:T(8,128)S(1)} collective-permute-done((f32[64,256]{1,0:T(8,128)S(1)}, f32[64,256]{1,0:T(8,128)S(1)}, u32[]{:S(2)}, u32[]{:S(2)}) %collective-permute-start.12) | collective-permute-done | bytes 65568 | tf_op jit(solution)/shard_map/ppermute | solution.py:270
  34.5 0.3 shard_map.99
  34.8 0.5 %collective-permute-start.13 = (f32[32,128]{1,0:T(8,128)S(1)}, f32[32,128]{1,0:T(8,128)S(1)}, u32[]{:S(2)}, u32[]{:S(2)}) collective-permute-start(f32[32,128]{1,0:T(8,128)S(1)} %get-tuple-element.38.own_ref), channel_id=1, source_target_pairs={{0,8},{1,13},{4,12},{5,9},{8,0},{9,5},{12,4},{13,1},{2,10},{3,15},... | collective-permute-start | bytes 49160 | tf_op jit(solution)/shard_map/ppermute | solution.py:322
  35.3 1.1 %collective-permute-start.15 = (f32[16,128]{1,0:T(8,128)S(1)}, f32[16,128]{1,0:T(8,128)S(1)}, u32[]{:S(2)}, u32[]{:S(2)}) collective-permute-start(f32[16,128]{1,0:T(8,128)S(1)} %get-tuple-element.41), channel_id=1, source_target_pairs={{0,4},{1,5},{4,0},{5,1},{8,12},{9,13},{12,8},{13,9},{2,6},{3,7},{6... | collective-permute-start | bytes 24584 | tf_op jit(solution)/shard_map/ppermute | solution.py:322
  36.3 3.1 %collective-permute-done.13.refs_0_ = f32[32,128]{1,0:T(8,128)S(1)} collective-permute-done((f32[32,128]{1,0:T(8,128)S(1)}, f32[32,128]{1,0:T(8,128)S(1)}, u32[]{:S(2)}, u32[]{:S(2)}) %collective-permute-start.13) | collective-permute-done | bytes 16416 | tf_op jit(solution)/shard_map/ppermute | solution.py:322
  39.4 0.5 %collective-permute-start.16 = (f32[16,128]{1,0:T(8,128)S(1)}, f32[16,128]{1,0:T(8,128)S(1)}, u32[]{:S(2)}, u32[]{:S(2)}) collective-permute-start(f32[16,128]{1,0:T(8,128)S(1)} %collective-permute-done.15.refs_2_), channel_id=1, source_target_pairs={{0,1},{1,0},{2,3},{3,2},{4,5},{5,4},{6,7},{7,6},{8,9},{9,8},{10,11... | collective-permute-start | bytes 24584 | tf_op jit(solution)/shard_map/ppermute | solution.py:325
  39.9 0.8 %collective-permute-done.16.refs_3_ = f32[16,128]{1,0:T(8,128)S(1)} collective-permute-done((f32[16,128]{1,0:T(8,128)S(1)}, f32[16,128]{1,0:T(8,128)S(1)}, u32[]{:S(2)}, u32[]{:S(2)}) %collective-permute-start.16) | collective-permute-done | bytes 8224 | tf_op jit(solution)/shard_map/ppermute | solution.py:325
  40.8 2.0 %shard_map.100 = (f32[64,256]{1,0:T(8,128)}, f32[64,64]{1,0:T(8,128)}, f32[64,64]{1,0:T(8,128)}) custom-call(f32[32,128]{1,0:T(8,128)S(1)} %get-tuple-element.38.own_ref, f32[64,256]{1,0:T(8,128)S(1)} %get-tuple-element.39.images_ref, f32[64,64]{1,0:T(8,128)S(1)} %get-tuple-element.40.d_ref, f32[32,128]{1,0:T(8,128)S(1)} %collective-permute-done.13.refs_0_, ...), custom_call_target="tpu_custom_call" | custom-call | flops 40000000 | bytes 1000000 | tf_op jit(solution)/shard_map/pallas_call | solution.py:373
  (9 shorter events, 0.0 us)
Async XLA Ops:
  0.6 2.0 %collective-permute-start.1 = (bf16[2,256,256]{2,1,0:T(8,128)(2,1)}, bf16[2,256,256]{2,1,0:T(8,128)(2,1)S(1)}, u32[]{:S(2)}, u32[]{:S(2)}) collective-permute-start(bf16[2,256,256]{2,1,0:T(8,128)(2,1)} %t_hbm.1), channel_id=1, source_target_pairs={{0,1},{1,0},{2,3},{3,2},{4,5},{5,4},{6,7},{7,6},{8,9},{9,8},{10,11... | collective-permute-start | bytes 786440 | tf_op jit(solution)/shard_map/ppermute | solution.py:294
  1.2 1.4 %collective-permute-start = (s32[2,2]{1,0:T(2,128)}, s32[2,2]{1,0:T(2,128)S(1)}, u32[]{:S(2)}, u32[]{:S(2)}) collective-permute-start(s32[2,2]{1,0:T(2,128)} %i_hbm.1), channel_id=1, source_target_pairs={{0,1},{1,0},{2,3},{3,2},{4,5},{5,4},{6,7},{7,6},{8,9},{9,8},{10,11... | collective-permute-start | bytes 56 | tf_op jit(solution)/shard_map/ppermute | solution.py:295
  2.8 7.6 %collective-permute-start.2 = (bf16[128,256]{1,0:T(8,128)(2,1)S(1)}, bf16[128,256]{1,0:T(8,128)(2,1)S(1)}, u32[]{:S(2)}, u32[]{:S(2)}) collective-permute-start(bf16[128,256]{1,0:T(8,128)(2,1)S(1)} %get-tuple-element.31), channel_id=1, source_target_pairs={{0,8},{1,13},{4,12},{5,9},{8,0},{9,5},{12,4},{13,1},{2,10},{3,15},... | collective-permute-start | bytes 196616 | tf_op jit(solution)/shard_map/ppermute | solution.py:322
  6.9 4.9 %collective-permute-start.4 = (bf16[256,128]{1,0:T(8,128)(2,1)S(1)}, bf16[256,128]{1,0:T(8,128)(2,1)S(1)}, u32[]{:S(2)}, u32[]{:S(2)}) collective-permute-start(bf16[256,128]{1,0:T(8,128)(2,1)S(1)} %get-tuple-element.32), channel_id=1, source_target_pairs={{0,4},{1,5},{4,0},{5,1},{8,12},{9,13},{12,8},{13,9},{2,6},{3,7},{6... | collective-permute-start | bytes 196616 | tf_op jit(solution)/shard_map/ppermute | solution.py:322
  10.4 1.4 %collective-permute-start.3 = (bf16[128,256]{1,0:T(8,128)(2,1)S(1)}, bf16[128,256]{1,0:T(8,128)(2,1)S(1)}, u32[]{:S(2)}, u32[]{:S(2)}) collective-permute-start(bf16[128,256]{1,0:T(8,128)(2,1)S(1)} %collective-permute-done.2.refs_0_), channel_id=1, source_target_pairs={{0,1},{1,0},{2,3},{3,2},{4,5},{5,4},{6,7},{7,6},{8,9},{9,8},{10,11... | collective-permute-start | bytes 196616 | tf_op jit(solution)/shard_map/ppermute | solution.py:325
  11.8 1.3 %collective-permute-start.5 = (bf16[256,128]{1,0:T(8,128)(2,1)S(1)}, bf16[256,128]{1,0:T(8,128)(2,1)S(1)}, u32[]{:S(2)}, u32[]{:S(2)}) collective-permute-start(bf16[256,128]{1,0:T(8,128)(2,1)S(1)} %collective-permute-done.4.refs_2_), channel_id=1, source_target_pairs={{0,1},{1,0},{2,3},{3,2},{4,5},{5,4},{6,7},{7,6},{8,9},{9,8},{10,11... | collective-permute-start | bytes 196616 | tf_op jit(solution)/shard_map/ppermute | solution.py:325
  13.8 6.1 %collective-permute-start.6 = (f32[112,256]{1,0:T(8,128)S(1)}, f32[112,256]{1,0:T(8,128)S(1)}, u32[]{:S(2)}, u32[]{:S(2)}) collective-permute-start(f32[112,256]{1,0:T(8,128)S(1)} %get-tuple-element.33.mine_ref), channel_id=1, source_target_pairs={{0,2},{2,0},{1,3},{3,1},{4,6},{6,4},{5,7},{7,5},{8,10},{10,8},{9,1... | collective-permute-start | bytes 344072 | tf_op jit(solution)/shard_map/ppermute | solution.py:270
  15.4 8.9 %collective-permute-start.7 = (bf16[320,256]{1,0:T(8,128)(2,1)S(1)}, bf16[320,256]{1,0:T(8,128)(2,1)S(1)}, u32[]{:S(2)}, u32[]{:S(2)}) collective-permute-start(bf16[320,256]{1,0:T(8,128)(2,1)S(1)} %get-tuple-element.26.high_ref), channel_id=1, source_target_pairs={{0,2},{2,0},{1,3},{3,1},{4,6},{6,4},{5,7},{7,5},{8,10},{10,8},{9,1... | collective-permute-start | bytes 491528 | tf_op jit(solution)/shard_map/ppermute | solution.py:270
  19.9 5.0 %collective-permute-start.10 = (bf16[128,256]{1,0:T(8,128)(2,1)S(1)}, bf16[128,256]{1,0:T(8,128)(2,1)S(1)}, u32[]{:S(2)}, u32[]{:S(2)}) collective-permute-start(bf16[128,256]{1,0:T(8,128)(2,1)S(1)} %get-tuple-element.35), channel_id=1, source_target_pairs={{0,4},{4,0},{8,12},{12,8},{1,5},{5,1},{9,13},{13,9},{2,6},{6,2},{1... | collective-permute-start | bytes 196616 | tf_op jit(solution)/shard_map/ppermute | solution.py:270
  21.5 6.5 %collective-permute-start.8 = (bf16[128,256]{1,0:T(8,128)(2,1)S(1)}, bf16[128,256]{1,0:T(8,128)(2,1)S(1)}, u32[]{:S(2)}, u32[]{:S(2)}) collective-permute-start(bf16[128,256]{1,0:T(8,128)(2,1)S(1)} %get-tuple-element.35), channel_id=1, source_target_pairs={{0,8},{4,12},{8,0},{12,4},{1,9},{5,13},{9,1},{13,5},{2,10},{6,14},... | collective-permute-start | bytes 196616 | tf_op jit(solution)/shard_map/ppermute | solution.py:270
  23.3 6.1 %collective-permute-start.9 = (bf16[128,256]{1,0:T(8,128)(2,1)S(1)}, bf16[128,256]{1,0:T(8,128)(2,1)S(1)}, u32[]{:S(2)}, u32[]{:S(2)}) collective-permute-start(bf16[128,256]{1,0:T(8,128)(2,1)S(1)} %get-tuple-element.35), channel_id=1, source_target_pairs={{0,12},{4,8},{8,4},{12,0},{1,13},{5,9},{9,5},{13,1},{2,14},{6,10},... | collective-permute-start | bytes 196616 | tf_op jit(solution)/shard_map/ppermute | solution.py:270
  29.9 4.6 %collective-permute-start.11 = (f32[192,256]{1,0:T(8,128)S(1)}, f32[192,256]{1,0:T(8,128)S(1)}, u32[]{:S(2)}, u32[]{:S(2)}) collective-permute-start(f32[192,256]{1,0:T(8,128)S(1)} %get-tuple-element.36.mine_ref), channel_id=1, source_target_pairs={{0,1},{1,0},{2,3},{3,2},{4,5},{5,4},{6,7},{7,6},{8,9},{9,8},{10,11... | collective-permute-start | bytes 589832 | tf_op jit(solution)/shard_map/ppermute | solution.py:368
  30.0 4.5 %collective-permute-start.12 = (f32[64,256]{1,0:T(8,128)S(1)}, f32[64,256]{1,0:T(8,128)S(1)}, u32[]{:S(2)}, u32[]{:S(2)}) collective-permute-start(f32[64,256]{1,0:T(8,128)S(1)} %get-tuple-element.37.y_ref), channel_id=1, source_target_pairs={{0,2},{2,0},{1,3},{3,1},{4,6},{6,4},{5,7},{7,5},{8,10},{10,8},{9,1... | collective-permute-start | bytes 196616 | tf_op jit(solution)/shard_map/ppermute | solution.py:270
  34.8 4.7 %collective-permute-start.13 = (f32[32,128]{1,0:T(8,128)S(1)}, f32[32,128]{1,0:T(8,128)S(1)}, u32[]{:S(2)}, u32[]{:S(2)}) collective-permute-start(f32[32,128]{1,0:T(8,128)S(1)} %get-tuple-element.38.own_ref), channel_id=1, source_target_pairs={{0,8},{1,13},{4,12},{5,9},{8,0},{9,5},{12,4},{13,1},{2,10},{3,15},... | collective-permute-start | bytes 49160 | tf_op jit(solution)/shard_map/ppermute | solution.py:322
  35.3 4.1 %collective-permute-start.15 = (f32[16,128]{1,0:T(8,128)S(1)}, f32[16,128]{1,0:T(8,128)S(1)}, u32[]{:S(2)}, u32[]{:S(2)}) collective-permute-start(f32[16,128]{1,0:T(8,128)S(1)} %get-tuple-element.41), channel_id=1, source_target_pairs={{0,4},{1,5},{4,0},{5,1},{8,12},{9,13},{12,8},{13,9},{2,6},{3,7},{6... | collective-permute-start | bytes 24584 | tf_op jit(solution)/shard_map/ppermute | solution.py:322
  39.4 1.3 %collective-permute-start.14 = (f32[32,128]{1,0:T(8,128)S(1)}, f32[32,128]{1,0:T(8,128)S(1)}, u32[]{:S(2)}, u32[]{:S(2)}) collective-permute-start(f32[32,128]{1,0:T(8,128)S(1)} %collective-permute-done.13.refs_0_), channel_id=1, source_target_pairs={{0,1},{1,0},{2,3},{3,2},{4,5},{5,4},{6,7},{7,6},{8,9},{9,8},{10,11... | collective-permute-start | bytes 49160 | tf_op jit(solution)/shard_map/ppermute | solution.py:325
  39.4 1.3 %collective-permute-start.16 = (f32[16,128]{1,0:T(8,128)S(1)}, f32[16,128]{1,0:T(8,128)S(1)}, u32[]{:S(2)}, u32[]{:S(2)}) collective-permute-start(f32[16,128]{1,0:T(8,128)S(1)} %collective-permute-done.15.refs_2_), channel_id=1, source_target_pairs={{0,1},{1,0},{2,3},{3,2},{4,5},{5,4},{6,7},{7,6},{8,9},{9,8},{10,11... | collective-permute-start | bytes 24584 | tf_op jit(solution)/shard_map/ppermute | solution.py:325

commit v7 on v6

--- a/solution.py
+++ b/solution.py
@@ -9,7 +9,7 @@
 
 f32 = jnp.float32
 bf16 = jnp.bfloat16
-GROUP = 16
+GROUPS = (16,)
 GRANT = 16 * 1024 * 1024
 NN = (((1,), (0,)), ((), ()))
 NT = (((1,), (1,)), ((), ()))
@@ -154,7 +154,9 @@
             first = band * columns
             inside = (target >= first) & (target < first + columns)
             source = jnp.where(inside, held, source)
-        y = y + dot_bf16(source.astype(bf16), tile, NT)
+        source = source.astype(bf16)
+        halves = [dot_bf16(source, tile[k * rows // 2 : (k + 1) * rows // 2], NT) for k in range(2)]
+        y = y + jnp.concatenate(halves, axis=1)
     y_ref[...] = y
     halves = split(y)
     stored = dot_split(halves, (high_ref[:width], low_ref[:width]), NT)
@@ -240,19 +242,21 @@
     m = jnp.concatenate([gram, pltpu.roll(gram, block, 1)], axis=0)
     m = jnp.where(left, m, jnp.where(column == row + block, 1.0, 0.0))
     finished = []
-    for start in range(0, block, GROUP):
+    while len(finished) < block:
+        start = len(finished)
+        group = min(GROUPS[start * len(GROUPS) // block], block - start)
         spread = [
-            jnp.broadcast_to(m[:, start + p : start + p + 1], m.shape) for p in range(GROUP)
+            jnp.broadcast_to(m[:, start + p : start + p + 1], m.shape) for p in range(group)
         ]
-        for p in range(GROUP):
+        for p in range(group):
             at = p % 8
-            root = lax.rsqrt(spread[p][at : at + 1])
-            lower = spread[p] * root
-            done = m[at : at + 1] * root
-            finished.append(done)
-            for q in range(p + 1, GROUP):
-                pivot = q - p + at
-                spread[q] = spread[q] - lower * lower[pivot : pivot + 1]
+            pivot = spread[p][at : at + 1]
+            lower = spread[p] * (1.0 / pivot)
+            done = m[at : at + 1]
+            finished.append(done * lax.rsqrt(pivot))
+            for q in range(p + 1, group):
+                other = q - p + at
+                spread[q] = spread[q] - lower * spread[p][other : other + 1]
             m = m - lower * done
             if at == 7:
                 m = m[8:]

time: 42.9 us -> 42.8 us (level)
  no operation moved by 1% of the time
where the time goes in v7:
time: 42.8 us; the launch traced here: 42.7 us
  waiting for transfers between devices  20.4 us (48%)
  starting transfers between devices  16.6 us (39%)
  Pallas kernels  5.08 us (12%)
  between operations  0.69 us (2%)
    ppermute x6, waiting for transfers between devices, exchange(): lax.ppermute(x, axis, [(i, i ^ distance) for i in range(lax.axis_size(axi...  11.9 us
    ppermute x6, starting transfers between devices, exchange(): lax.ppermute(x, axis, [(i, i ^ distance) for i in range(lax.axis_size(axi...  8.11 us
    ppermute x4, starting transfers between devices, serve(): received.append(lax.ppermute(send, ('rows', 'sub'), moves))  7.24 us
    ppermute x4, waiting for transfers between devices, serve(): received.append(lax.ppermute(send, ('rows', 'sub'), moves))  6.34 us
    pallas_call x1, Pallas kernels, local(): call(functools.partial(factor_kernel, pairs, total_rows), [(half, f32), (...  2.13 us
    ppermute x4, waiting for transfers between devices, serve(): swapped += [x, lax.ppermute(x, 'sub', swap)]  2.07 us
    pallas_call x1, Pallas kernels, local(): prepare(*(pltpu.with_memory_space_constraint(a, pltpu.HBM) for a in sourc...  1.29 us
  transfers between devices with their start and end apart: 17, of which 10 were waited for; matrix products, arithmetic and copies ran while one was open for 0% of the time, Pallas kernels for 3%

profile of v7, /device:TPU:0, one launch (start us, length us, event | category | flops | bytes accessed | tf_op | source)
XLA Modules:
  0.0 42.7 jit_solution(6067797728147319874)
XLA Ops:
  0.6 0.6 %collective-permute-start.1 = (bf16[2,256,256]{2,1,0:T(8,128)(2,1)}, bf16[2,256,256]{2,1,0:T(8,128)(2,1)S(1)}, u32[]{:S(2)}, u32[]{:S(2)}) collective-permute-start(bf16[2,256,256]{2,1,0:T(8,128)(2,1)} %t_hbm.1), channel_id=1, source_target_pairs={{0,1},{1,0},{2,3},{3,2},{4,5},{5,4},{6,7},{7,6},{8,9},{9,8},{10,11... | collective-permute-start | bytes 786440 | tf_op jit(solution)/shard_map/ppermute | solution.py:298
  1.2 0.1 collective-permute-start
  1.3 1.3 %shard_map.94 = (f32[64,256]{1,0:T(8,128)S(1)}, f32[2,32,256]{2,1,0:T(8,128)S(1)}, bf16[320,256]{1,0:T(8,128)(2,1)S(1)}, bf16[320,256]{1,0:T(8,128)(2,1)S(1)}, b...) custom-call(f32[64,256]{1,0:T(8,128)} %bitcast.12, f32[1,256]{1,0:T(1,128)} %bitcast.14, f32[64,256]{1,0:T(8,128)} %bitcast.13, ...), custom_call_target="tpu_custom_call" | custom-call | flops 40000000 | bytes 1000000 | tf_op jit(solution)/shard_map/pallas_call | solution.py:317
  2.6 0.0 collective-permute-done.j_ref
  2.6 0.2 shard_map.95
  2.8 4.1 %collective-permute-start.2 = (bf16[128,256]{1,0:T(8,128)(2,1)S(1)}, bf16[128,256]{1,0:T(8,128)(2,1)S(1)}, u32[]{:S(2)}, u32[]{:S(2)}) collective-permute-start(bf16[128,256]{1,0:T(8,128)(2,1)S(1)} %get-tuple-element.31), channel_id=1, source_target_pairs={{0,8},{1,13},{4,12},{5,9},{8,0},{9,5},{12,4},{13,1},{2,10},{3,15},... | collective-permute-start | bytes 196616 | tf_op jit(solution)/shard_map/ppermute | solution.py:326
  6.9 1.6 %collective-permute-start.4 = (bf16[256,128]{1,0:T(8,128)(2,1)S(1)}, bf16[256,128]{1,0:T(8,128)(2,1)S(1)}, u32[]{:S(2)}, u32[]{:S(2)}) collective-permute-start(bf16[256,128]{1,0:T(8,128)(2,1)S(1)} %get-tuple-element.32), channel_id=1, source_target_pairs={{0,4},{1,5},{4,0},{5,1},{8,12},{9,13},{12,8},{13,9},{2,6},{3,7},{6... | collective-permute-start | bytes 196616 | tf_op jit(solution)/shard_map/ppermute | solution.py:326
  8.5 1.9 %collective-permute-done.2.refs_0_ = bf16[128,256]{1,0:T(8,128)(2,1)S(1)} collective-permute-done((bf16[128,256]{1,0:T(8,128)(2,1)S(1)}, bf16[128,256]{1,0:T(8,128)(2,1)S(1)}, u32[]{:S(2)}, u32[]{:S(2)}) %collective-permute-start.2) | collective-permute-done | bytes 65568 | tf_op jit(solution)/shard_map/ppermute | solution.py:326
  10.4 1.3 %collective-permute-done.4.refs_2_ = bf16[256,128]{1,0:T(8,128)(2,1)S(1)} collective-permute-done((bf16[256,128]{1,0:T(8,128)(2,1)S(1)}, bf16[256,128]{1,0:T(8,128)(2,1)S(1)}, u32[]{:S(2)}, u32[]{:S(2)}) %collective-permute-start.4) | collective-permute-done | bytes 65568 | tf_op jit(solution)/shard_map/ppermute | solution.py:326
  11.8 0.0 collective-permute-start.5
  11.8 1.2 %collective-permute-done.5.refs_3_ = bf16[256,128]{1,0:T(8,128)(2,1)S(1)} collective-permute-done((bf16[256,128]{1,0:T(8,128)(2,1)S(1)}, bf16[256,128]{1,0:T(8,128)(2,1)S(1)}, u32[]{:S(2)}, u32[]{:S(2)}) %collective-permute-start.5) | collective-permute-done | bytes 65568 | tf_op jit(solution)/shard_map/ppermute | solution.py:329
  13.0 0.6 %shard_map.96 = (f32[64,256]{1,0:T(8,128)S(1)}, f32[112,256]{1,0:T(8,128)S(1)}) custom-call(s32[2,2]{1,0:T(2,128)S(1)} %get-tuple-element.24.i_ref, s32[2,2]{1,0:T(2,128)S(1)} %collective-permute-done.j_ref, f32[64,256]{1,0:T(8,128)S(1)} %get-tuple-element.25.base_ref, bf16[320,256]{1,0:T(8,128)(2,1)S(1)} %get-tuple-element.26.high_ref, ...), custom_call_target="tpu_custom_call" | custom-call | flops 40000000 | bytes 1000000 | tf_op jit(solution)/shard_map/pallas_call | solution.py:341
  13.6 1.6 %collective-permute-start.6 = (f32[112,256]{1,0:T(8,128)S(1)}, f32[112,256]{1,0:T(8,128)S(1)}, u32[]{:S(2)}, u32[]{:S(2)}) collective-permute-start(f32[112,256]{1,0:T(8,128)S(1)} %get-tuple-element.33.mine_ref), channel_id=1, source_target_pairs={{0,2},{2,0},{1,3},{3,1},{4,6},{6,4},{5,7},{7,5},{8,10},{10,8},{9,1... | collective-permute-start | bytes 344072 | tf_op jit(solution)/shard_map/ppermute | solution.py:274
  15.2 0.5 %collective-permute-start.7 = (bf16[320,256]{1,0:T(8,128)(2,1)S(1)}, bf16[320,256]{1,0:T(8,128)(2,1)S(1)}, u32[]{:S(2)}, u32[]{:S(2)}) collective-permute-start(bf16[320,256]{1,0:T(8,128)(2,1)S(1)} %get-tuple-element.26.high_ref), channel_id=1, source_target_pairs={{0,2},{2,0},{1,3},{3,1},{4,6},{6,4},{5,7},{7,5},{8,10},{10,8},{9,1... | collective-permute-start | bytes 491528 | tf_op jit(solution)/shard_map/ppermute | solution.py:274
  15.7 4.0 %collective-permute-done.6.other_ref = f32[112,256]{1,0:T(8,128)S(1)} collective-permute-done((f32[112,256]{1,0:T(8,128)S(1)}, f32[112,256]{1,0:T(8,128)S(1)}, u32[]{:S(2)}, u32[]{:S(2)}) %collective-permute-start.6) | collective-permute-done | bytes 114720 | tf_op jit(solution)/shard_map/ppermute | solution.py:274
  19.7 1.6 %collective-permute-start.10 = (bf16[128,256]{1,0:T(8,128)(2,1)S(1)}, bf16[128,256]{1,0:T(8,128)(2,1)S(1)}, u32[]{:S(2)}, u32[]{:S(2)}) collective-permute-start(bf16[128,256]{1,0:T(8,128)(2,1)S(1)} %get-tuple-element.35), channel_id=1, source_target_pairs={{0,4},{4,0},{8,12},{12,8},{1,5},{5,1},{9,13},{13,9},{2,6},{6,2},{1... | collective-permute-start | bytes 196616 | tf_op jit(solution)/shard_map/ppermute | solution.py:274
  21.3 1.8 %collective-permute-start.8 = (bf16[128,256]{1,0:T(8,128)(2,1)S(1)}, bf16[128,256]{1,0:T(8,128)(2,1)S(1)}, u32[]{:S(2)}, u32[]{:S(2)}) collective-permute-start(bf16[128,256]{1,0:T(8,128)(2,1)S(1)} %get-tuple-element.35), channel_id=1, source_target_pairs={{0,8},{4,12},{8,0},{12,4},{1,9},{5,13},{9,1},{13,5},{2,10},{6,14},... | collective-permute-start | bytes 196616 | tf_op jit(solution)/shard_map/ppermute | solution.py:274
  23.1 1.1 %collective-permute-start.9 = (bf16[128,256]{1,0:T(8,128)(2,1)S(1)}, bf16[128,256]{1,0:T(8,128)(2,1)S(1)}, u32[]{:S(2)}, u32[]{:S(2)}) collective-permute-start(bf16[128,256]{1,0:T(8,128)(2,1)S(1)} %get-tuple-element.35), channel_id=1, source_target_pairs={{0,12},{4,8},{8,4},{12,0},{1,13},{5,9},{9,5},{13,1},{2,14},{6,10},... | collective-permute-start | bytes 196616 | tf_op jit(solution)/shard_map/ppermute | solution.py:274
  24.2 0.5 %collective-permute-done.10.refs_2_ = bf16[128,256]{1,0:T(8,128)(2,1)S(1)} collective-permute-done((bf16[128,256]{1,0:T(8,128)(2,1)S(1)}, bf16[128,256]{1,0:T(8,128)(2,1)S(1)}, u32[]{:S(2)}, u32[]{:S(2)}) %collective-permute-start.10) | collective-permute-done | bytes 65568 | tf_op jit(solution)/shard_map/ppermute | solution.py:274
  24.7 3.1 %collective-permute-done.8.refs_0_ = bf16[128,256]{1,0:T(8,128)(2,1)S(1)} collective-permute-done((bf16[128,256]{1,0:T(8,128)(2,1)S(1)}, bf16[128,256]{1,0:T(8,128)(2,1)S(1)}, u32[]{:S(2)}, u32[]{:S(2)}) %collective-permute-start.8) | collective-permute-done | bytes 65568 | tf_op jit(solution)/shard_map/ppermute | solution.py:274
  27.8 1.4 %collective-permute-done.9.refs_1_ = bf16[128,256]{1,0:T(8,128)(2,1)S(1)} collective-permute-done((bf16[128,256]{1,0:T(8,128)(2,1)S(1)}, bf16[128,256]{1,0:T(8,128)(2,1)S(1)}, u32[]{:S(2)}, u32[]{:S(2)}) %collective-permute-start.9) | collective-permute-done | bytes 65568 | tf_op jit(solution)/shard_map/ppermute | solution.py:274
  29.2 0.5 %shard_map.98 = (f32[192,256]{1,0:T(8,128)S(1)}, f32[64,64]{1,0:T(8,128)S(1)}) custom-call(f32[112,256]{1,0:T(8,128)S(1)} %get-tuple-element.34.total_ref, bf16[320,256]{1,0:T(8,128)(2,1)S(1)} %get-tuple-element.26.high_ref, bf16[320,256]{1,0:T(8,128)(2,1)S(1)} %get-tuple-element.27.low_ref, bf16[320,256]{1,0:T(8,128)(2,1)S(1)} %collective-permute-done.7.near_ref, ...), custom_call_target="tpu_custom_call" | custom-call | flops 40000000 | bytes 1000000 | tf_op jit(solution)/shard_map/pallas_call | solution.py:367
  29.7 0.1 collective-permute-start.11
  29.8 1.6 %collective-permute-start.12 = (f32[64,256]{1,0:T(8,128)S(1)}, f32[64,256]{1,0:T(8,128)S(1)}, u32[]{:S(2)}, u32[]{:S(2)}) collective-permute-start(f32[64,256]{1,0:T(8,128)S(1)} %get-tuple-element.37.y_ref), channel_id=1, source_target_pairs={{0,2},{2,0},{1,3},{3,1},{4,6},{6,4},{5,7},{7,5},{8,10},{10,8},{9,1... | collective-permute-start | bytes 196616 | tf_op jit(solution)/shard_map/ppermute | solution.py:274
  31.4 2.9 %collective-permute-done.12.z_ref = f32[64,256]{1,0:T(8,128)S(1)} collective-permute-done((f32[64,256]{1,0:T(8,128)S(1)}, f32[64,256]{1,0:T(8,128)S(1)}, u32[]{:S(2)}, u32[]{:S(2)}) %collective-permute-start.12) | collective-permute-done | bytes 65568 | tf_op jit(solution)/shard_map/ppermute | solution.py:274
  34.3 0.3 shard_map.99
  34.6 0.5 %collective-permute-start.13 = (f32[32,128]{1,0:T(8,128)S(1)}, f32[32,128]{1,0:T(8,128)S(1)}, u32[]{:S(2)}, u32[]{:S(2)}) collective-permute-start(f32[32,128]{1,0:T(8,128)S(1)} %get-tuple-element.38.own_ref), channel_id=1, source_target_pairs={{0,8},{1,13},{4,12},{5,9},{8,0},{9,5},{12,4},{13,1},{2,10},{3,15},... | collective-permute-start | bytes 49160 | tf_op jit(solution)/shard_map/ppermute | solution.py:326
  35.1 1.1 %collective-permute-start.15 = (f32[16,128]{1,0:T(8,128)S(1)}, f32[16,128]{1,0:T(8,128)S(1)}, u32[]{:S(2)}, u32[]{:S(2)}) collective-permute-start(f32[16,128]{1,0:T(8,128)S(1)} %get-tuple-element.41), channel_id=1, source_target_pairs={{0,4},{1,5},{4,0},{5,1},{8,12},{9,13},{12,8},{13,9},{2,6},{3,7},{6... | collective-permute-start | bytes 24584 | tf_op jit(solution)/shard_map/ppermute | solution.py:326
  36.2 3.1 %collective-permute-done.13.refs_0_ = f32[32,128]{1,0:T(8,128)S(1)} collective-permute-done((f32[32,128]{1,0:T(8,128)S(1)}, f32[32,128]{1,0:T(8,128)S(1)}, u32[]{:S(2)}, u32[]{:S(2)}) %collective-permute-start.13) | collective-permute-done | bytes 16416 | tf_op jit(solution)/shard_map/ppermute | solution.py:326
  39.2 0.5 %collective-permute-start.16 = (f32[16,128]{1,0:T(8,128)S(1)}, f32[16,128]{1,0:T(8,128)S(1)}, u32[]{:S(2)}, u32[]{:S(2)}) collective-permute-start(f32[16,128]{1,0:T(8,128)S(1)} %collective-permute-done.15.refs_2_), channel_id=1, source_target_pairs={{0,1},{1,0},{2,3},{3,2},{4,5},{5,4},{6,7},{7,6},{8,9},{9,8},{10,11... | collective-permute-start | bytes 24584 | tf_op jit(solution)/shard_map/ppermute | solution.py:329
  39.7 0.8 %collective-permute-done.16.refs_3_ = f32[16,128]{1,0:T(8,128)S(1)} collective-permute-done((f32[16,128]{1,0:T(8,128)S(1)}, f32[16,128]{1,0:T(8,128)S(1)}, u32[]{:S(2)}, u32[]{:S(2)}) %collective-permute-start.16) | collective-permute-done | bytes 8224 | tf_op jit(solution)/shard_map/ppermute | solution.py:329
  40.6 2.1 %shard_map.100 = (f32[64,256]{1,0:T(8,128)}, f32[64,64]{1,0:T(8,128)}, f32[64,64]{1,0:T(8,128)}) custom-call(f32[32,128]{1,0:T(8,128)S(1)} %get-tuple-element.38.own_ref, f32[64,256]{1,0:T(8,128)S(1)} %get-tuple-element.39.images_ref, f32[64,64]{1,0:T(8,128)S(1)} %get-tuple-element.40.d_ref, f32[32,128]{1,0:T(8,128)S(1)} %collective-permute-done.13.refs_0_, ...), custom_call_target="tpu_custom_call" | custom-call | flops 40000000 | bytes 1000000 | tf_op jit(solution)/shard_map/pallas_call | solution.py:377
  (9 shorter events, 0.0 us)
Async XLA Ops:
  0.6 2.0 %collective-permute-start.1 = (bf16[2,256,256]{2,1,0:T(8,128)(2,1)}, bf16[2,256,256]{2,1,0:T(8,128)(2,1)S(1)}, u32[]{:S(2)}, u32[]{:S(2)}) collective-permute-start(bf16[2,256,256]{2,1,0:T(8,128)(2,1)} %t_hbm.1), channel_id=1, source_target_pairs={{0,1},{1,0},{2,3},{3,2},{4,5},{5,4},{6,7},{7,6},{8,9},{9,8},{10,11... | collective-permute-start | bytes 786440 | tf_op jit(solution)/shard_map/ppermute | solution.py:298
  1.2 1.4 %collective-permute-start = (s32[2,2]{1,0:T(2,128)}, s32[2,2]{1,0:T(2,128)S(1)}, u32[]{:S(2)}, u32[]{:S(2)}) collective-permute-start(s32[2,2]{1,0:T(2,128)} %i_hbm.1), channel_id=1, source_target_pairs={{0,1},{1,0},{2,3},{3,2},{4,5},{5,4},{6,7},{7,6},{8,9},{9,8},{10,11... | collective-permute-start | bytes 56 | tf_op jit(solution)/shard_map/ppermute | solution.py:299
  2.8 7.6 %collective-permute-start.2 = (bf16[128,256]{1,0:T(8,128)(2,1)S(1)}, bf16[128,256]{1,0:T(8,128)(2,1)S(1)}, u32[]{:S(2)}, u32[]{:S(2)}) collective-permute-start(bf16[128,256]{1,0:T(8,128)(2,1)S(1)} %get-tuple-element.31), channel_id=1, source_target_pairs={{0,8},{1,13},{4,12},{5,9},{8,0},{9,5},{12,4},{13,1},{2,10},{3,15},... | collective-permute-start | bytes 196616 | tf_op jit(solution)/shard_map/ppermute | solution.py:326
  6.9 4.9 %collective-permute-start.4 = (bf16[256,128]{1,0:T(8,128)(2,1)S(1)}, bf16[256,128]{1,0:T(8,128)(2,1)S(1)}, u32[]{:S(2)}, u32[]{:S(2)}) collective-permute-start(bf16[256,128]{1,0:T(8,128)(2,1)S(1)} %get-tuple-element.32), channel_id=1, source_target_pairs={{0,4},{1,5},{4,0},{5,1},{8,12},{9,13},{12,8},{13,9},{2,6},{3,7},{6... | collective-permute-start | bytes 196616 | tf_op jit(solution)/shard_map/ppermute | solution.py:326
  10.4 1.4 %collective-permute-start.3 = (bf16[128,256]{1,0:T(8,128)(2,1)S(1)}, bf16[128,256]{1,0:T(8,128)(2,1)S(1)}, u32[]{:S(2)}, u32[]{:S(2)}) collective-permute-start(bf16[128,256]{1,0:T(8,128)(2,1)S(1)} %collective-permute-done.2.refs_0_), channel_id=1, source_target_pairs={{0,1},{1,0},{2,3},{3,2},{4,5},{5,4},{6,7},{7,6},{8,9},{9,8},{10,11... | collective-permute-start | bytes 196616 | tf_op jit(solution)/shard_map/ppermute | solution.py:329
  11.8 1.3 %collective-permute-start.5 = (bf16[256,128]{1,0:T(8,128)(2,1)S(1)}, bf16[256,128]{1,0:T(8,128)(2,1)S(1)}, u32[]{:S(2)}, u32[]{:S(2)}) collective-permute-start(bf16[256,128]{1,0:T(8,128)(2,1)S(1)} %collective-permute-done.4.refs_2_), channel_id=1, source_target_pairs={{0,1},{1,0},{2,3},{3,2},{4,5},{5,4},{6,7},{7,6},{8,9},{9,8},{10,11... | collective-permute-start | bytes 196616 | tf_op jit(solution)/shard_map/ppermute | solution.py:329
  13.6 6.0 %collective-permute-start.6 = (f32[112,256]{1,0:T(8,128)S(1)}, f32[112,256]{1,0:T(8,128)S(1)}, u32[]{:S(2)}, u32[]{:S(2)}) collective-permute-start(f32[112,256]{1,0:T(8,128)S(1)} %get-tuple-element.33.mine_ref), channel_id=1, source_target_pairs={{0,2},{2,0},{1,3},{3,1},{4,6},{6,4},{5,7},{7,5},{8,10},{10,8},{9,1... | collective-permute-start | bytes 344072 | tf_op jit(solution)/shard_map/ppermute | solution.py:274
  15.2 8.9 %collective-permute-start.7 = (bf16[320,256]{1,0:T(8,128)(2,1)S(1)}, bf16[320,256]{1,0:T(8,128)(2,1)S(1)}, u32[]{:S(2)}, u32[]{:S(2)}) collective-permute-start(bf16[320,256]{1,0:T(8,128)(2,1)S(1)} %get-tuple-element.26.high_ref), channel_id=1, source_target_pairs={{0,2},{2,0},{1,3},{3,1},{4,6},{6,4},{5,7},{7,5},{8,10},{10,8},{9,1... | collective-permute-start | bytes 491528 | tf_op jit(solution)/shard_map/ppermute | solution.py:274
  19.7 5.0 %collective-permute-start.10 = (bf16[128,256]{1,0:T(8,128)(2,1)S(1)}, bf16[128,256]{1,0:T(8,128)(2,1)S(1)}, u32[]{:S(2)}, u32[]{:S(2)}) collective-permute-start(bf16[128,256]{1,0:T(8,128)(2,1)S(1)} %get-tuple-element.35), channel_id=1, source_target_pairs={{0,4},{4,0},{8,12},{12,8},{1,5},{5,1},{9,13},{13,9},{2,6},{6,2},{1... | collective-permute-start | bytes 196616 | tf_op jit(solution)/shard_map/ppermute | solution.py:274
  21.3 6.5 %collective-permute-start.8 = (bf16[128,256]{1,0:T(8,128)(2,1)S(1)}, bf16[128,256]{1,0:T(8,128)(2,1)S(1)}, u32[]{:S(2)}, u32[]{:S(2)}) collective-permute-start(bf16[128,256]{1,0:T(8,128)(2,1)S(1)} %get-tuple-element.35), channel_id=1, source_target_pairs={{0,8},{4,12},{8,0},{12,4},{1,9},{5,13},{9,1},{13,5},{2,10},{6,14},... | collective-permute-start | bytes 196616 | tf_op jit(solution)/shard_map/ppermute | solution.py:274
  23.1 6.1 %collective-permute-start.9 = (bf16[128,256]{1,0:T(8,128)(2,1)S(1)}, bf16[128,256]{1,0:T(8,128)(2,1)S(1)}, u32[]{:S(2)}, u32[]{:S(2)}) collective-permute-start(bf16[128,256]{1,0:T(8,128)(2,1)S(1)} %get-tuple-element.35), channel_id=1, source_target_pairs={{0,12},{4,8},{8,4},{12,0},{1,13},{5,9},{9,5},{13,1},{2,14},{6,10},... | collective-permute-start | bytes 196616 | tf_op jit(solution)/shard_map/ppermute | solution.py:274
  29.7 4.6 %collective-permute-start.11 = (f32[192,256]{1,0:T(8,128)S(1)}, f32[192,256]{1,0:T(8,128)S(1)}, u32[]{:S(2)}, u32[]{:S(2)}) collective-permute-start(f32[192,256]{1,0:T(8,128)S(1)} %get-tuple-element.36.mine_ref), channel_id=1, source_target_pairs={{0,1},{1,0},{2,3},{3,2},{4,5},{5,4},{6,7},{7,6},{8,9},{9,8},{10,11... | collective-permute-start | bytes 589832 | tf_op jit(solution)/shard_map/ppermute | solution.py:372
  29.8 4.5 %collective-permute-start.12 = (f32[64,256]{1,0:T(8,128)S(1)}, f32[64,256]{1,0:T(8,128)S(1)}, u32[]{:S(2)}, u32[]{:S(2)}) collective-permute-start(f32[64,256]{1,0:T(8,128)S(1)} %get-tuple-element.37.y_ref), channel_id=1, source_target_pairs={{0,2},{2,0},{1,3},{3,1},{4,6},{6,4},{5,7},{7,5},{8,10},{10,8},{9,1... | collective-permute-start | bytes 196616 | tf_op jit(solution)/shard_map/ppermute | solution.py:274
  34.6 4.7 %collective-permute-start.13 = (f32[32,128]{1,0:T(8,128)S(1)}, f32[32,128]{1,0:T(8,128)S(1)}, u32[]{:S(2)}, u32[]{:S(2)}) collective-permute-start(f32[32,128]{1,0:T(8,128)S(1)} %get-tuple-element.38.own_ref), channel_id=1, source_target_pairs={{0,8},{1,13},{4,12},{5,9},{8,0},{9,5},{12,4},{13,1},{2,10},{3,15},... | collective-permute-start | bytes 49160 | tf_op jit(solution)/shard_map/ppermute | solution.py:326
  35.1 4.1 %collective-permute-start.15 = (f32[16,128]{1,0:T(8,128)S(1)}, f32[16,128]{1,0:T(8,128)S(1)}, u32[]{:S(2)}, u32[]{:S(2)}) collective-permute-start(f32[16,128]{1,0:T(8,128)S(1)} %get-tuple-element.41), channel_id=1, source_target_pairs={{0,4},{1,5},{4,0},{5,1},{8,12},{9,13},{12,8},{13,9},{2,6},{3,7},{6... | collective-permute-start | bytes 24584 | tf_op jit(solution)/shard_map/ppermute | solution.py:326
  39.2 1.3 %collective-permute-start.14 = (f32[32,128]{1,0:T(8,128)S(1)}, f32[32,128]{1,0:T(8,128)S(1)}, u32[]{:S(2)}, u32[]{:S(2)}) collective-permute-start(f32[32,128]{1,0:T(8,128)S(1)} %collective-permute-done.13.refs_0_), channel_id=1, source_target_pairs={{0,1},{1,0},{2,3},{3,2},{4,5},{5,4},{6,7},{7,6},{8,9},{9,8},{10,11... | collective-permute-start | bytes 49160 | tf_op jit(solution)/shard_map/ppermute | solution.py:329
  39.2 1.3 %collective-permute-start.16 = (f32[16,128]{1,0:T(8,128)S(1)}, f32[16,128]{1,0:T(8,128)S(1)}, u32[]{:S(2)}, u32[]{:S(2)}) collective-permute-start(f32[16,128]{1,0:T(8,128)S(1)} %collective-permute-done.15.refs_2_), channel_id=1, source_target_pairs={{0,1},{1,0},{2,3},{3,2},{4,5},{5,4},{6,7},{7,6},{8,9},{9,8},{10,11... | collective-permute-start | bytes 24584 | tf_op jit(solution)/shard_map/ppermute | solution.py:329

commit v8 on v6

--- a/solution.py
+++ b/solution.py
@@ -27,6 +27,13 @@
 def dot_split(a, b, dims):
     (ah, al), (bh, bl) = a, b
     return dot_bf16(ah, bh, dims) + dot_bf16(ah, bl, dims) + dot_bf16(al, bh, dims)
+
+
+def dot_stacked(a, b, dims):
+    (ah, al), (bh, bl) = a, b
+    rows = ah.shape[0]
+    both = dot_bf16(jnp.concatenate([ah, al], axis=0), bh, dims)
+    return both[:rows] + both[rows:] + dot_bf16(ah, bl, dims)
 
 
 def fold(x, parts):
@@ -75,8 +82,8 @@
     ss = split(s_ref[...])
     for k, ref in enumerate((high_ref, low_ref)):
         ref[...] = jnp.concatenate([ss[k], xs[k]], axis=0)
-    base_ref[...] = e_ref[...] * x - dot_split(split(coupling), split(p_ref[...]), NN)
-    corr = dot_split(xs, ss, NT)
+    base_ref[...] = e_ref[...] * x - dot_stacked(split(coupling), split(p_ref[...]), NN)
+    corr = dot_stacked(xs, ss, NT)
     chunk = corr_ref.shape[1]
     for band in range(corr_ref.shape[0]):
         corr_ref[band] = corr[band * chunk : (band + 1) * chunk]
@@ -154,12 +161,14 @@
             first = band * columns
             inside = (target >= first) & (target < first + columns)
             source = jnp.where(inside, held, source)
-        y = y + dot_bf16(source.astype(bf16), tile, NT)
+        source = source.astype(bf16)
+        halves = [dot_bf16(source, tile[k * rows // 2 : (k + 1) * rows // 2], NT) for k in range(2)]
+        y = y + jnp.concatenate(halves, axis=1)
     y_ref[...] = y
     halves = split(y)
+    diagonal = fold(dot_split(halves, (high_ref[width:], low_ref[width:]), NT), parts)
     stored = dot_split(halves, (high_ref[:width], low_ref[:width]), NT)
-    diagonal = dot_split(halves, (high_ref[width:], low_ref[width:]), NT)
-    send_ref[...] = jnp.concatenate([stored, fold(diagonal, parts), corr], axis=0)
+    send_ref[...] = jnp.concatenate([stored, diagonal, corr], axis=0)
 
 
 def pack(total, block, small):
@@ -195,9 +204,14 @@
     even = jnp.bitwise_and(me, 1) == 0
     corr = jnp.concatenate([jnp.where(even, same, other), jnp.where(even, other, same)], axis=0)
     scale = 1.0 / total_rows
-    diagonal = unfold(diagonal * scale, parts)
+    diagonal = diagonal * scale
+    lane = lax.broadcasted_iota(jnp.int32, diagonal.shape, 1)
+    inside = [(lane >= k * block) & (lane < (k + 1) * block) for k in range(parts)]
+    spread = jnp.concatenate([jnp.where(k, diagonal, 0.0) for k in inside], axis=0)
+    many = [jnp.concatenate([h] * parts, axis=0) for h in split(corr * scale)]
+    projection = stored * scale - dot_split(split(spread), many, NN)
+    diagonal = unfold(diagonal, parts)
     diagonal_ref[...] = diagonal
-    projection = stored * scale - dot_split(split(diagonal), split(corr * scale), NN)
     weights = split(jnp.concatenate([projection, jnp.where(core == 0, diagonal, 0.0)], axis=1))
     for k, ref in enumerate((high_ref, near_ref)):
         rounded = dot_bf16(weights[0], ref[...], NN) + dot_bf16(weights[1], ref[...], NN)
@@ -213,8 +227,10 @@
     gram = 0.0
     for x in (images, z_ref[...] - removed[block : 2 * block]):
         halves = split(x)
-        gram = gram + dot_split(halves, halves, NT)
-    gram = fold(gram, 2)
+        twice = [jnp.concatenate([h, h], axis=0) for h in halves]
+        gram = gram + dot_stacked(halves, twice, NT)
+    left = lax.broadcasted_iota(jnp.int32, full_ref.shape, 1) < block
+    gram = jnp.where(left, gram[: block // 2], gram[block // 2 :])
     full_ref[...] = gram
     middle = half_ref.shape[0]
     half_ref[...] = jnp.where(lax.axis_index("sub") == 0, gram[:middle], gram[middle:])

time: 42.9 us -> 42.7 us (level)
  no operation moved by 1% of the time
where the time goes in v8:
time: 42.7 us; the launch traced here: 42.6 us
  waiting for transfers between devices  20.4 us (48%)
  starting transfers between devices  16.7 us (39%)
  Pallas kernels  4.85 us (11%)
  between operations  0.69 us (2%)
    ppermute x6, waiting for transfers between devices, exchange(): lax.ppermute(x, axis, [(i, i ^ distance) for i in range(lax.axis_size(axi...  11.9 us
    ppermute x6, starting transfers between devices, exchange(): lax.ppermute(x, axis, [(i, i ^ distance) for i in range(lax.axis_size(axi...  8.14 us
    ppermute x4, starting transfers between devices, serve(): received.append(lax.ppermute(send, ('rows', 'sub'), moves))  7.29 us
    ppermute x4, waiting for transfers between devices, serve(): received.append(lax.ppermute(send, ('rows', 'sub'), moves))  6.34 us
    ppermute x4, waiting for transfers between devices, serve(): swapped += [x, lax.ppermute(x, 'sub', swap)]  2.07 us
    pallas_call x1, Pallas kernels, local(): call(functools.partial(factor_kernel, pairs, total_rows), [(half, f32), (...  2.03 us
    pallas_call x1, Pallas kernels, local(): prepare(*(pltpu.with_memory_space_constraint(a, pltpu.HBM) for a in sourc...  1.27 us
  transfers between devices with their start and end apart: 17, of which 10 were waited for; matrix products, arithmetic and copies ran while one was open for 0% of the time, Pallas kernels for 3%

profile of v8, /device:TPU:0, one launch (start us, length us, event | category | flops | bytes accessed | tf_op | source)
XLA Modules:
  0.0 42.6 jit_solution(16322911806872522213)
XLA Ops:
  0.6 0.6 %collective-permute-start.1 = (bf16[2,256,256]{2,1,0:T(8,128)(2,1)}, bf16[2,256,256]{2,1,0:T(8,128)(2,1)S(1)}, u32[]{:S(2)}, u32[]{:S(2)}) collective-permute-start(bf16[2,256,256]{2,1,0:T(8,128)(2,1)} %t_hbm.1), channel_id=1, source_target_pairs={{0,1},{1,0},{2,3},{3,2},{4,5},{5,4},{6,7},{7,6},{8,9},{9,8},{10,11... | collective-permute-start | bytes 786440 | tf_op jit(solution)/shard_map/ppermute | solution.py:310
  1.2 0.1 collective-permute-start
  1.3 1.3 %shard_map.94 = (f32[64,256]{1,0:T(8,128)S(1)}, f32[2,32,256]{2,1,0:T(8,128)S(1)}, bf16[320,256]{1,0:T(8,128)(2,1)S(1)}, bf16[320,256]{1,0:T(8,128)(2,1)S(1)}, b...) custom-call(f32[64,256]{1,0:T(8,128)} %bitcast.12, f32[1,256]{1,0:T(1,128)} %bitcast.14, f32[64,256]{1,0:T(8,128)} %bitcast.13, ...), custom_call_target="tpu_custom_call" | custom-call | flops 40000000 | bytes 1000000 | tf_op jit(solution)/shard_map/pallas_call | solution.py:329
  2.5 0.0 collective-permute-done.j_ref
  2.6 0.2 shard_map.95
  2.8 4.1 %collective-permute-start.2 = (bf16[128,256]{1,0:T(8,128)(2,1)S(1)}, bf16[128,256]{1,0:T(8,128)(2,1)S(1)}, u32[]{:S(2)}, u32[]{:S(2)}) collective-permute-start(bf16[128,256]{1,0:T(8,128)(2,1)S(1)} %get-tuple-element.31), channel_id=1, source_target_pairs={{0,8},{1,13},{4,12},{5,9},{8,0},{9,5},{12,4},{13,1},{2,10},{3,15},... | collective-permute-start | bytes 196616 | tf_op jit(solution)/shard_map/ppermute | solution.py:338
  6.9 1.6 %collective-permute-start.4 = (bf16[256,128]{1,0:T(8,128)(2,1)S(1)}, bf16[256,128]{1,0:T(8,128)(2,1)S(1)}, u32[]{:S(2)}, u32[]{:S(2)}) collective-permute-start(bf16[256,128]{1,0:T(8,128)(2,1)S(1)} %get-tuple-element.32), channel_id=1, source_target_pairs={{0,4},{1,5},{4,0},{5,1},{8,12},{9,13},{12,8},{13,9},{2,6},{3,7},{6... | collective-permute-start | bytes 196616 | tf_op jit(solution)/shard_map/ppermute | solution.py:338
  8.4 1.9 %collective-permute-done.2.refs_0_ = bf16[128,256]{1,0:T(8,128)(2,1)S(1)} collective-permute-done((bf16[128,256]{1,0:T(8,128)(2,1)S(1)}, bf16[128,256]{1,0:T(8,128)(2,1)S(1)}, u32[]{:S(2)}, u32[]{:S(2)}) %collective-permute-start.2) | collective-permute-done | bytes 65568 | tf_op jit(solution)/shard_map/ppermute | solution.py:338
  10.4 1.3 %collective-permute-done.4.refs_2_ = bf16[256,128]{1,0:T(8,128)(2,1)S(1)} collective-permute-done((bf16[256,128]{1,0:T(8,128)(2,1)S(1)}, bf16[256,128]{1,0:T(8,128)(2,1)S(1)}, u32[]{:S(2)}, u32[]{:S(2)}) %collective-permute-start.4) | collective-permute-done | bytes 65568 | tf_op jit(solution)/shard_map/ppermute | solution.py:338
  11.7 0.0 collective-permute-start.5
  11.7 1.2 %collective-permute-done.5.refs_3_ = bf16[256,128]{1,0:T(8,128)(2,1)S(1)} collective-permute-done((bf16[256,128]{1,0:T(8,128)(2,1)S(1)}, bf16[256,128]{1,0:T(8,128)(2,1)S(1)}, u32[]{:S(2)}, u32[]{:S(2)}) %collective-permute-start.5) | collective-permute-done | bytes 65568 | tf_op jit(solution)/shard_map/ppermute | solution.py:341
  13.0 0.6 %shard_map.96 = (f32[64,256]{1,0:T(8,128)S(1)}, f32[112,256]{1,0:T(8,128)S(1)}) custom-call(s32[2,2]{1,0:T(2,128)S(1)} %get-tuple-element.24.i_ref, s32[2,2]{1,0:T(2,128)S(1)} %collective-permute-done.j_ref, f32[64,256]{1,0:T(8,128)S(1)} %get-tuple-element.25.base_ref, bf16[320,256]{1,0:T(8,128)(2,1)S(1)} %get-tuple-element.26.high_ref, ...), custom_call_target="tpu_custom_call" | custom-call | flops 40000000 | bytes 1000000 | tf_op jit(solution)/shard_map/pallas_call | solution.py:353
  13.6 1.6 %collective-permute-start.6 = (f32[112,256]{1,0:T(8,128)S(1)}, f32[112,256]{1,0:T(8,128)S(1)}, u32[]{:S(2)}, u32[]{:S(2)}) collective-permute-start(f32[112,256]{1,0:T(8,128)S(1)} %get-tuple-element.33.mine_ref), channel_id=1, source_target_pairs={{0,2},{2,0},{1,3},{3,1},{4,6},{6,4},{5,7},{7,5},{8,10},{10,8},{9,1... | collective-permute-start | bytes 344072 | tf_op jit(solution)/shard_map/ppermute | solution.py:286
  15.2 0.4 %collective-permute-start.7 = (bf16[320,256]{1,0:T(8,128)(2,1)S(1)}, bf16[320,256]{1,0:T(8,128)(2,1)S(1)}, u32[]{:S(2)}, u32[]{:S(2)}) collective-permute-start(bf16[320,256]{1,0:T(8,128)(2,1)S(1)} %get-tuple-element.26.high_ref), channel_id=1, source_target_pairs={{0,2},{2,0},{1,3},{3,1},{4,6},{6,4},{5,7},{7,5},{8,10},{10,8},{9,1... | collective-permute-start | bytes 491528 | tf_op jit(solution)/shard_map/ppermute | solution.py:286
  15.7 4.0 %collective-permute-done.6.other_ref = f32[112,256]{1,0:T(8,128)S(1)} collective-permute-done((f32[112,256]{1,0:T(8,128)S(1)}, f32[112,256]{1,0:T(8,128)S(1)}, u32[]{:S(2)}, u32[]{:S(2)}) %collective-permute-start.6) | collective-permute-done | bytes 114720 | tf_op jit(solution)/shard_map/ppermute | solution.py:286
  19.7 1.6 %collective-permute-start.10 = (bf16[128,256]{1,0:T(8,128)(2,1)S(1)}, bf16[128,256]{1,0:T(8,128)(2,1)S(1)}, u32[]{:S(2)}, u32[]{:S(2)}) collective-permute-start(bf16[128,256]{1,0:T(8,128)(2,1)S(1)} %get-tuple-element.35), channel_id=1, source_target_pairs={{0,4},{4,0},{8,12},{12,8},{1,5},{5,1},{9,13},{13,9},{2,6},{6,2},{1... | collective-permute-start | bytes 196616 | tf_op jit(solution)/shard_map/ppermute | solution.py:286
  21.3 1.8 %collective-permute-start.8 = (bf16[128,256]{1,0:T(8,128)(2,1)S(1)}, bf16[128,256]{1,0:T(8,128)(2,1)S(1)}, u32[]{:S(2)}, u32[]{:S(2)}) collective-permute-start(bf16[128,256]{1,0:T(8,128)(2,1)S(1)} %get-tuple-element.35), channel_id=1, source_target_pairs={{0,8},{4,12},{8,0},{12,4},{1,9},{5,13},{9,1},{13,5},{2,10},{6,14},... | collective-permute-start | bytes 196616 | tf_op jit(solution)/shard_map/ppermute | solution.py:286
  23.1 1.1 %collective-permute-start.9 = (bf16[128,256]{1,0:T(8,128)(2,1)S(1)}, bf16[128,256]{1,0:T(8,128)(2,1)S(1)}, u32[]{:S(2)}, u32[]{:S(2)}) collective-permute-start(bf16[128,256]{1,0:T(8,128)(2,1)S(1)} %get-tuple-element.35), channel_id=1, source_target_pairs={{0,12},{4,8},{8,4},{12,0},{1,13},{5,9},{9,5},{13,1},{2,14},{6,10},... | collective-permute-start | bytes 196616 | tf_op jit(solution)/shard_map/ppermute | solution.py:286
  24.2 0.5 %collective-permute-done.10.refs_2_ = bf16[128,256]{1,0:T(8,128)(2,1)S(1)} collective-permute-done((bf16[128,256]{1,0:T(8,128)(2,1)S(1)}, bf16[128,256]{1,0:T(8,128)(2,1)S(1)}, u32[]{:S(2)}, u32[]{:S(2)}) %collective-permute-start.10) | collective-permute-done | bytes 65568 | tf_op jit(solution)/shard_map/ppermute | solution.py:286
  24.6 3.2 %collective-permute-done.8.refs_0_ = bf16[128,256]{1,0:T(8,128)(2,1)S(1)} collective-permute-done((bf16[128,256]{1,0:T(8,128)(2,1)S(1)}, bf16[128,256]{1,0:T(8,128)(2,1)S(1)}, u32[]{:S(2)}, u32[]{:S(2)}) %collective-permute-start.8) | collective-permute-done | bytes 65568 | tf_op jit(solution)/shard_map/ppermute | solution.py:286
  27.8 1.4 %collective-permute-done.9.refs_1_ = bf16[128,256]{1,0:T(8,128)(2,1)S(1)} collective-permute-done((bf16[128,256]{1,0:T(8,128)(2,1)S(1)}, bf16[128,256]{1,0:T(8,128)(2,1)S(1)}, u32[]{:S(2)}, u32[]{:S(2)}) %collective-permute-start.9) | collective-permute-done | bytes 65568 | tf_op jit(solution)/shard_map/ppermute | solution.py:286
  29.2 0.5 %shard_map.98 = (f32[192,256]{1,0:T(8,128)S(1)}, f32[64,64]{1,0:T(8,128)S(1)}) custom-call(f32[112,256]{1,0:T(8,128)S(1)} %get-tuple-element.34.total_ref, bf16[320,256]{1,0:T(8,128)(2,1)S(1)} %get-tuple-element.26.high_ref, bf16[320,256]{1,0:T(8,128)(2,1)S(1)} %get-tuple-element.27.low_ref, bf16[320,256]{1,0:T(8,128)(2,1)S(1)} %collective-permute-done.7.near_ref, ...), custom_call_target="tpu_custom_call" | custom-call | flops 40000000 | bytes 1000000 | tf_op jit(solution)/shard_map/pallas_call | solution.py:379
  29.7 0.1 collective-permute-start.11
  29.8 1.6 %collective-permute-start.12 = (f32[64,256]{1,0:T(8,128)S(1)}, f32[64,256]{1,0:T(8,128)S(1)}, u32[]{:S(2)}, u32[]{:S(2)}) collective-permute-start(f32[64,256]{1,0:T(8,128)S(1)} %get-tuple-element.37.y_ref), channel_id=1, source_target_pairs={{0,2},{2,0},{1,3},{3,1},{4,6},{6,4},{5,7},{7,5},{8,10},{10,8},{9,1... | collective-permute-start | bytes 196616 | tf_op jit(solution)/shard_map/ppermute | solution.py:286
  31.4 2.9 %collective-permute-done.12.z_ref = f32[64,256]{1,0:T(8,128)S(1)} collective-permute-done((f32[64,256]{1,0:T(8,128)S(1)}, f32[64,256]{1,0:T(8,128)S(1)}, u32[]{:S(2)}, u32[]{:S(2)}) %collective-permute-start.12) | collective-permute-done | bytes 65568 | tf_op jit(solution)/shard_map/ppermute | solution.py:286
  34.3 0.2 shard_map.99
  34.5 0.6 %collective-permute-start.13 = (f32[32,128]{1,0:T(8,128)S(1)}, f32[32,128]{1,0:T(8,128)S(1)}, u32[]{:S(2)}, u32[]{:S(2)}) collective-permute-start(f32[32,128]{1,0:T(8,128)S(1)} %get-tuple-element.38.own_ref), channel_id=1, source_target_pairs={{0,8},{1,13},{4,12},{5,9},{8,0},{9,5},{12,4},{13,1},{2,10},{3,15},... | collective-permute-start | bytes 49160 | tf_op jit(solution)/shard_map/ppermute | solution.py:338
  35.1 1.1 %collective-permute-start.15 = (f32[16,128]{1,0:T(8,128)S(1)}, f32[16,128]{1,0:T(8,128)S(1)}, u32[]{:S(2)}, u32[]{:S(2)}) collective-permute-start(f32[16,128]{1,0:T(8,128)S(1)} %get-tuple-element.41), channel_id=1, source_target_pairs={{0,4},{1,5},{4,0},{5,1},{8,12},{9,13},{12,8},{13,9},{2,6},{3,7},{6... | collective-permute-start | bytes 24584 | tf_op jit(solution)/shard_map/ppermute | solution.py:338
  36.1 3.1 %collective-permute-done.13.refs_0_ = f32[32,128]{1,0:T(8,128)S(1)} collective-permute-done((f32[32,128]{1,0:T(8,128)S(1)}, f32[32,128]{1,0:T(8,128)S(1)}, u32[]{:S(2)}, u32[]{:S(2)}) %collective-permute-start.13) | collective-permute-done | bytes 16416 | tf_op jit(solution)/shard_map/ppermute | solution.py:338
  39.2 0.5 %collective-permute-start.16 = (f32[16,128]{1,0:T(8,128)S(1)}, f32[16,128]{1,0:T(8,128)S(1)}, u32[]{:S(2)}, u32[]{:S(2)}) collective-permute-start(f32[16,128]{1,0:T(8,128)S(1)} %collective-permute-done.15.refs_2_), channel_id=1, source_target_pairs={{0,1},{1,0},{2,3},{3,2},{4,5},{5,4},{6,7},{7,6},{8,9},{9,8},{10,11... | collective-permute-start | bytes 24584 | tf_op jit(solution)/shard_map/ppermute | solution.py:341
  39.7 0.8 %collective-permute-done.16.refs_3_ = f32[16,128]{1,0:T(8,128)S(1)} collective-permute-done((f32[16,128]{1,0:T(8,128)S(1)}, f32[16,128]{1,0:T(8,128)S(1)}, u32[]{:S(2)}, u32[]{:S(2)}) %collective-permute-start.16) | collective-permute-done | bytes 8224 | tf_op jit(solution)/shard_map/ppermute | solution.py:341
  40.6 2.0 %shard_map.100 = (f32[64,256]{1,0:T(8,128)}, f32[64,64]{1,0:T(8,128)}, f32[64,64]{1,0:T(8,128)}) custom-call(f32[32,128]{1,0:T(8,128)S(1)} %get-tuple-element.38.own_ref, f32[64,256]{1,0:T(8,128)S(1)} %get-tuple-element.39.images_ref, f32[64,64]{1,0:T(8,128)S(1)} %get-tuple-element.40.d_ref, f32[32,128]{1,0:T(8,128)S(1)} %collective-permute-done.13.refs_0_, ...), custom_call_target="tpu_custom_call" | custom-call | flops 40000000 | bytes 1000000 | tf_op jit(solution)/shard_map/pallas_call | solution.py:389
  (9 shorter events, 0.0 us)
Async XLA Ops:
  0.6 1.9 %collective-permute-start.1 = (bf16[2,256,256]{2,1,0:T(8,128)(2,1)}, bf16[2,256,256]{2,1,0:T(8,128)(2,1)S(1)}, u32[]{:S(2)}, u32[]{:S(2)}) collective-permute-start(bf16[2,256,256]{2,1,0:T(8,128)(2,1)} %t_hbm.1), channel_id=1, source_target_pairs={{0,1},{1,0},{2,3},{3,2},{4,5},{5,4},{6,7},{7,6},{8,9},{9,8},{10,11... | collective-permute-start | bytes 786440 | tf_op jit(solution)/shard_map/ppermute | solution.py:310
  1.2 1.4 %collective-permute-start = (s32[2,2]{1,0:T(2,128)}, s32[2,2]{1,0:T(2,128)S(1)}, u32[]{:S(2)}, u32[]{:S(2)}) collective-permute-start(s32[2,2]{1,0:T(2,128)} %i_hbm.1), channel_id=1, source_target_pairs={{0,1},{1,0},{2,3},{3,2},{4,5},{5,4},{6,7},{7,6},{8,9},{9,8},{10,11... | collective-permute-start | bytes 56 | tf_op jit(solution)/shard_map/ppermute | solution.py:311
  2.8 7.6 %collective-permute-start.2 = (bf16[128,256]{1,0:T(8,128)(2,1)S(1)}, bf16[128,256]{1,0:T(8,128)(2,1)S(1)}, u32[]{:S(2)}, u32[]{:S(2)}) collective-permute-start(bf16[128,256]{1,0:T(8,128)(2,1)S(1)} %get-tuple-element.31), channel_id=1, source_target_pairs={{0,8},{1,13},{4,12},{5,9},{8,0},{9,5},{12,4},{13,1},{2,10},{3,15},... | collective-permute-start | bytes 196616 | tf_op jit(solution)/shard_map/ppermute | solution.py:338
  6.9 4.9 %collective-permute-start.4 = (bf16[256,128]{1,0:T(8,128)(2,1)S(1)}, bf16[256,128]{1,0:T(8,128)(2,1)S(1)}, u32[]{:S(2)}, u32[]{:S(2)}) collective-permute-start(bf16[256,128]{1,0:T(8,128)(2,1)S(1)} %get-tuple-element.32), channel_id=1, source_target_pairs={{0,4},{1,5},{4,0},{5,1},{8,12},{9,13},{12,8},{13,9},{2,6},{3,7},{6... | collective-permute-start | bytes 196616 | tf_op jit(solution)/shard_map/ppermute | solution.py:338
  10.4 1.4 %collective-permute-start.3 = (bf16[128,256]{1,0:T(8,128)(2,1)S(1)}, bf16[128,256]{1,0:T(8,128)(2,1)S(1)}, u32[]{:S(2)}, u32[]{:S(2)}) collective-permute-start(bf16[128,256]{1,0:T(8,128)(2,1)S(1)} %collective-permute-done.2.refs_0_), channel_id=1, source_target_pairs={{0,1},{1,0},{2,3},{3,2},{4,5},{5,4},{6,7},{7,6},{8,9},{9,8},{10,11... | collective-permute-start | bytes 196616 | tf_op jit(solution)/shard_map/ppermute | solution.py:341
  11.7 1.3 %collective-permute-start.5 = (bf16[256,128]{1,0:T(8,128)(2,1)S(1)}, bf16[256,128]{1,0:T(8,128)(2,1)S(1)}, u32[]{:S(2)}, u32[]{:S(2)}) collective-permute-start(bf16[256,128]{1,0:T(8,128)(2,1)S(1)} %collective-permute-done.4.refs_2_), channel_id=1, source_target_pairs={{0,1},{1,0},{2,3},{3,2},{4,5},{5,4},{6,7},{7,6},{8,9},{9,8},{10,11... | collective-permute-start | bytes 196616 | tf_op jit(solution)/shard_map/ppermute | solution.py:341
  13.6 6.1 %collective-permute-start.6 = (f32[112,256]{1,0:T(8,128)S(1)}, f32[112,256]{1,0:T(8,128)S(1)}, u32[]{:S(2)}, u32[]{:S(2)}) collective-permute-start(f32[112,256]{1,0:T(8,128)S(1)} %get-tuple-element.33.mine_ref), channel_id=1, source_target_pairs={{0,2},{2,0},{1,3},{3,1},{4,6},{6,4},{5,7},{7,5},{8,10},{10,8},{9,1... | collective-permute-start | bytes 344072 | tf_op jit(solution)/shard_map/ppermute | solution.py:286
  15.2 8.9 %collective-permute-start.7 = (bf16[320,256]{1,0:T(8,128)(2,1)S(1)}, bf16[320,256]{1,0:T(8,128)(2,1)S(1)}, u32[]{:S(2)}, u32[]{:S(2)}) collective-permute-start(bf16[320,256]{1,0:T(8,128)(2,1)S(1)} %get-tuple-element.26.high_ref), channel_id=1, source_target_pairs={{0,2},{2,0},{1,3},{3,1},{4,6},{6,4},{5,7},{7,5},{8,10},{10,8},{9,1... | collective-permute-start | bytes 491528 | tf_op jit(solution)/shard_map/ppermute | solution.py:286
  19.7 4.9 %collective-permute-start.10 = (bf16[128,256]{1,0:T(8,128)(2,1)S(1)}, bf16[128,256]{1,0:T(8,128)(2,1)S(1)}, u32[]{:S(2)}, u32[]{:S(2)}) collective-permute-start(bf16[128,256]{1,0:T(8,128)(2,1)S(1)} %get-tuple-element.35), channel_id=1, source_target_pairs={{0,4},{4,0},{8,12},{12,8},{1,5},{5,1},{9,13},{13,9},{2,6},{6,2},{1... | collective-permute-start | bytes 196616 | tf_op jit(solution)/shard_map/ppermute | solution.py:286
  21.3 6.5 %collective-permute-start.8 = (bf16[128,256]{1,0:T(8,128)(2,1)S(1)}, bf16[128,256]{1,0:T(8,128)(2,1)S(1)}, u32[]{:S(2)}, u32[]{:S(2)}) collective-permute-start(bf16[128,256]{1,0:T(8,128)(2,1)S(1)} %get-tuple-element.35), channel_id=1, source_target_pairs={{0,8},{4,12},{8,0},{12,4},{1,9},{5,13},{9,1},{13,5},{2,10},{6,14},... | collective-permute-start | bytes 196616 | tf_op jit(solution)/shard_map/ppermute | solution.py:286
  23.1 6.1 %collective-permute-start.9 = (bf16[128,256]{1,0:T(8,128)(2,1)S(1)}, bf16[128,256]{1,0:T(8,128)(2,1)S(1)}, u32[]{:S(2)}, u32[]{:S(2)}) collective-permute-start(bf16[128,256]{1,0:T(8,128)(2,1)S(1)} %get-tuple-element.35), channel_id=1, source_target_pairs={{0,12},{4,8},{8,4},{12,0},{1,13},{5,9},{9,5},{13,1},{2,14},{6,10},... | collective-permute-start | bytes 196616 | tf_op jit(solution)/shard_map/ppermute | solution.py:286
  29.7 4.6 %collective-permute-start.11 = (f32[192,256]{1,0:T(8,128)S(1)}, f32[192,256]{1,0:T(8,128)S(1)}, u32[]{:S(2)}, u32[]{:S(2)}) collective-permute-start(f32[192,256]{1,0:T(8,128)S(1)} %get-tuple-element.36.mine_ref), channel_id=1, source_target_pairs={{0,1},{1,0},{2,3},{3,2},{4,5},{5,4},{6,7},{7,6},{8,9},{9,8},{10,11... | collective-permute-start | bytes 589832 | tf_op jit(solution)/shard_map/ppermute | solution.py:384
  29.8 4.5 %collective-permute-start.12 = (f32[64,256]{1,0:T(8,128)S(1)}, f32[64,256]{1,0:T(8,128)S(1)}, u32[]{:S(2)}, u32[]{:S(2)}) collective-permute-start(f32[64,256]{1,0:T(8,128)S(1)} %get-tuple-element.37.y_ref), channel_id=1, source_target_pairs={{0,2},{2,0},{1,3},{3,1},{4,6},{6,4},{5,7},{7,5},{8,10},{10,8},{9,1... | collective-permute-start | bytes 196616 | tf_op jit(solution)/shard_map/ppermute | solution.py:286
  34.5 4.7 %collective-permute-start.13 = (f32[32,128]{1,0:T(8,128)S(1)}, f32[32,128]{1,0:T(8,128)S(1)}, u32[]{:S(2)}, u32[]{:S(2)}) collective-permute-start(f32[32,128]{1,0:T(8,128)S(1)} %get-tuple-element.38.own_ref), channel_id=1, source_target_pairs={{0,8},{1,13},{4,12},{5,9},{8,0},{9,5},{12,4},{13,1},{2,10},{3,15},... | collective-permute-start | bytes 49160 | tf_op jit(solution)/shard_map/ppermute | solution.py:338
  35.1 4.1 %collective-permute-start.15 = (f32[16,128]{1,0:T(8,128)S(1)}, f32[16,128]{1,0:T(8,128)S(1)}, u32[]{:S(2)}, u32[]{:S(2)}) collective-permute-start(f32[16,128]{1,0:T(8,128)S(1)} %get-tuple-element.41), channel_id=1, source_target_pairs={{0,4},{1,5},{4,0},{5,1},{8,12},{9,13},{12,8},{13,9},{2,6},{3,7},{6... | collective-permute-start | bytes 24584 | tf_op jit(solution)/shard_map/ppermute | solution.py:338
  39.2 1.3 %collective-permute-start.14 = (f32[32,128]{1,0:T(8,128)S(1)}, f32[32,128]{1,0:T(8,128)S(1)}, u32[]{:S(2)}, u32[]{:S(2)}) collective-permute-start(f32[32,128]{1,0:T(8,128)S(1)} %collective-permute-done.13.refs_0_), channel_id=1, source_target_pairs={{0,1},{1,0},{2,3},{3,2},{4,5},{5,4},{6,7},{7,6},{8,9},{9,8},{10,11... | collective-permute-start | bytes 49160 | tf_op jit(solution)/shard_map/ppermute | solution.py:341
  39.2 1.3 %collective-permute-start.16 = (f32[16,128]{1,0:T(8,128)S(1)}, f32[16,128]{1,0:T(8,128)S(1)}, u32[]{:S(2)}, u32[]{:S(2)}) collective-permute-start(f32[16,128]{1,0:T(8,128)S(1)} %collective-permute-done.15.refs_2_), channel_id=1, source_target_pairs={{0,1},{1,0},{2,3},{3,2},{4,5},{5,4},{6,7},{7,6},{8,9},{9,8},{10,11... | collective-permute-start | bytes 24584 | tf_op jit(solution)/shard_map/ppermute | solution.py:341

commit v9 on v8

--- a/solution.py
+++ b/solution.py
@@ -123,7 +123,8 @@
     parity = jnp.bitwise_and(me, 1)
     outs[0][...] = jnp.concatenate([pushed(me), corr_ref[parity]], axis=0)
     for ref, pair in zip(outs[1:], pairs):
-        message = jnp.concatenate([x.astype(f32), pushed(target_band(me, core, pair))], axis=0)
+        products_of = split(pushed(target_band(me, core, pair)))
+        message = jnp.concatenate([h.astype(f32) for h in (x, *products_of)], axis=0)
         if pair[0] != pair[1]:
             ref[...] = message.astype(bf16)
         else:
@@ -145,15 +146,15 @@
         if pair[0] != pair[1]:
             found = [(target_band(me, core, pair), mine), (target_band(me, core, pair[::-1]), other)]
         else:
-            parts_of = mine[2 * block :]
+            parts_of = mine[3 * block :]
             count = parts_of.shape[0] // 2
             corr = corr + fold(parts_of[:count] + parts_of[count:], 2)
-            mine, other = mine[: 2 * block], other[: 2 * block]
+            mine, other = mine[: 3 * block], other[: 3 * block]
             first, second = jnp.where(core == 0, mine, other), jnp.where(core == 0, other, mine)
             found = [(jnp.bitwise_xor(me, pair[0]), jnp.concatenate([first, second], axis=1))]
         for band, message in found:
             blocks.append((band, message[0:block]))
-            y = y + message[block:]
+            y = y + (message[block : 2 * block] + message[2 * block :])
     tiles = [ref[k] for ref in (t_ref, u_ref) for k in range(ref.shape[0])]
     for target, tile in zip(tile_columns((i_ref, j_ref), (block, rows)), tiles):
         source = jnp.zeros((block, rows), f32)
@@ -171,17 +172,15 @@
     send_ref[...] = jnp.concatenate([stored, diagonal, corr], axis=0)
 
 
-def pack(total, block, small):
-    high, low = split(total[block : block + small])
-    message = [total[0:block], high.astype(f32), low.astype(f32), total[block + small :]]
-    return jnp.concatenate(message, axis=0).astype(bf16)
-
-
-def combine_kernel(block, small, mine_ref, other_ref, total_ref, *send_refs):
+def pack(total):
+    return jnp.concatenate([h.astype(f32) for h in split(total)], axis=0).astype(bf16)
+
+
+def combine_kernel(mine_ref, other_ref, total_ref, *send_refs):
     total = mine_ref[...] + other_ref[...]
     total_ref[...] = total
     for ref in send_refs:
-        ref[...] = pack(total, block, small)
+        ref[...] = pack(total)
 
 
 def project_kernel(steps, block, parts, total_rows, total_ref, high_ref, low_ref, near_ref, *refs):
@@ -193,10 +192,10 @@
     same, other = total[block + small :], jnp.zeros((block // 2, total.shape[1]), f32)
     for step, ref in zip(steps, received):
         message = ref[...].astype(f32)
+        message = message[: total.shape[0]] + message[total.shape[0] :]
         stored = stored + message[0:block]
         diagonal = diagonal + message[block : block + small]
-        diagonal = diagonal + message[block + small : block + 2 * small]
-        part = message[block + 2 * small :]
+        part = message[block + small :]
         if step % 2:
             other = other + part
         else:
@@ -344,7 +343,7 @@
     sends = call(
         functools.partial(push_kernel, pairs, columns),
         [((block + chunk, rows), f32)]
-        + [((2 * block, rows) if a != b else (4 * block, rows // 2), bf16) for a, b in pairs],
+        + [((3 * block, rows) if a != b else (5 * block, rows // 2), bf16) for a, b in pairs],
         "vvvvvv",
     )(index, other_index, high, corr, tiles, other_tiles)
     near = exchange(high, "cols", 1)
@@ -359,14 +358,14 @@
     late = exchange(y, "cols", 1)
     distances = [2**k for k in range(1, columns.bit_length() - 1)]
     total, *send = call(
-        functools.partial(combine_kernel, block, small),
+        combine_kernel,
         [((block + small + chunk, rows), f32)]
-        + [((block + 2 * small + chunk, rows), bf16)] * (not distances),
+        + [((2 * (block + small + chunk), rows), bf16)] * (not distances),
         "vv",
     )(mine, other)
     for distance in distances:
         total = total + exchange(total, "cols", distance)
-    send = send[0] if send else pack(total, block, small)
+    send = send[0] if send else pack(total)
     steps = [*range(2, bands), 1]
     received = []
     for step in steps:

time: 42.7 us -> 47.5 us (1.11)
  waiting for transfers between devices: 20.4 us -> 24.5 us
  starting transfers between devices: 16.7 us -> 17.2 us
    ppermute x6, waiting for transfers between devices: 11.9 us -> 14.3 us  [exchange(): lax.ppermute(x, axis, [(i, i ^ distance) for i in range(lax.axis_size(axi...]
    ppermute x4, waiting for transfers between devices: 6.34 us -> 7.76 us  [serve(): received.append(lax.ppermute(send, ('rows', 'sub'), moves))]
    ppermute x4, starting transfers between devices: 7.29 us -> 8.41 us  [serve(): received.append(lax.ppermute(send, ('rows', 'sub'), moves))]
    ppermute x4, starting transfers between devices: 0.52 us -> 0.01 us  [serve(): swapped += [x, lax.ppermute(x, 'sub', swap)]]
where the time goes in v9:
time: 47.5 us; the launch traced here: 47.3 us
  waiting for transfers between devices  24.5 us (52%)
  starting transfers between devices  17.2 us (36%)
  Pallas kernels  4.88 us (10%)
  between operations  0.69 us (1%)
    ppermute x6, waiting for transfers between devices, exchange(): lax.ppermute(x, axis, [(i, i ^ distance) for i in range(lax.axis_size(axi...  14.3 us
    ppermute x4, starting transfers between devices, serve(): received.append(lax.ppermute(send, ('rows', 'sub'), moves))  8.41 us
    ppermute x6, starting transfers between devices, exchange(): lax.ppermute(x, axis, [(i, i ^ distance) for i in range(lax.axis_size(axi...  8.11 us
    ppermute x4, waiting for transfers between devices, serve(): received.append(lax.ppermute(send, ('rows', 'sub'), moves))  7.76 us
    ppermute x4, waiting for transfers between devices, serve(): swapped += [x, lax.ppermute(x, 'sub', swap)]  2.45 us
    pallas_call x1, Pallas kernels, local(): call(functools.partial(factor_kernel, pairs, total_rows), [(half, f32), (...  2.03 us
    pallas_call x1, Pallas kernels, local(): prepare(*(pltpu.with_memory_space_constraint(a, pltpu.HBM) for a in sourc...  1.27 us
  transfers between devices with their start and end apart: 17, of which 10 were waited for; matrix products, arithmetic and copies ran while one was open for 0% of the time, Pallas kernels for 3%

profile of v9, /device:TPU:0, one launch (start us, length us, event | category | flops | bytes accessed | tf_op | source)
XLA Modules:
  0.0 47.3 jit_solution(4179090911020170354)
XLA Ops:
  0.6 0.6 %collective-permute-start.1 = (bf16[2,256,256]{2,1,0:T(8,128)(2,1)}, bf16[2,256,256]{2,1,0:T(8,128)(2,1)S(1)}, u32[]{:S(2)}, u32[]{:S(2)}) collective-permute-start(bf16[2,256,256]{2,1,0:T(8,128)(2,1)} %t_hbm.1), channel_id=1, source_target_pairs={{0,1},{1,0},{2,3},{3,2},{4,5},{5,4},{6,7},{7,6},{8,9},{9,8},{10,11... | collective-permute-start | bytes 786440 | tf_op jit(solution)/shard_map/ppermute | solution.py:309
  1.2 0.1 collective-permute-start
  1.3 1.3 %shard_map.94 = (f32[64,256]{1,0:T(8,128)S(1)}, f32[2,32,256]{2,1,0:T(8,128)S(1)}, bf16[320,256]{1,0:T(8,128)(2,1)S(1)}, bf16[320,256]{1,0:T(8,128)(2,1)S(1)}, b...) custom-call(f32[64,256]{1,0:T(8,128)} %bitcast.12, f32[1,256]{1,0:T(1,128)} %bitcast.14, f32[64,256]{1,0:T(8,128)} %bitcast.13, ...), custom_call_target="tpu_custom_call" | custom-call | flops 40000000 | bytes 1000000 | tf_op jit(solution)/shard_map/pallas_call | solution.py:328
  2.5 0.0 collective-permute-done.j_ref
  2.6 0.0 collective-permute-done.1.u_ref
  2.6 0.2 shard_map.95
  2.8 4.1 %collective-permute-start.2 = (bf16[192,256]{1,0:T(8,128)(2,1)S(1)}, bf16[192,256]{1,0:T(8,128)(2,1)S(1)}, u32[]{:S(2)}, u32[]{:S(2)}) collective-permute-start(bf16[192,256]{1,0:T(8,128)(2,1)S(1)} %get-tuple-element.31), channel_id=1, source_target_pairs={{0,8},{1,13},{4,12},{5,9},{8,0},{9,5},{12,4},{13,1},{2,10},{3,15},... | collective-permute-start | bytes 294920 | tf_op jit(solution)/shard_map/ppermute | solution.py:337
  6.9 1.6 %collective-permute-start.4 = (bf16[320,128]{1,0:T(8,128)(2,1)S(1)}, bf16[320,128]{1,0:T(8,128)(2,1)S(1)}, u32[]{:S(2)}, u32[]{:S(2)}) collective-permute-start(bf16[320,128]{1,0:T(8,128)(2,1)S(1)} %get-tuple-element.32), channel_id=1, source_target_pairs={{0,4},{1,5},{4,0},{5,1},{8,12},{9,13},{12,8},{13,9},{2,6},{3,7},{6... | collective-permute-start | bytes 245768 | tf_op jit(solution)/shard_map/ppermute | solution.py:337
  8.5 3.8 %collective-permute-done.2.refs_0_ = bf16[192,256]{1,0:T(8,128)(2,1)S(1)} collective-permute-done((bf16[192,256]{1,0:T(8,128)(2,1)S(1)}, bf16[192,256]{1,0:T(8,128)(2,1)S(1)}, u32[]{:S(2)}, u32[]{:S(2)}) %collective-permute-start.2) | collective-permute-done | bytes 98336 | tf_op jit(solution)/shard_map/ppermute | solution.py:337
  12.3 0.5 %collective-permute-done.4.refs_2_ = bf16[320,128]{1,0:T(8,128)(2,1)S(1)} collective-permute-done((bf16[320,128]{1,0:T(8,128)(2,1)S(1)}, bf16[320,128]{1,0:T(8,128)(2,1)S(1)}, u32[]{:S(2)}, u32[]{:S(2)}) %collective-permute-start.4) | collective-permute-done | bytes 81952 | tf_op jit(solution)/shard_map/ppermute | solution.py:337
  12.8 0.0 collective-permute-start.5
  12.8 1.3 %collective-permute-done.5.refs_3_ = bf16[320,128]{1,0:T(8,128)(2,1)S(1)} collective-permute-done((bf16[320,128]{1,0:T(8,128)(2,1)S(1)}, bf16[320,128]{1,0:T(8,128)(2,1)S(1)}, u32[]{:S(2)}, u32[]{:S(2)}) %collective-permute-start.5) | collective-permute-done | bytes 81952 | tf_op jit(solution)/shard_map/ppermute | solution.py:340
  14.1 0.6 %shard_map.96 = (f32[64,256]{1,0:T(8,128)S(1)}, f32[112,256]{1,0:T(8,128)S(1)}) custom-call(s32[2,2]{1,0:T(2,128)S(1)} %get-tuple-element.24.i_ref, s32[2,2]{1,0:T(2,128)S(1)} %collective-permute-done.j_ref, f32[64,256]{1,0:T(8,128)S(1)} %get-tuple-element.25.base_ref, bf16[320,256]{1,0:T(8,128)(2,1)S(1)} %get-tuple-element.26.high_ref, ...), custom_call_target="tpu_custom_call" | custom-call | flops 40000000 | bytes 1000000 | tf_op jit(solution)/shard_map/pallas_call | solution.py:352
  14.7 1.7 %collective-permute-start.6 = (f32[112,256]{1,0:T(8,128)S(1)}, f32[112,256]{1,0:T(8,128)S(1)}, u32[]{:S(2)}, u32[]{:S(2)}) collective-permute-start(f32[112,256]{1,0:T(8,128)S(1)} %get-tuple-element.33.mine_ref), channel_id=1, source_target_pairs={{0,2},{2,0},{1,3},{3,1},{4,6},{6,4},{5,7},{7,5},{8,10},{10,8},{9,1... | collective-permute-start | bytes 344072 | tf_op jit(solution)/shard_map/ppermute | solution.py:285
  16.4 0.4 collective-permute-start.7
  16.8 4.0 %collective-permute-done.6.other_ref = f32[112,256]{1,0:T(8,128)S(1)} collective-permute-done((f32[112,256]{1,0:T(8,128)S(1)}, f32[112,256]{1,0:T(8,128)S(1)}, u32[]{:S(2)}, u32[]{:S(2)}) %collective-permute-start.6) | collective-permute-done | bytes 114720 | tf_op jit(solution)/shard_map/ppermute | solution.py:285
  20.8 1.5 %collective-permute-start.10 = (bf16[224,256]{1,0:T(8,128)(2,1)S(1)}, bf16[224,256]{1,0:T(8,128)(2,1)S(1)}, u32[]{:S(2)}, u32[]{:S(2)}) collective-permute-start(bf16[224,256]{1,0:T(8,128)(2,1)S(1)} %get-tuple-element.35), channel_id=1, source_target_pairs={{0,4},{4,0},{8,12},{12,8},{1,5},{5,1},{9,13},{13,9},{2,6},{6,2},{1... | collective-permute-start | bytes 344072 | tf_op jit(solution)/shard_map/ppermute | solution.py:285
  22.3 1.9 %collective-permute-start.8 = (bf16[224,256]{1,0:T(8,128)(2,1)S(1)}, bf16[224,256]{1,0:T(8,128)(2,1)S(1)}, u32[]{:S(2)}, u32[]{:S(2)}) collective-permute-start(bf16[224,256]{1,0:T(8,128)(2,1)S(1)} %get-tuple-element.35), channel_id=1, source_target_pairs={{0,8},{4,12},{8,0},{12,4},{1,9},{5,13},{9,1},{13,5},{2,10},{6,14},... | collective-permute-start | bytes 344072 | tf_op jit(solution)/shard_map/ppermute | solution.py:285
  24.2 1.1 %collective-permute-start.9 = (bf16[224,256]{1,0:T(8,128)(2,1)S(1)}, bf16[224,256]{1,0:T(8,128)(2,1)S(1)}, u32[]{:S(2)}, u32[]{:S(2)}) collective-permute-start(bf16[224,256]{1,0:T(8,128)(2,1)S(1)} %get-tuple-element.35), channel_id=1, source_target_pairs={{0,12},{4,8},{8,4},{12,0},{1,13},{5,9},{9,5},{13,1},{2,14},{6,10},... | collective-permute-start | bytes 344072 | tf_op jit(solution)/shard_map/ppermute | solution.py:285
  25.3 1.2 %collective-permute-done.10.refs_2_ = bf16[224,256]{1,0:T(8,128)(2,1)S(1)} collective-permute-done((bf16[224,256]{1,0:T(8,128)(2,1)S(1)}, bf16[224,256]{1,0:T(8,128)(2,1)S(1)}, u32[]{:S(2)}, u32[]{:S(2)}) %collective-permute-start.10) | collective-permute-done | bytes 114720 | tf_op jit(solution)/shard_map/ppermute | solution.py:285
  26.5 6.1 %collective-permute-done.8.refs_0_ = bf16[224,256]{1,0:T(8,128)(2,1)S(1)} collective-permute-done((bf16[224,256]{1,0:T(8,128)(2,1)S(1)}, bf16[224,256]{1,0:T(8,128)(2,1)S(1)}, u32[]{:S(2)}, u32[]{:S(2)}) %collective-permute-start.8) | collective-permute-done | bytes 114720 | tf_op jit(solution)/shard_map/ppermute | solution.py:285
  32.6 0.5 %shard_map.98 = (f32[192,256]{1,0:T(8,128)S(1)}, f32[64,64]{1,0:T(8,128)S(1)}) custom-call(f32[112,256]{1,0:T(8,128)S(1)} %get-tuple-element.34.total_ref, bf16[320,256]{1,0:T(8,128)(2,1)S(1)} %get-tuple-element.26.high_ref, bf16[320,256]{1,0:T(8,128)(2,1)S(1)} %get-tuple-element.27.low_ref, bf16[320,256]{1,0:T(8,128)(2,1)S(1)} %collective-permute-done.7.near_ref, ...), custom_call_target="tpu_custom_call" | custom-call | flops 40000000 | bytes 1000000 | tf_op jit(solution)/shard_map/pallas_call | solution.py:378
  33.1 0.1 collective-permute-start.11
  33.2 1.6 %collective-permute-start.12 = (f32[64,256]{1,0:T(8,128)S(1)}, f32[64,256]{1,0:T(8,128)S(1)}, u32[]{:S(2)}, u32[]{:S(2)}) collective-permute-start(f32[64,256]{1,0:T(8,128)S(1)} %get-tuple-element.37.y_ref), channel_id=1, source_target_pairs={{0,2},{2,0},{1,3},{3,1},{4,6},{6,4},{5,7},{7,5},{8,10},{10,8},{9,1... | collective-permute-start | bytes 196616 | tf_op jit(solution)/shard_map/ppermute | solution.py:285
  34.8 2.9 %collective-permute-done.12.z_ref = f32[64,256]{1,0:T(8,128)S(1)} collective-permute-done((f32[64,256]{1,0:T(8,128)S(1)}, f32[64,256]{1,0:T(8,128)S(1)}, u32[]{:S(2)}, u32[]{:S(2)}) %collective-permute-start.12) | collective-permute-done | bytes 65568 | tf_op jit(solution)/shard_map/ppermute | solution.py:285
  37.7 0.2 shard_map.99
  37.9 2.5 %collective-permute-start.13 = (f32[32,128]{1,0:T(8,128)S(1)}, f32[32,128]{1,0:T(8,128)S(1)}, u32[]{:S(2)}, u32[]{:S(2)}) collective-permute-start(f32[32,128]{1,0:T(8,128)S(1)} %get-tuple-element.38.own_ref), channel_id=1, source_target_pairs={{0,8},{1,13},{4,12},{5,9},{8,0},{9,5},{12,4},{13,1},{2,10},{3,15},... | collective-permute-start | bytes 49160 | tf_op jit(solution)/shard_map/ppermute | solution.py:337
  40.5 0.2 collective-permute-start.15
  40.7 1.9 %collective-permute-done.13.refs_0_ = f32[32,128]{1,0:T(8,128)S(1)} collective-permute-done((f32[32,128]{1,0:T(8,128)S(1)}, f32[32,128]{1,0:T(8,128)S(1)}, u32[]{:S(2)}, u32[]{:S(2)}) %collective-permute-start.13) | collective-permute-done | bytes 16416 | tf_op jit(solution)/shard_map/ppermute | solution.py:337
  42.6 1.5 %collective-permute-done.15.refs_2_ = f32[16,128]{1,0:T(8,128)S(1)} collective-permute-done((f32[16,128]{1,0:T(8,128)S(1)}, f32[16,128]{1,0:T(8,128)S(1)}, u32[]{:S(2)}, u32[]{:S(2)}) %collective-permute-start.15) | collective-permute-done | bytes 8224 | tf_op jit(solution)/shard_map/ppermute | solution.py:337
  44.1 1.2 %collective-permute-done.16.refs_3_ = f32[16,128]{1,0:T(8,128)S(1)} collective-permute-done((f32[16,128]{1,0:T(8,128)S(1)}, f32[16,128]{1,0:T(8,128)S(1)}, u32[]{:S(2)}, u32[]{:S(2)}) %collective-permute-start.16) | collective-permute-done | bytes 8224 | tf_op jit(solution)/shard_map/ppermute | solution.py:340
  45.3 2.0 %shard_map.100 = (f32[64,256]{1,0:T(8,128)}, f32[64,64]{1,0:T(8,128)}, f32[64,64]{1,0:T(8,128)}) custom-call(f32[32,128]{1,0:T(8,128)S(1)} %get-tuple-element.38.own_ref, f32[64,256]{1,0:T(8,128)S(1)} %get-tuple-element.39.images_ref, f32[64,64]{1,0:T(8,128)S(1)} %get-tuple-element.40.d_ref, f32[32,128]{1,0:T(8,128)S(1)} %collective-permute-done.13.refs_0_, ...), custom_call_target="tpu_custom_call" | custom-call | flops 40000000 | bytes 1000000 | tf_op jit(solution)/shard_map/pallas_call | solution.py:388
  (9 shorter events, 0.0 us)
Async XLA Ops:
  0.6 1.9 %collective-permute-start.1 = (bf16[2,256,256]{2,1,0:T(8,128)(2,1)}, bf16[2,256,256]{2,1,0:T(8,128)(2,1)S(1)}, u32[]{:S(2)}, u32[]{:S(2)}) collective-permute-start(bf16[2,256,256]{2,1,0:T(8,128)(2,1)} %t_hbm.1), channel_id=1, source_target_pairs={{0,1},{1,0},{2,3},{3,2},{4,5},{5,4},{6,7},{7,6},{8,9},{9,8},{10,11... | collective-permute-start | bytes 786440 | tf_op jit(solution)/shard_map/ppermute | solution.py:309
  1.2 1.4 %collective-permute-start = (s32[2,2]{1,0:T(2,128)}, s32[2,2]{1,0:T(2,128)S(1)}, u32[]{:S(2)}, u32[]{:S(2)}) collective-permute-start(s32[2,2]{1,0:T(2,128)} %i_hbm.1), channel_id=1, source_target_pairs={{0,1},{1,0},{2,3},{3,2},{4,5},{5,4},{6,7},{7,6},{8,9},{9,8},{10,11... | collective-permute-start | bytes 56 | tf_op jit(solution)/shard_map/ppermute | solution.py:310
  2.8 9.5 %collective-permute-start.2 = (bf16[192,256]{1,0:T(8,128)(2,1)S(1)}, bf16[192,256]{1,0:T(8,128)(2,1)S(1)}, u32[]{:S(2)}, u32[]{:S(2)}) collective-permute-start(bf16[192,256]{1,0:T(8,128)(2,1)S(1)} %get-tuple-element.31), channel_id=1, source_target_pairs={{0,8},{1,13},{4,12},{5,9},{8,0},{9,5},{12,4},{13,1},{2,10},{3,15},... | collective-permute-start | bytes 294920 | tf_op jit(solution)/shard_map/ppermute | solution.py:337
  6.9 5.9 %collective-permute-start.4 = (bf16[320,128]{1,0:T(8,128)(2,1)S(1)}, bf16[320,128]{1,0:T(8,128)(2,1)S(1)}, u32[]{:S(2)}, u32[]{:S(2)}) collective-permute-start(bf16[320,128]{1,0:T(8,128)(2,1)S(1)} %get-tuple-element.32), channel_id=1, source_target_pairs={{0,4},{1,5},{4,0},{5,1},{8,12},{9,13},{12,8},{13,9},{2,6},{3,7},{6... | collective-permute-start | bytes 245768 | tf_op jit(solution)/shard_map/ppermute | solution.py:337
  12.3 1.8 %collective-permute-start.3 = (bf16[192,256]{1,0:T(8,128)(2,1)S(1)}, bf16[192,256]{1,0:T(8,128)(2,1)S(1)}, u32[]{:S(2)}, u32[]{:S(2)}) collective-permute-start(bf16[192,256]{1,0:T(8,128)(2,1)S(1)} %collective-permute-done.2.refs_0_), channel_id=1, source_target_pairs={{0,1},{1,0},{2,3},{3,2},{4,5},{5,4},{6,7},{7,6},{8,9},{9,8},{10,11... | collective-permute-start | bytes 294920 | tf_op jit(solution)/shard_map/ppermute | solution.py:340
  12.8 1.3 %collective-permute-start.5 = (bf16[320,128]{1,0:T(8,128)(2,1)S(1)}, bf16[320,128]{1,0:T(8,128)(2,1)S(1)}, u32[]{:S(2)}, u32[]{:S(2)}) collective-permute-start(bf16[320,128]{1,0:T(8,128)(2,1)S(1)} %collective-permute-done.4.refs_2_), channel_id=1, source_target_pairs={{0,1},{1,0},{2,3},{3,2},{4,5},{5,4},{6,7},{7,6},{8,9},{9,8},{10,11... | collective-permute-start | bytes 245768 | tf_op jit(solution)/shard_map/ppermute | solution.py:340
  14.7 6.1 %collective-permute-start.6 = (f32[112,256]{1,0:T(8,128)S(1)}, f32[112,256]{1,0:T(8,128)S(1)}, u32[]{:S(2)}, u32[]{:S(2)}) collective-permute-start(f32[112,256]{1,0:T(8,128)S(1)} %get-tuple-element.33.mine_ref), channel_id=1, source_target_pairs={{0,2},{2,0},{1,3},{3,1},{4,6},{6,4},{5,7},{7,5},{8,10},{10,8},{9,1... | collective-permute-start | bytes 344072 | tf_op jit(solution)/shard_map/ppermute | solution.py:285
  16.4 8.8 %collective-permute-start.7 = (bf16[320,256]{1,0:T(8,128)(2,1)S(1)}, bf16[320,256]{1,0:T(8,128)(2,1)S(1)}, u32[]{:S(2)}, u32[]{:S(2)}) collective-permute-start(bf16[320,256]{1,0:T(8,128)(2,1)S(1)} %get-tuple-element.26.high_ref), channel_id=1, source_target_pairs={{0,2},{2,0},{1,3},{3,1},{4,6},{6,4},{5,7},{7,5},{8,10},{10,8},{9,1... | collective-permute-start | bytes 491528 | tf_op jit(solution)/shard_map/ppermute | solution.py:285
  20.8 5.7 %collective-permute-start.10 = (bf16[224,256]{1,0:T(8,128)(2,1)S(1)}, bf16[224,256]{1,0:T(8,128)(2,1)S(1)}, u32[]{:S(2)}, u32[]{:S(2)}) collective-permute-start(bf16[224,256]{1,0:T(8,128)(2,1)S(1)} %get-tuple-element.35), channel_id=1, source_target_pairs={{0,4},{4,0},{8,12},{12,8},{1,5},{5,1},{9,13},{13,9},{2,6},{6,2},{1... | collective-permute-start | bytes 344072 | tf_op jit(solution)/shard_map/ppermute | solution.py:285
  22.3 10.3 %collective-permute-start.8 = (bf16[224,256]{1,0:T(8,128)(2,1)S(1)}, bf16[224,256]{1,0:T(8,128)(2,1)S(1)}, u32[]{:S(2)}, u32[]{:S(2)}) collective-permute-start(bf16[224,256]{1,0:T(8,128)(2,1)S(1)} %get-tuple-element.35), channel_id=1, source_target_pairs={{0,8},{4,12},{8,0},{12,4},{1,9},{5,13},{9,1},{13,5},{2,10},{6,14},... | collective-permute-start | bytes 344072 | tf_op jit(solution)/shard_map/ppermute | solution.py:285
  24.2 8.4 %collective-permute-start.9 = (bf16[224,256]{1,0:T(8,128)(2,1)S(1)}, bf16[224,256]{1,0:T(8,128)(2,1)S(1)}, u32[]{:S(2)}, u32[]{:S(2)}) collective-permute-start(bf16[224,256]{1,0:T(8,128)(2,1)S(1)} %get-tuple-element.35), channel_id=1, source_target_pairs={{0,12},{4,8},{8,4},{12,0},{1,13},{5,9},{9,5},{13,1},{2,14},{6,10},... | collective-permute-start | bytes 344072 | tf_op jit(solution)/shard_map/ppermute | solution.py:285
  33.1 4.6 %collective-permute-start.11 = (f32[192,256]{1,0:T(8,128)S(1)}, f32[192,256]{1,0:T(8,128)S(1)}, u32[]{:S(2)}, u32[]{:S(2)}) collective-permute-start(f32[192,256]{1,0:T(8,128)S(1)} %get-tuple-element.36.mine_ref), channel_id=1, source_target_pairs={{0,1},{1,0},{2,3},{3,2},{4,5},{5,4},{6,7},{7,6},{8,9},{9,8},{10,11... | collective-permute-start | bytes 589832 | tf_op jit(solution)/shard_map/ppermute | solution.py:383
  33.2 4.5 %collective-permute-start.12 = (f32[64,256]{1,0:T(8,128)S(1)}, f32[64,256]{1,0:T(8,128)S(1)}, u32[]{:S(2)}, u32[]{:S(2)}) collective-permute-start(f32[64,256]{1,0:T(8,128)S(1)} %get-tuple-element.37.y_ref), channel_id=1, source_target_pairs={{0,2},{2,0},{1,3},{3,1},{4,6},{6,4},{5,7},{7,5},{8,10},{10,8},{9,1... | collective-permute-start | bytes 196616 | tf_op jit(solution)/shard_map/ppermute | solution.py:285
  37.9 4.7 %collective-permute-start.13 = (f32[32,128]{1,0:T(8,128)S(1)}, f32[32,128]{1,0:T(8,128)S(1)}, u32[]{:S(2)}, u32[]{:S(2)}) collective-permute-start(f32[32,128]{1,0:T(8,128)S(1)} %get-tuple-element.38.own_ref), channel_id=1, source_target_pairs={{0,8},{1,13},{4,12},{5,9},{8,0},{9,5},{12,4},{13,1},{2,10},{3,15},... | collective-permute-start | bytes 49160 | tf_op jit(solution)/shard_map/ppermute | solution.py:337
  40.5 3.7 %collective-permute-start.15 = (f32[16,128]{1,0:T(8,128)S(1)}, f32[16,128]{1,0:T(8,128)S(1)}, u32[]{:S(2)}, u32[]{:S(2)}) collective-permute-start(f32[16,128]{1,0:T(8,128)S(1)} %get-tuple-element.41), channel_id=1, source_target_pairs={{0,4},{1,5},{4,0},{5,1},{8,12},{9,13},{12,8},{13,9},{2,6},{3,7},{6... | collective-permute-start | bytes 24584 | tf_op jit(solution)/shard_map/ppermute | solution.py:337
  42.6 2.7 %collective-permute-start.14 = (f32[32,128]{1,0:T(8,128)S(1)}, f32[32,128]{1,0:T(8,128)S(1)}, u32[]{:S(2)}, u32[]{:S(2)}) collective-permute-start(f32[32,128]{1,0:T(8,128)S(1)} %collective-permute-done.13.refs_0_), channel_id=1, source_target_pairs={{0,1},{1,0},{2,3},{3,2},{4,5},{5,4},{6,7},{7,6},{8,9},{9,8},{10,11... | collective-permute-start | bytes 49160 | tf_op jit(solution)/shard_map/ppermute | solution.py:340
  44.1 1.2 %collective-permute-start.16 = (f32[16,128]{1,0:T(8,128)S(1)}, f32[16,128]{1,0:T(8,128)S(1)}, u32[]{:S(2)}, u32[]{:S(2)}) collective-permute-start(f32[16,128]{1,0:T(8,128)S(1)} %collective-permute-done.15.refs_2_), channel_id=1, source_target_pairs={{0,1},{1,0},{2,3},{3,2},{4,5},{5,4},{6,7},{7,6},{8,9},{9,8},{10,11... | collective-permute-start | bytes 24584 | tf_op jit(solution)/shard_map/ppermute | solution.py:340

commit v10 on v8

--- a/solution.py
+++ b/solution.py
@@ -61,7 +61,7 @@
 
 def prepare_kernel(
     x_hbm, e_hbm, p_hbm, c_hbm, s_hbm, t_hbm, i_hbm,
-    base_ref, corr_ref, high_ref, low_ref, t_ref, i_ref,
+    base_ref, high_ref, low_ref, t_ref, i_ref,
     x_ref, e_ref, p_ref, c_ref, s_ref, sems,
 ):
     pairs = (
@@ -80,13 +80,10 @@
     x = x_ref[...]
     xs = split(x)
     ss = split(s_ref[...])
-    for k, ref in enumerate((high_ref, low_ref)):
-        ref[...] = jnp.concatenate([ss[k], xs[k]], axis=0)
     base_ref[...] = e_ref[...] * x - dot_stacked(split(coupling), split(p_ref[...]), NN)
-    corr = dot_stacked(xs, ss, NT)
-    chunk = corr_ref.shape[1]
-    for band in range(corr_ref.shape[0]):
-        corr_ref[band] = corr[band * chunk : (band + 1) * chunk]
+    corr = split(dot_stacked(xs, ss, NT))
+    high_ref[...] = jnp.concatenate([ss[0], xs[0], *corr], axis=0)
+    low_ref[...] = jnp.concatenate([ss[1], xs[1]], axis=0)
     for copy in copies[5:]:
         copy.wait()
 
@@ -104,10 +101,10 @@
     return jnp.bitwise_xor(me, jnp.where(core == 0, pair[0], pair[1]))
 
 
-def push_kernel(pairs, columns, i_ref, j_ref, high_ref, corr_ref, t_ref, u_ref, *outs):
-    width, rows = corr_ref.shape[2], high_ref.shape[1]
-    block = high_ref.shape[0] - width
-    x = high_ref[width:]
+def push_kernel(pairs, columns, i_ref, j_ref, high_ref, t_ref, u_ref, *outs):
+    block, rows = outs[0].shape
+    width = high_ref.shape[0] - 3 * block
+    x = high_ref[width : width + block]
     me, core = lax.axis_index("rows"), lax.axis_index("sub")
     targets = tile_columns((i_ref, j_ref), (block, rows))
     products = [dot_bf16(x, ref[k], NN) for ref in (t_ref, u_ref) for k in range(ref.shape[0])]
@@ -120,35 +117,30 @@
             total = total + jnp.where(inside, product, 0.0)
         return total
 
-    parity = jnp.bitwise_and(me, 1)
-    outs[0][...] = jnp.concatenate([pushed(me), corr_ref[parity]], axis=0)
+    outs[0][...] = pushed(me)
     for ref, pair in zip(outs[1:], pairs):
         message = jnp.concatenate([x.astype(f32), pushed(target_band(me, core, pair))], axis=0)
-        if pair[0] != pair[1]:
-            ref[...] = message.astype(bf16)
-        else:
+        if pair[0] == pair[1]:
             message = jnp.where(core == 0, message[:, : rows // 2], message[:, rows // 2 :])
-            halves = [unfold(h.astype(f32), 2) for h in split(corr_ref[1 - parity])]
-            ref[...] = jnp.concatenate([message, *halves], axis=0).astype(bf16)
-
-
-def image_kernel(pairs, columns, parts, i_ref, j_ref, base_ref, high_ref, low_ref, t_ref, u_ref, own_ref, *refs):
-    received, (y_ref, send_ref) = refs[:-2], refs[-2:]
+        ref[...] = message.astype(bf16)
+
+
+def image_kernel(pairs, columns, parts, i_ref, j_ref, base_ref, high_ref, low_ref, near_ref, t_ref, u_ref, own_ref, *refs):
+    received, (y_ref, send_ref, corr_ref, part_ref) = refs[:-4], refs[-4:]
     block, rows = base_ref.shape
-    width = high_ref.shape[0] - block
+    width = low_ref.shape[0] - block
     me, core = lax.axis_index("rows"), lax.axis_index("sub")
-    y = base_ref[...] + own_ref[0:block]
-    corr = own_ref[block:]
-    blocks = [(me, high_ref[width:].astype(f32))]
+    y = base_ref[...] + own_ref[...]
+    halves = [r[k : k + block].astype(f32) for r in (high_ref, near_ref) for k in (width + block, width + 2 * block)]
+    corr = (halves[0] + halves[1]) + (halves[2] + halves[3])
+    corr_ref[...] = corr
+    part_ref[...] = corr.astype(bf16)
+    blocks = [(me, high_ref[width : width + block].astype(f32))]
     for k, pair in enumerate(pairs):
         mine, other = received[2 * k][...].astype(f32), received[2 * k + 1][...].astype(f32)
         if pair[0] != pair[1]:
             found = [(target_band(me, core, pair), mine), (target_band(me, core, pair[::-1]), other)]
         else:
-            parts_of = mine[2 * block :]
-            count = parts_of.shape[0] // 2
-            corr = corr + fold(parts_of[:count] + parts_of[count:], 2)
-            mine, other = mine[: 2 * block], other[: 2 * block]
             first, second = jnp.where(core == 0, mine, other), jnp.where(core == 0, other, mine)
             found = [(jnp.bitwise_xor(me, pair[0]), jnp.concatenate([first, second], axis=1))]
         for band, message in found:
@@ -166,43 +158,38 @@
         y = y + jnp.concatenate(halves, axis=1)
     y_ref[...] = y
     halves = split(y)
-    diagonal = fold(dot_split(halves, (high_ref[width:], low_ref[width:]), NT), parts)
+    diagonal = fold(dot_split(halves, (high_ref[width : width + block], low_ref[width:]), NT), parts)
     stored = dot_split(halves, (high_ref[:width], low_ref[:width]), NT)
-    send_ref[...] = jnp.concatenate([stored, diagonal, corr], axis=0)
-
-
-def pack(total, block, small):
-    high, low = split(total[block : block + small])
-    message = [total[0:block], high.astype(f32), low.astype(f32), total[block + small :]]
+    send_ref[...] = jnp.concatenate([stored, diagonal], axis=0)
+
+
+def pack(total, block):
+    high, low = split(total[block:])
+    message = [total[0:block], high.astype(f32), low.astype(f32)]
     return jnp.concatenate(message, axis=0).astype(bf16)
 
 
-def combine_kernel(block, small, mine_ref, other_ref, total_ref, *send_refs):
+def combine_kernel(block, mine_ref, other_ref, total_ref, *send_refs):
     total = mine_ref[...] + other_ref[...]
     total_ref[...] = total
     for ref in send_refs:
-        ref[...] = pack(total, block, small)
-
-
-def project_kernel(steps, block, parts, total_rows, total_ref, high_ref, low_ref, near_ref, *refs):
+        ref[...] = pack(total, block)
+
+
+def project_kernel(block, parts, total_rows, total_ref, corr_ref, high_ref, low_ref, near_ref, *refs):
     received, (out_ref, diagonal_ref) = refs[:-2], refs[-2:]
-    me, core = lax.axis_index("rows"), lax.axis_index("sub")
+    core = lax.axis_index("sub")
+    count = len(received) // 2
     small = block // parts
+    corr = corr_ref[...]
+    for ref in received[count:]:
+        corr = corr + ref[...].astype(f32)
     total = total_ref[...]
-    stored, diagonal = total[0:block], total[block : block + small]
-    same, other = total[block + small :], jnp.zeros((block // 2, total.shape[1]), f32)
-    for step, ref in zip(steps, received):
+    stored, diagonal = total[0:block], total[block:]
+    for ref in received[:count]:
         message = ref[...].astype(f32)
         stored = stored + message[0:block]
-        diagonal = diagonal + message[block : block + small]
-        diagonal = diagonal + message[block + small : block + 2 * small]
-        part = message[block + 2 * small :]
-        if step % 2:
-            other = other + part
-        else:
-            same = same + part
-    even = jnp.bitwise_and(me, 1) == 0
-    corr = jnp.concatenate([jnp.where(even, same, other), jnp.where(even, other, same)], axis=0)
+        diagonal = diagonal + (message[block : block + small] + message[block + small :])
     scale = 1.0 / total_rows
     diagonal = diagonal * scale
     lane = lax.broadcasted_iota(jnp.int32, diagonal.shape, 1)
@@ -214,7 +201,8 @@
     diagonal_ref[...] = diagonal
     weights = split(jnp.concatenate([projection, jnp.where(core == 0, diagonal, 0.0)], axis=1))
     for k, ref in enumerate((high_ref, near_ref)):
-        rounded = dot_bf16(weights[0], ref[...], NN) + dot_bf16(weights[1], ref[...], NN)
+        stacked = ref[: low_ref.shape[0]]
+        rounded = dot_bf16(weights[0], stacked, NN) + dot_bf16(weights[1], stacked, NN)
         out_ref[k * block : (k + 1) * block, :] = rounded
     out_ref[2 * block :, :] = dot_bf16(weights[0], low_ref[...], NN)
 
@@ -302,7 +290,6 @@
     width = stored * block
     total_rows = rows * bands * columns
     parts = width // block
-    chunk = block // 2
     assert rows == tile_values.shape[1] and cores == 2 and width == rows
     assert bands > 1 and columns > 1 and bands & (bands - 1) == 0 and columns & (columns - 1) == 0
     half = (block, rows)
@@ -312,7 +299,7 @@
     prepare = call(
         prepare_kernel,
         [
-            (half, f32), ((2, chunk, width), f32), *[((width + block, rows), bf16)] * 2,
+            (half, f32), ((width + 3 * block, rows), bf16), ((width + block, rows), bf16),
             (tile_values.shape, bf16), (tile_index.shape, jnp.int32),
         ],
         "hhhhhhh",
@@ -326,7 +313,7 @@
         start_block.T, onsite_energy.reshape(1, rows), previous_block.T, previous_coupling,
         stored_basis.transpose(0, 2, 1).reshape(width, rows), tile_values, tile_index,
     )
-    base, corr, high, low, tiles, index = prepare(
+    base, high, low, tiles, index = prepare(
         *(pltpu.with_memory_space_constraint(a, pltpu.HBM) for a in sources)
     )
     pairs = [(step - 1, step) for step in range(bands - 1, 1, -2)] + [(1, 1)]
@@ -343,40 +330,42 @@
 
     sends = call(
         functools.partial(push_kernel, pairs, columns),
-        [((block + chunk, rows), f32)]
-        + [((2 * block, rows) if a != b else (4 * block, rows // 2), bf16) for a, b in pairs],
-        "vvvvvv",
-    )(index, other_index, high, corr, tiles, other_tiles)
+        [(half, f32)] + [((2 * block, rows if a != b else rows // 2), bf16) for a, b in pairs],
+        "vvvvv",
+    )(index, other_index, high, tiles, other_tiles)
     near = exchange(high, "cols", 1)
     received = serve(sends[1:])
     small = block // parts
-    y, mine = call(
+    y, mine, corr, part = call(
         functools.partial(image_kernel, pairs, columns, parts),
-        [(half, f32), ((block + small + chunk, rows), f32)],
-        "v" * (8 + len(received)),
-    )(index, other_index, base, high, low, tiles, other_tiles, sends[0], *received)
+        [(half, f32), ((block + small, rows), f32), (half, f32), (half, bf16)],
+        "v" * (9 + len(received)),
+    )(index, other_index, base, high, low, near, tiles, other_tiles, sends[0], *received)
     other = exchange(mine, "cols", 1)
     late = exchange(y, "cols", 1)
     distances = [2**k for k in range(1, columns.bit_length() - 1)]
     total, *send = call(
-        functools.partial(combine_kernel, block, small),
-        [((block + small + chunk, rows), f32)]
-        + [((block + 2 * small + chunk, rows), bf16)] * (not distances),
+        functools.partial(combine_kernel, block),
+        [((block + small, rows), f32)]
+        + [((block + 2 * small, rows), bf16)] * (not distances),
         "vv",
     )(mine, other)
     for distance in distances:
         total = total + exchange(total, "cols", distance)
-    send = send[0] if send else pack(total, block, small)
+        corr = corr + exchange(corr, "cols", distance)
+        part = corr.astype(bf16)
+    send = send[0] if send else pack(total, block)
     steps = [*range(2, bands), 1]
     received = []
-    for step in steps:
-        received.append(exchange(send, "rows", step))
+    for message in (send, part):
+        for step in steps:
+            received.append(exchange(message, "rows", step))
     project = call(
-        functools.partial(project_kernel, steps, block, parts, total_rows),
+        functools.partial(project_kernel, block, parts, total_rows),
         [((3 * block, rows), f32), ((block, block), f32)],
-        "v" * (3 + bands),
-    )
-    removed, diagonal = project(total, high, low, near, *received)
+        "v" * (5 + len(received)),
+    )
+    removed, diagonal = project(total, corr, high, low, near, *received)
     images, full, part = call(
         gram_kernel,
         [(half, f32), ((block // 2, 2 * block), f32), ((block // 4, 2 * block), f32)],

time: 42.7 us -> 45.3 us (1.061)
  starting transfers between devices: 16.7 us -> 21 us
  waiting for transfers between devices: 20.4 us -> 18.5 us
    ppermute x6 -> x9, starting transfers between devices: 8.14 us -> 12.5 us  [exchange(): lax.ppermute(x, axis, [(i, i ^ distance) for i in range(lax.axis_size(axi...]
    ppermute x4, waiting for transfers between devices: 6.34 us -> 4.88 us  [serve(): received.append(lax.ppermute(send, ('rows', 'sub'), moves))]
    ppermute x6 -> x9, waiting for transfers between devices: 11.9 us -> 10.9 us  [exchange(): lax.ppermute(x, axis, [(i, i ^ distance) for i in range(lax.axis_size(axi...]
    ppermute x1, waiting for transfers between devices: 0.02 us -> 0.95 us  [local(): other_index = lax.ppermute(tile_index, 'sub', swap)]
  transfers between devices with their start and end apart: 17 -> 20, of which waited for: 10 -> 10; matrix products, arithmetic and copies ran while one was open for 0% -> 0% of each run, Pallas kernels for 3% -> 3%
where the time goes in v10:
time: 45.3 us; the launch traced here: 45.1 us
  starting transfers between devices  21 us (46%)
  waiting for transfers between devices  18.5 us (41%)
  Pallas kernels  4.87 us (11%)
  between operations  0.71 us (2%)
    ppermute x9, starting transfers between devices, exchange(): lax.ppermute(x, axis, [(i, i ^ distance) for i in range(lax.axis_size(axi...  12.5 us
    ppermute x9, waiting for transfers between devices, exchange(): lax.ppermute(x, axis, [(i, i ^ distance) for i in range(lax.axis_size(axi...  10.9 us
    ppermute x4, starting transfers between devices, serve(): received.append(lax.ppermute(send, ('rows', 'sub'), moves))  6.97 us
    ppermute x4, waiting for transfers between devices, serve(): received.append(lax.ppermute(send, ('rows', 'sub'), moves))  4.88 us
    pallas_call x1, Pallas kernels, local(): call(functools.partial(factor_kernel, pairs, total_rows), [(half, f32), (...  2.03 us
    ppermute x4, waiting for transfers between devices, serve(): swapped += [x, lax.ppermute(x, 'sub', swap)]  1.83 us
    pallas_call x1, Pallas kernels, local(): prepare(*(pltpu.with_memory_space_constraint(a, pltpu.HBM) for a in sourc...  1.27 us
    ppermute x1, waiting for transfers between devices, local(): other_index = lax.ppermute(tile_index, 'sub', swap)  0.95 us
  transfers between devices with their start and end apart: 20, of which 10 were waited for; matrix products, arithmetic and copies ran while one was open for 0% of the time, Pallas kernels for 3%

profile of v10, /device:TPU:0, one launch (start us, length us, event | category | flops | bytes accessed | tf_op | source)
XLA Modules:
  0.0 45.1 jit_solution(16729357243727965123)
XLA Ops:
  0.6 0.6 %collective-permute-start.2 = (bf16[2,256,256]{2,1,0:T(8,128)(2,1)}, bf16[2,256,256]{2,1,0:T(8,128)(2,1)S(1)}, u32[]{:S(2)}, u32[]{:S(2)}) collective-permute-start(bf16[2,256,256]{2,1,0:T(8,128)(2,1)} %t_hbm.1), channel_id=1, source_target_pairs={{0,1},{1,0},{2,3},{3,2},{4,5},{5,4},{6,7},{7,6},{8,9},{9,8},{10,11... | collective-permute-start | bytes 786440 | tf_op jit(solution)/shard_map/ppermute | solution.py:297
  1.2 1.3 %shard_map.94 = (f32[64,256]{1,0:T(8,128)S(1)}, bf16[448,256]{1,0:T(8,128)(2,1)S(1)}, bf16[320,256]{1,0:T(8,128)(2,1)S(1)}, bf16[2,256,256]{2,1,0:T(8,128)(2,1)S(1)}, s32[2,2]{1,0:T(2,128)S(1)}) custom-call(f32[64,256]{1,0:T(8,128)} %bitcast.12, f32[1,256]{1,0:T(1,128)} %bitcast.14, f32[64,256]{1,0:T(8,128)} %bitcast.13, f32[64,64]{1,0:T(8,128)} %c_hbm.1, ...), custom_call_target="tpu_custom_call" | custom-call | flops 40000000 | bytes 1000000 | tf_op jit(solution)/shard_map/pallas_call | solution.py:316
  2.5 2.6 %collective-permute-start.1 = (bf16[448,256]{1,0:T(8,128)(2,1)S(1)}, bf16[448,256]{1,0:T(8,128)(2,1)S(1)}, u32[]{:S(2)}, u32[]{:S(2)}) collective-permute-start(bf16[448,256]{1,0:T(8,128)(2,1)S(1)} %get-tuple-element.27.high_ref), channel_id=1, source_target_pairs={{0,2},{2,0},{1,3},{3,1},{4,6},{6,4},{5,7},{7,5},{8,10},{10,8},{9,1... | collective-permute-start | bytes 688136 | tf_op jit(solution)/shard_map/ppermute | solution.py:274
  5.0 0.2 collective-permute-start
  5.3 0.9 %collective-permute-done.j_ref = s32[2,2]{1,0:T(2,128)S(1)} collective-permute-done((s32[2,2]{1,0:T(2,128)S(1)}, s32[2,2]{1,0:T(2,128)S(1)}, u32[]{:S(2)}, u32[]{:S(2)}) %collective-permute-start) | collective-permute-done | bytes 48 | tf_op jit(solution)/shard_map/ppermute | solution.py:298
  6.2 0.2 shard_map.95
  6.4 2.7 %collective-permute-start.3 = (bf16[128,256]{1,0:T(8,128)(2,1)S(1)}, bf16[128,256]{1,0:T(8,128)(2,1)S(1)}, u32[]{:S(2)}, u32[]{:S(2)}) collective-permute-start(bf16[128,256]{1,0:T(8,128)(2,1)S(1)} %get-tuple-element.31), channel_id=1, source_target_pairs={{0,8},{1,13},{4,12},{5,9},{8,0},{9,5},{12,4},{13,1},{2,10},{3,15},... | collective-permute-start | bytes 196616 | tf_op jit(solution)/shard_map/ppermute | solution.py:325
  9.1 1.6 %collective-permute-start.5 = (bf16[128,128]{1,0:T(8,128)(2,1)S(1)}, bf16[128,128]{1,0:T(8,128)(2,1)S(1)}, u32[]{:S(2)}, u32[]{:S(2)}) collective-permute-start(bf16[128,128]{1,0:T(8,128)(2,1)S(1)} %get-tuple-element.32), channel_id=1, source_target_pairs={{0,4},{1,5},{4,0},{5,1},{8,12},{9,13},{12,8},{13,9},{2,6},{3,7},{6... | collective-permute-start | bytes 98312 | tf_op jit(solution)/shard_map/ppermute | solution.py:325
  10.7 2.6 %collective-permute-done.3.refs_0_ = bf16[128,256]{1,0:T(8,128)(2,1)S(1)} collective-permute-done((bf16[128,256]{1,0:T(8,128)(2,1)S(1)}, bf16[128,256]{1,0:T(8,128)(2,1)S(1)}, u32[]{:S(2)}, u32[]{:S(2)}) %collective-permute-start.3) | collective-permute-done | bytes 65568 | tf_op jit(solution)/shard_map/ppermute | solution.py:325
  13.2 0.3 collective-permute-done.5.refs_2_
  13.7 1.0 %collective-permute-done.6.refs_3_ = bf16[128,128]{1,0:T(8,128)(2,1)S(1)} collective-permute-done((bf16[128,128]{1,0:T(8,128)(2,1)S(1)}, bf16[128,128]{1,0:T(8,128)(2,1)S(1)}, u32[]{:S(2)}, u32[]{:S(2)}) %collective-permute-start.6) | collective-permute-done | bytes 32800 | tf_op jit(solution)/shard_map/ppermute | solution.py:328
  14.7 0.6 %shard_map.96 = (f32[64,256]{1,0:T(8,128)S(1)}, f32[80,256]{1,0:T(8,128)S(1)}, f32[64,256]{1,0:T(8,128)S(1)}, bf16[64,256]{1,0:T(8,128)(2,1)S(1)}) custom-call(s32[2,2]{1,0:T(2,128)S(1)} %get-tuple-element.25.i_ref, s32[2,2]{1,0:T(2,128)S(1)} %collective-permute-done.j_ref, f32[64,256]{1,0:T(8,128)S(1)} %get-tuple-element.26.base_ref, ...), custom_call_target="tpu_custom_call" | custom-call | flops 40000000 | bytes 1000000 | tf_op jit(solution)/shard_map/pallas_call | solution.py:339
  15.4 0.8 %collective-permute-start.7 = (f32[80,256]{1,0:T(8,128)S(1)}, f32[80,256]{1,0:T(8,128)S(1)}, u32[]{:S(2)}, u32[]{:S(2)}) collective-permute-start(f32[80,256]{1,0:T(8,128)S(1)} %get-tuple-element.33.mine_ref), channel_id=1, source_target_pairs={{0,2},{2,0},{1,3},{3,1},{4,6},{6,4},{5,7},{7,5},{8,10},{10,8},{9,1... | collective-permute-start | bytes 245768 | tf_op jit(solution)/shard_map/ppermute | solution.py:274
  16.2 1.2 %collective-permute-start.13 = (bf16[64,256]{1,0:T(8,128)(2,1)S(1)}, bf16[64,256]{1,0:T(8,128)(2,1)S(1)}, u32[]{:S(2)}, u32[]{:S(2)}) collective-permute-start(bf16[64,256]{1,0:T(8,128)(2,1)S(1)} %get-tuple-element.37), channel_id=1, source_target_pairs={{0,4},{4,0},{8,12},{12,8},{1,5},{5,1},{9,13},{13,9},{2,6},{6,2},{1... | collective-permute-start | bytes 98312 | tf_op jit(solution)/shard_map/ppermute | solution.py:274
  17.4 2.6 %collective-permute-done.7.other_ref = f32[80,256]{1,0:T(8,128)S(1)} collective-permute-done((f32[80,256]{1,0:T(8,128)S(1)}, f32[80,256]{1,0:T(8,128)S(1)}, u32[]{:S(2)}, u32[]{:S(2)}) %collective-permute-start.7) | collective-permute-done | bytes 81952 | tf_op jit(solution)/shard_map/ppermute | solution.py:274
  20.0 1.2 %collective-permute-start.10 = (bf16[96,256]{1,0:T(8,128)(2,1)S(1)}, bf16[96,256]{1,0:T(8,128)(2,1)S(1)}, u32[]{:S(2)}, u32[]{:S(2)}) collective-permute-start(bf16[96,256]{1,0:T(8,128)(2,1)S(1)} %get-tuple-element.36), channel_id=1, source_target_pairs={{0,4},{4,0},{8,12},{12,8},{1,5},{5,1},{9,13},{13,9},{2,6},{6,2},{1... | collective-permute-start | bytes 147464 | tf_op jit(solution)/shard_map/ppermute | solution.py:274
  21.3 2.2 %collective-permute-start.9 = (bf16[96,256]{1,0:T(8,128)(2,1)S(1)}, bf16[96,256]{1,0:T(8,128)(2,1)S(1)}, u32[]{:S(2)}, u32[]{:S(2)}) collective-permute-start(bf16[96,256]{1,0:T(8,128)(2,1)S(1)} %get-tuple-element.36), channel_id=1, source_target_pairs={{0,12},{4,8},{8,4},{12,0},{1,13},{5,9},{9,5},{13,1},{2,14},{6,10},... | collective-permute-start | bytes 147464 | tf_op jit(solution)/shard_map/ppermute | solution.py:274
  23.5 0.5 %collective-permute-start.8 = (bf16[96,256]{1,0:T(8,128)(2,1)S(1)}, bf16[96,256]{1,0:T(8,128)(2,1)S(1)}, u32[]{:S(2)}, u32[]{:S(2)}) collective-permute-start(bf16[96,256]{1,0:T(8,128)(2,1)S(1)} %get-tuple-element.36), channel_id=1, source_target_pairs={{0,8},{4,12},{8,0},{12,4},{1,9},{5,13},{9,1},{13,5},{2,10},{6,14},... | collective-permute-start | bytes 147464 | tf_op jit(solution)/shard_map/ppermute | solution.py:274
  24.0 2.9 %collective-permute-start.12 = (bf16[64,256]{1,0:T(8,128)(2,1)S(1)}, bf16[64,256]{1,0:T(8,128)(2,1)S(1)}, u32[]{:S(2)}, u32[]{:S(2)}) collective-permute-start(bf16[64,256]{1,0:T(8,128)(2,1)S(1)} %get-tuple-element.37), channel_id=1, source_target_pairs={{0,12},{4,8},{8,4},{12,0},{1,13},{5,9},{9,5},{13,1},{2,14},{6,10},... | collective-permute-start | bytes 98312 | tf_op jit(solution)/shard_map/ppermute | solution.py:274
  26.9 0.2 collective-permute-start.11
  27.1 2.6 %collective-permute-done.12.refs_4_ = bf16[64,256]{1,0:T(8,128)(2,1)S(1)} collective-permute-done((bf16[64,256]{1,0:T(8,128)(2,1)S(1)}, bf16[64,256]{1,0:T(8,128)(2,1)S(1)}, u32[]{:S(2)}, u32[]{:S(2)}) %collective-permute-start.12) | collective-permute-done | bytes 32800 | tf_op jit(solution)/shard_map/ppermute | solution.py:274
  29.8 1.9 %collective-permute-done.11.refs_3_ = bf16[64,256]{1,0:T(8,128)(2,1)S(1)} collective-permute-done((bf16[64,256]{1,0:T(8,128)(2,1)S(1)}, bf16[64,256]{1,0:T(8,128)(2,1)S(1)}, u32[]{:S(2)}, u32[]{:S(2)}) %collective-permute-start.11) | collective-permute-done | bytes 32800 | tf_op jit(solution)/shard_map/ppermute | solution.py:274
  31.7 0.5 %shard_map.98 = (f32[192,256]{1,0:T(8,128)S(1)}, f32[64,64]{1,0:T(8,128)S(1)}) custom-call(f32[80,256]{1,0:T(8,128)S(1)} %get-tuple-element.34.total_ref, f32[64,256]{1,0:T(8,128)S(1)} %get-tuple-element.35.corr_ref, bf16[448,256]{1,0:T(8,128)(2,1)S(1)} %get-tuple-element.27.high_ref, bf16[320,256]{1,0:T(8,128)(2,1)S(1)} %get-tuple-element.28.low_ref, ...), custom_call_target="tpu_custom_call" | custom-call | flops 40000000 | bytes 1000000 | tf_op jit(solution)/shard_map/pallas_call | solution.py:368
  32.3 0.8 %collective-permute-start.15 = (f32[64,256]{1,0:T(8,128)S(1)}, f32[64,256]{1,0:T(8,128)S(1)}, u32[]{:S(2)}, u32[]{:S(2)}) collective-permute-start(f32[64,256]{1,0:T(8,128)S(1)} %get-tuple-element.39.y_ref), channel_id=1, source_target_pairs={{0,2},{2,0},{1,3},{3,1},{4,6},{6,4},{5,7},{7,5},{8,10},{10,8},{9,1... | collective-permute-start | bytes 196616 | tf_op jit(solution)/shard_map/ppermute | solution.py:274
  33.1 3.7 %collective-permute-done.15.z_ref = f32[64,256]{1,0:T(8,128)S(1)} collective-permute-done((f32[64,256]{1,0:T(8,128)S(1)}, f32[64,256]{1,0:T(8,128)S(1)}, u32[]{:S(2)}, u32[]{:S(2)}) %collective-permute-start.15) | collective-permute-done | bytes 65568 | tf_op jit(solution)/shard_map/ppermute | solution.py:274
  36.8 0.2 shard_map.99
  37.0 0.9 %collective-permute-start.16 = (f32[32,128]{1,0:T(8,128)S(1)}, f32[32,128]{1,0:T(8,128)S(1)}, u32[]{:S(2)}, u32[]{:S(2)}) collective-permute-start(f32[32,128]{1,0:T(8,128)S(1)} %get-tuple-element.40.own_ref), channel_id=1, source_target_pairs={{0,8},{1,13},{4,12},{5,9},{8,0},{9,5},{12,4},{13,1},{2,10},{3,15},... | collective-permute-start | bytes 49160 | tf_op jit(solution)/shard_map/ppermute | solution.py:325
  38.0 1.8 %collective-permute-start.18 = (f32[16,128]{1,0:T(8,128)S(1)}, f32[16,128]{1,0:T(8,128)S(1)}, u32[]{:S(2)}, u32[]{:S(2)}) collective-permute-start(f32[16,128]{1,0:T(8,128)S(1)} %get-tuple-element.43), channel_id=1, source_target_pairs={{0,4},{1,5},{4,0},{5,1},{8,12},{9,13},{12,8},{13,9},{2,6},{3,7},{6... | collective-permute-start | bytes 24584 | tf_op jit(solution)/shard_map/ppermute | solution.py:325
  39.8 2.0 %collective-permute-done.16.refs_0_ = f32[32,128]{1,0:T(8,128)S(1)} collective-permute-done((f32[32,128]{1,0:T(8,128)S(1)}, f32[32,128]{1,0:T(8,128)S(1)}, u32[]{:S(2)}, u32[]{:S(2)}) %collective-permute-start.16) | collective-permute-done | bytes 16416 | tf_op jit(solution)/shard_map/ppermute | solution.py:325
  41.8 0.5 %collective-permute-start.19 = (f32[16,128]{1,0:T(8,128)S(1)}, f32[16,128]{1,0:T(8,128)S(1)}, u32[]{:S(2)}, u32[]{:S(2)}) collective-permute-start(f32[16,128]{1,0:T(8,128)S(1)} %collective-permute-done.18.refs_2_), channel_id=1, source_target_pairs={{0,1},{1,0},{2,3},{3,2},{4,5},{5,4},{6,7},{7,6},{8,9},{9,8},{10,11... | collective-permute-start | bytes 24584 | tf_op jit(solution)/shard_map/ppermute | solution.py:328
  42.2 0.8 %collective-permute-done.19.refs_3_ = f32[16,128]{1,0:T(8,128)S(1)} collective-permute-done((f32[16,128]{1,0:T(8,128)S(1)}, f32[16,128]{1,0:T(8,128)S(1)}, u32[]{:S(2)}, u32[]{:S(2)}) %collective-permute-start.19) | collective-permute-done | bytes 8224 | tf_op jit(solution)/shard_map/ppermute | solution.py:328
  43.1 2.0 %shard_map.100 = (f32[64,256]{1,0:T(8,128)}, f32[64,64]{1,0:T(8,128)}, f32[64,64]{1,0:T(8,128)}) custom-call(f32[32,128]{1,0:T(8,128)S(1)} %get-tuple-element.40.own_ref, f32[64,256]{1,0:T(8,128)S(1)} %get-tuple-element.41.images_ref, f32[64,64]{1,0:T(8,128)S(1)} %get-tuple-element.42.d_ref, f32[32,128]{1,0:T(8,128)S(1)} %collective-permute-done.16.refs_0_, ...), custom_call_target="tpu_custom_call" | custom-call | flops 40000000 | bytes 1000000 | tf_op jit(solution)/shard_map/pallas_call | solution.py:378
  (17 shorter events, 0.4 us)
Async XLA Ops:
  0.6 5.6 %collective-permute-start.2 = (bf16[2,256,256]{2,1,0:T(8,128)(2,1)}, bf16[2,256,256]{2,1,0:T(8,128)(2,1)S(1)}, u32[]{:S(2)}, u32[]{:S(2)}) collective-permute-start(bf16[2,256,256]{2,1,0:T(8,128)(2,1)} %t_hbm.1), channel_id=1, source_target_pairs={{0,1},{1,0},{2,3},{3,2},{4,5},{5,4},{6,7},{7,6},{8,9},{9,8},{10,11... | collective-permute-start | bytes 786440 | tf_op jit(solution)/shard_map/ppermute | solution.py:297
  2.5 2.6 %copy-start = (s32[2,2]{1,0:T(2,128)S(1)}, s32[2,2]{1,0:T(2,128)}, u32[]{:S(2)}) copy-start(s32[2,2]{1,0:T(2,128)} %i_hbm.1) | copy-start | bytes 52
  2.5 11.3 %collective-permute-start.1 = (bf16[448,256]{1,0:T(8,128)(2,1)S(1)}, bf16[448,256]{1,0:T(8,128)(2,1)S(1)}, u32[]{:S(2)}, u32[]{:S(2)}) collective-permute-start(bf16[448,256]{1,0:T(8,128)(2,1)S(1)} %get-tuple-element.27.high_ref), channel_id=1, source_target_pairs={{0,2},{2,0},{1,3},{3,1},{4,6},{6,4},{5,7},{7,5},{8,10},{10,8},{9,1... | collective-permute-start | bytes 688136 | tf_op jit(solution)/shard_map/ppermute | solution.py:274
  5.0 1.2 %collective-permute-start = (s32[2,2]{1,0:T(2,128)S(1)}, s32[2,2]{1,0:T(2,128)S(1)}, u32[]{:S(2)}, u32[]{:S(2)}) collective-permute-start(s32[2,2]{1,0:T(2,128)S(1)} %copy-done), channel_id=1, source_target_pairs={{0,1},{1,0},{2,3},{3,2},{4,5},{5,4},{6,7},{7,6},{8,9},{9,8},{10,11... | collective-permute-start | bytes 56 | tf_op jit(solution)/shard_map/ppermute | solution.py:298
  6.4 6.8 %collective-permute-start.3 = (bf16[128,256]{1,0:T(8,128)(2,1)S(1)}, bf16[128,256]{1,0:T(8,128)(2,1)S(1)}, u32[]{:S(2)}, u32[]{:S(2)}) collective-permute-start(bf16[128,256]{1,0:T(8,128)(2,1)S(1)} %get-tuple-element.31), channel_id=1, source_target_pairs={{0,8},{1,13},{4,12},{5,9},{8,0},{9,5},{12,4},{13,1},{2,10},{3,15},... | collective-permute-start | bytes 196616 | tf_op jit(solution)/shard_map/ppermute | solution.py:325
  9.1 4.4 %collective-permute-start.5 = (bf16[128,128]{1,0:T(8,128)(2,1)S(1)}, bf16[128,128]{1,0:T(8,128)(2,1)S(1)}, u32[]{:S(2)}, u32[]{:S(2)}) collective-permute-start(bf16[128,128]{1,0:T(8,128)(2,1)S(1)} %get-tuple-element.32), channel_id=1, source_target_pairs={{0,4},{1,5},{4,0},{5,1},{8,12},{9,13},{12,8},{13,9},{2,6},{3,7},{6... | collective-permute-start | bytes 98312 | tf_op jit(solution)/shard_map/ppermute | solution.py:325
  13.2 1.5 %collective-permute-start.4 = (bf16[128,256]{1,0:T(8,128)(2,1)S(1)}, bf16[128,256]{1,0:T(8,128)(2,1)S(1)}, u32[]{:S(2)}, u32[]{:S(2)}) collective-permute-start(bf16[128,256]{1,0:T(8,128)(2,1)S(1)} %collective-permute-done.3.refs_0_), channel_id=1, source_target_pairs={{0,1},{1,0},{2,3},{3,2},{4,5},{5,4},{6,7},{7,6},{8,9},{9,8},{10,11... | collective-permute-start | bytes 196616 | tf_op jit(solution)/shard_map/ppermute | solution.py:328
  13.5 1.2 %collective-permute-start.6 = (bf16[128,128]{1,0:T(8,128)(2,1)S(1)}, bf16[128,128]{1,0:T(8,128)(2,1)S(1)}, u32[]{:S(2)}, u32[]{:S(2)}) collective-permute-start(bf16[128,128]{1,0:T(8,128)(2,1)S(1)} %collective-permute-done.5.refs_2_), channel_id=1, source_target_pairs={{0,1},{1,0},{2,3},{3,2},{4,5},{5,4},{6,7},{7,6},{8,9},{9,8},{10,11... | collective-permute-start | bytes 98312 | tf_op jit(solution)/shard_map/ppermute | solution.py:328
  15.4 4.6 %collective-permute-start.7 = (f32[80,256]{1,0:T(8,128)S(1)}, f32[80,256]{1,0:T(8,128)S(1)}, u32[]{:S(2)}, u32[]{:S(2)}) collective-permute-start(f32[80,256]{1,0:T(8,128)S(1)} %get-tuple-element.33.mine_ref), channel_id=1, source_target_pairs={{0,2},{2,0},{1,3},{3,1},{4,6},{6,4},{5,7},{7,5},{8,10},{10,8},{9,1... | collective-permute-start | bytes 245768 | tf_op jit(solution)/shard_map/ppermute | solution.py:274
  16.2 10.7 %collective-permute-start.13 = (bf16[64,256]{1,0:T(8,128)(2,1)S(1)}, bf16[64,256]{1,0:T(8,128)(2,1)S(1)}, u32[]{:S(2)}, u32[]{:S(2)}) collective-permute-start(bf16[64,256]{1,0:T(8,128)(2,1)S(1)} %get-tuple-element.37), channel_id=1, source_target_pairs={{0,4},{4,0},{8,12},{12,8},{1,5},{5,1},{9,13},{13,9},{2,6},{6,2},{1... | collective-permute-start | bytes 98312 | tf_op jit(solution)/shard_map/ppermute | solution.py:274
  20.0 11.7 %collective-permute-start.10 = (bf16[96,256]{1,0:T(8,128)(2,1)S(1)}, bf16[96,256]{1,0:T(8,128)(2,1)S(1)}, u32[]{:S(2)}, u32[]{:S(2)}) collective-permute-start(bf16[96,256]{1,0:T(8,128)(2,1)S(1)} %get-tuple-element.36), channel_id=1, source_target_pairs={{0,4},{4,0},{8,12},{12,8},{1,5},{5,1},{9,13},{13,9},{2,6},{6,2},{1... | collective-permute-start | bytes 147464 | tf_op jit(solution)/shard_map/ppermute | solution.py:274
  21.3 10.5 %collective-permute-start.9 = (bf16[96,256]{1,0:T(8,128)(2,1)S(1)}, bf16[96,256]{1,0:T(8,128)(2,1)S(1)}, u32[]{:S(2)}, u32[]{:S(2)}) collective-permute-start(bf16[96,256]{1,0:T(8,128)(2,1)S(1)} %get-tuple-element.36), channel_id=1, source_target_pairs={{0,12},{4,8},{8,4},{12,0},{1,13},{5,9},{9,5},{13,1},{2,14},{6,10},... | collective-permute-start | bytes 147464 | tf_op jit(solution)/shard_map/ppermute | solution.py:274
  23.5 8.2 %collective-permute-start.8 = (bf16[96,256]{1,0:T(8,128)(2,1)S(1)}, bf16[96,256]{1,0:T(8,128)(2,1)S(1)}, u32[]{:S(2)}, u32[]{:S(2)}) collective-permute-start(bf16[96,256]{1,0:T(8,128)(2,1)S(1)} %get-tuple-element.36), channel_id=1, source_target_pairs={{0,8},{4,12},{8,0},{12,4},{1,9},{5,13},{9,1},{13,5},{2,10},{6,14},... | collective-permute-start | bytes 147464 | tf_op jit(solution)/shard_map/ppermute | solution.py:274
  24.0 5.8 %collective-permute-start.12 = (bf16[64,256]{1,0:T(8,128)(2,1)S(1)}, bf16[64,256]{1,0:T(8,128)(2,1)S(1)}, u32[]{:S(2)}, u32[]{:S(2)}) collective-permute-start(bf16[64,256]{1,0:T(8,128)(2,1)S(1)} %get-tuple-element.37), channel_id=1, source_target_pairs={{0,12},{4,8},{8,4},{12,0},{1,13},{5,9},{9,5},{13,1},{2,14},{6,10},... | collective-permute-start | bytes 98312 | tf_op jit(solution)/shard_map/ppermute | solution.py:274
  26.9 4.8 %collective-permute-start.11 = (bf16[64,256]{1,0:T(8,128)(2,1)S(1)}, bf16[64,256]{1,0:T(8,128)(2,1)S(1)}, u32[]{:S(2)}, u32[]{:S(2)}) collective-permute-start(bf16[64,256]{1,0:T(8,128)(2,1)S(1)} %get-tuple-element.37), channel_id=1, source_target_pairs={{0,8},{4,12},{8,0},{12,4},{1,9},{5,13},{9,1},{13,5},{2,10},{6,14},... | collective-permute-start | bytes 98312 | tf_op jit(solution)/shard_map/ppermute | solution.py:274
  32.2 4.6 %collective-permute-start.14 = (f32[192,256]{1,0:T(8,128)S(1)}, f32[192,256]{1,0:T(8,128)S(1)}, u32[]{:S(2)}, u32[]{:S(2)}) collective-permute-start(f32[192,256]{1,0:T(8,128)S(1)} %get-tuple-element.38.mine_ref), channel_id=1, source_target_pairs={{0,1},{1,0},{2,3},{3,2},{4,5},{5,4},{6,7},{7,6},{8,9},{9,8},{10,11... | collective-permute-start | bytes 589832 | tf_op jit(solution)/shard_map/ppermute | solution.py:373
  32.3 4.5 %collective-permute-start.15 = (f32[64,256]{1,0:T(8,128)S(1)}, f32[64,256]{1,0:T(8,128)S(1)}, u32[]{:S(2)}, u32[]{:S(2)}) collective-permute-start(f32[64,256]{1,0:T(8,128)S(1)} %get-tuple-element.39.y_ref), channel_id=1, source_target_pairs={{0,2},{2,0},{1,3},{3,1},{4,6},{6,4},{5,7},{7,5},{8,10},{10,8},{9,1... | collective-permute-start | bytes 196616 | tf_op jit(solution)/shard_map/ppermute | solution.py:274
  37.0 4.7 %collective-permute-start.16 = (f32[32,128]{1,0:T(8,128)S(1)}, f32[32,128]{1,0:T(8,128)S(1)}, u32[]{:S(2)}, u32[]{:S(2)}) collective-permute-start(f32[32,128]{1,0:T(8,128)S(1)} %get-tuple-element.40.own_ref), channel_id=1, source_target_pairs={{0,8},{1,13},{4,12},{5,9},{8,0},{9,5},{12,4},{13,1},{2,10},{3,15},... | collective-permute-start | bytes 49160 | tf_op jit(solution)/shard_map/ppermute | solution.py:325
  38.0 3.8 %collective-permute-start.18 = (f32[16,128]{1,0:T(8,128)S(1)}, f32[16,128]{1,0:T(8,128)S(1)}, u32[]{:S(2)}, u32[]{:S(2)}) collective-permute-start(f32[16,128]{1,0:T(8,128)S(1)} %get-tuple-element.43), channel_id=1, source_target_pairs={{0,4},{1,5},{4,0},{5,1},{8,12},{9,13},{12,8},{13,9},{2,6},{3,7},{6... | collective-permute-start | bytes 24584 | tf_op jit(solution)/shard_map/ppermute | solution.py:325
  41.7 1.3 %collective-permute-start.17 = (f32[32,128]{1,0:T(8,128)S(1)}, f32[32,128]{1,0:T(8,128)S(1)}, u32[]{:S(2)}, u32[]{:S(2)}) collective-permute-start(f32[32,128]{1,0:T(8,128)S(1)} %collective-permute-done.16.refs_0_), channel_id=1, source_target_pairs={{0,1},{1,0},{2,3},{3,2},{4,5},{5,4},{6,7},{7,6},{8,9},{9,8},{10,11... | collective-permute-start | bytes 49160 | tf_op jit(solution)/shard_map/ppermute | solution.py:328
  41.8 1.3 %collective-permute-start.19 = (f32[16,128]{1,0:T(8,128)S(1)}, f32[16,128]{1,0:T(8,128)S(1)}, u32[]{:S(2)}, u32[]{:S(2)}) collective-permute-start(f32[16,128]{1,0:T(8,128)S(1)} %collective-permute-done.18.refs_2_), channel_id=1, source_target_pairs={{0,1},{1,0},{2,3},{3,2},{4,5},{5,4},{6,7},{7,6},{8,9},{9,8},{10,11... | collective-permute-start | bytes 24584 | tf_op jit(solution)/shard_map/ppermute | solution.py:328

commit v11 on v10

--- a/solution.py
+++ b/solution.py
@@ -125,16 +125,12 @@
         ref[...] = message.astype(bf16)
 
 
-def image_kernel(pairs, columns, parts, i_ref, j_ref, base_ref, high_ref, low_ref, near_ref, t_ref, u_ref, own_ref, *refs):
-    received, (y_ref, send_ref, corr_ref, part_ref) = refs[:-4], refs[-4:]
+def image_kernel(pairs, columns, parts, i_ref, j_ref, base_ref, high_ref, low_ref, t_ref, u_ref, own_ref, *refs):
+    received, (y_ref, send_ref) = refs[:-2], refs[-2:]
     block, rows = base_ref.shape
     width = low_ref.shape[0] - block
     me, core = lax.axis_index("rows"), lax.axis_index("sub")
     y = base_ref[...] + own_ref[...]
-    halves = [r[k : k + block].astype(f32) for r in (high_ref, near_ref) for k in (width + block, width + 2 * block)]
-    corr = (halves[0] + halves[1]) + (halves[2] + halves[3])
-    corr_ref[...] = corr
-    part_ref[...] = corr.astype(bf16)
     blocks = [(me, high_ref[width : width + block].astype(f32))]
     for k, pair in enumerate(pairs):
         mine, other = received[2 * k][...].astype(f32), received[2 * k + 1][...].astype(f32)
@@ -161,6 +157,17 @@
     diagonal = fold(dot_split(halves, (high_ref[width : width + block], low_ref[width:]), NT), parts)
     stored = dot_split(halves, (high_ref[:width], low_ref[:width]), NT)
     send_ref[...] = jnp.concatenate([stored, diagonal], axis=0)
+
+
+def stored_kernel(high_ref, near_ref, corr_ref, part_ref):
+    block = corr_ref.shape[0]
+    start = high_ref.shape[0] - 2 * block
+    corr = 0.0
+    for ref in (high_ref, near_ref):
+        halves = ref[start:].astype(f32)
+        corr = corr + (halves[:block] + halves[block:])
+    corr_ref[...] = corr
+    part_ref[...] = corr.astype(bf16)
 
 
 def pack(total, block):
@@ -336,11 +343,13 @@
     near = exchange(high, "cols", 1)
     received = serve(sends[1:])
     small = block // parts
-    y, mine, corr, part = call(
+    y, mine = call(
         functools.partial(image_kernel, pairs, columns, parts),
-        [(half, f32), ((block + small, rows), f32), (half, f32), (half, bf16)],
-        "v" * (9 + len(received)),
-    )(index, other_index, base, high, low, near, tiles, other_tiles, sends[0], *received)
+        [(half, f32), ((block + small, rows), f32)],
+        "v" * (8 + len(received)),
+    )(index, other_index, base, high, low, tiles, other_tiles, sends[0], *received)
+    sum_stored = call(stored_kernel, [(half, f32), (half, bf16)], "vv")
+    corr, part = sum_stored(high, near)
     other = exchange(mine, "cols", 1)
     late = exchange(y, "cols", 1)
     distances = [2**k for k in range(1, columns.bit_length() - 1)]

time: 45.3 us -> 45.3 us (level)
  transfers between devices with their start and end apart: 20 -> 20, of which waited for: 10 -> 10; matrix products, arithmetic and copies ran while one was open for 0% -> 0% of each run, Pallas kernels for 3% -> 5%
where the time goes in v11:
time: 45.3 us; the launch traced here: 45.1 us
  starting transfers between devices  21.1 us (47%)
  waiting for transfers between devices  18.5 us (41%)
  Pallas kernels  4.88 us (11%)
  between operations  0.71 us (2%)
    ppermute x9, starting transfers between devices, exchange(): lax.ppermute(x, axis, [(i, i ^ distance) for i in range(lax.axis_size(axi...  12.6 us
    ppermute x9, waiting for transfers between devices, exchange(): lax.ppermute(x, axis, [(i, i ^ distance) for i in range(lax.axis_size(axi...  10.8 us
    ppermute x4, starting transfers between devices, serve(): received.append(lax.ppermute(send, ('rows', 'sub'), moves))  6.95 us
    ppermute x4, waiting for transfers between devices, serve(): received.append(lax.ppermute(send, ('rows', 'sub'), moves))  4.89 us
    pallas_call x1, Pallas kernels, local(): call(functools.partial(factor_kernel, pairs, total_rows), [(half, f32), (...  2.03 us
    ppermute x4, waiting for transfers between devices, serve(): swapped += [x, lax.ppermute(x, 'sub', swap)]  1.83 us
    pallas_call x1, Pallas kernels, local(): prepare(*(pltpu.with_memory_space_constraint(a, pltpu.HBM) for a in sourc...  1.27 us
    ppermute x1, waiting for transfers between devices, local(): other_index = lax.ppermute(tile_index, 'sub', swap)  0.95 us
  transfers between devices with their start and end apart: 20, of which 10 were waited for; matrix products, arithmetic and copies ran while one was open for 0% of the time, Pallas kernels for 5%

profile of v11, /device:TPU:0, one launch (start us, length us, event | category | flops | bytes accessed | tf_op | source)
XLA Modules:
  0.0 45.1 jit_solution(10086922309871903723)
XLA Ops:
  0.6 0.6 %collective-permute-start.1 = (bf16[2,256,256]{2,1,0:T(8,128)(2,1)}, bf16[2,256,256]{2,1,0:T(8,128)(2,1)S(1)}, u32[]{:S(2)}, u32[]{:S(2)}) collective-permute-start(bf16[2,256,256]{2,1,0:T(8,128)(2,1)} %t_hbm.1), channel_id=1, source_target_pairs={{0,1},{1,0},{2,3},{3,2},{4,5},{5,4},{6,7},{7,6},{8,9},{9,8},{10,11... | collective-permute-start | bytes 786440 | tf_op jit(solution)/shard_map/ppermute | solution.py:304
  1.2 1.3 %shard_map.94 = (f32[64,256]{1,0:T(8,128)S(1)}, bf16[448,256]{1,0:T(8,128)(2,1)S(1)}, bf16[320,256]{1,0:T(8,128)(2,1)S(1)}, bf16[2,256,256]{2,1,0:T(8,128)(2,1)S(1)}, s32[2,2]{1,0:T(2,128)S(1)}) custom-call(f32[64,256]{1,0:T(8,128)} %bitcast.12, f32[1,256]{1,0:T(1,128)} %bitcast.14, f32[64,256]{1,0:T(8,128)} %bitcast.13, f32[64,64]{1,0:T(8,128)} %c_hbm.1, ...), custom_call_target="tpu_custom_call" | custom-call | flops 40000000 | bytes 1000000 | tf_op jit(solution)/shard_map/pallas_call | solution.py:323
  2.5 2.6 %collective-permute-start.7 = (bf16[448,256]{1,0:T(8,128)(2,1)S(1)}, bf16[448,256]{1,0:T(8,128)(2,1)S(1)}, u32[]{:S(2)}, u32[]{:S(2)}) collective-permute-start(bf16[448,256]{1,0:T(8,128)(2,1)S(1)} %get-tuple-element.27.high_ref), channel_id=1, source_target_pairs={{0,2},{2,0},{1,3},{3,1},{4,6},{6,4},{5,7},{7,5},{8,10},{10,8},{9,1... | collective-permute-start | bytes 688136 | tf_op jit(solution)/shard_map/ppermute | solution.py:281
  5.0 0.2 collective-permute-start
  5.3 0.9 %collective-permute-done.j_ref = s32[2,2]{1,0:T(2,128)S(1)} collective-permute-done((s32[2,2]{1,0:T(2,128)S(1)}, s32[2,2]{1,0:T(2,128)S(1)}, u32[]{:S(2)}, u32[]{:S(2)}) %collective-permute-start) | collective-permute-done | bytes 48 | tf_op jit(solution)/shard_map/ppermute | solution.py:305
  6.2 0.2 shard_map.95
  6.4 2.7 %collective-permute-start.2 = (bf16[128,256]{1,0:T(8,128)(2,1)S(1)}, bf16[128,256]{1,0:T(8,128)(2,1)S(1)}, u32[]{:S(2)}, u32[]{:S(2)}) collective-permute-start(bf16[128,256]{1,0:T(8,128)(2,1)S(1)} %get-tuple-element.31), channel_id=1, source_target_pairs={{0,8},{1,13},{4,12},{5,9},{8,0},{9,5},{12,4},{13,1},{2,10},{3,15},... | collective-permute-start | bytes 196616 | tf_op jit(solution)/shard_map/ppermute | solution.py:332
  9.1 1.6 %collective-permute-start.4 = (bf16[128,128]{1,0:T(8,128)(2,1)S(1)}, bf16[128,128]{1,0:T(8,128)(2,1)S(1)}, u32[]{:S(2)}, u32[]{:S(2)}) collective-permute-start(bf16[128,128]{1,0:T(8,128)(2,1)S(1)} %get-tuple-element.32), channel_id=1, source_target_pairs={{0,4},{1,5},{4,0},{5,1},{8,12},{9,13},{12,8},{13,9},{2,6},{3,7},{6... | collective-permute-start | bytes 98312 | tf_op jit(solution)/shard_map/ppermute | solution.py:332
  10.7 2.6 %collective-permute-done.2.refs_0_ = bf16[128,256]{1,0:T(8,128)(2,1)S(1)} collective-permute-done((bf16[128,256]{1,0:T(8,128)(2,1)S(1)}, bf16[128,256]{1,0:T(8,128)(2,1)S(1)}, u32[]{:S(2)}, u32[]{:S(2)}) %collective-permute-start.2) | collective-permute-done | bytes 65568 | tf_op jit(solution)/shard_map/ppermute | solution.py:332
  13.2 0.3 collective-permute-done.4.refs_2_
  13.7 1.0 %collective-permute-done.5.refs_3_ = bf16[128,128]{1,0:T(8,128)(2,1)S(1)} collective-permute-done((bf16[128,128]{1,0:T(8,128)(2,1)S(1)}, bf16[128,128]{1,0:T(8,128)(2,1)S(1)}, u32[]{:S(2)}, u32[]{:S(2)}) %collective-permute-start.5) | collective-permute-done | bytes 32800 | tf_op jit(solution)/shard_map/ppermute | solution.py:335
  14.7 0.6 %shard_map.96 = (f32[64,256]{1,0:T(8,128)S(1)}, f32[80,256]{1,0:T(8,128)S(1)}) custom-call(s32[2,2]{1,0:T(2,128)S(1)} %get-tuple-element.25.i_ref, s32[2,2]{1,0:T(2,128)S(1)} %collective-permute-done.j_ref, f32[64,256]{1,0:T(8,128)S(1)} %get-tuple-element.26.base_ref, bf16[448,256]{1,0:T(8,128)(2,1)S(1)} %get-tuple-element.27.high_ref, ...), custom_call_target="tpu_custom_call" | custom-call | flops 40000000 | bytes 1000000 | tf_op jit(solution)/shard_map/pallas_call | solution.py:346
  15.4 0.8 %collective-permute-start.6 = (f32[80,256]{1,0:T(8,128)S(1)}, f32[80,256]{1,0:T(8,128)S(1)}, u32[]{:S(2)}, u32[]{:S(2)}) collective-permute-start(f32[80,256]{1,0:T(8,128)S(1)} %get-tuple-element.33.mine_ref), channel_id=1, source_target_pairs={{0,2},{2,0},{1,3},{3,1},{4,6},{6,4},{5,7},{7,5},{8,10},{10,8},{9,1... | collective-permute-start | bytes 245768 | tf_op jit(solution)/shard_map/ppermute | solution.py:281
  16.2 1.3 %collective-permute-start.13 = (bf16[64,256]{1,0:T(8,128)(2,1)S(1)}, bf16[64,256]{1,0:T(8,128)(2,1)S(1)}, u32[]{:S(2)}, u32[]{:S(2)}) collective-permute-start(bf16[64,256]{1,0:T(8,128)(2,1)S(1)} %get-tuple-element.37), channel_id=1, source_target_pairs={{0,4},{4,0},{8,12},{12,8},{1,5},{5,1},{9,13},{13,9},{2,6},{6,2},{1... | collective-permute-start | bytes 98312 | tf_op jit(solution)/shard_map/ppermute | solution.py:281
  17.5 2.5 %collective-permute-done.6.other_ref = f32[80,256]{1,0:T(8,128)S(1)} collective-permute-done((f32[80,256]{1,0:T(8,128)S(1)}, f32[80,256]{1,0:T(8,128)S(1)}, u32[]{:S(2)}, u32[]{:S(2)}) %collective-permute-start.6) | collective-permute-done | bytes 81952 | tf_op jit(solution)/shard_map/ppermute | solution.py:281
  20.0 1.2 %collective-permute-start.10 = (bf16[96,256]{1,0:T(8,128)(2,1)S(1)}, bf16[96,256]{1,0:T(8,128)(2,1)S(1)}, u32[]{:S(2)}, u32[]{:S(2)}) collective-permute-start(bf16[96,256]{1,0:T(8,128)(2,1)S(1)} %get-tuple-element.36), channel_id=1, source_target_pairs={{0,4},{4,0},{8,12},{12,8},{1,5},{5,1},{9,13},{13,9},{2,6},{6,2},{1... | collective-permute-start | bytes 147464 | tf_op jit(solution)/shard_map/ppermute | solution.py:281
  21.2 2.2 %collective-permute-start.9 = (bf16[96,256]{1,0:T(8,128)(2,1)S(1)}, bf16[96,256]{1,0:T(8,128)(2,1)S(1)}, u32[]{:S(2)}, u32[]{:S(2)}) collective-permute-start(bf16[96,256]{1,0:T(8,128)(2,1)S(1)} %get-tuple-element.36), channel_id=1, source_target_pairs={{0,12},{4,8},{8,4},{12,0},{1,13},{5,9},{9,5},{13,1},{2,14},{6,10},... | collective-permute-start | bytes 147464 | tf_op jit(solution)/shard_map/ppermute | solution.py:281
  23.5 0.5 %collective-permute-start.8 = (bf16[96,256]{1,0:T(8,128)(2,1)S(1)}, bf16[96,256]{1,0:T(8,128)(2,1)S(1)}, u32[]{:S(2)}, u32[]{:S(2)}) collective-permute-start(bf16[96,256]{1,0:T(8,128)(2,1)S(1)} %get-tuple-element.36), channel_id=1, source_target_pairs={{0,8},{4,12},{8,0},{12,4},{1,9},{5,13},{9,1},{13,5},{2,10},{6,14},... | collective-permute-start | bytes 147464 | tf_op jit(solution)/shard_map/ppermute | solution.py:281
  24.0 2.9 %collective-permute-start.12 = (bf16[64,256]{1,0:T(8,128)(2,1)S(1)}, bf16[64,256]{1,0:T(8,128)(2,1)S(1)}, u32[]{:S(2)}, u32[]{:S(2)}) collective-permute-start(bf16[64,256]{1,0:T(8,128)(2,1)S(1)} %get-tuple-element.37), channel_id=1, source_target_pairs={{0,12},{4,8},{8,4},{12,0},{1,13},{5,9},{9,5},{13,1},{2,14},{6,10},... | collective-permute-start | bytes 98312 | tf_op jit(solution)/shard_map/ppermute | solution.py:281
  26.9 0.2 collective-permute-start.11
  27.1 2.7 %collective-permute-done.12.refs_4_ = bf16[64,256]{1,0:T(8,128)(2,1)S(1)} collective-permute-done((bf16[64,256]{1,0:T(8,128)(2,1)S(1)}, bf16[64,256]{1,0:T(8,128)(2,1)S(1)}, u32[]{:S(2)}, u32[]{:S(2)}) %collective-permute-start.12) | collective-permute-done | bytes 32800 | tf_op jit(solution)/shard_map/ppermute | solution.py:281
  29.8 1.9 %collective-permute-done.11.refs_3_ = bf16[64,256]{1,0:T(8,128)(2,1)S(1)} collective-permute-done((bf16[64,256]{1,0:T(8,128)(2,1)S(1)}, bf16[64,256]{1,0:T(8,128)(2,1)S(1)}, u32[]{:S(2)}, u32[]{:S(2)}) %collective-permute-start.11) | collective-permute-done | bytes 32800 | tf_op jit(solution)/shard_map/ppermute | solution.py:281
  31.7 0.5 %shard_map.99 = (f32[192,256]{1,0:T(8,128)S(1)}, f32[64,64]{1,0:T(8,128)S(1)}) custom-call(f32[80,256]{1,0:T(8,128)S(1)} %get-tuple-element.34.total_ref, f32[64,256]{1,0:T(8,128)S(1)} %get-tuple-element.35.corr_ref, bf16[448,256]{1,0:T(8,128)(2,1)S(1)} %get-tuple-element.27.high_ref, bf16[320,256]{1,0:T(8,128)(2,1)S(1)} %get-tuple-element.28.low_ref, ...), custom_call_target="tpu_custom_call" | custom-call | flops 40000000 | bytes 1000000 | tf_op jit(solution)/shard_map/pallas_call | solution.py:377
  32.3 0.8 %collective-permute-start.15 = (f32[64,256]{1,0:T(8,128)S(1)}, f32[64,256]{1,0:T(8,128)S(1)}, u32[]{:S(2)}, u32[]{:S(2)}) collective-permute-start(f32[64,256]{1,0:T(8,128)S(1)} %get-tuple-element.39.y_ref), channel_id=1, source_target_pairs={{0,2},{2,0},{1,3},{3,1},{4,6},{6,4},{5,7},{7,5},{8,10},{10,8},{9,1... | collective-permute-start | bytes 196616 | tf_op jit(solution)/shard_map/ppermute | solution.py:281
  33.1 3.7 %collective-permute-done.15.z_ref = f32[64,256]{1,0:T(8,128)S(1)} collective-permute-done((f32[64,256]{1,0:T(8,128)S(1)}, f32[64,256]{1,0:T(8,128)S(1)}, u32[]{:S(2)}, u32[]{:S(2)}) %collective-permute-start.15) | collective-permute-done | bytes 65568 | tf_op jit(solution)/shard_map/ppermute | solution.py:281
  36.8 0.2 shard_map.100
  37.0 0.9 %collective-permute-start.16 = (f32[32,128]{1,0:T(8,128)S(1)}, f32[32,128]{1,0:T(8,128)S(1)}, u32[]{:S(2)}, u32[]{:S(2)}) collective-permute-start(f32[32,128]{1,0:T(8,128)S(1)} %get-tuple-element.40.own_ref), channel_id=1, source_target_pairs={{0,8},{1,13},{4,12},{5,9},{8,0},{9,5},{12,4},{13,1},{2,10},{3,15},... | collective-permute-start | bytes 49160 | tf_op jit(solution)/shard_map/ppermute | solution.py:332
  37.9 1.8 %collective-permute-start.18 = (f32[16,128]{1,0:T(8,128)S(1)}, f32[16,128]{1,0:T(8,128)S(1)}, u32[]{:S(2)}, u32[]{:S(2)}) collective-permute-start(f32[16,128]{1,0:T(8,128)S(1)} %get-tuple-element.43), channel_id=1, source_target_pairs={{0,4},{1,5},{4,0},{5,1},{8,12},{9,13},{12,8},{13,9},{2,6},{3,7},{6... | collective-permute-start | bytes 24584 | tf_op jit(solution)/shard_map/ppermute | solution.py:332
  39.7 2.0 %collective-permute-done.16.refs_0_ = f32[32,128]{1,0:T(8,128)S(1)} collective-permute-done((f32[32,128]{1,0:T(8,128)S(1)}, f32[32,128]{1,0:T(8,128)S(1)}, u32[]{:S(2)}, u32[]{:S(2)}) %collective-permute-start.16) | collective-permute-done | bytes 16416 | tf_op jit(solution)/shard_map/ppermute | solution.py:332
  41.8 0.5 %collective-permute-start.19 = (f32[16,128]{1,0:T(8,128)S(1)}, f32[16,128]{1,0:T(8,128)S(1)}, u32[]{:S(2)}, u32[]{:S(2)}) collective-permute-start(f32[16,128]{1,0:T(8,128)S(1)} %collective-permute-done.18.refs_2_), channel_id=1, source_target_pairs={{0,1},{1,0},{2,3},{3,2},{4,5},{5,4},{6,7},{7,6},{8,9},{9,8},{10,11... | collective-permute-start | bytes 24584 | tf_op jit(solution)/shard_map/ppermute | solution.py:335
  42.2 0.8 %collective-permute-done.19.refs_3_ = f32[16,128]{1,0:T(8,128)S(1)} collective-permute-done((f32[16,128]{1,0:T(8,128)S(1)}, f32[16,128]{1,0:T(8,128)S(1)}, u32[]{:S(2)}, u32[]{:S(2)}) %collective-permute-start.19) | collective-permute-done | bytes 8224 | tf_op jit(solution)/shard_map/ppermute | solution.py:335
  43.1 2.0 %shard_map.101 = (f32[64,256]{1,0:T(8,128)}, f32[64,64]{1,0:T(8,128)}, f32[64,64]{1,0:T(8,128)}) custom-call(f32[32,128]{1,0:T(8,128)S(1)} %get-tuple-element.40.own_ref, f32[64,256]{1,0:T(8,128)S(1)} %get-tuple-element.41.images_ref, f32[64,64]{1,0:T(8,128)S(1)} %get-tuple-element.42.d_ref, f32[32,128]{1,0:T(8,128)S(1)} %collective-permute-done.16.refs_0_, ...), custom_call_target="tpu_custom_call" | custom-call | flops 40000000 | bytes 1000000 | tf_op jit(solution)/shard_map/pallas_call | solution.py:387
  (18 shorter events, 0.4 us)
Async XLA Ops:
  0.6 5.6 %collective-permute-start.1 = (bf16[2,256,256]{2,1,0:T(8,128)(2,1)}, bf16[2,256,256]{2,1,0:T(8,128)(2,1)S(1)}, u32[]{:S(2)}, u32[]{:S(2)}) collective-permute-start(bf16[2,256,256]{2,1,0:T(8,128)(2,1)} %t_hbm.1), channel_id=1, source_target_pairs={{0,1},{1,0},{2,3},{3,2},{4,5},{5,4},{6,7},{7,6},{8,9},{9,8},{10,11... | collective-permute-start | bytes 786440 | tf_op jit(solution)/shard_map/ppermute | solution.py:304
  2.5 2.6 %copy-start = (s32[2,2]{1,0:T(2,128)S(1)}, s32[2,2]{1,0:T(2,128)}, u32[]{:S(2)}) copy-start(s32[2,2]{1,0:T(2,128)} %i_hbm.1) | copy-start | bytes 52
  2.5 13.7 %collective-permute-start.7 = (bf16[448,256]{1,0:T(8,128)(2,1)S(1)}, bf16[448,256]{1,0:T(8,128)(2,1)S(1)}, u32[]{:S(2)}, u32[]{:S(2)}) collective-permute-start(bf16[448,256]{1,0:T(8,128)(2,1)S(1)} %get-tuple-element.27.high_ref), channel_id=1, source_target_pairs={{0,2},{2,0},{1,3},{3,1},{4,6},{6,4},{5,7},{7,5},{8,10},{10,8},{9,1... | collective-permute-start | bytes 688136 | tf_op jit(solution)/shard_map/ppermute | solution.py:281
  5.0 1.2 %collective-permute-start = (s32[2,2]{1,0:T(2,128)S(1)}, s32[2,2]{1,0:T(2,128)S(1)}, u32[]{:S(2)}, u32[]{:S(2)}) collective-permute-start(s32[2,2]{1,0:T(2,128)S(1)} %copy-done), channel_id=1, source_target_pairs={{0,1},{1,0},{2,3},{3,2},{4,5},{5,4},{6,7},{7,6},{8,9},{9,8},{10,11... | collective-permute-start | bytes 56 | tf_op jit(solution)/shard_map/ppermute | solution.py:305
  6.4 6.8 %collective-permute-start.2 = (bf16[128,256]{1,0:T(8,128)(2,1)S(1)}, bf16[128,256]{1,0:T(8,128)(2,1)S(1)}, u32[]{:S(2)}, u32[]{:S(2)}) collective-permute-start(bf16[128,256]{1,0:T(8,128)(2,1)S(1)} %get-tuple-element.31), channel_id=1, source_target_pairs={{0,8},{1,13},{4,12},{5,9},{8,0},{9,5},{12,4},{13,1},{2,10},{3,15},... | collective-permute-start | bytes 196616 | tf_op jit(solution)/shard_map/ppermute | solution.py:332
  9.1 4.4 %collective-permute-start.4 = (bf16[128,128]{1,0:T(8,128)(2,1)S(1)}, bf16[128,128]{1,0:T(8,128)(2,1)S(1)}, u32[]{:S(2)}, u32[]{:S(2)}) collective-permute-start(bf16[128,128]{1,0:T(8,128)(2,1)S(1)} %get-tuple-element.32), channel_id=1, source_target_pairs={{0,4},{1,5},{4,0},{5,1},{8,12},{9,13},{12,8},{13,9},{2,6},{3,7},{6... | collective-permute-start | bytes 98312 | tf_op jit(solution)/shard_map/ppermute | solution.py:332
  13.2 1.5 %collective-permute-start.3 = (bf16[128,256]{1,0:T(8,128)(2,1)S(1)}, bf16[128,256]{1,0:T(8,128)(2,1)S(1)}, u32[]{:S(2)}, u32[]{:S(2)}) collective-permute-start(bf16[128,256]{1,0:T(8,128)(2,1)S(1)} %collective-permute-done.2.refs_0_), channel_id=1, source_target_pairs={{0,1},{1,0},{2,3},{3,2},{4,5},{5,4},{6,7},{7,6},{8,9},{9,8},{10,11... | collective-permute-start | bytes 196616 | tf_op jit(solution)/shard_map/ppermute | solution.py:335
  13.5 1.2 %collective-permute-start.5 = (bf16[128,128]{1,0:T(8,128)(2,1)S(1)}, bf16[128,128]{1,0:T(8,128)(2,1)S(1)}, u32[]{:S(2)}, u32[]{:S(2)}) collective-permute-start(bf16[128,128]{1,0:T(8,128)(2,1)S(1)} %collective-permute-done.4.refs_2_), channel_id=1, source_target_pairs={{0,1},{1,0},{2,3},{3,2},{4,5},{5,4},{6,7},{7,6},{8,9},{9,8},{10,11... | collective-permute-start | bytes 98312 | tf_op jit(solution)/shard_map/ppermute | solution.py:335
  15.4 4.6 %collective-permute-start.6 = (f32[80,256]{1,0:T(8,128)S(1)}, f32[80,256]{1,0:T(8,128)S(1)}, u32[]{:S(2)}, u32[]{:S(2)}) collective-permute-start(f32[80,256]{1,0:T(8,128)S(1)} %get-tuple-element.33.mine_ref), channel_id=1, source_target_pairs={{0,2},{2,0},{1,3},{3,1},{4,6},{6,4},{5,7},{7,5},{8,10},{10,8},{9,1... | collective-permute-start | bytes 245768 | tf_op jit(solution)/shard_map/ppermute | solution.py:281
  16.2 10.7 %collective-permute-start.13 = (bf16[64,256]{1,0:T(8,128)(2,1)S(1)}, bf16[64,256]{1,0:T(8,128)(2,1)S(1)}, u32[]{:S(2)}, u32[]{:S(2)}) collective-permute-start(bf16[64,256]{1,0:T(8,128)(2,1)S(1)} %get-tuple-element.37), channel_id=1, source_target_pairs={{0,4},{4,0},{8,12},{12,8},{1,5},{5,1},{9,13},{13,9},{2,6},{6,2},{1... | collective-permute-start | bytes 98312 | tf_op jit(solution)/shard_map/ppermute | solution.py:281
  20.0 11.7 %collective-permute-start.10 = (bf16[96,256]{1,0:T(8,128)(2,1)S(1)}, bf16[96,256]{1,0:T(8,128)(2,1)S(1)}, u32[]{:S(2)}, u32[]{:S(2)}) collective-permute-start(bf16[96,256]{1,0:T(8,128)(2,1)S(1)} %get-tuple-element.36), channel_id=1, source_target_pairs={{0,4},{4,0},{8,12},{12,8},{1,5},{5,1},{9,13},{13,9},{2,6},{6,2},{1... | collective-permute-start | bytes 147464 | tf_op jit(solution)/shard_map/ppermute | solution.py:281
  21.2 10.5 %collective-permute-start.9 = (bf16[96,256]{1,0:T(8,128)(2,1)S(1)}, bf16[96,256]{1,0:T(8,128)(2,1)S(1)}, u32[]{:S(2)}, u32[]{:S(2)}) collective-permute-start(bf16[96,256]{1,0:T(8,128)(2,1)S(1)} %get-tuple-element.36), channel_id=1, source_target_pairs={{0,12},{4,8},{8,4},{12,0},{1,13},{5,9},{9,5},{13,1},{2,14},{6,10},... | collective-permute-start | bytes 147464 | tf_op jit(solution)/shard_map/ppermute | solution.py:281
  23.5 8.2 %collective-permute-start.8 = (bf16[96,256]{1,0:T(8,128)(2,1)S(1)}, bf16[96,256]{1,0:T(8,128)(2,1)S(1)}, u32[]{:S(2)}, u32[]{:S(2)}) collective-permute-start(bf16[96,256]{1,0:T(8,128)(2,1)S(1)} %get-tuple-element.36), channel_id=1, source_target_pairs={{0,8},{4,12},{8,0},{12,4},{1,9},{5,13},{9,1},{13,5},{2,10},{6,14},... | collective-permute-start | bytes 147464 | tf_op jit(solution)/shard_map/ppermute | solution.py:281
  24.0 5.8 %collective-permute-start.12 = (bf16[64,256]{1,0:T(8,128)(2,1)S(1)}, bf16[64,256]{1,0:T(8,128)(2,1)S(1)}, u32[]{:S(2)}, u32[]{:S(2)}) collective-permute-start(bf16[64,256]{1,0:T(8,128)(2,1)S(1)} %get-tuple-element.37), channel_id=1, source_target_pairs={{0,12},{4,8},{8,4},{12,0},{1,13},{5,9},{9,5},{13,1},{2,14},{6,10},... | collective-permute-start | bytes 98312 | tf_op jit(solution)/shard_map/ppermute | solution.py:281
  26.9 4.8 %collective-permute-start.11 = (bf16[64,256]{1,0:T(8,128)(2,1)S(1)}, bf16[64,256]{1,0:T(8,128)(2,1)S(1)}, u32[]{:S(2)}, u32[]{:S(2)}) collective-permute-start(bf16[64,256]{1,0:T(8,128)(2,1)S(1)} %get-tuple-element.37), channel_id=1, source_target_pairs={{0,8},{4,12},{8,0},{12,4},{1,9},{5,13},{9,1},{13,5},{2,10},{6,14},... | collective-permute-start | bytes 98312 | tf_op jit(solution)/shard_map/ppermute | solution.py:281
  32.2 4.6 %collective-permute-start.14 = (f32[192,256]{1,0:T(8,128)S(1)}, f32[192,256]{1,0:T(8,128)S(1)}, u32[]{:S(2)}, u32[]{:S(2)}) collective-permute-start(f32[192,256]{1,0:T(8,128)S(1)} %get-tuple-element.38.mine_ref), channel_id=1, source_target_pairs={{0,1},{1,0},{2,3},{3,2},{4,5},{5,4},{6,7},{7,6},{8,9},{9,8},{10,11... | collective-permute-start | bytes 589832 | tf_op jit(solution)/shard_map/ppermute | solution.py:382
  32.3 4.5 %collective-permute-start.15 = (f32[64,256]{1,0:T(8,128)S(1)}, f32[64,256]{1,0:T(8,128)S(1)}, u32[]{:S(2)}, u32[]{:S(2)}) collective-permute-start(f32[64,256]{1,0:T(8,128)S(1)} %get-tuple-element.39.y_ref), channel_id=1, source_target_pairs={{0,2},{2,0},{1,3},{3,1},{4,6},{6,4},{5,7},{7,5},{8,10},{10,8},{9,1... | collective-permute-start | bytes 196616 | tf_op jit(solution)/shard_map/ppermute | solution.py:281
  37.0 4.7 %collective-permute-start.16 = (f32[32,128]{1,0:T(8,128)S(1)}, f32[32,128]{1,0:T(8,128)S(1)}, u32[]{:S(2)}, u32[]{:S(2)}) collective-permute-start(f32[32,128]{1,0:T(8,128)S(1)} %get-tuple-element.40.own_ref), channel_id=1, source_target_pairs={{0,8},{1,13},{4,12},{5,9},{8,0},{9,5},{12,4},{13,1},{2,10},{3,15},... | collective-permute-start | bytes 49160 | tf_op jit(solution)/shard_map/ppermute | solution.py:332
  37.9 3.8 %collective-permute-start.18 = (f32[16,128]{1,0:T(8,128)S(1)}, f32[16,128]{1,0:T(8,128)S(1)}, u32[]{:S(2)}, u32[]{:S(2)}) collective-permute-start(f32[16,128]{1,0:T(8,128)S(1)} %get-tuple-element.43), channel_id=1, source_target_pairs={{0,4},{1,5},{4,0},{5,1},{8,12},{9,13},{12,8},{13,9},{2,6},{3,7},{6... | collective-permute-start | bytes 24584 | tf_op jit(solution)/shard_map/ppermute | solution.py:332
  41.7 1.3 %collective-permute-start.17 = (f32[32,128]{1,0:T(8,128)S(1)}, f32[32,128]{1,0:T(8,128)S(1)}, u32[]{:S(2)}, u32[]{:S(2)}) collective-permute-start(f32[32,128]{1,0:T(8,128)S(1)} %collective-permute-done.16.refs_0_), channel_id=1, source_target_pairs={{0,1},{1,0},{2,3},{3,2},{4,5},{5,4},{6,7},{7,6},{8,9},{9,8},{10,11... | collective-permute-start | bytes 49160 | tf_op jit(solution)/shard_map/ppermute | solution.py:335
  41.8 1.3 %collective-permute-start.19 = (f32[16,128]{1,0:T(8,128)S(1)}, f32[16,128]{1,0:T(8,128)S(1)}, u32[]{:S(2)}, u32[]{:S(2)}) collective-permute-start(f32[16,128]{1,0:T(8,128)S(1)} %collective-permute-done.18.refs_2_), channel_id=1, source_target_pairs={{0,1},{1,0},{2,3},{3,2},{4,5},{5,4},{6,7},{7,6},{8,9},{9,8},{10,11... | collective-permute-start | bytes 24584 | tf_op jit(solution)/shard_map/ppermute | solution.py:335

commit v12 on v8

--- a/solution.py
+++ b/solution.py
@@ -123,7 +123,8 @@
     parity = jnp.bitwise_and(me, 1)
     outs[0][...] = jnp.concatenate([pushed(me), corr_ref[parity]], axis=0)
     for ref, pair in zip(outs[1:], pairs):
-        message = jnp.concatenate([x.astype(f32), pushed(target_band(me, core, pair))], axis=0)
+        products_of = split(pushed(target_band(me, core, pair)))
+        message = jnp.concatenate([h.astype(f32) for h in (x, *products_of)], axis=0)
         if pair[0] != pair[1]:
             ref[...] = message.astype(bf16)
         else:
@@ -145,15 +146,15 @@
         if pair[0] != pair[1]:
             found = [(target_band(me, core, pair), mine), (target_band(me, core, pair[::-1]), other)]
         else:
-            parts_of = mine[2 * block :]
+            parts_of = mine[3 * block :]
             count = parts_of.shape[0] // 2
             corr = corr + fold(parts_of[:count] + parts_of[count:], 2)
-            mine, other = mine[: 2 * block], other[: 2 * block]
+            mine, other = mine[: 3 * block], other[: 3 * block]
             first, second = jnp.where(core == 0, mine, other), jnp.where(core == 0, other, mine)
             found = [(jnp.bitwise_xor(me, pair[0]), jnp.concatenate([first, second], axis=1))]
         for band, message in found:
             blocks.append((band, message[0:block]))
-            y = y + message[block:]
+            y = y + (message[block : 2 * block] + message[2 * block :])
     tiles = [ref[k] for ref in (t_ref, u_ref) for k in range(ref.shape[0])]
     for target, tile in zip(tile_columns((i_ref, j_ref), (block, rows)), tiles):
         source = jnp.zeros((block, rows), f32)
@@ -344,7 +345,7 @@
     sends = call(
         functools.partial(push_kernel, pairs, columns),
         [((block + chunk, rows), f32)]
-        + [((2 * block, rows) if a != b else (4 * block, rows // 2), bf16) for a, b in pairs],
+        + [((3 * block, rows) if a != b else (5 * block, rows // 2), bf16) for a, b in pairs],
         "vvvvvv",
     )(index, other_index, high, corr, tiles, other_tiles)
     near = exchange(high, "cols", 1)

time: 42.7 us -> 43.8 us (1.026)
  waiting for transfers between devices: 20.4 us -> 21.4 us
    ppermute x4, waiting for transfers between devices: 6.34 us -> 7.35 us  [serve(): received.append(lax.ppermute(send, ('rows', 'sub'), moves))]
where the time goes in v12:
time: 43.8 us; the launch traced here: 43.6 us
  waiting for transfers between devices  21.4 us (49%)
  starting transfers between devices  16.7 us (38%)
  Pallas kernels  4.86 us (11%)
  between operations  0.69 us (2%)
    ppermute x6, waiting for transfers between devices, exchange(): lax.ppermute(x, axis, [(i, i ^ distance) for i in range(lax.axis_size(axi...  11.9 us
    ppermute x6, starting transfers between devices, exchange(): lax.ppermute(x, axis, [(i, i ^ distance) for i in range(lax.axis_size(axi...  8.11 us
    ppermute x4, starting transfers between devices, serve(): received.append(lax.ppermute(send, ('rows', 'sub'), moves))  7.35 us
    ppermute x4, waiting for transfers between devices, serve(): received.append(lax.ppermute(send, ('rows', 'sub'), moves))  7.35 us
    ppermute x4, waiting for transfers between devices, serve(): swapped += [x, lax.ppermute(x, 'sub', swap)]  2.11 us
    pallas_call x1, Pallas kernels, local(): call(functools.partial(factor_kernel, pairs, total_rows), [(half, f32), (...  2.03 us
    pallas_call x1, Pallas kernels, local(): prepare(*(pltpu.with_memory_space_constraint(a, pltpu.HBM) for a in sourc...  1.27 us
  transfers between devices with their start and end apart: 17, of which 10 were waited for; matrix products, arithmetic and copies ran while one was open for 0% of the time, Pallas kernels for 3%

profile of v12, /device:TPU:0, one launch (start us, length us, event | category | flops | bytes accessed | tf_op | source)
XLA Modules:
  0.0 43.6 jit_solution(9695201337597712552)
XLA Ops:
  0.6 0.6 %collective-permute-start.1 = (bf16[2,256,256]{2,1,0:T(8,128)(2,1)}, bf16[2,256,256]{2,1,0:T(8,128)(2,1)S(1)}, u32[]{:S(2)}, u32[]{:S(2)}) collective-permute-start(bf16[2,256,256]{2,1,0:T(8,128)(2,1)} %t_hbm.1), channel_id=1, source_target_pairs={{0,1},{1,0},{2,3},{3,2},{4,5},{5,4},{6,7},{7,6},{8,9},{9,8},{10,11... | collective-permute-start | bytes 786440 | tf_op jit(solution)/shard_map/ppermute | solution.py:311
  1.2 0.1 collective-permute-start
  1.3 1.3 %shard_map.94 = (f32[64,256]{1,0:T(8,128)S(1)}, f32[2,32,256]{2,1,0:T(8,128)S(1)}, bf16[320,256]{1,0:T(8,128)(2,1)S(1)}, bf16[320,256]{1,0:T(8,128)(2,1)S(1)}, b...) custom-call(f32[64,256]{1,0:T(8,128)} %bitcast.12, f32[1,256]{1,0:T(1,128)} %bitcast.14, f32[64,256]{1,0:T(8,128)} %bitcast.13, ...), custom_call_target="tpu_custom_call" | custom-call | flops 40000000 | bytes 1000000 | tf_op jit(solution)/shard_map/pallas_call | solution.py:330
  2.5 0.0 collective-permute-done.j_ref
  2.6 0.0 collective-permute-done.1.u_ref
  2.6 0.2 shard_map.95
  2.8 4.1 %collective-permute-start.2 = (bf16[192,256]{1,0:T(8,128)(2,1)S(1)}, bf16[192,256]{1,0:T(8,128)(2,1)S(1)}, u32[]{:S(2)}, u32[]{:S(2)}) collective-permute-start(bf16[192,256]{1,0:T(8,128)(2,1)S(1)} %get-tuple-element.31), channel_id=1, source_target_pairs={{0,8},{1,13},{4,12},{5,9},{8,0},{9,5},{12,4},{13,1},{2,10},{3,15},... | collective-permute-start | bytes 294920 | tf_op jit(solution)/shard_map/ppermute | solution.py:339
  6.9 1.6 %collective-permute-start.4 = (bf16[320,128]{1,0:T(8,128)(2,1)S(1)}, bf16[320,128]{1,0:T(8,128)(2,1)S(1)}, u32[]{:S(2)}, u32[]{:S(2)}) collective-permute-start(bf16[320,128]{1,0:T(8,128)(2,1)S(1)} %get-tuple-element.32), channel_id=1, source_target_pairs={{0,4},{1,5},{4,0},{5,1},{8,12},{9,13},{12,8},{13,9},{2,6},{3,7},{6... | collective-permute-start | bytes 245768 | tf_op jit(solution)/shard_map/ppermute | solution.py:339
  8.5 3.8 %collective-permute-done.2.refs_0_ = bf16[192,256]{1,0:T(8,128)(2,1)S(1)} collective-permute-done((bf16[192,256]{1,0:T(8,128)(2,1)S(1)}, bf16[192,256]{1,0:T(8,128)(2,1)S(1)}, u32[]{:S(2)}, u32[]{:S(2)}) %collective-permute-start.2) | collective-permute-done | bytes 98336 | tf_op jit(solution)/shard_map/ppermute | solution.py:339
  12.3 0.5 %collective-permute-done.4.refs_2_ = bf16[320,128]{1,0:T(8,128)(2,1)S(1)} collective-permute-done((bf16[320,128]{1,0:T(8,128)(2,1)S(1)}, bf16[320,128]{1,0:T(8,128)(2,1)S(1)}, u32[]{:S(2)}, u32[]{:S(2)}) %collective-permute-start.4) | collective-permute-done | bytes 81952 | tf_op jit(solution)/shard_map/ppermute | solution.py:339
  12.8 1.3 %collective-permute-done.5.refs_3_ = bf16[320,128]{1,0:T(8,128)(2,1)S(1)} collective-permute-done((bf16[320,128]{1,0:T(8,128)(2,1)S(1)}, bf16[320,128]{1,0:T(8,128)(2,1)S(1)}, u32[]{:S(2)}, u32[]{:S(2)}) %collective-permute-start.5) | collective-permute-done | bytes 81952 | tf_op jit(solution)/shard_map/ppermute | solution.py:342
  14.1 0.6 %shard_map.96 = (f32[64,256]{1,0:T(8,128)S(1)}, f32[112,256]{1,0:T(8,128)S(1)}) custom-call(s32[2,2]{1,0:T(2,128)S(1)} %get-tuple-element.24.i_ref, s32[2,2]{1,0:T(2,128)S(1)} %collective-permute-done.j_ref, f32[64,256]{1,0:T(8,128)S(1)} %get-tuple-element.25.base_ref, bf16[320,256]{1,0:T(8,128)(2,1)S(1)} %get-tuple-element.26.high_ref, ...), custom_call_target="tpu_custom_call" | custom-call | flops 40000000 | bytes 1000000 | tf_op jit(solution)/shard_map/pallas_call | solution.py:354
  14.7 1.7 %collective-permute-start.6 = (f32[112,256]{1,0:T(8,128)S(1)}, f32[112,256]{1,0:T(8,128)S(1)}, u32[]{:S(2)}, u32[]{:S(2)}) collective-permute-start(f32[112,256]{1,0:T(8,128)S(1)} %get-tuple-element.33.mine_ref), channel_id=1, source_target_pairs={{0,2},{2,0},{1,3},{3,1},{4,6},{6,4},{5,7},{7,5},{8,10},{10,8},{9,1... | collective-permute-start | bytes 344072 | tf_op jit(solution)/shard_map/ppermute | solution.py:287
  16.4 0.4 collective-permute-start.7
  16.8 4.0 %collective-permute-done.6.other_ref = f32[112,256]{1,0:T(8,128)S(1)} collective-permute-done((f32[112,256]{1,0:T(8,128)S(1)}, f32[112,256]{1,0:T(8,128)S(1)}, u32[]{:S(2)}, u32[]{:S(2)}) %collective-permute-start.6) | collective-permute-done | bytes 114720 | tf_op jit(solution)/shard_map/ppermute | solution.py:287
  20.8 1.5 %collective-permute-start.10 = (bf16[128,256]{1,0:T(8,128)(2,1)S(1)}, bf16[128,256]{1,0:T(8,128)(2,1)S(1)}, u32[]{:S(2)}, u32[]{:S(2)}) collective-permute-start(bf16[128,256]{1,0:T(8,128)(2,1)S(1)} %get-tuple-element.35), channel_id=1, source_target_pairs={{0,4},{4,0},{8,12},{12,8},{1,5},{5,1},{9,13},{13,9},{2,6},{6,2},{1... | collective-permute-start | bytes 196616 | tf_op jit(solution)/shard_map/ppermute | solution.py:287
  22.3 1.9 %collective-permute-start.8 = (bf16[128,256]{1,0:T(8,128)(2,1)S(1)}, bf16[128,256]{1,0:T(8,128)(2,1)S(1)}, u32[]{:S(2)}, u32[]{:S(2)}) collective-permute-start(bf16[128,256]{1,0:T(8,128)(2,1)S(1)} %get-tuple-element.35), channel_id=1, source_target_pairs={{0,8},{4,12},{8,0},{12,4},{1,9},{5,13},{9,1},{13,5},{2,10},{6,14},... | collective-permute-start | bytes 196616 | tf_op jit(solution)/shard_map/ppermute | solution.py:287
  24.2 1.1 %collective-permute-start.9 = (bf16[128,256]{1,0:T(8,128)(2,1)S(1)}, bf16[128,256]{1,0:T(8,128)(2,1)S(1)}, u32[]{:S(2)}, u32[]{:S(2)}) collective-permute-start(bf16[128,256]{1,0:T(8,128)(2,1)S(1)} %get-tuple-element.35), channel_id=1, source_target_pairs={{0,12},{4,8},{8,4},{12,0},{1,13},{5,9},{9,5},{13,1},{2,14},{6,10},... | collective-permute-start | bytes 196616 | tf_op jit(solution)/shard_map/ppermute | solution.py:287
  25.3 0.4 collective-permute-done.10.refs_2_
  25.7 3.2 %collective-permute-done.8.refs_0_ = bf16[128,256]{1,0:T(8,128)(2,1)S(1)} collective-permute-done((bf16[128,256]{1,0:T(8,128)(2,1)S(1)}, bf16[128,256]{1,0:T(8,128)(2,1)S(1)}, u32[]{:S(2)}, u32[]{:S(2)}) %collective-permute-start.8) | collective-permute-done | bytes 65568 | tf_op jit(solution)/shard_map/ppermute | solution.py:287
  28.9 1.4 %collective-permute-done.9.refs_1_ = bf16[128,256]{1,0:T(8,128)(2,1)S(1)} collective-permute-done((bf16[128,256]{1,0:T(8,128)(2,1)S(1)}, bf16[128,256]{1,0:T(8,128)(2,1)S(1)}, u32[]{:S(2)}, u32[]{:S(2)}) %collective-permute-start.9) | collective-permute-done | bytes 65568 | tf_op jit(solution)/shard_map/ppermute | solution.py:287
  30.3 0.5 %shard_map.98 = (f32[192,256]{1,0:T(8,128)S(1)}, f32[64,64]{1,0:T(8,128)S(1)}) custom-call(f32[112,256]{1,0:T(8,128)S(1)} %get-tuple-element.34.total_ref, bf16[320,256]{1,0:T(8,128)(2,1)S(1)} %get-tuple-element.26.high_ref, bf16[320,256]{1,0:T(8,128)(2,1)S(1)} %get-tuple-element.27.low_ref, bf16[320,256]{1,0:T(8,128)(2,1)S(1)} %collective-permute-done.7.near_ref, ...), custom_call_target="tpu_custom_call" | custom-call | flops 40000000 | bytes 1000000 | tf_op jit(solution)/shard_map/pallas_call | solution.py:380
  30.7 0.1 collective-permute-start.11
  30.8 1.6 %collective-permute-start.12 = (f32[64,256]{1,0:T(8,128)S(1)}, f32[64,256]{1,0:T(8,128)S(1)}, u32[]{:S(2)}, u32[]{:S(2)}) collective-permute-start(f32[64,256]{1,0:T(8,128)S(1)} %get-tuple-element.37.y_ref), channel_id=1, source_target_pairs={{0,2},{2,0},{1,3},{3,1},{4,6},{6,4},{5,7},{7,5},{8,10},{10,8},{9,1... | collective-permute-start | bytes 196616 | tf_op jit(solution)/shard_map/ppermute | solution.py:287
  32.4 2.9 %collective-permute-done.12.z_ref = f32[64,256]{1,0:T(8,128)S(1)} collective-permute-done((f32[64,256]{1,0:T(8,128)S(1)}, f32[64,256]{1,0:T(8,128)S(1)}, u32[]{:S(2)}, u32[]{:S(2)}) %collective-permute-start.12) | collective-permute-done | bytes 65568 | tf_op jit(solution)/shard_map/ppermute | solution.py:287
  35.3 0.2 shard_map.99
  35.6 0.6 %collective-permute-start.13 = (f32[32,128]{1,0:T(8,128)S(1)}, f32[32,128]{1,0:T(8,128)S(1)}, u32[]{:S(2)}, u32[]{:S(2)}) collective-permute-start(f32[32,128]{1,0:T(8,128)S(1)} %get-tuple-element.38.own_ref), channel_id=1, source_target_pairs={{0,8},{1,13},{4,12},{5,9},{8,0},{9,5},{12,4},{13,1},{2,10},{3,15},... | collective-permute-start | bytes 49160 | tf_op jit(solution)/shard_map/ppermute | solution.py:339
  36.2 1.1 %collective-permute-start.15 = (f32[16,128]{1,0:T(8,128)S(1)}, f32[16,128]{1,0:T(8,128)S(1)}, u32[]{:S(2)}, u32[]{:S(2)}) collective-permute-start(f32[16,128]{1,0:T(8,128)S(1)} %get-tuple-element.41), channel_id=1, source_target_pairs={{0,4},{1,5},{4,0},{5,1},{8,12},{9,13},{12,8},{13,9},{2,6},{3,7},{6... | collective-permute-start | bytes 24584 | tf_op jit(solution)/shard_map/ppermute | solution.py:339
  37.3 3.0 %collective-permute-done.13.refs_0_ = f32[32,128]{1,0:T(8,128)S(1)} collective-permute-done((f32[32,128]{1,0:T(8,128)S(1)}, f32[32,128]{1,0:T(8,128)S(1)}, u32[]{:S(2)}, u32[]{:S(2)}) %collective-permute-start.13) | collective-permute-done | bytes 16416 | tf_op jit(solution)/shard_map/ppermute | solution.py:339
  40.3 0.5 %collective-permute-start.16 = (f32[16,128]{1,0:T(8,128)S(1)}, f32[16,128]{1,0:T(8,128)S(1)}, u32[]{:S(2)}, u32[]{:S(2)}) collective-permute-start(f32[16,128]{1,0:T(8,128)S(1)} %collective-permute-done.15.refs_2_), channel_id=1, source_target_pairs={{0,1},{1,0},{2,3},{3,2},{4,5},{5,4},{6,7},{7,6},{8,9},{9,8},{10,11... | collective-permute-start | bytes 24584 | tf_op jit(solution)/shard_map/ppermute | solution.py:342
  40.8 0.8 %collective-permute-done.16.refs_3_ = f32[16,128]{1,0:T(8,128)S(1)} collective-permute-done((f32[16,128]{1,0:T(8,128)S(1)}, f32[16,128]{1,0:T(8,128)S(1)}, u32[]{:S(2)}, u32[]{:S(2)}) %collective-permute-start.16) | collective-permute-done | bytes 8224 | tf_op jit(solution)/shard_map/ppermute | solution.py:342
  41.6 2.0 %shard_map.100 = (f32[64,256]{1,0:T(8,128)}, f32[64,64]{1,0:T(8,128)}, f32[64,64]{1,0:T(8,128)}) custom-call(f32[32,128]{1,0:T(8,128)S(1)} %get-tuple-element.38.own_ref, f32[64,256]{1,0:T(8,128)S(1)} %get-tuple-element.39.images_ref, f32[64,64]{1,0:T(8,128)S(1)} %get-tuple-element.40.d_ref, f32[32,128]{1,0:T(8,128)S(1)} %collective-permute-done.13.refs_0_, ...), custom_call_target="tpu_custom_call" | custom-call | flops 40000000 | bytes 1000000 | tf_op jit(solution)/shard_map/pallas_call | solution.py:390
  (9 shorter events, 0.0 us)
Async XLA Ops:
  0.6 1.9 %collective-permute-start.1 = (bf16[2,256,256]{2,1,0:T(8,128)(2,1)}, bf16[2,256,256]{2,1,0:T(8,128)(2,1)S(1)}, u32[]{:S(2)}, u32[]{:S(2)}) collective-permute-start(bf16[2,256,256]{2,1,0:T(8,128)(2,1)} %t_hbm.1), channel_id=1, source_target_pairs={{0,1},{1,0},{2,3},{3,2},{4,5},{5,4},{6,7},{7,6},{8,9},{9,8},{10,11... | collective-permute-start | bytes 786440 | tf_op jit(solution)/shard_map/ppermute | solution.py:311
  1.2 1.4 %collective-permute-start = (s32[2,2]{1,0:T(2,128)}, s32[2,2]{1,0:T(2,128)S(1)}, u32[]{:S(2)}, u32[]{:S(2)}) collective-permute-start(s32[2,2]{1,0:T(2,128)} %i_hbm.1), channel_id=1, source_target_pairs={{0,1},{1,0},{2,3},{3,2},{4,5},{5,4},{6,7},{7,6},{8,9},{9,8},{10,11... | collective-permute-start | bytes 56 | tf_op jit(solution)/shard_map/ppermute | solution.py:312
  2.8 9.5 %collective-permute-start.2 = (bf16[192,256]{1,0:T(8,128)(2,1)S(1)}, bf16[192,256]{1,0:T(8,128)(2,1)S(1)}, u32[]{:S(2)}, u32[]{:S(2)}) collective-permute-start(bf16[192,256]{1,0:T(8,128)(2,1)S(1)} %get-tuple-element.31), channel_id=1, source_target_pairs={{0,8},{1,13},{4,12},{5,9},{8,0},{9,5},{12,4},{13,1},{2,10},{3,15},... | collective-permute-start | bytes 294920 | tf_op jit(solution)/shard_map/ppermute | solution.py:339
  6.9 5.9 %collective-permute-start.4 = (bf16[320,128]{1,0:T(8,128)(2,1)S(1)}, bf16[320,128]{1,0:T(8,128)(2,1)S(1)}, u32[]{:S(2)}, u32[]{:S(2)}) collective-permute-start(bf16[320,128]{1,0:T(8,128)(2,1)S(1)} %get-tuple-element.32), channel_id=1, source_target_pairs={{0,4},{1,5},{4,0},{5,1},{8,12},{9,13},{12,8},{13,9},{2,6},{3,7},{6... | collective-permute-start | bytes 245768 | tf_op jit(solution)/shard_map/ppermute | solution.py:339
  12.3 1.8 %collective-permute-start.3 = (bf16[192,256]{1,0:T(8,128)(2,1)S(1)}, bf16[192,256]{1,0:T(8,128)(2,1)S(1)}, u32[]{:S(2)}, u32[]{:S(2)}) collective-permute-start(bf16[192,256]{1,0:T(8,128)(2,1)S(1)} %collective-permute-done.2.refs_0_), channel_id=1, source_target_pairs={{0,1},{1,0},{2,3},{3,2},{4,5},{5,4},{6,7},{7,6},{8,9},{9,8},{10,11... | collective-permute-start | bytes 294920 | tf_op jit(solution)/shard_map/ppermute | solution.py:342
  12.8 1.3 %collective-permute-start.5 = (bf16[320,128]{1,0:T(8,128)(2,1)S(1)}, bf16[320,128]{1,0:T(8,128)(2,1)S(1)}, u32[]{:S(2)}, u32[]{:S(2)}) collective-permute-start(bf16[320,128]{1,0:T(8,128)(2,1)S(1)} %collective-permute-done.4.refs_2_), channel_id=1, source_target_pairs={{0,1},{1,0},{2,3},{3,2},{4,5},{5,4},{6,7},{7,6},{8,9},{9,8},{10,11... | collective-permute-start | bytes 245768 | tf_op jit(solution)/shard_map/ppermute | solution.py:342
  14.7 6.1 %collective-permute-start.6 = (f32[112,256]{1,0:T(8,128)S(1)}, f32[112,256]{1,0:T(8,128)S(1)}, u32[]{:S(2)}, u32[]{:S(2)}) collective-permute-start(f32[112,256]{1,0:T(8,128)S(1)} %get-tuple-element.33.mine_ref), channel_id=1, source_target_pairs={{0,2},{2,0},{1,3},{3,1},{4,6},{6,4},{5,7},{7,5},{8,10},{10,8},{9,1... | collective-permute-start | bytes 344072 | tf_op jit(solution)/shard_map/ppermute | solution.py:287
  16.4 8.8 %collective-permute-start.7 = (bf16[320,256]{1,0:T(8,128)(2,1)S(1)}, bf16[320,256]{1,0:T(8,128)(2,1)S(1)}, u32[]{:S(2)}, u32[]{:S(2)}) collective-permute-start(bf16[320,256]{1,0:T(8,128)(2,1)S(1)} %get-tuple-element.26.high_ref), channel_id=1, source_target_pairs={{0,2},{2,0},{1,3},{3,1},{4,6},{6,4},{5,7},{7,5},{8,10},{10,8},{9,1... | collective-permute-start | bytes 491528 | tf_op jit(solution)/shard_map/ppermute | solution.py:287
  20.8 4.9 %collective-permute-start.10 = (bf16[128,256]{1,0:T(8,128)(2,1)S(1)}, bf16[128,256]{1,0:T(8,128)(2,1)S(1)}, u32[]{:S(2)}, u32[]{:S(2)}) collective-permute-start(bf16[128,256]{1,0:T(8,128)(2,1)S(1)} %get-tuple-element.35), channel_id=1, source_target_pairs={{0,4},{4,0},{8,12},{12,8},{1,5},{5,1},{9,13},{13,9},{2,6},{6,2},{1... | collective-permute-start | bytes 196616 | tf_op jit(solution)/shard_map/ppermute | solution.py:287
  22.3 6.6 %collective-permute-start.8 = (bf16[128,256]{1,0:T(8,128)(2,1)S(1)}, bf16[128,256]{1,0:T(8,128)(2,1)S(1)}, u32[]{:S(2)}, u32[]{:S(2)}) collective-permute-start(bf16[128,256]{1,0:T(8,128)(2,1)S(1)} %get-tuple-element.35), channel_id=1, source_target_pairs={{0,8},{4,12},{8,0},{12,4},{1,9},{5,13},{9,1},{13,5},{2,10},{6,14},... | collective-permute-start | bytes 196616 | tf_op jit(solution)/shard_map/ppermute | solution.py:287
  24.2 6.1 %collective-permute-start.9 = (bf16[128,256]{1,0:T(8,128)(2,1)S(1)}, bf16[128,256]{1,0:T(8,128)(2,1)S(1)}, u32[]{:S(2)}, u32[]{:S(2)}) collective-permute-start(bf16[128,256]{1,0:T(8,128)(2,1)S(1)} %get-tuple-element.35), channel_id=1, source_target_pairs={{0,12},{4,8},{8,4},{12,0},{1,13},{5,9},{9,5},{13,1},{2,14},{6,10},... | collective-permute-start | bytes 196616 | tf_op jit(solution)/shard_map/ppermute | solution.py:287
  30.7 4.6 %collective-permute-start.11 = (f32[192,256]{1,0:T(8,128)S(1)}, f32[192,256]{1,0:T(8,128)S(1)}, u32[]{:S(2)}, u32[]{:S(2)}) collective-permute-start(f32[192,256]{1,0:T(8,128)S(1)} %get-tuple-element.36.mine_ref), channel_id=1, source_target_pairs={{0,1},{1,0},{2,3},{3,2},{4,5},{5,4},{6,7},{7,6},{8,9},{9,8},{10,11... | collective-permute-start | bytes 589832 | tf_op jit(solution)/shard_map/ppermute | solution.py:385
  30.8 4.5 %collective-permute-start.12 = (f32[64,256]{1,0:T(8,128)S(1)}, f32[64,256]{1,0:T(8,128)S(1)}, u32[]{:S(2)}, u32[]{:S(2)}) collective-permute-start(f32[64,256]{1,0:T(8,128)S(1)} %get-tuple-element.37.y_ref), channel_id=1, source_target_pairs={{0,2},{2,0},{1,3},{3,1},{4,6},{6,4},{5,7},{7,5},{8,10},{10,8},{9,1... | collective-permute-start | bytes 196616 | tf_op jit(solution)/shard_map/ppermute | solution.py:287
  35.6 4.7 %collective-permute-start.13 = (f32[32,128]{1,0:T(8,128)S(1)}, f32[32,128]{1,0:T(8,128)S(1)}, u32[]{:S(2)}, u32[]{:S(2)}) collective-permute-start(f32[32,128]{1,0:T(8,128)S(1)} %get-tuple-element.38.own_ref), channel_id=1, source_target_pairs={{0,8},{1,13},{4,12},{5,9},{8,0},{9,5},{12,4},{13,1},{2,10},{3,15},... | collective-permute-start | bytes 49160 | tf_op jit(solution)/shard_map/ppermute | solution.py:339
  36.2 4.1 %collective-permute-start.15 = (f32[16,128]{1,0:T(8,128)S(1)}, f32[16,128]{1,0:T(8,128)S(1)}, u32[]{:S(2)}, u32[]{:S(2)}) collective-permute-start(f32[16,128]{1,0:T(8,128)S(1)} %get-tuple-element.41), channel_id=1, source_target_pairs={{0,4},{1,5},{4,0},{5,1},{8,12},{9,13},{12,8},{13,9},{2,6},{3,7},{6... | collective-permute-start | bytes 24584 | tf_op jit(solution)/shard_map/ppermute | solution.py:339
  40.3 1.3 %collective-permute-start.14 = (f32[32,128]{1,0:T(8,128)S(1)}, f32[32,128]{1,0:T(8,128)S(1)}, u32[]{:S(2)}, u32[]{:S(2)}) collective-permute-start(f32[32,128]{1,0:T(8,128)S(1)} %collective-permute-done.13.refs_0_), channel_id=1, source_target_pairs={{0,1},{1,0},{2,3},{3,2},{4,5},{5,4},{6,7},{7,6},{8,9},{9,8},{10,11... | collective-permute-start | bytes 49160 | tf_op jit(solution)/shard_map/ppermute | solution.py:342
  40.3 1.3 %collective-permute-start.16 = (f32[16,128]{1,0:T(8,128)S(1)}, f32[16,128]{1,0:T(8,128)S(1)}, u32[]{:S(2)}, u32[]{:S(2)}) collective-permute-start(f32[16,128]{1,0:T(8,128)S(1)} %collective-permute-done.15.refs_2_), channel_id=1, source_target_pairs={{0,1},{1,0},{2,3},{3,2},{4,5},{5,4},{6,7},{7,6},{8,9},{9,8},{10,11... | collective-permute-start | bytes 24584 | tf_op jit(solution)/shard_map/ppermute | solution.py:342
